TPU v7x, 32 devices: a whole 2x2x4 slice. The times are simulated.
32 devices in a mesh: dp: 8 (over z, y), fsdp: 4 (over x, core).
Axes of the slice: x: 2, y: 2, z: 4, core: 2. Of those that a mesh axis runs over, the one named last changes fastest.
Arguments:
- states: bfloat16 [20480, 1280], P(('dp', 'fsdp')), may hold values from -0.1796875 to 0.1796875
- teacher: float32 [20480, 1280], P(('dp', 'fsdp')), may hold values from -0.18 to 0.18
- parent_ids: int32 [160], P('dp'), may hold values from -1 to 159, as said below
- valid_mask: int32 [20480], P(('dp', 'fsdp')), may hold values from 0 to 1, as said below
- w_query: bfloat16 [1280, 1280], P(('dp', 'fsdp')), may hold values from -0.15625 to 0.15625
- w_key: bfloat16 [1280, 1280], P(('dp', 'fsdp')), may hold values from -0.15625 to 0.15625
- w_value: bfloat16 [1280, 1280], P(('dp', 'fsdp')), may hold values from -0.15625 to 0.15625
- w_out: bfloat16 [1280, 1280], P(('dp', 'fsdp')), may hold values from -0.15625 to 0.15625
- w_up: bfloat16 [1280, 5120], P(('dp', 'fsdp')), may hold values from -0.15625 to 0.15625
- w_gate: bfloat16 [1280, 5120], P(('dp', 'fsdp')), may hold values from -0.15625 to 0.15625
- w_down: bfloat16 [5120, 1280], P(('dp', 'fsdp')), may hold values from -0.078125 to 0.078125
- qk_scale: bfloat16 [1280], P(('dp', 'fsdp')), may hold values from 0.69921875 to 1.5
- attn_rate: bfloat16 [1280], P(('dp', 'fsdp')), may hold values from 0.099609375 to 0.59765625
- mlp_rate: bfloat16 [1280], P(('dp', 'fsdp')), may hold values from 0.099609375 to 0.59765625
- up_scale: bfloat16 [5120], P(('dp', 'fsdp')), may hold values from 0.5 to 2
- gate_scale: bfloat16 [5120], P(('dp', 'fsdp')), may hold values from 0.5 to 2
Outputs:
- out_states: bfloat16 [20480, 1280], P(('dp', 'fsdp'))
- loss: float32 [], replicated
- grad_states: float32 [20480, 1280], P(('dp', 'fsdp'))
- grad_query: float32 [1280, 1280], P(('dp', 'fsdp'))
- grad_key: float32 [1280, 1280], P(('dp', 'fsdp'))
- grad_value: float32 [1280, 1280], P(('dp', 'fsdp'))
- grad_out: float32 [1280, 1280], P(('dp', 'fsdp'))
- grad_up: float32 [1280, 5120], P(('dp', 'fsdp'))
- grad_gate: float32 [1280, 5120], P(('dp', 'fsdp'))
- grad_down: float32 [5120, 1280], P(('dp', 'fsdp'))
- grad_qk_scale: float32 [1280], P(('dp', 'fsdp'))
- grad_attn_rate: float32 [1280], P(('dp', 'fsdp'))
- grad_mlp_rate: float32 [1280], P(('dp', 'fsdp'))
- grad_up_scale: float32 [5120], P(('dp', 'fsdp'))
- grad_gate_scale: float32 [5120], P(('dp', 'fsdp'))
Inputs may be any that keep to these rules, and one draw needn't show every extreme that they name: `parent_ids`: the blocks form runs of 20 in order; a parent is a block of the same run. Each run holds 1 trees of 20 blocks placed at random: a chain of 8 trunk blocks, four branch blocks whose parent is the trunk's last, and two leaf blocks under each branch; every other block has no parent. `valid_mask`: 1 on a leading part of each block, never empty, 0 after it.
All inputs are finite; a program needn't handle non-finite values.
Results may differ from a plain program's by a relative error of at most 0.017.
Values may be sent and summed in bfloat16 or wider, within the bound.
A program may use at most 576 MiB of HBM per device.

v0:
```python
import math

import jax
import jax.numpy as jnp
from jax import lax
from jax.sharding import PartitionSpec as P

D = 1280
HEADS = 20
HEAD_DIM = 64
FF = 5120
BLOCK = 128
DEPTH = 10


EPS = 1e-06


def unit_rows(vector):
    inverse = lax.rsqrt(jnp.sum(vector * vector, axis=-1, keepdims=True) + EPS)
    return (vector * inverse, inverse)


def unit_back(grad, unit, inverse):
    return (grad - unit * jnp.sum(grad * unit, axis=-1, keepdims=True)) * inverse


def project(left, right):
    return jnp.dot(left, right, preferred_element_type=jnp.float32)


def project_back(grad, weight):
    return jnp.einsum("te,de->td", grad, weight, preferred_element_type=jnp.float32)


def ancestors(local_parent):
    column = jnp.arange(local_parent.shape[0], dtype=jnp.int32)
    columns = [column]
    for depth_step in range(DEPTH - 1):
        column = jnp.where(column >= 0, local_parent[jnp.maximum(column, 0)], -1)
        columns.append(column)
    return jnp.stack(columns, axis=1)


def head_back(grad_flat, unit, inverse, scale):
    scaled = (grad_flat * scale).reshape(unit.shape)
    raw = unit_back(scaled, unit, inverse).reshape(grad_flat.shape)
    scale_grad = jnp.sum(grad_flat * unit.reshape(grad_flat.shape), axis=0)
    return (raw, scale_grad)


def local(
    states,
    teacher,
    parent_ids,
    valid_mask,
    w_query,
    w_key,
    w_value,
    w_out,
    w_up,
    w_gate,
    w_down,
    qk_scale,
    attn_rate,
    mlp_rate,
    up_scale,
    gate_scale,
):
    rows_dev = states.shape[0]
    blocks_dev = rows_dev // BLOCK
    width_rows = w_query.shape[0]
    span = DEPTH * BLOCK
    factor = math.sqrt(HEAD_DIM)
    root_width = math.sqrt(D)
    mask_f = valid_mask.astype(jnp.float32)
    qkv_local = jnp.concatenate((w_query, w_key, w_value), axis=1)
    scal_width_local = jnp.stack((qk_scale, attn_rate, mlp_rate), axis=1)
    piece_qkv = lax.all_gather(qkv_local, ("dp", "fsdp"), axis=0, tiled=True)
    piece_out = lax.all_gather(w_out, ("dp", "fsdp"), axis=0, tiled=True)
    piece_scal = lax.all_gather(scal_width_local, ("dp", "fsdp"), axis=0, tiled=True)
    lefts = states
    total = jnp.dot(lefts, piece_qkv, preferred_element_type=jnp.float32)
    scal_whole = piece_scal
    qkv_raw = total
    scal_width = scal_whole
    scale_qk = scal_width[:, 0].astype(jnp.float32)
    rate_attn = scal_width[:, 1].astype(jnp.float32)
    rate_mlp = scal_width[:, 2].astype(jnp.float32)
    query_raw = qkv_raw[:, :D]
    key_raw = qkv_raw[:, D : 2 * D]
    values = qkv_raw[:, 2 * D :].astype(jnp.bfloat16)
    query_unit, query_inv = unit_rows(query_raw.reshape(rows_dev, HEADS, HEAD_DIM))
    key_unit, key_inv = unit_rows(key_raw.reshape(rows_dev, HEADS, HEAD_DIM))
    query_n = (query_unit.reshape(rows_dev, D) * scale_qk).astype(jnp.bfloat16)
    key_n = (key_unit.reshape(rows_dev, D) * scale_qk).astype(jnp.bfloat16)
    key_group, value_group = (
        lax.all_gather(key_n, "fsdp", axis=0, tiled=True),
        lax.all_gather(values, "fsdp", axis=0, tiled=True),
    )
    group_blocks = parent_ids.shape[0]
    group_base = lax.axis_index("dp") * group_blocks
    local_parent = jnp.where(parent_ids >= 0, parent_ids - group_base, -1)
    paths_all = ancestors(local_parent)
    own_first = lax.axis_index("fsdp") * blocks_dev
    paths = lax.dynamic_slice_in_dim(paths_all, own_first, blocks_dev, 0)
    safe_paths = jnp.maximum(paths, 0)
    key_rows = key_group.reshape(group_blocks, BLOCK, D)[safe_paths].reshape(
        blocks_dev, span, HEADS, HEAD_DIM
    )
    value_rows = value_group.reshape(group_blocks, BLOCK, D)[safe_paths].reshape(
        blocks_dev, span, HEADS, HEAD_DIM
    )
    slot_of = jnp.arange(span, dtype=jnp.int32) // BLOCK
    offset = jnp.arange(span, dtype=jnp.int32) % BLOCK
    row_pos = jnp.arange(BLOCK, dtype=jnp.int32)
    causal = offset[None, :] <= row_pos[:, None]
    is_live = jnp.take(paths, slot_of, axis=1) >= 0
    allowed = jnp.where(slot_of[None, None, :] == 0, causal[None], is_live[:, None, :])[:, None]
    query_heads = query_n.reshape(blocks_dev, BLOCK, HEADS, HEAD_DIM)
    scores = factor * jnp.einsum(
        "bqhd,bkhd->bhqk", query_heads, key_rows, preferred_element_type=jnp.float32
    )
    scores = jnp.where(allowed, scores, jnp.float32(-1e30))
    row_max = jnp.max(scores, axis=-1, keepdims=True)
    powers = jnp.exp(scores - row_max)
    row_sum = jnp.sum(powers, axis=-1, keepdims=True)
    probs_b = (powers / row_sum).astype(jnp.bfloat16)
    log_total = row_max + jnp.log(row_sum)
    mixed = jnp.einsum("bhqk,bkhd->bqhd", probs_b, value_rows, preferred_element_type=jnp.float32)
    mixed = mixed.reshape(rows_dev, D).astype(jnp.bfloat16)
    inputs = states.astype(jnp.float32)
    attn = project(mixed, piece_out)
    attn_unit, attn_inv = unit_rows(attn)
    hidden, hidden_inv = unit_rows(inputs + rate_attn * (attn_unit - inputs))
    hidden_b = hidden.astype(jnp.bfloat16)
    ffn_local = jnp.concatenate((w_up, w_gate), axis=1)
    scal_hidden_local = jnp.concatenate(
        (up_scale.reshape(width_rows, 4), gate_scale.reshape(width_rows, 4)), axis=1
    )
    piece_ffn = lax.all_gather(ffn_local, ("dp", "fsdp"), axis=0, tiled=True)
    piece_scal = lax.all_gather(scal_hidden_local, ("dp", "fsdp"), axis=0, tiled=True)
    lefts = hidden_b
    total = jnp.dot(lefts, piece_ffn, preferred_element_type=jnp.float32)
    scal_whole = piece_scal
    scale_up = scal_whole[:, :4].reshape(FF).astype(jnp.float32)
    scale_gate = scal_whole[:, 4:].reshape(FF).astype(jnp.float32)
    up_proj = total[:, :FF]
    gate_proj = total[:, FF:]
    upscaled = up_proj * scale_up
    gated = gate_proj * scale_gate * root_width
    sigmoid_gate = jax.nn.sigmoid(gated)
    act = (upscaled * (gated * sigmoid_gate)).astype(jnp.bfloat16)
    lefts = act
    down = jnp.dot(
        lefts,
        lax.all_gather(w_down, ("dp", "fsdp"), axis=0, tiled=True),
        preferred_element_type=jnp.float32,
    )
    down_unit, down_inv = unit_rows(down)
    result, result_inv = unit_rows(hidden + rate_mlp * (down_unit - hidden))
    loss_local = jnp.sum(mask_f[:, None] * (result - teacher) ** 2)
    valid_count, loss_sum = lax.psum((jnp.sum(mask_f), loss_local), ("dp", "fsdp"))
    loss = loss_sum / valid_count
    g_result = 2.0 * mask_f[:, None] * (result - teacher) / valid_count
    g_last = unit_back(g_result, result, result_inv)
    g_hidden = g_last * (1.0 - rate_mlp)
    g_rate_mlp = jnp.sum(g_last * (down_unit - hidden), axis=0)
    g_down = unit_back(g_last * rate_mlp, down_unit, down_inv).astype(jnp.bfloat16)
    g_act = jnp.einsum(
        "te,fe->tf",
        g_down,
        lax.all_gather(w_down, ("dp", "fsdp"), axis=0, tiled=True),
        preferred_element_type=jnp.float32,
    )
    g_upscaled = g_act * (gated * sigmoid_gate)
    g_gated = g_act * upscaled * sigmoid_gate * (1.0 + gated * (1.0 - sigmoid_gate))
    grad_up_scale = jnp.sum(g_upscaled * up_proj, axis=0)
    grad_gate_scale = jnp.sum(g_gated * gate_proj * root_width, axis=0)
    g_up = (g_upscaled * scale_up).astype(jnp.bfloat16)
    g_gate = (g_gated * scale_gate * root_width).astype(jnp.bfloat16)
    g_both = jnp.concatenate((g_up, g_gate), axis=1)
    g_hidden = g_hidden + jnp.einsum(
        "tc,dc->td",
        g_both,
        lax.all_gather(ffn_local, ("dp", "fsdp"), axis=0, tiled=True),
        preferred_element_type=jnp.float32,
    )
    scal_terms = jnp.concatenate(
        (grad_up_scale.reshape(D, 4), grad_gate_scale.reshape(D, 4)), axis=1
    )
    lefts = hidden_b
    main = jnp.einsum("td,tc->dc", lefts, g_both, preferred_element_type=jnp.float32)
    ffn_share = lax.psum_scatter(
        jnp.concatenate((main, scal_terms), axis=1), ("dp", "fsdp"), scatter_dimension=0, tiled=True
    )
    lefts = act
    grad_down = lax.psum_scatter(
        jnp.einsum("tf,te->fe", lefts, g_down, preferred_element_type=jnp.float32),
        ("dp", "fsdp"),
        scatter_dimension=0,
        tiled=True,
    )
    g_pre = unit_back(g_hidden, hidden, hidden_inv)
    g_states = g_pre * (1.0 - rate_attn)
    g_rate_attn = jnp.sum(g_pre * (attn_unit - inputs), axis=0)
    g_attn = unit_back(g_pre * rate_attn, attn_unit, attn_inv).astype(jnp.bfloat16)
    g_mixed = project_back(g_attn, piece_out).astype(jnp.bfloat16)
    scores = factor * jnp.einsum(
        "bqhd,bkhd->bhqk", query_heads, key_rows, preferred_element_type=jnp.float32
    )
    probs = jnp.where(allowed, jnp.exp(scores - log_total), jnp.float32(0.0))
    probs_again = probs.astype(jnp.bfloat16)
    g_heads = g_mixed.reshape(blocks_dev, BLOCK, HEADS, HEAD_DIM)
    g_probs = jnp.einsum("bqhd,bkhd->bhqk", g_heads, value_rows, preferred_element_type=jnp.float32)
    delta = jnp.sum(probs * g_probs, axis=-1, keepdims=True)
    g_scores = (probs * (g_probs - delta)).astype(jnp.bfloat16)
    g_query_n = factor * jnp.einsum(
        "bhqk,bkhd->bqhd", g_scores, key_rows, preferred_element_type=jnp.float32
    )
    g_key_rows = factor * jnp.einsum(
        "bhqk,bqhd->bkhd", g_scores, query_heads, preferred_element_type=jnp.float32
    )
    g_value_rows = jnp.einsum(
        "bhqk,bqhd->bkhd", probs_again, g_heads, preferred_element_type=jnp.float32
    )
    flat_paths = safe_paths.reshape(blocks_dev * DEPTH)
    g_key_group = (
        jnp.zeros((group_blocks, BLOCK, D), jnp.float32)
        .at[flat_paths]
        .add(g_key_rows.reshape(blocks_dev * DEPTH, BLOCK, D))
    )
    g_value_group = (
        jnp.zeros((group_blocks, BLOCK, D), jnp.float32)
        .at[flat_paths]
        .add(g_value_rows.reshape(blocks_dev * DEPTH, BLOCK, D))
    )
    g_key_n, g_values = (
        lax.psum_scatter(
            g_key_group.reshape(group_blocks * BLOCK, D).astype(jnp.bfloat16),
            "fsdp",
            scatter_dimension=0,
            tiled=True,
        ).astype(jnp.float32),
        lax.psum_scatter(
            g_value_group.reshape(group_blocks * BLOCK, D).astype(jnp.bfloat16),
            "fsdp",
            scatter_dimension=0,
            tiled=True,
        ).astype(jnp.float32),
    )
    g_query_raw, scale_from_query = head_back(
        g_query_n.reshape(rows_dev, D), query_unit, query_inv, scale_qk
    )
    g_key_raw, scale_from_key = head_back(g_key_n, key_unit, key_inv, scale_qk)
    grad_qk_scale = scale_from_query + scale_from_key
    g_qkv = jnp.concatenate(
        (
            g_query_raw.astype(jnp.bfloat16),
            g_key_raw.astype(jnp.bfloat16),
            g_values.astype(jnp.bfloat16),
        ),
        axis=1,
    )
    g_states = g_states + jnp.einsum(
        "tc,dc->td",
        g_qkv,
        lax.all_gather(qkv_local, ("dp", "fsdp"), axis=0, tiled=True),
        preferred_element_type=jnp.float32,
    )
    vector_terms = jnp.stack((grad_qk_scale, g_rate_attn, g_rate_mlp), axis=1)
    lefts = states
    main = jnp.einsum("td,tc->dc", lefts, g_qkv, preferred_element_type=jnp.float32)
    outer = jnp.einsum("td,tc->dc", mixed, g_attn, preferred_element_type=jnp.float32)
    attn_share = lax.psum_scatter(
        jnp.concatenate((main, outer, vector_terms), axis=1),
        ("dp", "fsdp"),
        scatter_dimension=0,
        tiled=True,
    )
    return (
        result.astype(jnp.bfloat16),
        loss,
        g_states,
        attn_share[:, :D],
        attn_share[:, D : 2 * D],
        attn_share[:, 2 * D : 3 * D],
        attn_share[:, 3 * D : 4 * D],
        ffn_share[:, :FF],
        ffn_share[:, FF : 2 * FF],
        grad_down,
        attn_share[:, 4 * D],
        attn_share[:, 4 * D + 1],
        attn_share[:, 4 * D + 2],
        ffn_share[:, 2 * FF : 2 * FF + 4].reshape(-1),
        ffn_share[:, 2 * FF + 4 : 2 * FF + 8].reshape(-1),
    )


def solution(mesh):
    placed = (
        P(("dp", "fsdp"), None),
        P(("dp", "fsdp"), None),
        P("dp"),
        P(("dp", "fsdp")),
        P(("dp", "fsdp"), None),
        P(("dp", "fsdp"), None),
        P(("dp", "fsdp"), None),
        P(("dp", "fsdp"), None),
        P(("dp", "fsdp"), None),
        P(("dp", "fsdp"), None),
        P(("dp", "fsdp"), None),
        P(("dp", "fsdp")),
        P(("dp", "fsdp")),
        P(("dp", "fsdp")),
        P(("dp", "fsdp")),
        P(("dp", "fsdp")),
    )
    return jax.shard_map(
        local,
        mesh=mesh,
        in_specs=placed,
        out_specs=(
            P(("dp", "fsdp"), None),
            P(),
            P(("dp", "fsdp"), None),
            P(("dp", "fsdp"), None),
            P(("dp", "fsdp"), None),
            P(("dp", "fsdp"), None),
            P(("dp", "fsdp"), None),
            P(("dp", "fsdp"), None),
            P(("dp", "fsdp"), None),
            P(("dp", "fsdp"), None),
            P(("dp", "fsdp")),
            P(("dp", "fsdp")),
            P(("dp", "fsdp")),
            P(("dp", "fsdp")),
            P(("dp", "fsdp")),
        ),
        check_vma=False,
    )
```

profile of v0, /device:TPU:4, one launch (start us, length us, event | category | flops | bytes accessed | tf_op | source)
XLA Modules:
  0.0 2935.7 jit_solution(9725263483345402264)
XLA Ops:
  9.0 87.5 %all-gather.9.cloned.1.call-done = bf16[1280,3840]{1,0:T(8,128)(2,1)} async-done(((bf16[40,3840]{1,0:T(8,128)(2,1)}), bf16[1280,3840]{1,0:T(8,128)(2,1)}) %all-gather.9.cloned.1.call-update) | async-done | bytes 9830416 | tf_op jit(solution)/shard_map/all_gather | solution.py:79
  113.0 35.5 %all-gather = bf16[32,40,3]{1,2,0:T(4,128)(2,1)S(1)} all-gather(bf16[1,40,3]{1,2,0:T(4,128)(2,1)S(1)} %maximum_bitcast_fusion.1), channel_id=1, replica_groups=mesh['dp'=8,'fsdp'=4] {'dp','fsdp'}, dimensions={0}, use_global_device_ids=true | all-gather | bytes 7920 | tf_op jit(solution)/shard_map/all_gather | solution.py:81
  181.1 37.2 %all-gather.1 = bf16[32,40,8]{1,2,0:T(8,128)(2,1)S(1)} all-gather(bf16[1,40,8]{1,2,0:T(8,128)(2,1)S(1)} %maximum_bitcast_fusion), channel_id=1, replica_groups=mesh['dp'=8,'fsdp'=4] {'dp','fsdp'}, dimensions={0}, use_global_device_ids=true | all-gather | bytes 21120 | tf_op jit(solution)/shard_map/all_gather | solution.py:142
  220.9 42.3 %psum.15 = f32[]{:T(128)} all-reduce(f32[]{:T(128)} %get-tuple-element.167), channel_id=1, replica_groups=mesh['dp'=8,'fsdp'=4] {'dp','fsdp'}, use_global_device_ids=true, to_apply=%region_11.12 | all-reduce | flops 1 | bytes 8 | tf_op jit(solution)/shard_map/psum | solution.py:163
  289.0 46.2 %reshape.933 = bf16[5,1280,20,64]{3,2,1,0:T(8,128)(2,1)} reshape(bf16[50,128,1280]{2,1,0:T(8,128)(2,1)} %gather_fusion.9) | data formatting | bytes 32768000 | tf_op jit(solution)/shard_map/reshape | solution.py:111
  335.3 47.0 %copy.213 = bf16[5,1280,20,64]{1,3,2,0:T(8,128)(2,1)} copy(bf16[5,1280,20,64]{3,2,1,0:T(8,128)(2,1)} %reshape.933) | data formatting | bytes 32768000 | tf_op jit(solution)/shard_map/reshape | solution.py:111
  402.4 46.3 %reshape.934 = bf16[5,1280,20,64]{3,2,1,0:T(8,128)(2,1)} reshape(bf16[50,128,1280]{2,1,0:T(8,128)(2,1)} %gather_fusion.11) | data formatting | bytes 32768000 | tf_op jit(solution)/shard_map/reshape | solution.py:108
  448.7 46.7 %copy.212 = bf16[5,1280,20,64]{1,3,2,0:T(8,128)(2,1)} copy(bf16[5,1280,20,64]{3,2,1,0:T(8,128)(2,1)} %reshape.934) | data formatting | bytes 32768000 | tf_op jit(solution)/shard_map/reshape | solution.py:108
  546.9 31.6 %fusion.32 = bf16[5,128,20,64]{1,3,2,0:T(8,128)(2,1)} fusion(bf16[5,1280,20,64]{1,3,2,0:T(8,128)(2,1)} %copy.213, f32[5,20,128,1280]{3,2,1,0:T(8,128)} %get-tuple-element.169, f32[5,20,128]{2,1,0:T(8,128)S(1)} %fusion.1, f32[5,20,128]{2,1,0:T(8,128)S(1)} %get-tuple-element.168, pred[5,128,1280]{2,1,0:T(8,128)(4,1)S(1)} %broadcast_select_fusion), kind=kOutput, calls=%fused_computation.107 | convolution fusion | flops 2179891200 | bytes 84480000 | tf_op jit(solution)/shard_map/bhqk,bkhd->bqhd/dot_general | solution.py:130
  740.3 55.0 %multiply_reduce_fusion = (f32[5,20,128]{2,1,0:T(8,128)}, f32[5,20,128,1280]{3,2,1,0:T(8,128)}) fusion(f32[5,20,128,1280]{3,2,1,0:T(8,128)} %get-tuple-element.169, f32[5,20,128]{2,1,0:T(8,128)S(1)} %copy-done.32, pred[5,128,1280]{2,1,0:T(8,128)(4,1)S(1)} %copy-done.6, bf16[5,128,20,64]{1,3,2,0:T(8,128)(2,1)S(1)} %copy.221, bf16[5,1280,20,64]{1,3,2,0:T(8,128)(2,1)} %copy.213), kind=kOutput, calls=%fused_computation.16 | convolution fusion | flops 2179059200 | bytes 150016000 | tf_op jit(solution)/shard_map/bqhd,bkhd->bhqk/dot_general | solution.py:215
  795.2 52.9 %multiply_convert_fusion = bf16[5,20,128,1280]{3,2,1,0:T(8,128)(2,1)} fusion(f32[5,20,128,1280]{3,2,1,0:T(8,128)} %get-tuple-element.177, f32[5,20,128,1280]{3,2,1,0:T(8,128)} %get-tuple-element.169, f32[5,20,128]{2,1,0:T(8,128)} %get-tuple-element.176, f32[5,20,128]{2,1,0:T(8,128)S(1)} %copy-done.32, pred[5,128,1280]{2,1,0:T(8,128)(4,1)S(1)} %copy-done.6), kind=kLoop, calls=%fused_computation.15 | loop fusion | flops 98304000 | bytes 164761600 | tf_op jit(solution)/shard_map/convert_element_type | solution.py:217
  869.1 53.4 %copy.240 = f32[5,1280,20,64]{3,2,1,0:T(8,128)} copy(f32[5,1280,20,64]{1,3,2,0:T(8,128)} %multiply_bitcast_fusion) | data formatting | bytes 65536000 | tf_op jit(solution)/shard_map/reshape | solution.py:231
  922.5 57.4 %reshape.925 = f32[50,128,1280]{2,1,0:T(8,128)} reshape(f32[5,1280,20,64]{3,2,1,0:T(8,128)} %copy.240) | data formatting | bytes 65536000 | tf_op jit(solution)/shard_map/reshape | solution.py:231
  986.0 65.5 %scatter_fusion = f32[20,128,1280]{2,1,0:T(8,128)} fusion(f32[20,128,1280]{2,1,0:T(8,128)} %broadcast.941.clone.1, s32[50]{0:T(128)S(1)} %copy-done.55, f32[50,128,1280]{2,1,0:T(8,128)} %reshape.925), kind=kCustom, calls=%fused_computation.12 | custom fusion | flops 8192000 | bytes 98304200 | tf_op jit(solution)/shard_map/scatter-add | solution.py:231
  1061.1 38.7 %fusion.10 = f32[5,1280,20,64]{1,3,2,0:T(8,128)} fusion(bf16[5,128,20,64]{1,3,2,0:T(8,128)(2,1)S(1)} %copy-done.12, f32[5,20,128,1280]{3,2,1,0:T(8,128)} %get-tuple-element.169, f32[5,20,128]{2,1,0:T(8,128)S(1)} %copy-done.32, pred[5,128,1280]{2,1,0:T(8,128)(4,1)S(1)} %copy-done.6), kind=kOutput, calls=%fused_computation.30 | convolution fusion | flops 2162688000 | bytes 100812800 | tf_op jit(solution)/shard_map/bhqk,bqhd->bkhd/dot_general | solution.py:224
  1099.8 53.5 %copy.241 = f32[5,1280,20,64]{3,2,1,0:T(8,128)} copy(f32[5,1280,20,64]{1,3,2,0:T(8,128)} %fusion.10) | data formatting | bytes 65536000 | tf_op jit(solution)/shard_map/reshape | solution.py:236
  1153.3 57.4 %reshape.926 = f32[50,128,1280]{2,1,0:T(8,128)} reshape(f32[5,1280,20,64]{3,2,1,0:T(8,128)} %copy.241) | data formatting | bytes 65536000 | tf_op jit(solution)/shard_map/reshape | solution.py:236
  1216.8 65.4 %scatter_fusion.1 = f32[20,128,1280]{2,1,0:T(8,128)} fusion(f32[20,128,1280]{2,1,0:T(8,128)} %broadcast.941.clone, s32[50]{0:T(128)S(1)} %copy-done.55, f32[50,128,1280]{2,1,0:T(8,128)} %reshape.926), kind=kCustom, calls=%fused_computation.13 | custom fusion | flops 8192000 | bytes 98304200 | tf_op jit(solution)/shard_map/scatter-add | solution.py:236
  1328.8 31.7 %fusion.14 = f32[1280,10240]{1,0:T(8,128)} fusion(bf16[640,5120]{1,0:T(8,128)(2,1)} %multiply_convert_fusion.1, bf16[640,5120]{1,0:T(8,128)(2,1)} %get-tuple-element.148, f32[640,1280]{1,0:T(8,128)S(1)} %copy-done.1, f32[640]{0:T(1024)S(1)} %copy-done.23), kind=kOutput, calls=%fused_computation.43 | convolution fusion | flops 16805068800 | bytes 68815360 | tf_op jit(solution)/shard_map/td,tc->dc/dot_general | solution.py:193
  1360.5 55.9 %concatenate.27 = f32[1280,10248]{1,0:T(8,128)} concatenate(f32[1280,10240]{1,0:T(8,128)} %fusion.14, f32[1280,4]{1,0:T(8,128)} %reshape.794, f32[1280,4]{1,0:T(8,128)} %reshape.795), dimensions={1} | concatenate | bytes 104939520 | tf_op jit(solution)/shard_map/concatenate | solution.py:195
  1455.6 60.2 %concatenate.26 = f32[1280,5123]{0,1:T(8,128)} concatenate(f32[1280,3840]{0,1:T(8,128)} %convolution_bitcast_fusion, f32[1280,1280]{0,1:T(8,128)} %fusion.27, f32[1280,1]{0,1:T(1,128)S(1)} %add.198, f32[1280,1]{0,1:T(1,128)S(1)} %stack.40, f32[1280,1]{0,1:T(1,128)S(1)} %stack.41), dimensions={1} | concatenate | bytes 52459520 | tf_op jit(solution)/shard_map/concatenate | solution.py:276
  1534.9 48.0 %psum.14 = f32[]{:T(128)} all-reduce(f32[]{:T(128)} %get-tuple-element.114), channel_id=1, replica_groups=mesh['dp'=8,'fsdp'=4] {'dp','fsdp'}, use_global_device_ids=true, to_apply=%region_9.10 | all-reduce | flops 1 | bytes 8 | tf_op jit(solution)/shard_map/psum | solution.py:163
  1597.9 1048.7 %all-reduce.5.cloned.1.call-done = (f32[1280,5123]{0,1:T(8,128)}, f32[1280,10248]{1,0:T(8,128)}) async-done(((f32[1280,5123]{0,1:T(8,128)}, f32[1280,10248]{1,0:T(8,128)}), (f32[1280,5123]{0,1:T(8,128)}, f32[1280,10248]{1,0:T(8,128)})) %all-reduce.5.cloned.1.call-update) | async-done | bytes 78699536
  2659.9 267.4 %reduce-scatter.9.cloned.1.call-done = f32[160,1280]{1,0:T(8,128)} async-done(((f32[5120,1280]{1,0:T(8,128)}), f32[160,1280]{1,0:T(8,128)}) %reduce-scatter.9.cloned.1.call-update) | async-done | bytes 819216 | tf_op jit(solution)/shard_map/reduce_scatter | solution.py:198
  (314 shorter events, 486.4 us)
Async XLA Ops:
  7.2 89.4 %all-gather.9.cloned.1.call-start = ((), (), s32[]{:S(2)}) async-start(), calls=%async_computation.3 | async-start | bytes 10137600 | tf_op jit(solution)/shard_map/all_gather | solution.py:79
  9.0 259.4 %all-gather.11.cloned.1.call-start = ((), (), s32[]{:S(2)}) async-start(), calls=%async_computation.4 | async-start | bytes 8192000 | tf_op jit(solution)/shard_map/all_gather | solution.py:99
  112.9 269.4 %all-gather.13.cloned.1.call-start = ((), (), s32[]{:S(2)}) async-start(), calls=%async_computation.5 | async-start | bytes 8192000 | tf_op jit(solution)/shard_map/all_gather | solution.py:98
  149.2 113.9 %copy-start.35 = (f32[1280]{0:T(1024)}, f32[1280]{0:T(1024)S(1)}, u32[]{:S(2)}) copy-start(f32[1280]{0:T(1024)S(1)} %get-tuple-element.116) | copy-start | bytes 15364
  164.7 416.7 %all-gather.15.cloned.1.call-start = ((), (), s32[]{:S(2)}) async-start(), calls=%async_computation.6 | async-start | bytes 3379200 | tf_op jit(solution)/shard_map/all_gather | solution.py:80
  165.3 423.8 %all-gather.17.cloned.1.call-start = ((), (), s32[]{:S(2)}) async-start(), calls=%async_computation.7 | async-start | bytes 27033600 | tf_op jit(solution)/shard_map/all_gather | solution.py:141
  166.3 462.6 %all-gather.19.cloned.1.call-start = ((), (), s32[]{:S(2)}) async-start(), calls=%async_computation.8 | async-start | bytes 13516800 | tf_op jit(solution)/shard_map/all_gather | solution.py:157
  166.9 1256.4 %reduce-scatter.11.cloned.1.call-start = ((), (), s32[]{:S(2)}) async-start(), calls=%async_computation.10 | async-start | bytes 8192000
  264.6 282.3 %copy-start.5 = (pred[5,128,1280]{2,1,0:T(8,128)(4,1)}, pred[5,128,1280]{2,1,0:T(8,128)(4,1)S(1)}, u32[]{:S(2)}) copy-start(pred[5,128,1280]{2,1,0:T(8,128)(4,1)S(1)} %broadcast_select_fusion) | copy-start | bytes 2457604
  268.4 227.1 %copy-start.9 = (bf16[5,128,20,64]{1,0,3,2:T(8,128)(2,1)}, bf16[5,128,20,64]{1,0,3,2:T(8,128)(2,1)S(1)}, u32[]{:S(2)}) copy-start(bf16[5,128,20,64]{1,0,3,2:T(8,128)(2,1)S(1)} %reshape.781) | copy-start | bytes 4915204
  588.4 131.2 %copy-start = (f32[640,1280]{1,0:T(8,128)}, f32[640,1280]{1,0:T(8,128)S(1)}, u32[]{:S(2)}) copy-start(f32[640,1280]{1,0:T(8,128)S(1)} %get-tuple-element.127) | copy-start | bytes 9830404
  588.4 131.2 %copy-start.22 = (f32[640]{0:T(1024)}, f32[640]{0:T(1024)S(1)}, u32[]{:S(2)}) copy-start(f32[640]{0:T(1024)S(1)} %add_rsqrt_fusion.4) | copy-start | bytes 7684
  589.1 27.2 copy-start.40
  589.1 27.2 copy-start.43
  654.1 29.7 %copy-start.25 = (bf16[640,1280]{1,0:T(8,128)(2,1)}, bf16[640,1280]{1,0:T(8,128)(2,1)S(1)}, u32[]{:S(2)}) copy-start(bf16[640,1280]{1,0:T(8,128)(2,1)S(1)} %multiply_convert_fusion.5) | copy-start | bytes 4915204
  693.0 26.7 copy-start.38
  693.0 26.7 copy-start.45
  740.3 55.0 %copy-start.11 = (bf16[5,128,20,64]{1,3,2,0:T(8,128)(2,1)}, bf16[5,128,20,64]{1,3,2,0:T(8,128)(2,1)S(1)}, u32[]{:S(2)}) copy-start(bf16[5,128,20,64]{1,3,2,0:T(8,128)(2,1)S(1)} %copy.221) | copy-start | bytes 4915204
  795.2 52.9 %copy-start.10 = (bf16[5,128,20,64]{1,0,3,2:T(8,128)(2,1)S(1)}, bf16[5,128,20,64]{1,0,3,2:T(8,128)(2,1)}, u32[]{:S(2)}) copy-start(bf16[5,128,20,64]{1,0,3,2:T(8,128)(2,1)} %copy-done.9) | copy-start | bytes 4915204
  1059.7 376.7 %reduce-scatter.13.cloned.1.call-start = ((), (), s32[]{:S(2)}) async-start(), calls=%async_computation.11 | async-start | bytes 8192000
  1290.5 1356.1 %all-reduce.5.cloned.1.call-start = ((), (), s32[]{:S(2)}) async-start(), calls=%async_computation.12 | async-start | bytes 158679040
  1360.5 55.9 %copy-start.21 = (bf16[5,128,20,64]{1,0,3,2:T(8,128)(2,1)S(1)}, bf16[5,128,20,64]{1,0,3,2:T(8,128)(2,1)}, u32[]{:S(2)}) copy-start(bf16[5,128,20,64]{1,0,3,2:T(8,128)(2,1)} %copy-done.20) | copy-start | bytes 4915204
  1515.8 1411.5 %reduce-scatter.9.cloned.1.call-start = ((), (), s32[]{:S(2)}) async-start(), calls=%async_computation.9 | async-start | bytes 27033600 | tf_op jit(solution)/shard_map/reduce_scatter | solution.py:198
  1534.2 50.0 %copy-start.15 = (f32[640,1280]{1,0:T(8,128)S(1)}, f32[640,1280]{1,0:T(8,128)}, u32[]{:S(2)}) copy-start(f32[640,1280]{1,0:T(8,128)} %copy-done.14) | copy-start | bytes 9830404
  (51 other events, 235.2 us)
Sparse Core Ops, SparseCore 0:
  11.5 85.0 all-gather.8
  113.0 46.5 all-gather.10
  164.8 48.0 all-gather.12
  215.6 59.4 all-gather.14
  278.4 158.5 all-gather.16
  439.7 96.6 all-gather.18
  1059.9 61.9 reduce-scatter.10
  1290.6 63.5 reduce-scatter.12
  1516.0 1130.6 all-reduce.4
  2649.4 277.8 reduce-scatter.8
where the time goes:
time: 2960 us; the launch traced here: 2940 us
  waiting for transfers between devices  1400 us (47%)
  local copies, waits for them, and re-layouts  656 us (22%)
  matrix products  400 us (14%)
  other arithmetic  294 us (10%)
  blocking collectives  163 us (6%)
    unnamed x13, waiting for transfers between devices  1050 us
    reduce_scatter x1, waiting for transfers between devices, local(): lax.psum_scatter(jnp.einsum('tf,te->fe', lefts, g_down, preferred_element...  267 us
    reshape x2, local copies, waits for them, and re-layouts, local(): g_value_rows.reshape(blocks_dev * DEPTH, BLOCK, D)  111 us
    reshape x2, local copies, waits for them, and re-layouts, local(): g_key_rows.reshape(blocks_dev * DEPTH, BLOCK, D)  111 us
    reshape x2, local copies, waits for them, and re-layouts, local(): value_group.reshape(group_blocks, BLOCK, D)[safe_paths]  93.2 us
    reshape x2, local copies, waits for them, and re-layouts, local(): key_group.reshape(group_blocks, BLOCK, D)[safe_paths]  93 us
    psum x2, blocking collectives, local(): lax.psum((jnp.sum(mask_f), loss_local), ('dp', 'fsdp'))  90.3 us
    all_gather x1, waiting for transfers between devices, local(): piece_qkv = lax.all_gather(qkv_local, ('dp', 'fsdp'), axis=0, tiled=True)  87.5 us
  transfers between devices with their start and end apart: 10, of which 3 were waited for; matrix products, arithmetic and copies ran while one was open for 28% of the time, Pallas kernels for 0%

commit v1 on v0

--- a/solution.py
+++ b/solution.py
@@ -1,9 +1,13 @@
+import functools
 import math
 
 import jax
 import jax.numpy as jnp
 from jax import lax
+from jax.experimental import pallas as pl
+from jax.experimental.pallas import tpu as pltpu
 from jax.sharding import PartitionSpec as P
+
 
 D = 1280
 HEADS = 20
@@ -49,7 +53,7 @@
     return (raw, scale_grad)
 
 
-def local(
+def general(
     states,
     teacher,
     parent_ids,
@@ -296,6 +300,441 @@
         ffn_share[:, 2 * FF + 4 : 2 * FF + 8].reshape(-1),
     )
 
+TRUNK = 8
+NB = 20
+TOK = NB * BLOCK
+F32 = jnp.float32
+BF = jnp.bfloat16
+
+
+def head_norm(raw):
+    inv = lax.rsqrt(jnp.sum(raw * raw, axis=0, keepdims=True) + EPS)
+    return raw * inv, inv
+
+def tri(size):
+    key = lax.broadcasted_iota(jnp.int32, (size, size), 0)
+    query = lax.broadcasted_iota(jnp.int32, (size, size), 1)
+    return key, query
+
+def chunks():
+    out = []
+    for j in range(TRUNK // 2):
+        parts = [(0, 256 * j, "all")] if j else []
+        out.append((256 * j, parts + [(256 * j, 256, "causal")]))
+    for j in range(2):
+        start = TRUNK * BLOCK + 256 * j
+        out.append((start, [(0, 1024, "all"), (start, 256, "pair")]))
+    for j in range(4):
+        start = (TRUNK + 4) * BLOCK + 256 * j
+        out.append((start, [(0, 1024, "all"), ((TRUNK + j) * BLOCK, 128, "all"), (start, 256, "pair")]))
+    return out
+
+def masked(kind, value):
+    if kind == "all":
+        return value
+    key, query = tri(256)
+    keep = key <= query
+    if kind == "pair":
+        keep = keep & ((key < 128) == (query < 128))
+    return jnp.where(keep, value, jnp.zeros_like(value))
+
+def nn(a, b):
+    return lax.dot_general(a, b, (((1,), (0,)), ((), ())), preferred_element_type=F32)
+
+def fwd_kernel(perm_ref, qkv_ref, scale_ref, mixed_ref, sum_ref, qs, ks, vs):
+    scale = scale_ref[0]
+    for i in range(NB):
+        lanes = pl.ds(pl.multiple_of(perm_ref[i] * BLOCK, BLOCK), BLOCK)
+        here = slice(i * BLOCK, (i + 1) * BLOCK)
+        q_unit, _ = head_norm(qkv_ref[0, :, lanes])
+        k_unit, _ = head_norm(qkv_ref[1, :, lanes])
+        qs[:, here] = (q_unit * scale).astype(BF) * BF(8.0)
+        ks[here, :] = (k_unit * scale).astype(BF).T
+        vs[0:64, here] = qkv_ref[2, :, lanes].astype(BF)
+    vs[64:80, :] = jnp.ones((16, TOK), BF)
+    for start, parts in chunks():
+        query = qs[:, start:start + 256]
+        acc = jnp.zeros((80, 256), F32)
+        for kstart, count, kind in parts:
+            scores = nn(ks[kstart:kstart + count, :], query)
+            powers = masked(kind, jnp.exp(scores)).astype(BF)
+            acc = acc + nn(vs[:, kstart:kstart + count], powers)
+        total = acc[64:65, :]
+        result = (acc[0:64, :] / total).astype(BF)
+        for half in range(2):
+            lanes = pl.ds(pl.multiple_of(perm_ref[start // BLOCK + half] * BLOCK, BLOCK), BLOCK)
+            cut = slice(half * BLOCK, (half + 1) * BLOCK)
+            mixed_ref[:, lanes] = result[:, cut]
+            sum_ref[0, :, lanes] = jnp.broadcast_to(1.0 / total[:, cut], (8, BLOCK))
+
+def attn_fwd(perm, qkv, scale):
+    heads = qkv.shape[1] // HEAD_DIM
+    return pl.pallas_call(
+        fwd_kernel,
+        grid_spec=pltpu.PrefetchScalarGridSpec(
+            num_scalar_prefetch=1,
+            grid=(heads,),
+            in_specs=[
+                pl.BlockSpec((3, HEAD_DIM, TOK), lambda h, p: (0, h, 0)),
+                pl.BlockSpec((1, HEAD_DIM, 1), lambda h, p: (h, 0, 0)),
+            ],
+            out_specs=[
+                pl.BlockSpec((HEAD_DIM, TOK), lambda h, p: (h, 0)),
+                pl.BlockSpec((1, 8, TOK), lambda h, p: (h, 0, 0)),
+            ],
+            scratch_shapes=[
+                pltpu.VMEM((HEAD_DIM, TOK), BF),
+                pltpu.VMEM((TOK, HEAD_DIM), BF),
+                pltpu.VMEM((80, TOK), BF),
+            ],
+        ),
+        out_shape=[
+            jax.ShapeDtypeStruct((heads * HEAD_DIM, TOK), BF),
+            jax.ShapeDtypeStruct((heads, 8, TOK), F32),
+        ],
+        compiler_params=pltpu.CompilerParams(vmem_limit_bytes=48 << 20),
+        name="tree_attention",
+        cost_estimate=pl.CostEstimate(flops=heads * 2 * 2 * 64 * 256 * 10752, bytes_accessed=12 << 20, transcendentals=heads * 256 * 10752),
+    )(perm, qkv, scale)
+
+def bwd_kernel(perm_ref, qkv_ref, scale_ref, sum_ref, mixed_ref, g_ref, out_ref, gscale_ref,
+               qT, q, k, kT, v, gT, g, dq, dk, dv, delta, inv):
+    scale = scale_ref[0]
+    for i in range(NB):
+        lanes = pl.ds(pl.multiple_of(perm_ref[i] * BLOCK, BLOCK), BLOCK)
+        here = slice(i * BLOCK, (i + 1) * BLOCK)
+        q_unit, _ = head_norm(qkv_ref[0, :, lanes])
+        k_unit, _ = head_norm(qkv_ref[1, :, lanes])
+        q8 = (q_unit * scale).astype(BF) * BF(8.0)
+        qT[:, here] = q8
+        q[here, :] = q8.T
+        kn = (k_unit * scale).astype(BF)
+        kT[:, here] = kn
+        k[here, :] = kn.T
+        v[here, :] = qkv_ref[2, :, lanes].astype(BF).T
+        gh = g_ref[:, lanes]
+        gT[:, here] = gh
+        g[here, :] = gh.T
+        delta[:, here] = jnp.sum(gh.astype(F32) * mixed_ref[:, lanes].astype(F32), axis=0, keepdims=True)
+        inv[:, here] = sum_ref[0, 0:1, lanes]
+    dk[...] = jnp.zeros_like(dk)
+    dv[...] = jnp.zeros_like(dv)
+    for start, parts in chunks():
+        span = slice(start, start + 256)
+        query, grad = qT[:, span], gT[:, span]
+        query_rows, grad_rows = q[span, :], g[span, :]
+        scale_row, delta_row = inv[:, span], delta[:, span]
+        acc = jnp.zeros((64, 256), F32)
+        for kstart, count, kind in parts:
+            keys = slice(kstart, kstart + count)
+            probs = masked(kind, jnp.exp(nn(k[keys, :], query)) * scale_row)
+            g_probs = nn(v[keys, :], grad)
+            g_scores = (probs * (g_probs - delta_row)).astype(BF)
+            dv[keys, :] += nn(probs.astype(BF), grad_rows)
+            dk[keys, :] += nn(g_scores, query_rows)
+            acc = acc + nn(kT[:, keys], g_scores)
+        dq[:, span] = acc * 8.0
+    g_scale = jnp.zeros((64, BLOCK), F32)
+    for i in range(NB):
+        lanes = pl.ds(pl.multiple_of(perm_ref[i] * BLOCK, BLOCK), BLOCK)
+        here = slice(i * BLOCK, (i + 1) * BLOCK)
+        for which, grad in ((0, dq[:, here]), (1, dk[here, :].T)):
+            unit, inverse = head_norm(qkv_ref[which, :, lanes])
+            g_scale = g_scale + grad * unit
+            scaled = grad * scale
+            raw = (scaled - unit * jnp.sum(scaled * unit, axis=0, keepdims=True)) * inverse
+            out_ref[which, :, lanes] = raw.astype(BF)
+        out_ref[2, :, lanes] = dv[here, :].T.astype(BF)
+    gscale_ref[0] = jnp.sum(g_scale, axis=1, keepdims=True)
+
+def attn_bwd(perm, qkv, scale, sums, mixed, g_mixed):
+    heads = qkv.shape[1] // HEAD_DIM
+    row = lambda h, p: (h, 0)
+    return pl.pallas_call(
+        bwd_kernel,
+        grid_spec=pltpu.PrefetchScalarGridSpec(
+            num_scalar_prefetch=1,
+            grid=(heads,),
+            in_specs=[
+                pl.BlockSpec((3, HEAD_DIM, TOK), lambda h, p: (0, h, 0)),
+                pl.BlockSpec((1, HEAD_DIM, 1), lambda h, p: (h, 0, 0)),
+                pl.BlockSpec((1, 8, TOK), lambda h, p: (h, 0, 0)),
+                pl.BlockSpec((HEAD_DIM, TOK), row),
+                pl.BlockSpec((HEAD_DIM, TOK), row),
+            ],
+            out_specs=[
+                pl.BlockSpec((3, HEAD_DIM, TOK), lambda h, p: (0, h, 0)),
+                pl.BlockSpec((1, HEAD_DIM, 1), lambda h, p: (h, 0, 0)),
+            ],
+            scratch_shapes=[
+                pltpu.VMEM((HEAD_DIM, TOK), BF),
+                pltpu.VMEM((TOK, HEAD_DIM), BF),
+                pltpu.VMEM((TOK, HEAD_DIM), BF),
+                pltpu.VMEM((HEAD_DIM, TOK), BF),
+                pltpu.VMEM((TOK, HEAD_DIM), BF),
+                pltpu.VMEM((HEAD_DIM, TOK), BF),
+                pltpu.VMEM((TOK, HEAD_DIM), BF),
+                pltpu.VMEM((HEAD_DIM, TOK), F32),
+                pltpu.VMEM((TOK, HEAD_DIM), F32),
+                pltpu.VMEM((TOK, HEAD_DIM), F32),
+                pltpu.VMEM((1, TOK), F32),
+                pltpu.VMEM((1, TOK), F32),
+            ],
+        ),
+        out_shape=[
+            jax.ShapeDtypeStruct((3, heads * HEAD_DIM, TOK), BF),
+            jax.ShapeDtypeStruct((heads, HEAD_DIM, 1), F32),
+        ],
+        compiler_params=pltpu.CompilerParams(vmem_limit_bytes=48 << 20),
+        name="tree_attention_grad",
+        cost_estimate=pl.CostEstimate(flops=heads * 5 * 2 * 64 * 256 * 10752, bytes_accessed=20 << 20, transcendentals=heads * 256 * 10752),
+    )(perm, qkv, scale, sums, mixed, g_mixed)
+
+
+def order_kernel(where_ref, parent_ref, perm_ref, branch_ref, leaf_ref):
+    base, me = where_ref[0], where_ref[1]
+
+    def parent_of(block):
+        return jnp.where(block >= 0, parent_ref[jnp.maximum(block, 0)] - base, -1)
+
+    def depth_of(block):
+        def climb(step, state):
+            at, depth = state
+            at = jnp.where(at >= 0, jnp.maximum(parent_of(at), -1), -1)
+            return at, depth + (at >= 0).astype(jnp.int32)
+
+        return lax.fori_loop(0, DEPTH - 1, climb, (block, jnp.int32(0)))[1]
+
+    def relative(block):
+        return jnp.bitwise_xor(block // 5, me) * 5 + block % 5
+
+    def first(block, count):
+        depth = depth_of(block)
+        is_branch = depth == TRUNK
+        branch_ref[block] = count
+        leaf_ref[block] = 0
+
+        @pl.when(depth <= TRUNK)
+        def _():
+            perm_ref[jnp.where(is_branch, TRUNK + count, depth)] = relative(block)
+
+        return count + is_branch.astype(jnp.int32)
+
+    lax.fori_loop(0, NB, first, jnp.int32(0))
+
+    def second(block, carry):
+        @pl.when(depth_of(block) > TRUNK)
+        def _():
+            parent = jnp.maximum(parent_of(block), 0)
+            seen = leaf_ref[parent]
+            perm_ref[TRUNK + 4 + 2 * branch_ref[parent] + seen] = relative(block)
+            leaf_ref[parent] = seen + 1
+
+        return carry
+
+    lax.fori_loop(0, NB, second, jnp.int32(0))
+
+
+def tree_order(where, parents):
+    smem = pl.BlockSpec(memory_space=pltpu.SMEM)
+    return pl.pallas_call(
+        order_kernel,
+        in_specs=[smem, smem],
+        out_specs=smem,
+        out_shape=jax.ShapeDtypeStruct((NB,), jnp.int32),
+        scratch_shapes=[pltpu.SMEM((NB,), jnp.int32), pltpu.SMEM((NB,), jnp.int32)],
+        name="tree_order",
+    )(where, parents)
+
+
+def swap(value, step):
+    return lax.ppermute(value, "fsdp", [(i, i ^ step) for i in range(4)])
+
+
+def gather_tokens(mine):
+    across = swap(mine, 2)
+    return jnp.concatenate((mine, swap(mine, 1), across, swap(across, 1)), axis=0)
+
+
+def reduce_tokens(share):
+    rows = share.shape[0] // 4
+    part = [share[i * rows : (i + 1) * rows] for i in range(4)]
+    other = swap(jnp.concatenate((part[3], part[1]), axis=0).astype(BF), 1)
+    far = part[2] + other[:rows]
+    near = part[0] + other[rows:]
+    return near + swap(far.astype(BF), 2)
+
+
+def dot(left, right, contract):
+    return lax.dot_general(left, right, ((contract[:1], contract[1:]), ((), ())), preferred_element_type=F32)
+
+
+def local(
+    states,
+    teacher,
+    parent_ids,
+    valid_mask,
+    w_query,
+    w_key,
+    w_value,
+    w_out,
+    w_up,
+    w_gate,
+    w_down,
+    qk_scale,
+    attn_rate,
+    mlp_rate,
+    up_scale,
+    gate_scale,
+):
+    both = ("dp", "fsdp")
+    dps, tps = 8, 4
+    rows_w = w_query.shape[0]
+    cols = D // tps
+    hid = FF // tps
+    ff_rows = FF // (dps * tps)
+    me = lax.axis_index("fsdp")
+    root_width = math.sqrt(D)
+    mask_f = valid_mask.astype(F32)
+    group_base = lax.axis_index("dp") * NB
+    perm = tree_order(jnp.stack((group_base, me)).astype(jnp.int32), parent_ids)
+
+    tokens = gather_tokens(states)
+
+    count = jnp.sum(valid_mask)
+    first_row = jnp.arange(rows_w, dtype=jnp.int32) == 0
+    small = jnp.stack(
+        (
+            qk_scale,
+            attn_rate,
+            mlp_rate,
+            jnp.where(first_row, count // 128, 0).astype(BF),
+            jnp.where(first_row, count % 128, 0).astype(BF),
+        ),
+        axis=1,
+    )
+    qkv_send = jnp.concatenate(
+        [w.reshape(rows_w, tps, cols).transpose(1, 0, 2) for w in (w_query, w_key, w_value)]
+        + [jnp.broadcast_to(small[None], (tps, rows_w, 5))],
+        axis=2,
+    )
+    qkv_group = lax.all_to_all(qkv_send, "fsdp", 0, 0, tiled=True).reshape(tps * rows_w, 3 * cols + 5)
+    qkv_group = jnp.concatenate(
+        (qkv_group, up_scale[:, None], gate_scale[:, None], jnp.zeros((tps * rows_w, 57), BF)), axis=1
+    )
+    first = lax.all_gather(qkv_group, "dp", axis=0, tiled=True)
+    ug_send = jnp.concatenate(
+        [
+            w.reshape(rows_w, dps, tps, ff_rows).transpose(2, 0, 1, 3).reshape(tps, rows_w, hid)
+            for w in (w_up, w_gate)
+        ],
+        axis=2,
+    )
+    ug_group = lax.all_to_all(ug_send, "fsdp", 0, 0, tiled=True).reshape(tps * rows_w, 2 * hid)
+    spread = [(j, tps * (j % dps) + j // dps) for j in range(dps * tps)]
+    out_mine = lax.ppermute(w_out, both, spread)
+    w_ug = lax.all_gather(ug_group, "dp", axis=0, tiled=True)
+    w_o = lax.all_gather(out_mine, "dp", axis=0, tiled=True)
+    w_d = lax.all_gather(w_down, "dp", axis=0, tiled=True)
+
+    w_qkv = first[:, : 3 * cols]
+    small_all = first[:, 3 * cols :].astype(F32)
+    rate_attn = small_all[:, 1]
+    rate_mlp = small_all[:, 2]
+    valid_count = 128.0 * jnp.sum(small_all[:, 3]) + jnp.sum(small_all[:, 4])
+    scale_up = small_all[:, 5]
+    scale_gate = small_all[:, 6]
+    scale_qk = lax.dynamic_slice_in_dim(small_all[:, 0], me * cols, cols).reshape(cols // HEAD_DIM, HEAD_DIM, 1)
+
+    qkv = dot(w_qkv, tokens, (0, 1)).reshape(3, cols, TOK)
+    mixed, sums = attn_fwd(perm, qkv, scale_qk)
+    attn = reduce_tokens(dot(mixed, w_o, (0, 0)))
+    inputs = states.astype(F32)
+    attn_unit, attn_inv = unit_rows(attn)
+    hidden, hidden_inv = unit_rows(inputs + rate_attn * (attn_unit - inputs))
+    hidden_all = gather_tokens(hidden.astype(BF))
+    raw = dot(hidden_all, w_ug, (1, 0))
+    up_proj, gate_proj = raw[:, :hid], raw[:, hid:]
+    upscaled = up_proj * scale_up
+    gated = gate_proj * scale_gate * root_width
+    sigmoid_gate = jax.nn.sigmoid(gated)
+    act = (upscaled * (gated * sigmoid_gate)).astype(BF)
+    down = reduce_tokens(dot(act, w_d, (1, 0)))
+    down_unit, down_inv = unit_rows(down)
+    result, result_inv = unit_rows(hidden + rate_mlp * (down_unit - hidden))
+    loss_local = jnp.sum(mask_f[:, None] * (result - teacher) ** 2)
+    loss_parts = lax.all_gather(jnp.broadcast_to(loss_local, (1, 128)), both, axis=0, tiled=True)
+    loss = jnp.sum(loss_parts[:, 0]) / valid_count
+
+    g_result = 2.0 * mask_f[:, None] * (result - teacher) / valid_count
+    g_last = unit_back(g_result, result, result_inv)
+    g_rate_mlp = jnp.sum(g_last * (down_unit - hidden), axis=0)
+    g_down = unit_back(g_last * rate_mlp, down_unit, down_inv).astype(BF)
+    g_down_all = gather_tokens(g_down)
+    g_act = dot(g_down_all, w_d, (1, 1))
+    g_upscaled = g_act * (gated * sigmoid_gate)
+    g_gated = g_act * upscaled * sigmoid_gate * (1.0 + gated * (1.0 - sigmoid_gate))
+    grad_up_scale = jnp.sum(g_upscaled * up_proj, axis=0)
+    grad_gate_scale = jnp.sum(g_gated * gate_proj * root_width, axis=0)
+    g_ug = jnp.concatenate(
+        ((g_upscaled * scale_up).astype(BF), (g_gated * scale_gate * root_width).astype(BF)), axis=1
+    )
+    g_hidden = g_last * (1.0 - rate_mlp) + reduce_tokens(dot(g_ug, w_ug, (1, 1)))
+    grad_down = lax.psum_scatter(
+        dot(act, g_down_all, (0, 0)).astype(BF), "dp", scatter_dimension=0, tiled=True
+    ).astype(F32)
+    grad_ug = lax.psum_scatter(dot(hidden_all, g_ug, (0, 0)).astype(BF), "dp", scatter_dimension=0, tiled=True)
+
+    g_pre = unit_back(g_hidden, hidden, hidden_inv)
+    g_rate_attn = jnp.sum(g_pre * (attn_unit - inputs), axis=0)
+    g_attn = unit_back(g_pre * rate_attn, attn_unit, attn_inv).astype(BF)
+    g_attn_all = gather_tokens(g_attn)
+    g_mixed = dot(w_o, g_attn_all, (1, 1)).astype(BF)
+    g_qkv, g_scale = attn_bwd(perm, qkv, scale_qk, sums, mixed, g_mixed)
+    g_qkv = g_qkv.reshape(3 * cols, TOK)
+    grad_states = g_pre * (1.0 - rate_attn) + reduce_tokens(dot(g_qkv, w_qkv, (0, 1)))
+    grad_out = lax.psum_scatter(dot(mixed, g_attn_all, (1, 0)).astype(BF), "dp", scatter_dimension=0, tiled=True)
+    grad_qkv = lax.psum_scatter(dot(tokens, g_qkv, (0, 1)).astype(BF), "dp", scatter_dimension=0, tiled=True)
+
+    slot = jnp.arange(tps, dtype=jnp.int32) == me
+    qk_rows = jnp.where(slot[:, None], g_scale.reshape(1, cols), 0.0).reshape(dps * tps, rows_w)
+    ff_terms = [
+        jnp.where(slot[None, :, None], term.reshape(dps, 1, ff_rows), 0.0).reshape(dps * tps, ff_rows)
+        for term in (grad_up_scale, grad_gate_scale)
+    ]
+    vectors = jnp.concatenate(
+        [g_rate_attn.reshape(dps * tps, rows_w), g_rate_mlp.reshape(dps * tps, rows_w), qk_rows]
+        + ff_terms
+        + [jnp.zeros((dps * tps, 512 - 3 * rows_w - 2 * ff_rows), F32)],
+        axis=1,
+    )
+    vector_share = lax.psum_scatter(vectors, both, scatter_dimension=0, tiled=True)[0]
+
+    grad_out = lax.ppermute(grad_out, both, [(b, a) for a, b in spread]).astype(F32)
+    ug_back = lax.all_to_all(grad_ug, "fsdp", 0, 0, tiled=True).reshape(tps, rows_w, 2, dps, ff_rows)
+    ug_back = ug_back.transpose(2, 1, 3, 0, 4).reshape(2, rows_w, FF).astype(F32)
+    qkv_back = lax.all_to_all(grad_qkv, "fsdp", 0, 0, tiled=True).reshape(tps, rows_w, 3, cols)
+    qkv_back = qkv_back.transpose(2, 1, 0, 3).reshape(3, rows_w, D).astype(F32)
+    cuts = (0, rows_w, 2 * rows_w, 3 * rows_w, 3 * rows_w + ff_rows, 3 * rows_w + 2 * ff_rows)
+    v = [vector_share[a:b] for a, b in zip(cuts, cuts[1:])]
+    return (
+        result.astype(BF),
+        loss,
+        grad_states,
+        qkv_back[0],
+        qkv_back[1],
+        qkv_back[2],
+        grad_out,
+        ug_back[0],
+        ug_back[1],
+        grad_down,
+        v[2],
+        v[0],
+        v[1],
+        v[3],
+        v[4],
+    )
+
 
 def solution(mesh):
     placed = (
@@ -316,8 +755,9 @@
         P(("dp", "fsdp")),
         P(("dp", "fsdp")),
     )
+    quick = mesh.shape["fsdp"] == 4 and mesh.shape["dp"] == 8
     return jax.shard_map(
-        local,
+        local if quick else general,
         mesh=mesh,
         in_specs=placed,
         out_specs=(

time: 2960 us -> 1170 us (0.40)
  waiting for transfers between devices: 1400 us -> 598 us
  local copies, waits for them, and re-layouts: 656 us -> 69 us
  other arithmetic: 294 us -> 67.7 us
  matrix products: 400 us -> 182 us
  Pallas kernels: 0 us -> 79.8 us
  blocking collectives: 163 us -> 102 us
  starting transfers between devices: 0.41 us -> 37.8 us
    unnamed x13 -> x9, waiting for transfers between devices: 1050 us -> 122 us
    reshape x21 -> x11, local copies, waits for them, and re-layouts: 428 us -> 7.35 us  [the longest x6 4 us: local(): w.reshape(rows_w, dps, tps, ff_rows).transpose(2, 0, 1, 3)]
    ppermute x0 -> x22, waiting for transfers between devices: none -> 280 us  [the longest x20 272 us: swap(): return lax.ppermute(value, 'fsdp', [(i, i ^ step) for i in range(4)])]
    dot_general x18 -> x12, matrix products: 400 us -> 182 us  [dot(): lax.dot_general(left, right, ((contract[:1], contract[1:]), ((), ())), pr...]
    scatter-add x2 -> x0, other arithmetic: 131 us -> none  [the longest x1 65.5 us: local(): g_key_group = jnp.zeros((group_blocks, BLOCK, D), jnp.float32).at[flat_pa...]
    concatenate x2 -> x4, local copies, waits for them, and re-layouts: 116 us -> 4.39 us  [the longest x1 2.75 us: gather_tokens(): jnp.concatenate((mine, swap(mine, 1), across, swap(across, 1)), axis=0)]
    reduce_scatter x1 -> x4, waiting for transfers between devices: 267 us -> 173 us  [the longest x1 113 us: local(): lax.psum_scatter(dot(hidden_all, g_ug, (0, 0)).astype(BF), 'dp', scatter_...]
    psum x2 -> x0, blocking collectives: 90.3 us -> none  [local(): lax.psum((jnp.sum(mask_f), loss_local), ('dp', 'fsdp'))]
  transfers between devices with their start and end apart: 10 -> 34, of which waited for: 3 -> 20; matrix products, arithmetic and copies ran while one was open for 28% -> 15% of each run, Pallas kernels for 0% -> 3%
where the time goes in v1:
time: 1170 us; the launch traced here: 1160 us
  waiting for transfers between devices  598 us (51%)
  matrix products  182 us (16%)
  blocking collectives  102 us (9%)
  Pallas kernels  79.8 us (7%)
  local copies, waits for them, and re-layouts  69 us (6%)
  other arithmetic  67.7 us (6%)
  starting transfers between devices  37.8 us (3%)
  between operations  21 us (2%)
    ppermute x20, waiting for transfers between devices, swap(): return lax.ppermute(value, 'fsdp', [(i, i ^ step) for i in range(4)])  272 us
    dot_general x12, matrix products, dot(): lax.dot_general(left, right, ((contract[:1], contract[1:]), ((), ())), pr...  182 us
    unnamed x9, waiting for transfers between devices  122 us
    reduce_scatter x1, waiting for transfers between devices, local(): lax.psum_scatter(dot(hidden_all, g_ug, (0, 0)).astype(BF), 'dp', scatter_...  113 us
    unnamed x1, blocking collectives  69.8 us
    reduce_scatter x1, waiting for transfers between devices, local(): lax.psum_scatter(dot(mixed, g_attn_all, (1, 0)).astype(BF), 'dp', scatter...  60.6 us
    pallas_call x1, Pallas kernels, attn_bwd(): pl.pallas_call(bwd_kernel, grid_spec=pltpu.PrefetchScalarGridSpec(num_sca...  48.7 us
    unnamed x105, local copies, waits for them, and re-layouts  34.6 us
  transfers between devices with their start and end apart: 34, of which 20 were waited for; matrix products, arithmetic and copies ran while one was open for 15% of the time, Pallas kernels for 3%

profile of v1, /device:TPU:4, one launch (start us, length us, event | category | flops | bytes accessed | tf_op | source)
XLA Modules:
  0.0 1156.7 jit_solution(1387074628174424576)
XLA Ops:
  32.0 33.0 %collective-permute-done.1 = bf16[640,1280]{1,0:T(8,128)(2,1)} collective-permute-done((bf16[640,1280]{1,0:T(8,128)(2,1)S(1)}, bf16[640,1280]{1,0:T(8,128)(2,1)}, u32[]{:S(2)}, u32[]{:S(2)}) %collective-permute-start.1) | collective-permute-done | bytes 1638432 | tf_op jit(solution)/shard_map/ppermute | solution.py:551
  82.3 32.2 %all_gather.16 = bf16[320,1280]{1,0:T(8,128)(2,1)S(1)} all-gather(bf16[40,1280]{1,0:T(8,128)(2,1)S(1)} %collective-permute-done.3), channel_id=1, replica_groups=mesh['dp'=8,'fsdp'=4] {'dp'}, dimensions={0}, use_global_device_ids=true | all-gather | bytes 921600 | tf_op jit(solution)/shard_map/all_gather | solution.py:637
  126.8 12.0 %fusion.15 = f32[960,2560]{1,0:T(8,128)} fusion(bf16[2560,1280]{1,0:T(8,128)(2,1)S(1)} %copy-done.31, bf16[1280,1024]{1,0:T(8,128)(2,1)} %all-gather.4.cloned.1.call-done), kind=kOutput, calls=%fused_computation.69 | convolution fusion | flops 6291456000 | bytes 19005440 | tf_op jit(solution)/shard_map/dot_general | solution.py:569
  138.8 24.7 %tree_attention.1 = (bf16[320,2560]{1,0:T(8,128)(2,1)S(1)}, f32[5,8,2560]{2,1,0:T(8,128)S(1)}) custom-call(s32[20]{0:T(128)S(1)} %copy-done.4, f32[3,320,2560]{2,1,0:T(8,128)} %bitcast.77, f32[5,64,1]{2,1,0:T(8,128)S(1)} %bitcast.57), custom_call_target="tpu_custom_call" | custom-call | flops 3523215360 | bytes 12582912 | tf_op jit(solution)/shard_map/tree_attention/pallas_call | solution.py:372
  184.4 33.3 %collective-permute-done.5 = bf16[640,1280]{0,1:T(8,128)(2,1)} collective-permute-done((bf16[640,1280]{0,1:T(8,128)(2,1)}, bf16[640,1280]{0,1:T(8,128)(2,1)}, u32[]{:S(2)}, u32[]{:S(2)}) %collective-permute-start.5) | collective-permute-done | bytes 1638432 | tf_op jit(solution)/shard_map/ppermute | solution.py:551
  227.0 35.7 %collective-permute-done.7 = bf16[640,1280]{0,1:T(8,128)(2,1)} collective-permute-done((bf16[640,1280]{0,1:T(8,128)(2,1)S(1)}, bf16[640,1280]{0,1:T(8,128)(2,1)}, u32[]{:S(2)}, u32[]{:S(2)}) %collective-permute-start.7) | collective-permute-done | bytes 1638432 | tf_op jit(solution)/shard_map/ppermute | solution.py:551
  266.5 26.8 %fusion.18 = f32[2560,2560]{1,0:T(8,128)} fusion(bf16[1280,2560]{1,0:T(8,128)(2,1)} %all-gather.6.cloned.1.call-done, bf16[640,1280]{0,1:T(8,128)(2,1)} %collective-permute-done.8, bf16[640,1280]{0,1:T(8,128)(2,1)} %collective-permute-done.7, bf16[640,1280]{0,1:T(8,128)(2,1)} %collective-permute-done.6, bf16[640,1280]{0,1:T(8,128)(2,1)S(1)} %multiply_convert_fusion.6), kind=kOutput, calls=%fused_computation.72 | convolution fusion | flops 16803430400 | bytes 39321600 | tf_op jit(solution)/shard_map/dot_general | solution.py:569
  293.3 13.7 %multiply_convert_fusion.2 = bf16[2560,1280]{1,0:T(8,128)(2,1)} fusion(f32[2560,2560]{1,0:T(8,128)} %fusion.18, f32[1280]{0:T(1024)S(1)} %get-tuple-element.94, f32[1280]{0:T(1024)S(1)} %get-tuple-element.93), kind=kLoop, calls=%fused_computation.6 | loop fusion | flops 29491200 | bytes 32778240 | tf_op jit(solution)/shard_map/convert_element_type | solution.py:661
  306.9 17.9 %all-gather.8.cloned.1.call-done = bf16[1280,1280]{1,0:T(8,128)(2,1)} async-done(((bf16[160,1280]{1,0:T(8,128)(2,1)}), bf16[1280,1280]{1,0:T(8,128)(2,1)}) %all-gather.8.cloned.1.call-update) | async-done | bytes 3276816 | tf_op jit(solution)/shard_map/all_gather | solution.py:638
  324.9 15.0 %fusion.40 = (bf16[2560,1280]{0,1:T(8,128)(2,1)S(1)}, f32[2560,1280]{0,1:T(8,128)}) fusion(bf16[2560,1280]{1,0:T(8,128)(2,1)} %multiply_convert_fusion.2, bf16[1280,1280]{1,0:T(8,128)(2,1)} %all-gather.8.cloned.1.call-done), kind=kOutput, calls=%fused_computation.125 | convolution fusion | flops 8391884800 | bytes 29491200 | tf_op jit(solution)/shard_map/dot_general | solution.py:569
  357.2 30.6 %collective-permute-done.10 = bf16[640,1280]{0,1:T(8,128)(2,1)} collective-permute-done((bf16[640,1280]{0,1:T(8,128)(2,1)S(1)}, bf16[640,1280]{0,1:T(8,128)(2,1)}, u32[]{:S(2)}, u32[]{:S(2)}) %collective-permute-start.10) | collective-permute-done | bytes 1638432 | tf_op jit(solution)/shard_map/ppermute | solution.py:551
  402.2 35.5 %collective-permute-done.12 = bf16[640,1280]{0,1:T(8,128)(2,1)S(1)} collective-permute-done((bf16[640,1280]{0,1:T(8,128)(2,1)S(1)}, bf16[640,1280]{0,1:T(8,128)(2,1)S(1)}, u32[]{:S(2)}, u32[]{:S(2)}) %collective-permute-start.12) | collective-permute-done | bytes 1638432 | tf_op jit(solution)/shard_map/ppermute | solution.py:551
  441.4 27.3 %multiply_reduce_fusion = (f32[1280]{0:T(1024)S(1)}, f32[1280]{0:T(1024)S(1)}, f32[2560,1280]{1,0:T(8,128)}, bf16[2560,1280]{1,0:T(8,128)(2,1)}) fusion(f32[2560,2560]{1,0:T(8,128)} %fusion.18, f32[1280]{0:T(1024)S(1)} %get-tuple-element.93, f32[1280]{0:T(1024)S(1)} %get-tuple-element.94, bf16[1280,1280]{1,0:T(8,128)(2,1)} %all-gather.8.cloned.1.call-done, ...), kind=kOutput, calls=%fused_computation.1 | convolution fusion | flops 8483633152 | bytes 55726080 | tf_op jit(solution)/shard_map/dot_general | solution.py:569
  477.5 26.2 %fusion.41 = (bf16[2560,1280]{0,1:T(8,128)(2,1)}, f32[2560,1280]{0,1:T(8,128)}) fusion(bf16[1280,2560]{1,0:T(8,128)(2,1)} %all-gather.6.cloned.1.call-done, bf16[2560,1280]{1,0:T(8,128)(2,1)} %multiply_convert_fusion, bf16[2560,1280]{1,0:T(8,128)(2,1)} %get-tuple-element.110), kind=kOutput, calls=%fused_computation.126 | convolution fusion | flops 16806707200 | bytes 39321600 | tf_op jit(solution)/shard_map/dot_general | solution.py:569
  514.4 36.4 %collective-permute-done.15 = bf16[640,1280]{0,1:T(8,128)(2,1)S(1)} collective-permute-done((bf16[640,1280]{0,1:T(8,128)(2,1)S(1)}, bf16[640,1280]{0,1:T(8,128)(2,1)S(1)}, u32[]{:S(2)}, u32[]{:S(2)}) %collective-permute-start.15) | collective-permute-done | bytes 1638432 | tf_op jit(solution)/shard_map/ppermute | solution.py:551
  558.0 35.5 %collective-permute-done.17 = bf16[640,1280]{0,1:T(8,128)(2,1)S(1)} collective-permute-done((bf16[640,1280]{0,1:T(8,128)(2,1)S(1)}, bf16[640,1280]{0,1:T(8,128)(2,1)S(1)}, u32[]{:S(2)}, u32[]{:S(2)}) %collective-permute-start.17) | collective-permute-done | bytes 1638432 | tf_op jit(solution)/shard_map/ppermute | solution.py:551
  602.2 48.7 %tree_attention_grad.1 = (bf16[3,320,2560]{2,1,0:T(8,128)(2,1)}, f32[5,64,1]{2,1,0:T(8,128)S(1)}) custom-call(s32[20]{0:T(128)S(1)} %copy-done.5, f32[3,320,2560]{2,1,0:T(8,128)} %bitcast.78, f32[5,64,1]{2,1,0:T(8,128)S(1)} %bitcast.58, f32[5,8,2560]{2,1,0:T(8,128)S(1)} %get-tuple-element.20.sum_ref, bf16[320,2560]{1,0:T(8,128)(2,1)S(1)} %copy-done.1, ...), custom_call_target="tpu_custom_call" | custom-call | flops 8808038400 | bytes 20971520 | tf_op jit(solution)/shard_map/tree_attention_grad/pallas_call | solution.py:453
  650.8 10.3 convolution_convert_fusion.3
  661.2 15.8 %convolution_convert_fusion.1 = bf16[1280,1280]{1,0:T(8,128)(2,1)} fusion(bf16[2560,1280]{1,0:T(8,128)(2,1)} %multiply_convert_fusion.2, bf16[640,1280]{0,1:T(8,128)(2,1)} %collective-permute-done.13, bf16[640,1280]{0,1:T(8,128)(2,1)} %copy-done.40, bf16[640,1280]{0,1:T(8,128)(2,1)} %copy-done.41, bf16[640,1280]{0,1:T(8,128)(2,1)} %copy-done.29), kind=kOutput, calls=%fused_computation.13 | convolution fusion | flops 8416460800 | bytes 16384000 | tf_op jit(solution)/shard_map/dot_general | solution.py:569
  685.1 24.9 %convolution_convert_fusion = bf16[1280,2560]{1,0:T(8,128)(2,1)} fusion(bf16[2560,1280]{1,0:T(8,128)(2,1)} %multiply_convert_fusion, bf16[2560,1280]{1,0:T(8,128)(2,1)} %get-tuple-element.110, bf16[640,1280]{0,1:T(8,128)(2,1)} %collective-permute-done.8, bf16[640,1280]{0,1:T(8,128)(2,1)} %collective-permute-done.7, ...), kind=kOutput, calls=%fused_computation.11 | convolution fusion | flops 16832921600 | bytes 26214400 | tf_op jit(solution)/shard_map/dot_general | solution.py:569
  735.5 69.8 %all-reduce = f32[32]{0:T(128)S(1)} all-reduce(f32[32]{0:T(128)S(1)} %dynamic-update-slice), channel_id=2, replica_groups=mesh['dp'=8,'fsdp'=4] {'dp','fsdp'}, use_global_device_ids=true, to_apply=%add | all-reduce | flops 32 | bytes 256
  812.1 121.5 %all-reduce.4.cloned.1.call-done = f32[32,512]{1,0:T(8,128)} async-done(((f32[32,512]{1,0:T(8,128)}), f32[32,512]{1,0:T(8,128)}) %all-reduce.4.cloned.1.call-update) | async-done | bytes 65552
  935.0 60.6 %reduce-scatter.7.cloned.1.call-done = bf16[40,1280]{1,0:T(8,128)(2,1)} async-done(((bf16[320,1280]{1,0:T(8,128)(2,1)}), bf16[40,1280]{1,0:T(8,128)(2,1)}) %reduce-scatter.7.cloned.1.call-update) | async-done | bytes 102416 | tf_op jit(solution)/shard_map/reduce_scatter | solution.py:696
  1007.7 112.6 %reduce-scatter.9.cloned.1.call-done = bf16[160,2560]{1,0:T(8,128)(2,1)} async-done(((bf16[1280,2560]{1,0:T(8,128)(2,1)}), bf16[160,2560]{1,0:T(8,128)(2,1)}) %reduce-scatter.9.cloned.1.call-update) | async-done | bytes 819216 | tf_op jit(solution)/shard_map/reduce_scatter | solution.py:686
  (272 shorter events, 235.6 us)
Async XLA Ops:
  19.9 103.7 %all-gather.4.cloned.1.call-start = ((), (), s32[]{:S(2)}) async-start(), calls=%async_computation.8 | async-start | bytes 2949120 | tf_op jit(solution)/shard_map/all_gather | solution.py:625
  27.5 37.5 %collective-permute-start.1 = (bf16[640,1280]{1,0:T(8,128)(2,1)S(1)}, bf16[640,1280]{1,0:T(8,128)(2,1)}, u32[]{:S(2)}, u32[]{:S(2)}) collective-permute-start(bf16[640,1280]{1,0:T(8,128)(2,1)S(1)} %copy-done.19), channel_id=1, source_target_pairs={{0,2},{1,3},{2,0},{3,1},{4,6},{5,7},{6,4},{7,5},{8,10},{9,11},{10,... | collective-permute-start | bytes 4915208 | tf_op jit(solution)/shard_map/ppermute | solution.py:551
  27.9 87.5 %collective-permute-start = (bf16[640,1280]{1,0:T(8,128)(2,1)S(1)}, bf16[640,1280]{1,0:T(8,128)(2,1)}, u32[]{:S(2)}, u32[]{:S(2)}) collective-permute-start(bf16[640,1280]{1,0:T(8,128)(2,1)S(1)} %copy-done.19), channel_id=1, source_target_pairs={{0,1},{1,0},{2,3},{3,2},{4,5},{5,4},{6,7},{7,6},{8,9},{9,8},{10,11... | collective-permute-start | bytes 4915208 | tf_op jit(solution)/shard_map/ppermute | solution.py:551
  65.0 55.9 %collective-permute-start.2 = (bf16[640,1280]{1,0:T(8,128)(2,1)}, bf16[640,1280]{1,0:T(8,128)(2,1)}, u32[]{:S(2)}, u32[]{:S(2)}) collective-permute-start(bf16[640,1280]{1,0:T(8,128)(2,1)} %collective-permute-done.1), channel_id=1, source_target_pairs={{0,1},{1,0},{2,3},{3,2},{4,5},{5,4},{6,7},{7,6},{8,9},{9,8},{10,11... | collective-permute-start | bytes 4915208 | tf_op jit(solution)/shard_map/ppermute | solution.py:551
  65.9 48.5 %all-to-all-start.1 = ((bf16[4,40,2560]{2,1,0:T(8,128)(2,1)}), bf16[4,40,2560]{2,1,0:T(8,128)(2,1)S(1)}, u32[]{:S(2)}, u32[]{:S(2)}) async-start(bf16[4,40,2560]{2,1,0:T(8,128)(2,1)} %pad_maximum_fusion.16), calls=%async_computation.1 | async-start | bytes 1638400 | tf_op jit(solution)/shard_map/all_to_all | solution.py:633
  69.4 193.3 %all-gather.6.cloned.1.call-start = ((), (), s32[]{:S(2)}) async-start(), calls=%async_computation.9 | async-start | bytes 7372800 | tf_op jit(solution)/shard_map/all_gather | solution.py:636
  115.4 209.5 %all-gather.8.cloned.1.call-start = ((), (), s32[]{:S(2)}) async-start(), calls=%async_computation.10 | async-start | bytes 3686400 | tf_op jit(solution)/shard_map/all_gather | solution.py:638
  176.0 41.8 %collective-permute-start.5 = (bf16[640,1280]{0,1:T(8,128)(2,1)}, bf16[640,1280]{0,1:T(8,128)(2,1)}, u32[]{:S(2)}, u32[]{:S(2)}) collective-permute-start(bf16[640,1280]{0,1:T(8,128)(2,1)} %fusion.11), channel_id=1, source_target_pairs={{0,2},{1,3},{2,0},{3,1},{4,6},{5,7},{6,4},{7,5},{8,10},{9,11},{10,... | collective-permute-start | bytes 4915208 | tf_op jit(solution)/shard_map/ppermute | solution.py:551
  225.1 37.5 %collective-permute-start.7 = (bf16[640,1280]{0,1:T(8,128)(2,1)S(1)}, bf16[640,1280]{0,1:T(8,128)(2,1)}, u32[]{:S(2)}, u32[]{:S(2)}) collective-permute-start(bf16[640,1280]{0,1:T(8,128)(2,1)S(1)} %multiply_convert_fusion.6), channel_id=1, source_target_pairs={{0,2},{1,3},{2,0},{3,1},{4,6},{5,7},{6,4},{7,5},{8,10},{9,11},{10,... | collective-permute-start | bytes 4915208 | tf_op jit(solution)/shard_map/ppermute | solution.py:551
  227.0 35.8 %collective-permute-start.6 = (bf16[640,1280]{0,1:T(8,128)(2,1)S(1)}, bf16[640,1280]{0,1:T(8,128)(2,1)}, u32[]{:S(2)}, u32[]{:S(2)}) collective-permute-start(bf16[640,1280]{0,1:T(8,128)(2,1)S(1)} %multiply_convert_fusion.6), channel_id=1, source_target_pairs={{0,1},{1,0},{2,3},{3,2},{4,5},{5,4},{6,7},{7,6},{8,9},{9,8},{10,11... | collective-permute-start | bytes 4915208 | tf_op jit(solution)/shard_map/ppermute | solution.py:551
  262.7 468.7 %reduce-scatter.5.cloned.1.call-start = ((), (), s32[]{:S(2)}) async-start(), calls=%async_computation.11 | async-start | bytes 2949120 | tf_op jit(solution)/shard_map/reduce_scatter | solution.py:697
  349.8 38.0 %collective-permute-start.10 = (bf16[640,1280]{0,1:T(8,128)(2,1)S(1)}, bf16[640,1280]{0,1:T(8,128)(2,1)}, u32[]{:S(2)}, u32[]{:S(2)}) collective-permute-start(bf16[640,1280]{0,1:T(8,128)(2,1)S(1)} %fusion.9), channel_id=1, source_target_pairs={{0,2},{1,3},{2,0},{3,1},{4,6},{5,7},{6,4},{7,5},{8,10},{9,11},{10,... | collective-permute-start | bytes 4915208 | tf_op jit(solution)/shard_map/ppermute | solution.py:551
  400.8 37.0 %collective-permute-start.12 = (bf16[640,1280]{0,1:T(8,128)(2,1)S(1)}, bf16[640,1280]{0,1:T(8,128)(2,1)S(1)}, u32[]{:S(2)}, u32[]{:S(2)}) collective-permute-start(bf16[640,1280]{0,1:T(8,128)(2,1)S(1)} %multiply_convert_fusion.4), channel_id=1, source_target_pairs={{0,2},{1,3},{2,0},{3,1},{4,6},{5,7},{6,4},{7,5},{8,10},{9,11},{10,... | collective-permute-start | bytes 4915208 | tf_op jit(solution)/shard_map/ppermute | solution.py:551
  402.2 35.6 %collective-permute-start.11 = (bf16[640,1280]{0,1:T(8,128)(2,1)S(1)}, bf16[640,1280]{0,1:T(8,128)(2,1)S(1)}, u32[]{:S(2)}, u32[]{:S(2)}) collective-permute-start(bf16[640,1280]{0,1:T(8,128)(2,1)S(1)} %multiply_convert_fusion.4), channel_id=1, source_target_pairs={{0,1},{1,0},{2,3},{3,2},{4,5},{5,4},{6,7},{7,6},{8,9},{9,8},{10,11... | collective-permute-start | bytes 4915208 | tf_op jit(solution)/shard_map/ppermute | solution.py:551
  512.9 37.9 %collective-permute-start.15 = (bf16[640,1280]{0,1:T(8,128)(2,1)S(1)}, bf16[640,1280]{0,1:T(8,128)(2,1)S(1)}, u32[]{:S(2)}, u32[]{:S(2)}) collective-permute-start(bf16[640,1280]{0,1:T(8,128)(2,1)S(1)} %fusion.6), channel_id=1, source_target_pairs={{0,2},{1,3},{2,0},{3,1},{4,6},{5,7},{6,4},{7,5},{8,10},{9,11},{10,... | collective-permute-start | bytes 4915208 | tf_op jit(solution)/shard_map/ppermute | solution.py:551
  556.5 37.1 %collective-permute-start.17 = (bf16[640,1280]{0,1:T(8,128)(2,1)S(1)}, bf16[640,1280]{0,1:T(8,128)(2,1)S(1)}, u32[]{:S(2)}, u32[]{:S(2)}) collective-permute-start(bf16[640,1280]{0,1:T(8,128)(2,1)S(1)} %multiply_convert_fusion.3), channel_id=1, source_target_pairs={{0,2},{1,3},{2,0},{3,1},{4,6},{5,7},{6,4},{7,5},{8,10},{9,11},{10,... | collective-permute-start | bytes 4915208 | tf_op jit(solution)/shard_map/ppermute | solution.py:551
  558.0 35.6 %collective-permute-start.16 = (bf16[640,1280]{0,1:T(8,128)(2,1)S(1)}, bf16[640,1280]{0,1:T(8,128)(2,1)S(1)}, u32[]{:S(2)}, u32[]{:S(2)}) collective-permute-start(bf16[640,1280]{0,1:T(8,128)(2,1)S(1)} %multiply_convert_fusion.3), channel_id=1, source_target_pairs={{0,1},{1,0},{2,3},{3,2},{4,5},{5,4},{6,7},{7,6},{8,9},{9,8},{10,11... | collective-permute-start | bytes 4915208 | tf_op jit(solution)/shard_map/ppermute | solution.py:551
  661.2 148.9 %reduce-scatter.11.cloned.1.call-start = ((), (), s32[]{:S(2)}) async-start(), calls=%async_computation.14 | async-start | bytes 3686400 | tf_op jit(solution)/shard_map/reduce_scatter | solution.py:683
  677.1 256.5 %all-reduce.4.cloned.1.call-start = ((), (), s32[]{:S(2)}) async-start(), calls=%async_computation.15 | async-start | bytes 131072
  679.2 316.3 %reduce-scatter.7.cloned.1.call-start = ((), (), s32[]{:S(2)}) async-start(), calls=%async_computation.12 | async-start | bytes 921600 | tf_op jit(solution)/shard_map/reduce_scatter | solution.py:696
  685.0 435.3 %reduce-scatter.9.cloned.1.call-start = ((), (), s32[]{:S(2)}) async-start(), calls=%async_computation.13 | async-start | bytes 7372800 | tf_op jit(solution)/shard_map/reduce_scatter | solution.py:686
  729.2 395.5 %collective-permute-start.20 = (bf16[640,1280]{0,1:T(8,128)(2,1)}, bf16[640,1280]{0,1:T(8,128)(2,1)}, u32[]{:S(2)}, u32[]{:S(2)}) collective-permute-start(bf16[640,1280]{0,1:T(8,128)(2,1)} %fusion.3), channel_id=1, source_target_pairs={{0,2},{1,3},{2,0},{3,1},{4,6},{5,7},{6,4},{7,5},{8,10},{9,11},{10,... | collective-permute-start | bytes 4915208 | tf_op jit(solution)/shard_map/ppermute | solution.py:551
  731.3 389.0 %all-to-all-start.2 = ((bf16[4,40,960]{2,1,0:T(8,128)(2,1)}), bf16[4,40,960]{2,1,0:T(8,128)(2,1)}, u32[]{:S(2)}, u32[]{:S(2)}) async-start(bf16[4,40,960]{2,1,0:T(8,128)(2,1)} %bitcast.71), calls=%async_computation.3 | async-start | bytes 655360 | tf_op jit(solution)/shard_map/all_to_all | solution.py:716
  1120.3 19.2 %all-to-all-start.3 = ((bf16[4,40,2560]{2,1,0:T(8,128)(2,1)}), bf16[4,40,2560]{2,1,0:T(8,128)(2,1)}, u32[]{:S(2)}, u32[]{:S(2)}) async-start(bf16[4,40,2560]{2,1,0:T(8,128)(2,1)} %bitcast.65), calls=%async_computation.6 | async-start | bytes 1638400 | tf_op jit(solution)/shard_map/all_to_all | solution.py:714
  (58 other events, 1551.8 us)
Sparse Core Ops, SparseCore 0:
  27.6 53.5 all-gather.3
  115.5 106.0 all-gather.5
  262.8 62.0 all-gather.7
  661.3 69.4 reduce-scatter.4
  734.2 75.5 reduce-scatter.10
  816.7 116.8 all-reduce.3
  937.9 57.6 reduce-scatter.6
  999.2 121.0 reduce-scatter.8

commit v2 on v1

--- a/solution.py
+++ b/solution.py
@@ -491,6 +491,268 @@
     )(perm, qkv, scale, sums, mixed, g_mixed)
 
 
+MESH = pl.DeviceIdType.MESH
+
+
+def ring_place():
+    dp = lax.axis_index("dp")
+    z, y = dp // 2, dp % 2
+    return z + y * (7 - 2 * z)
+
+
+def ring_dp(place):
+    place = (place + 16) % 8
+    y = place // 4
+    return 2 * (place + y * (7 - 2 * place)) + y
+
+
+def greet(peers):
+    barrier = pltpu.get_barrier_semaphore()
+    for peer in peers:
+        pl.semaphore_signal(barrier, inc=1, device_id=peer, device_id_type=MESH)
+    pl.semaphore_wait(barrier, len(peers))
+
+
+def group_peers():
+    me = lax.axis_index("fsdp")
+    core = 1 - 2 * (me % 2)
+    chip = 2 - 4 * (me // 2)
+    return {"fsdp": me + core}, {"fsdp": me + chip}, {"fsdp": me + core + chip}
+
+
+def send(src, dst, send_sem, recv_sem, peer):
+    return pltpu.make_async_remote_copy(
+        src_ref=src, dst_ref=dst, send_sem=send_sem, recv_sem=recv_sem, device_id=peer, device_id_type=MESH
+    )
+
+
+def first_kernel(states, qkv_send, extra, out_piece, tokens, weights, out_w, own_sem, tok_send, tok_recv,
+                 a2a_send, a2a_recv, ring_send, ring_recv):
+    me, dp = lax.axis_index("fsdp"), lax.axis_index("dp")
+    place = ring_place()
+    sibling, across, corner = group_peers()
+    right, left = {"dp": ring_dp(place + 1)}, {"dp": ring_dp(place - 1)}
+    greet([sibling, across, corner, right, left])
+    rows = states.shape[0] // 2
+    halves = [pl.ds(0, rows), pl.ds(rows, rows)]
+
+    exchange = []
+    for i, peer in enumerate((sibling, across, corner)):
+        copy = send(qkv_send.at[peer["fsdp"]], weights.at[dp, me], a2a_send.at[i], a2a_recv.at[i], peer)
+        copy.start()
+        exchange.append(copy)
+    far = []
+    for i, half in enumerate(halves):
+        copy = send(states.at[half], tokens.at[2, half], tok_send.at[i], tok_recv.at[i], across)
+        copy.start()
+        far.append(copy)
+    near = send(states, tokens.at[1], tok_send.at[2], tok_recv.at[2], sibling)
+    near.start()
+    own = pltpu.make_async_copy(states, tokens.at[0], own_sem.at[0])
+    own.start()
+    weights[dp, me] = qkv_send[me]
+    out_w[dp] = out_piece[...]
+    for copy in exchange:
+        copy.wait()
+    lanes = pl.ds(weights.shape[3] - 128, 128)
+    weights[dp, :, :, lanes] = weights[dp, :, :, lanes] + extra[...]
+
+    def hop(step, carry):
+        to_right, to_left = ring_dp(place - step), ring_dp(place + step)
+        copies = [
+            send(weights.at[to_right, pl.ds(0, 2)], weights.at[to_right, pl.ds(0, 2)],
+                 ring_send.at[0, step], ring_recv.at[0, step], right),
+            send(weights.at[to_left, pl.ds(2, 2)], weights.at[to_left, pl.ds(2, 2)],
+                 ring_send.at[1, step], ring_recv.at[1, step], left),
+            send(out_w.at[to_right, :, pl.ds(0, 640)], out_w.at[to_right, :, pl.ds(0, 640)],
+                 ring_send.at[2, step], ring_recv.at[2, step], right),
+            send(out_w.at[to_left, :, pl.ds(640, 640)], out_w.at[to_left, :, pl.ds(640, 640)],
+                 ring_send.at[3, step], ring_recv.at[3, step], left),
+        ]
+        for copy in copies:
+            copy.start()
+        for copy in copies:
+            copy.wait()
+        return carry
+
+    lax.fori_loop(0, 4, hop, 0)
+    passed = []
+    for i, half in enumerate(halves):
+        far[i].wait()
+        copy = send(tokens.at[2, half], tokens.at[3, half], tok_send.at[3 + i], tok_recv.at[3 + i], sibling)
+        copy.start()
+        passed.append(copy)
+    lax.fori_loop(4, 7, hop, 0)
+    near.wait()
+    own.wait()
+    for copy in passed:
+        copy.wait()
+
+
+def first_exchange(states, qkv_send, extra, out_piece):
+    tps, rows_w, width = qkv_send.shape
+    vmem, hbm = pl.BlockSpec(memory_space=pltpu.VMEM), pl.BlockSpec(memory_space=pl.ANY)
+    return pl.pallas_call(
+        first_kernel,
+        in_specs=[hbm, vmem, vmem, vmem],
+        out_specs=[hbm, vmem, vmem],
+        out_shape=[
+            jax.ShapeDtypeStruct((4,) + states.shape, BF),
+            jax.ShapeDtypeStruct((8, tps, rows_w, width), BF),
+            jax.ShapeDtypeStruct((8,) + out_piece.shape, BF),
+        ],
+        scratch_shapes=[
+            pltpu.SemaphoreType.DMA((1,)),
+            pltpu.SemaphoreType.DMA((5,)),
+            pltpu.SemaphoreType.DMA((5,)),
+            pltpu.SemaphoreType.DMA((3,)),
+            pltpu.SemaphoreType.DMA((3,)),
+            pltpu.SemaphoreType.DMA((4, 7)),
+            pltpu.SemaphoreType.DMA((4, 7)),
+        ],
+        compiler_params=pltpu.CompilerParams(
+            collective_id=1, has_side_effects=True, vmem_limit_bytes=32 << 20
+        ),
+        cost_estimate=pl.CostEstimate(flops=0, bytes_accessed=150 << 20, transcendentals=0),
+        name="first_exchange",
+    )(states, qkv_send, extra, out_piece)
+
+
+def last_kernel(share, base, grads, vectors, g_states, qkv_rows, out_rows, vec_own,
+                core_buf, far_buf, x_buf, ring_buf, vec_buf, row_buf, vec_part, vec_in,
+                core_send, core_recv, x_send, x_recv, ring_send, ring_recv, a2a_send, a2a_recv):
+    me, dp = lax.axis_index("fsdp"), lax.axis_index("dp")
+    place = ring_place()
+    sibling, across, corner = group_peers()
+    right, left = {"dp": ring_dp(place + 1)}, {"dp": ring_dp(place - 1)}
+    greet([sibling, across, corner, right, left])
+    half = grads.shape[1] // 2
+    rows = share.shape[1] // 4
+
+    def first_hop():
+        to_right, to_left = ring_dp(place - 1), ring_dp(place + 1)
+        return [
+            send(grads.at[to_right, pl.ds(0, half)], ring_buf.at[0, 0], ring_send.at[0, 0], ring_recv.at[0, 0], right),
+            send(grads.at[to_left, pl.ds(half, half)], ring_buf.at[1, 0], ring_send.at[1, 0], ring_recv.at[1, 0], left),
+            send(vectors.at[to_right], vec_buf.at[0], ring_send.at[2, 0], ring_recv.at[2, 0], right),
+        ]
+
+    def later_hop(step):
+        return [
+            send(ring_buf.at[0, step - 1], ring_buf.at[0, step], ring_send.at[0, step], ring_recv.at[0, step], right),
+            send(ring_buf.at[1, step - 1], ring_buf.at[1, step], ring_send.at[1, step], ring_recv.at[1, step], left),
+            send(vec_buf.at[step - 1], vec_buf.at[step], ring_send.at[2, step], ring_recv.at[2, step], right),
+        ]
+
+    core = [
+        send(share.at[3], core_buf.at[0], core_send.at[0], core_recv.at[0], sibling),
+        send(share.at[1], core_buf.at[1], core_send.at[1], core_recv.at[1], sibling),
+    ]
+    core[0].start()
+    opening = first_hop()
+    for copy in opening:
+        copy.start()
+    core[1].start()
+    core[0].wait()
+    far = []
+    for i in range(4):
+        span = pl.ds(i * rows, rows)
+        far_buf[span] = (share[2, span].astype(F32) + core_buf[0, span].astype(F32)).astype(BF)
+        copy = send(far_buf.at[span], x_buf.at[span], x_send.at[i], x_recv.at[i], across)
+        copy.start()
+        far.append(copy)
+    for copy in opening:
+        copy.wait()
+
+    def hop(step, carry):
+        to_right, to_left = ring_dp(place - 1 - step), ring_dp(place + 1 + step)
+        ring_buf[0, step - 1] = (
+            ring_buf[0, step - 1].astype(F32) + grads[to_right, pl.ds(0, half)].astype(F32)
+        ).astype(BF)
+        ring_buf[1, step - 1] = (
+            ring_buf[1, step - 1].astype(F32) + grads[to_left, pl.ds(half, half)].astype(F32)
+        ).astype(BF)
+        vec_buf[step - 1] = vec_buf[step - 1] + vectors[to_right]
+        copies = later_hop(step)
+        for copy in copies:
+            copy.start()
+        for copy in copies:
+            copy.wait()
+        return carry
+
+    lax.fori_loop(1, 7, hop, 0)
+    quarter = half // 2
+    for side in range(2):
+        total = ring_buf[side, 6].astype(F32) + grads[dp, pl.ds(side * half, half)].astype(F32)
+        for i in range(2):
+            piece = total[i * quarter : (i + 1) * quarter]
+            row_buf[2 * side + i] = piece.astype(BF)
+            out_rows[2 * side + i] = piece
+    vec_part[...] = vec_buf[6] + vectors[dp]
+    exchange = []
+    for i, peer in enumerate((sibling, across, corner)):
+        to = peer["fsdp"]
+        copies = [
+            send(row_buf.at[to], qkv_rows.at[me], a2a_send.at[i], a2a_recv.at[i], peer),
+            send(vec_part.at[to], vec_in.at[me], a2a_send.at[3 + i], a2a_recv.at[3 + i], peer),
+        ]
+        for copy in copies:
+            copy.start()
+        exchange += copies
+    qkv_rows[me] = row_buf[me]
+    vec_in[me] = vec_part[me]
+    core[1].wait()
+    for i in range(4):
+        span = pl.ds(i * rows, rows)
+        far[i].wait()
+        g_states[span] = base[span] + (
+            share[0, span].astype(F32) + core_buf[1, span].astype(F32) + x_buf[span].astype(F32)
+        )
+    for copy in exchange:
+        copy.wait()
+    vec_own[...] = vec_in[0] + vec_in[1] + vec_in[2] + vec_in[3]
+
+
+def last_exchange(share, base, grads, vectors):
+    half, cols = grads.shape[1] // 2, grads.shape[2]
+    rows_w = grads.shape[1] // 4
+    vmem = pl.BlockSpec(memory_space=pltpu.VMEM)
+    return pl.pallas_call(
+        last_kernel,
+        in_specs=[vmem] * 4,
+        out_specs=[vmem] * 4,
+        out_shape=[
+            jax.ShapeDtypeStruct(base.shape, F32),
+            jax.ShapeDtypeStruct((4, rows_w, cols), BF),
+            jax.ShapeDtypeStruct((4, rows_w, cols), F32),
+            jax.ShapeDtypeStruct(vectors.shape[2:], F32),
+        ],
+        scratch_shapes=[
+            pltpu.VMEM((2,) + share.shape[1:], BF),
+            pltpu.VMEM(share.shape[1:], BF),
+            pltpu.VMEM(share.shape[1:], BF),
+            pltpu.VMEM((2, 7, half, cols), BF),
+            pltpu.VMEM((7,) + vectors.shape[1:], F32),
+            pltpu.VMEM((4, rows_w, cols), BF),
+            pltpu.VMEM(vectors.shape[1:], F32),
+            pltpu.VMEM(vectors.shape[1:], F32),
+            pltpu.SemaphoreType.DMA((2,)),
+            pltpu.SemaphoreType.DMA((2,)),
+            pltpu.SemaphoreType.DMA((4,)),
+            pltpu.SemaphoreType.DMA((4,)),
+            pltpu.SemaphoreType.DMA((3, 7)),
+            pltpu.SemaphoreType.DMA((3, 7)),
+            pltpu.SemaphoreType.DMA((6,)),
+            pltpu.SemaphoreType.DMA((6,)),
+        ],
+        compiler_params=pltpu.CompilerParams(
+            collective_id=2, has_side_effects=True, vmem_limit_bytes=52 << 20
+        ),
+        cost_estimate=pl.CostEstimate(flops=0, bytes_accessed=150 << 20, transcendentals=0),
+        name="last_exchange",
+    )(share, base, grads, vectors)
+
+
 def order_kernel(where_ref, parent_ref, perm_ref, branch_ref, leaf_ref):
     base, me = where_ref[0], where_ref[1]
 
@@ -599,8 +861,6 @@
     group_base = lax.axis_index("dp") * NB
     perm = tree_order(jnp.stack((group_base, me)).astype(jnp.int32), parent_ids)
 
-    tokens = gather_tokens(states)
-
     count = jnp.sum(valid_mask)
     first_row = jnp.arange(rows_w, dtype=jnp.int32) == 0
     small = jnp.stack(
@@ -613,16 +873,18 @@
         ),
         axis=1,
     )
+    small = jnp.pad(small, ((0, 0), (0, 59)))
     qkv_send = jnp.concatenate(
         [w.reshape(rows_w, tps, cols).transpose(1, 0, 2) for w in (w_query, w_key, w_value)]
-        + [jnp.broadcast_to(small[None], (tps, rows_w, 5))],
+        + [jnp.broadcast_to(small[None], (tps, rows_w, 64))],
         axis=2,
     )
-    qkv_group = lax.all_to_all(qkv_send, "fsdp", 0, 0, tiled=True).reshape(tps * rows_w, 3 * cols + 5)
-    qkv_group = jnp.concatenate(
-        (qkv_group, up_scale[:, None], gate_scale[:, None], jnp.zeros((tps * rows_w, 57), BF)), axis=1
-    )
-    first = lax.all_gather(qkv_group, "dp", axis=0, tiled=True)
+    extra = jnp.pad(jnp.stack((up_scale, gate_scale), axis=1), ((0, 0), (69, 57))).reshape(tps, rows_w, 128)
+    spread = [(j, tps * (j % dps) + j // dps) for j in range(dps * tps)]
+    tokens, first, w_o = first_exchange(states, qkv_send, extra, lax.ppermute(w_out, both, spread))
+    tokens = tokens.reshape(TOK, D)
+    first = first.reshape(D, 1024)
+    w_o = w_o.reshape(cols, D)
     ug_send = jnp.concatenate(
         [
             w.reshape(rows_w, dps, tps, ff_rows).transpose(2, 0, 1, 3).reshape(tps, rows_w, hid)
@@ -631,10 +893,7 @@
         axis=2,
     )
     ug_group = lax.all_to_all(ug_send, "fsdp", 0, 0, tiled=True).reshape(tps * rows_w, 2 * hid)
-    spread = [(j, tps * (j % dps) + j // dps) for j in range(dps * tps)]
-    out_mine = lax.ppermute(w_out, both, spread)
     w_ug = lax.all_gather(ug_group, "dp", axis=0, tiled=True)
-    w_o = lax.all_gather(out_mine, "dp", axis=0, tiled=True)
     w_d = lax.all_gather(w_down, "dp", axis=0, tiled=True)
 
     w_qkv = first[:, : 3 * cols]
@@ -663,8 +922,6 @@
     down_unit, down_inv = unit_rows(down)
     result, result_inv = unit_rows(hidden + rate_mlp * (down_unit - hidden))
     loss_local = jnp.sum(mask_f[:, None] * (result - teacher) ** 2)
-    loss_parts = lax.all_gather(jnp.broadcast_to(loss_local, (1, 128)), both, axis=0, tiled=True)
-    loss = jnp.sum(loss_parts[:, 0]) / valid_count
 
     g_result = 2.0 * mask_f[:, None] * (result - teacher) / valid_count
     g_last = unit_back(g_result, result, result_inv)
@@ -679,11 +936,16 @@
     g_ug = jnp.concatenate(
         ((g_upscaled * scale_up).astype(BF), (g_gated * scale_gate * root_width).astype(BF)), axis=1
     )
-    g_hidden = g_last * (1.0 - rate_mlp) + reduce_tokens(dot(g_ug, w_ug, (1, 1)))
-    grad_down = lax.psum_scatter(
-        dot(act, g_down_all, (0, 0)).astype(BF), "dp", scatter_dimension=0, tiled=True
-    ).astype(F32)
-    grad_ug = lax.psum_scatter(dot(hidden_all, g_ug, (0, 0)).astype(BF), "dp", scatter_dimension=0, tiled=True)
+    back_hidden, part_down, part_ug = lax.optimization_barrier(
+        (
+            reduce_tokens(dot(g_ug, w_ug, (1, 1))),
+            dot(act, g_down_all, (0, 0)).astype(BF),
+            dot(hidden_all, g_ug, (0, 0)).astype(BF),
+        )
+    )
+    g_hidden = g_last * (1.0 - rate_mlp) + back_hidden
+    grad_ug = lax.psum_scatter(part_ug, "dp", scatter_dimension=0, tiled=True)
+    grad_down = lax.psum_scatter(part_down, "dp", scatter_dimension=0, tiled=True).astype(F32)
 
     g_pre = unit_back(g_hidden, hidden, hidden_inv)
     g_rate_attn = jnp.sum(g_pre * (attn_unit - inputs), axis=0)
@@ -692,10 +954,6 @@
     g_mixed = dot(w_o, g_attn_all, (1, 1)).astype(BF)
     g_qkv, g_scale = attn_bwd(perm, qkv, scale_qk, sums, mixed, g_mixed)
     g_qkv = g_qkv.reshape(3 * cols, TOK)
-    grad_states = g_pre * (1.0 - rate_attn) + reduce_tokens(dot(g_qkv, w_qkv, (0, 1)))
-    grad_out = lax.psum_scatter(dot(mixed, g_attn_all, (1, 0)).astype(BF), "dp", scatter_dimension=0, tiled=True)
-    grad_qkv = lax.psum_scatter(dot(tokens, g_qkv, (0, 1)).astype(BF), "dp", scatter_dimension=0, tiled=True)
-
     slot = jnp.arange(tps, dtype=jnp.int32) == me
     qk_rows = jnp.where(slot[:, None], g_scale.reshape(1, cols), 0.0).reshape(dps * tps, rows_w)
     ff_terms = [
@@ -705,21 +963,26 @@
     vectors = jnp.concatenate(
         [g_rate_attn.reshape(dps * tps, rows_w), g_rate_mlp.reshape(dps * tps, rows_w), qk_rows]
         + ff_terms
-        + [jnp.zeros((dps * tps, 512 - 3 * rows_w - 2 * ff_rows), F32)],
+        + [jnp.broadcast_to(loss_local, (dps * tps, 512 - 3 * rows_w - 2 * ff_rows))],
         axis=1,
-    )
-    vector_share = lax.psum_scatter(vectors, both, scatter_dimension=0, tiled=True)[0]
-
-    grad_out = lax.ppermute(grad_out, both, [(b, a) for a, b in spread]).astype(F32)
+    ).reshape(dps, tps, 4, 128)
+    share = dot(g_qkv, w_qkv, (0, 1)).astype(BF).reshape(tps, TOK // tps, D)
+    part_out = dot(mixed, g_attn_all, (1, 0)).astype(BF).reshape(dps, rows_w, tps, cols).transpose(0, 2, 1, 3)
+    part_qkv = dot(tokens, g_qkv, (0, 1)).astype(BF).reshape(dps, tps * rows_w, 3 * cols)
+    parts = jnp.concatenate((part_qkv, part_out.reshape(dps, tps * rows_w, cols)), axis=2)
+    grad_states, qkv_back, out_back, vector_share = last_exchange(share, g_pre * (1.0 - rate_attn), parts, vectors)
+    vector_share = vector_share.reshape(512)
+    out_back = out_back[:, :, 3 * cols :].transpose(1, 0, 2).reshape(rows_w, D)
+    grad_out = lax.ppermute(out_back, both, [(b, a) for a, b in spread])
     ug_back = lax.all_to_all(grad_ug, "fsdp", 0, 0, tiled=True).reshape(tps, rows_w, 2, dps, ff_rows)
     ug_back = ug_back.transpose(2, 1, 3, 0, 4).reshape(2, rows_w, FF).astype(F32)
-    qkv_back = lax.all_to_all(grad_qkv, "fsdp", 0, 0, tiled=True).reshape(tps, rows_w, 3, cols)
+    qkv_back = qkv_back[:, :, : 3 * cols].reshape(tps, rows_w, 3, cols)
     qkv_back = qkv_back.transpose(2, 1, 0, 3).reshape(3, rows_w, D).astype(F32)
     cuts = (0, rows_w, 2 * rows_w, 3 * rows_w, 3 * rows_w + ff_rows, 3 * rows_w + 2 * ff_rows)
     v = [vector_share[a:b] for a, b in zip(cuts, cuts[1:])]
     return (
         result.astype(BF),
-        loss,
+        vector_share[-1] / valid_count,
         grad_states,
         qkv_back[0],
         qkv_back[1],

time: 1170 us -> 837 us (0.72)
  waiting for transfers between devices: 598 us -> 260 us
  Pallas kernels: 79.8 us -> 214 us
  blocking collectives: 102 us -> 0 us
  starting transfers between devices: 37.8 us -> 24 us
    reduce_scatter x4 -> x2, waiting for transfers between devices: 173 us -> 0.01 us  [the longest x1 0.01 us: local(): grad_ug = lax.psum_scatter(part_ug, 'dp', scatter_dimension=0, tiled=True)]
    pallas_call x0 -> x2, Pallas kernels: none -> 134 us  [the longest x1 74.4 us: last_exchange(): pl.pallas_call(last_kernel, in_specs=[vmem] * 4, out_specs=[vmem] * 4, ou...]
    unnamed x9 -> x4, waiting for transfers between devices: 122 us -> 0.07 us
    unnamed x1 -> x0, blocking collectives: 69.8 us -> none
    ppermute x20 -> x15, waiting for transfers between devices: 272 us -> 222 us  [swap(): return lax.ppermute(value, 'fsdp', [(i, i ^ step) for i in range(4)])]
    all_gather x1 -> x0, blocking collectives: 32.2 us -> none  [local(): w_o = lax.all_gather(out_mine, 'dp', axis=0, tiled=True)]
    unnamed x105 -> x107, local copies, waits for them, and re-layouts: 34.6 us -> 20.3 us
  transfers between devices with their start and end apart: 34 -> 23, of which waited for: 20 -> 14; matrix products, arithmetic and copies ran while one was open for 15% -> 23% of each run, Pallas kernels for 3% -> 26%
where the time goes in v2:
time: 837 us; the launch traced here: 833 us
  waiting for transfers between devices  260 us (31%)
  Pallas kernels  214 us (26%)
  matrix products  184 us (22%)
  other arithmetic  70.6 us (8%)
  local copies, waits for them, and re-layouts  60 us (7%)
  starting transfers between devices  24 us (3%)
  between operations  20.7 us (2%)
    ppermute x15, waiting for transfers between devices, swap(): return lax.ppermute(value, 'fsdp', [(i, i ^ step) for i in range(4)])  222 us
    dot_general x12, matrix products, dot(): lax.dot_general(left, right, ((contract[:1], contract[1:]), ((), ())), pr...  184 us
    pallas_call x1, Pallas kernels, last_exchange(): pl.pallas_call(last_kernel, in_specs=[vmem] * 4, out_specs=[vmem] * 4, ou...  74.4 us
    pallas_call x1, Pallas kernels, first_exchange(): pl.pallas_call(first_kernel, in_specs=[hbm, vmem, vmem, vmem], out_specs=...  59.8 us
    pallas_call x1, Pallas kernels, attn_bwd(): pl.pallas_call(bwd_kernel, grid_spec=pltpu.PrefetchScalarGridSpec(num_sca...  48.3 us
    pallas_call x1, Pallas kernels, attn_fwd(): pl.pallas_call(fwd_kernel, grid_spec=pltpu.PrefetchScalarGridSpec(num_sca...  24.7 us
    all_gather x1, waiting for transfers between devices, local(): w_d = lax.all_gather(w_down, 'dp', axis=0, tiled=True)  23 us
    unnamed x107, local copies, waits for them, and re-layouts  20.3 us
  transfers between devices with their start and end apart: 23, of which 14 were waited for; matrix products, arithmetic and copies ran while one was open for 23% of the time, Pallas kernels for 26%

profile of v2, /device:TPU:4, one launch (start us, length us, event | category | flops | bytes accessed | tf_op | source)
XLA Modules:
  0.0 832.5 jit_solution(16956168263611106833)
XLA Ops:
  33.7 59.8 %first_exchange.1 = (bf16[4,640,1280]{2,1,0:T(8,128)(2,1)S(1)}, bf16[8,4,40,1024]{3,2,1,0:T(8,128)(2,1)S(1)}, bf16[8,40,1280]{2,1,0:T(8,128)(2,1)S(1)}) custom-call(bf16[640,1280]{1,0:T(8,128)(2,1)S(1)} %copy-done, bf16[4,40,1024]{2,1,0:T(8,128)(2,1)S(1)} %pad_maximum_fusion.17.qkv_send, bf16[4,40,128]{2,1,0:T(8,128)(2,1)S(1)} %bitcast.69, ...), custom_call_target="tpu_custom_call" | custom-call | bytes 157286400 | tf_op jit(solution)/shard_map/first_exchange/pallas_call | solution.py:595
  103.6 11.7 %fusion.33.qkv_ref = f32[3,320,2560]{2,1,0:T(8,128)} fusion(bf16[3,320,1280]{2,1,0:T(8,128)(2,1)} %bitcast.82, bf16[2560,1280,1]{1,0,2:T(8,128)(2,1)} %bitcast.73), kind=kOutput, calls=%fused_computation.118 | convolution fusion | flops 6291456000 | bytes 18841600 | tf_op jit(solution)/shard_map/dot_general | solution.py:831
  115.4 24.7 %tree_attention.1 = (bf16[320,2560]{1,0:T(8,128)(2,1)S(1)}, f32[5,8,2560]{2,1,0:T(8,128)S(1)}) custom-call(s32[20]{0:T(128)S(1)} %copy-done.9, f32[3,320,2560]{2,1,0:T(8,128)} %fusion.33.qkv_ref, f32[5,64,1]{2,1,0:T(8,128)S(1)} %reshape.243.scale_ref), custom_call_target="tpu_custom_call" | custom-call | flops 3523215360 | bytes 12582912 | tf_op jit(solution)/shard_map/tree_attention/pallas_call | solution.py:372
  140.1 6.7 fusion.30
  161.5 36.0 %collective-permute-done.2 = bf16[640,1280]{1,0:T(8,128)(2,1)S(1)} collective-permute-done((bf16[640,1280]{1,0:T(8,128)(2,1)S(1)}, bf16[640,1280]{1,0:T(8,128)(2,1)S(1)}, u32[]{:S(2)}, u32[]{:S(2)}) %collective-permute-start.2) | collective-permute-done | bytes 1638432 | tf_op jit(solution)/shard_map/ppermute | solution.py:813
  205.2 36.0 %collective-permute-done.4 = bf16[640,1280]{1,0:T(8,128)(2,1)} collective-permute-done((bf16[640,1280]{1,0:T(8,128)(2,1)S(1)}, bf16[640,1280]{1,0:T(8,128)(2,1)}, u32[]{:S(2)}, u32[]{:S(2)}) %collective-permute-start.4) | collective-permute-done | bytes 1638432 | tf_op jit(solution)/shard_map/ppermute | solution.py:813
  249.9 26.8 %fusion.10 = f32[2560,2560]{1,0:T(8,128)} fusion(bf16[1280,2560]{1,0:T(8,128)(2,1)} %all-gather.3.cloned.1.call-done, bf16[640,1280]{1,0:T(8,128)(2,1)} %collective-permute-done.5, bf16[640,1280]{1,0:T(8,128)(2,1)} %collective-permute-done.4, bf16[640,1280]{1,0:T(8,128)(2,1)} %collective-permute-done.3, bf16[640,1280]{1,0:T(8,128)(2,1)S(1)} %multiply_convert_fusion.6), kind=kOutput, calls=%fused_computation.66 | convolution fusion | flops 16803430400 | bytes 39321600 | tf_op jit(solution)/shard_map/dot_general | solution.py:831
  276.7 12.5 %multiply_convert_fusion.2 = bf16[2560,1280]{1,0:T(8,128)(2,1)} fusion(f32[2560,2560]{1,0:T(8,128)} %fusion.10, f32[1280]{0:T(1024)S(1)} %get-tuple-element.54, f32[1280]{0:T(1024)S(1)} %get-tuple-element.53), kind=kLoop, calls=%fused_computation.6 | loop fusion | flops 29491200 | bytes 32778240 | tf_op jit(solution)/shard_map/convert_element_type | solution.py:920
  289.2 23.0 %all-gather.5.cloned.1.call-done = bf16[1280,1280]{1,0:T(8,128)(2,1)} async-done(((bf16[160,1280]{1,0:T(8,128)(2,1)}), bf16[1280,1280]{1,0:T(8,128)(2,1)}) %all-gather.5.cloned.1.call-update) | async-done | bytes 3276816 | tf_op jit(solution)/shard_map/all_gather | solution.py:897
  312.2 12.2 %fusion.31 = (bf16[2560,1280]{1,0:T(8,128)(2,1)S(1)}, f32[2560,1280]{1,0:T(8,128)S(1)}) fusion(bf16[2560,1280]{1,0:T(8,128)(2,1)} %multiply_convert_fusion.2, bf16[1280,1280]{1,0:T(8,128)(2,1)} %all-gather.5.cloned.1.call-done), kind=kOutput, calls=%fused_computation.116 | convolution fusion | flops 8391884800 | bytes 29491200 | tf_op jit(solution)/shard_map/dot_general | solution.py:831
  335.3 35.2 %collective-permute-done.7 = bf16[640,1280]{1,0:T(8,128)(2,1)} collective-permute-done((bf16[640,1280]{1,0:T(8,128)(2,1)S(1)}, bf16[640,1280]{1,0:T(8,128)(2,1)}, u32[]{:S(2)}, u32[]{:S(2)}) %collective-permute-start.7) | collective-permute-done | bytes 1638432 | tf_op jit(solution)/shard_map/ppermute | solution.py:813
  385.3 35.5 %collective-permute-done.9 = bf16[640,1280]{1,0:T(8,128)(2,1)S(1)} collective-permute-done((bf16[640,1280]{1,0:T(8,128)(2,1)S(1)}, bf16[640,1280]{1,0:T(8,128)(2,1)S(1)}, u32[]{:S(2)}, u32[]{:S(2)}) %collective-permute-start.9) | collective-permute-done | bytes 1638432 | tf_op jit(solution)/shard_map/ppermute | solution.py:813
  424.4 28.6 %multiply_reduce_fusion = (f32[1280]{0:T(1024)S(1)}, f32[1280]{0:T(1024)S(1)}, f32[2560,1280]{1,0:T(8,128)}, bf16[2560,1280]{1,0:T(8,128)(2,1)}) fusion(f32[2560,2560]{1,0:T(8,128)} %fusion.10, f32[1280]{0:T(1024)S(1)} %get-tuple-element.53, f32[1280]{0:T(1024)S(1)} %get-tuple-element.54, bf16[1280,1280]{1,0:T(8,128)(2,1)} %all-gather.5.cloned.1.call-done, ...), kind=kOutput, calls=%fused_computation.1 | convolution fusion | flops 8483633152 | bytes 55726080 | tf_op jit(solution)/shard_map/dot_general | solution.py:831
  453.0 8.8 %multiply_convert_fusion = bf16[2560,1280]{1,0:T(8,128)(2,1)} fusion(f32[2560,1280]{1,0:T(8,128)} %get-tuple-element.57, f32[1280]{0:T(1024)S(1)} %get-tuple-element.53), kind=kLoop, calls=%fused_computation.3 | loop fusion | flops 9830400 | bytes 19665920 | tf_op jit(solution)/shard_map/convert_element_type | solution.py:937
  461.8 24.6 %fusion.32 = (bf16[2560,1280]{1,0:T(8,128)(2,1)}, f32[2560,1280]{1,0:T(8,128)}) fusion(bf16[1280,2560]{1,0:T(8,128)(2,1)} %all-gather.3.cloned.1.call-done, bf16[2560,1280]{1,0:T(8,128)(2,1)} %multiply_convert_fusion, bf16[2560,1280]{1,0:T(8,128)(2,1)} %get-tuple-element.69), kind=kOutput, calls=%fused_computation.117 | convolution fusion | flops 16806707200 | bytes 39321600 | tf_op jit(solution)/shard_map/dot_general | solution.py:831
  490.7 27.0 %convolution_convert_fusion.1 = bf16[1280,2560]{1,0:T(8,128)(2,1)} fusion(bf16[2560,1280]{1,0:T(8,128)(2,1)} %multiply_convert_fusion, bf16[2560,1280]{1,0:T(8,128)(2,1)} %get-tuple-element.69, bf16[640,1280]{1,0:T(8,128)(2,1)} %collective-permute-done.5, bf16[640,1280]{1,0:T(8,128)(2,1)} %collective-permute-done.4, ...), kind=kOutput, calls=%fused_computation.12 | convolution fusion | flops 16832921600 | bytes 26214400 | tf_op jit(solution)/shard_map/dot_general | solution.py:831
  523.3 13.8 %convolution_convert_fusion.2 = bf16[1280,1280]{1,0:T(8,128)(2,1)} fusion(bf16[2560,1280]{1,0:T(8,128)(2,1)} %multiply_convert_fusion.2, bf16[640,1280]{1,0:T(8,128)(2,1)} %collective-permute-done.10, bf16[640,1280]{1,0:T(8,128)(2,1)S(1)} %copy-done.46, bf16[640,1280]{1,0:T(8,128)(2,1)S(1)} %copy-done.48, bf16[640,1280]{1,0:T(8,128)(2,1)S(1)} %copy-done.26), kind=kOutput, calls=%fused_computation.14 | convolution fusion | flops 8416460800 | bytes 16384000 | tf_op jit(solution)/shard_map/dot_general | solution.py:831
  537.1 23.0 %collective-permute-done.12 = bf16[640,1280]{1,0:T(8,128)(2,1)S(1)} collective-permute-done((bf16[640,1280]{1,0:T(8,128)(2,1)}, bf16[640,1280]{1,0:T(8,128)(2,1)S(1)}, u32[]{:S(2)}, u32[]{:S(2)}) %collective-permute-start.12) | collective-permute-done | bytes 1638432 | tf_op jit(solution)/shard_map/ppermute | solution.py:813
  580.3 36.1 %collective-permute-done.14 = bf16[640,1280]{1,0:T(8,128)(2,1)} collective-permute-done((bf16[640,1280]{1,0:T(8,128)(2,1)}, bf16[640,1280]{1,0:T(8,128)(2,1)}, u32[]{:S(2)}, u32[]{:S(2)}) %collective-permute-start.14) | collective-permute-done | bytes 1638432 | tf_op jit(solution)/shard_map/ppermute | solution.py:813
  625.6 48.3 %tree_attention_grad.1 = (bf16[3,320,2560]{2,1,0:T(8,128)(2,1)}, f32[5,64,1]{2,1,0:T(8,128)S(1)}) custom-call(s32[20]{0:T(128)S(1)} %copy-done.10, f32[3,320,2560]{2,1,0:T(8,128)} %fusion.33.qkv_ref, f32[5,64,1]{2,1,0:T(8,128)S(1)} %reshape.243.scale_ref, f32[5,8,2560]{2,1,0:T(8,128)S(1)} %get-tuple-element.33.sum_ref, bf16[320,2560]{1,0:T(8,128)(2,1)S(1)} %copy-done.5, ...), custom_call_target="tpu_custom_call" | custom-call | flops 8808038400 | bytes 20971520 | tf_op jit(solution)/shard_map/tree_attention_grad/pallas_call | solution.py:453
  675.0 11.6 %convolution_convert_fusion.4 = bf16[1280,960]{0,1:T(8,128)(2,1)} fusion(bf16[960,2560]{1,0:T(8,128)(2,1)} %bitcast.88, bf16[2560,1280]{1,0:T(8,128)(2,1)} %bitcast.74), kind=kOutput, calls=%fused_computation.21 | convolution fusion | flops 6292684800 | bytes 13926400 | tf_op jit(solution)/shard_map/dot_general | solution.py:831
  701.8 10.8 %convolution_convert_fusion = bf16[2560,1280]{1,0:T(8,128)(2,1)} fusion(bf16[960,2560]{1,0:T(8,128)(2,1)} %bitcast.89, bf16[1280,1024]{1,0:T(8,128)(2,1)S(1)} %bitcast.66), kind=kOutput, calls=%fused_computation.11 | convolution fusion | flops 6294732800 | bytes 14090240 | tf_op jit(solution)/shard_map/dot_general | solution.py:831
  712.6 74.4 %last_exchange.1 = (f32[640,1280]{1,0:T(8,128)}, bf16[4,40,1280]{2,1,0:T(8,128)(2,1)S(1)}, f32[4,40,1280]{2,1,0:T(8,128)S(1)}, f32[4,128]{1,0:T(4,128)S(1)}) custom-call(bf16[4,640,1280]{2,1,0:T(8,128)(2,1)} %bitcast.77, f32[640,1280]{1,0:T(8,128)} %get-tuple-element.58.base, bf16[8,160,1280]{2,1,0:T(8,128)(2,1)} %pad_maximum_fusion.9.grads, ...), custom_call_target="tpu_custom_call" | custom-call | bytes 157286400 | tf_op jit(solution)/shard_map/last_exchange/pallas_call | solution.py:720
  799.8 10.2 %collective-permute-done.16 = f32[40,1280]{1,0:T(8,128)S(1)} collective-permute-done((f32[40,1280]{1,0:T(8,128)S(1)}, f32[40,1280]{1,0:T(8,128)S(1)}, u32[]{:S(2)}, u32[]{:S(2)}) %collective-permute-start.16) | collective-permute-done | bytes 204832 | tf_op jit(solution)/shard_map/ppermute | solution.py:976
  (257 shorter events, 174.3 us)
Async XLA Ops:
  7.2 26.5 %collective-permute-start = (bf16[40,1280]{1,0:T(8,128)(2,1)}, bf16[40,1280]{1,0:T(8,128)(2,1)S(1)}, u32[]{:S(2)}, u32[]{:S(2)}) collective-permute-start(bf16[40,1280]{1,0:T(8,128)(2,1)} %param.23), channel_id=1, source_target_pairs={{0,0},{1,4},{2,8},{3,12},{4,16},{5,20},{6,24},{7,28},{8,1},{9,5},{... | collective-permute-start | bytes 307208 | tf_op jit(solution)/shard_map/ppermute | solution.py:884
  16.9 131.8 %all-to-all-start = ((bf16[4,40,2560]{2,1,0:T(8,128)(2,1)}), bf16[4,40,2560]{2,1,0:T(8,128)(2,1)}, u32[]{:S(2)}, u32[]{:S(2)}) async-start(bf16[4,40,2560]{2,1,0:T(8,128)(2,1)} %pad_maximum_fusion.16), calls=%async_computation | async-start | bytes 1638400 | tf_op jit(solution)/shard_map/all_to_all | solution.py:895
  21.1 228.8 %all-gather.3.cloned.1.call-start = ((), (), s32[]{:S(2)}) async-start(), calls=%async_computation.4 | async-start | bytes 7372800 | tf_op jit(solution)/shard_map/all_gather | solution.py:896
  148.7 163.6 %all-gather.5.cloned.1.call-start = ((), (), s32[]{:S(2)}) async-start(), calls=%async_computation.5 | async-start | bytes 3686400 | tf_op jit(solution)/shard_map/all_gather | solution.py:897
  151.1 5.9 collective-permute-start.1
  159.7 37.9 %collective-permute-start.2 = (bf16[640,1280]{1,0:T(8,128)(2,1)S(1)}, bf16[640,1280]{1,0:T(8,128)(2,1)S(1)}, u32[]{:S(2)}, u32[]{:S(2)}) collective-permute-start(bf16[640,1280]{1,0:T(8,128)(2,1)S(1)} %fusion.6), channel_id=1, source_target_pairs={{0,2},{1,3},{2,0},{3,1},{4,6},{5,7},{6,4},{7,5},{8,10},{9,11},{10,... | collective-permute-start | bytes 4915208 | tf_op jit(solution)/shard_map/ppermute | solution.py:813
  161.5 220.5 %copy-start.28 = (f32[1280]{0:T(1024)}, f32[1280]{0:T(1024)S(1)}, u32[]{:S(2)}) copy-start(f32[1280]{0:T(1024)S(1)} %get-tuple-element.55) | copy-start | bytes 15364
  204.0 37.3 %collective-permute-start.4 = (bf16[640,1280]{1,0:T(8,128)(2,1)S(1)}, bf16[640,1280]{1,0:T(8,128)(2,1)}, u32[]{:S(2)}, u32[]{:S(2)}) collective-permute-start(bf16[640,1280]{1,0:T(8,128)(2,1)S(1)} %multiply_convert_fusion.6), channel_id=1, source_target_pairs={{0,2},{1,3},{2,0},{3,1},{4,6},{5,7},{6,4},{7,5},{8,10},{9,11},{10,... | collective-permute-start | bytes 4915208 | tf_op jit(solution)/shard_map/ppermute | solution.py:813
  205.2 36.1 %collective-permute-start.3 = (bf16[640,1280]{1,0:T(8,128)(2,1)S(1)}, bf16[640,1280]{1,0:T(8,128)(2,1)}, u32[]{:S(2)}, u32[]{:S(2)}) collective-permute-start(bf16[640,1280]{1,0:T(8,128)(2,1)S(1)} %multiply_convert_fusion.6), channel_id=1, source_target_pairs={{0,1},{1,0},{2,3},{3,2},{4,5},{5,4},{6,7},{7,6},{8,9},{9,8},{10,11... | collective-permute-start | bytes 4915208 | tf_op jit(solution)/shard_map/ppermute | solution.py:813
  241.3 3.8 collective-permute-start.5
  241.3 549.5 %reduce-scatter.3.cloned.1.call-start = ((), (), s32[]{:S(2)}) async-start(), calls=%async_computation.6 | async-start | bytes 7372800 | tf_op jit(solution)/shard_map/reduce_scatter | solution.py:947
  324.9 5.9 collective-permute-start.6
  332.5 37.9 %collective-permute-start.7 = (bf16[640,1280]{1,0:T(8,128)(2,1)S(1)}, bf16[640,1280]{1,0:T(8,128)(2,1)}, u32[]{:S(2)}, u32[]{:S(2)}) collective-permute-start(bf16[640,1280]{1,0:T(8,128)(2,1)S(1)} %fusion.4), channel_id=1, source_target_pairs={{0,2},{1,3},{2,0},{3,1},{4,6},{5,7},{6,4},{7,5},{8,10},{9,11},{10,... | collective-permute-start | bytes 4915208 | tf_op jit(solution)/shard_map/ppermute | solution.py:813
  383.8 37.0 %collective-permute-start.9 = (bf16[640,1280]{1,0:T(8,128)(2,1)S(1)}, bf16[640,1280]{1,0:T(8,128)(2,1)S(1)}, u32[]{:S(2)}, u32[]{:S(2)}) collective-permute-start(bf16[640,1280]{1,0:T(8,128)(2,1)S(1)} %multiply_convert_fusion.4), channel_id=1, source_target_pairs={{0,2},{1,3},{2,0},{3,1},{4,6},{5,7},{6,4},{7,5},{8,10},{9,11},{10,... | collective-permute-start | bytes 4915208 | tf_op jit(solution)/shard_map/ppermute | solution.py:813
  385.3 35.5 %collective-permute-start.8 = (bf16[640,1280]{1,0:T(8,128)(2,1)S(1)}, bf16[640,1280]{1,0:T(8,128)(2,1)S(1)}, u32[]{:S(2)}, u32[]{:S(2)}) collective-permute-start(bf16[640,1280]{1,0:T(8,128)(2,1)S(1)} %multiply_convert_fusion.4), channel_id=1, source_target_pairs={{0,1},{1,0},{2,3},{3,2},{4,5},{5,4},{6,7},{7,6},{8,9},{9,8},{10,11... | collective-permute-start | bytes 4915208 | tf_op jit(solution)/shard_map/ppermute | solution.py:813
  420.8 3.6 collective-permute-start.10
  490.5 27.2 %collective-permute-start.11 = (bf16[1280,1280]{1,0:T(8,128)(2,1)}, bf16[1280,1280]{1,0:T(8,128)(2,1)}, u32[]{:S(2)}, u32[]{:S(2)}) collective-permute-start(bf16[1280,1280]{1,0:T(8,128)(2,1)} %pad_maximum_fusion.8), channel_id=1, source_target_pairs={{0,1},{1,0},{2,3},{3,2},{4,5},{5,4},{6,7},{7,6},{8,9},{9,8},{10,11... | collective-permute-start | bytes 9830408 | tf_op jit(solution)/shard_map/ppermute | solution.py:813
  521.8 38.3 %collective-permute-start.12 = (bf16[640,1280]{1,0:T(8,128)(2,1)}, bf16[640,1280]{1,0:T(8,128)(2,1)S(1)}, u32[]{:S(2)}, u32[]{:S(2)}) collective-permute-start(bf16[640,1280]{1,0:T(8,128)(2,1)} %fusion.2), channel_id=1, source_target_pairs={{0,2},{1,3},{2,0},{3,1},{4,6},{5,7},{6,4},{7,5},{8,10},{9,11},{10,... | collective-permute-start | bytes 4915208 | tf_op jit(solution)/shard_map/ppermute | solution.py:813
  564.7 245.4 %reduce-scatter.5.cloned.1.call-start = ((), (), s32[]{:S(2)}) async-start(), calls=%async_computation.7 | async-start | bytes 3686400 | tf_op jit(solution)/shard_map/reduce_scatter | solution.py:948
  578.9 37.6 %collective-permute-start.14 = (bf16[640,1280]{1,0:T(8,128)(2,1)}, bf16[640,1280]{1,0:T(8,128)(2,1)}, u32[]{:S(2)}, u32[]{:S(2)}) collective-permute-start(bf16[640,1280]{1,0:T(8,128)(2,1)} %multiply_convert_fusion.3), channel_id=1, source_target_pairs={{0,2},{1,3},{2,0},{3,1},{4,6},{5,7},{6,4},{7,5},{8,10},{9,11},{10,... | collective-permute-start | bytes 4915208 | tf_op jit(solution)/shard_map/ppermute | solution.py:813
  580.3 36.9 %collective-permute-start.13 = (bf16[640,1280]{1,0:T(8,128)(2,1)}, bf16[640,1280]{1,0:T(8,128)(2,1)}, u32[]{:S(2)}, u32[]{:S(2)}) collective-permute-start(bf16[640,1280]{1,0:T(8,128)(2,1)} %multiply_convert_fusion.3), channel_id=1, source_target_pairs={{0,1},{1,0},{2,3},{3,2},{4,5},{5,4},{6,7},{7,6},{8,9},{9,8},{10,11... | collective-permute-start | bytes 4915208 | tf_op jit(solution)/shard_map/ppermute | solution.py:813
  616.5 3.8 collective-permute-start.15
  790.9 21.2 %all-to-all-start.1 = ((bf16[4,40,2560]{2,1,0:T(8,128)(2,1)}), bf16[4,40,2560]{2,1,0:T(8,128)(2,1)S(1)}, u32[]{:S(2)}, u32[]{:S(2)}) async-start(bf16[4,40,2560]{2,1,0:T(8,128)(2,1)} %bitcast.83), calls=%async_computation.2 | async-start | bytes 1638400 | tf_op jit(solution)/shard_map/all_to_all | solution.py:977
  794.8 15.3 %collective-permute-start.16 = (f32[40,1280]{1,0:T(8,128)S(1)}, f32[40,1280]{1,0:T(8,128)S(1)}, u32[]{:S(2)}, u32[]{:S(2)}) collective-permute-start(f32[40,1280]{1,0:T(8,128)S(1)} %reshape.239), channel_id=1, source_target_pairs={{0,0},{4,1},{8,2},{12,3},{16,4},{20,5},{24,6},{28,7},{1,8},{5,9},{... | collective-permute-start | bytes 614408 | tf_op jit(solution)/shard_map/ppermute | solution.py:976
  (50 other events, 746.8 us)
Sparse Core Ops, SparseCore 0:
  148.8 101.0 all-gather.2
  252.0 60.1 all-gather.4
  564.8 121.1 reduce-scatter.2
  689.9 87.8 reduce-scatter.4

commit v3 on v2

--- a/solution.py
+++ b/solution.py
@@ -618,7 +618,7 @@
     )(states, qkv_send, extra, out_piece)
 
 
-def last_kernel(share, base, grads, vectors, g_states, qkv_rows, out_rows, vec_own,
+def last_kernel(share, base, grads, down, vectors, g_states, qkv_rows, out_rows, down_rows, vec_own,
                 core_buf, far_buf, x_buf, ring_buf, vec_buf, row_buf, vec_part, vec_in,
                 core_send, core_recv, x_send, x_recv, ring_send, ring_recv, a2a_send, a2a_recv):
     me, dp = lax.axis_index("fsdp"), lax.axis_index("dp")
@@ -626,14 +626,13 @@
     sibling, across, corner = group_peers()
     right, left = {"dp": ring_dp(place + 1)}, {"dp": ring_dp(place - 1)}
     greet([sibling, across, corner, right, left])
-    half = grads.shape[1] // 2
     rows = share.shape[1] // 4
 
     def first_hop():
         to_right, to_left = ring_dp(place - 1), ring_dp(place + 1)
         return [
-            send(grads.at[to_right, pl.ds(0, half)], ring_buf.at[0, 0], ring_send.at[0, 0], ring_recv.at[0, 0], right),
-            send(grads.at[to_left, pl.ds(half, half)], ring_buf.at[1, 0], ring_send.at[1, 0], ring_recv.at[1, 0], left),
+            send(grads.at[to_right], ring_buf.at[0, 0], ring_send.at[0, 0], ring_recv.at[0, 0], right),
+            send(down.at[to_left], ring_buf.at[1, 0], ring_send.at[1, 0], ring_recv.at[1, 0], left),
             send(vectors.at[to_right], vec_buf.at[0], ring_send.at[2, 0], ring_recv.at[2, 0], right),
         ]
 
@@ -667,10 +666,10 @@
     def hop(step, carry):
         to_right, to_left = ring_dp(place - 1 - step), ring_dp(place + 1 + step)
         ring_buf[0, step - 1] = (
-            ring_buf[0, step - 1].astype(F32) + grads[to_right, pl.ds(0, half)].astype(F32)
+            ring_buf[0, step - 1].astype(F32) + grads[to_right].astype(F32)
         ).astype(BF)
         ring_buf[1, step - 1] = (
-            ring_buf[1, step - 1].astype(F32) + grads[to_left, pl.ds(half, half)].astype(F32)
+            ring_buf[1, step - 1].astype(F32) + down[to_left].astype(F32)
         ).astype(BF)
         vec_buf[step - 1] = vec_buf[step - 1] + vectors[to_right]
         copies = later_hop(step)
@@ -681,13 +680,13 @@
         return carry
 
     lax.fori_loop(1, 7, hop, 0)
-    quarter = half // 2
-    for side in range(2):
-        total = ring_buf[side, 6].astype(F32) + grads[dp, pl.ds(side * half, half)].astype(F32)
-        for i in range(2):
-            piece = total[i * quarter : (i + 1) * quarter]
-            row_buf[2 * side + i] = piece.astype(BF)
-            out_rows[2 * side + i] = piece
+    total = ring_buf[0, 6].astype(F32) + grads[dp].astype(F32)
+    quarter = total.shape[0] // 4
+    for i in range(4):
+        piece = total[i * quarter : (i + 1) * quarter]
+        row_buf[i] = piece.astype(BF)
+        out_rows[i] = piece
+    down_rows[...] = ring_buf[1, 6].astype(F32) + down[dp].astype(F32)
     vec_part[...] = vec_buf[6] + vectors[dp]
     exchange = []
     for i, peer in enumerate((sibling, across, corner)):
@@ -713,25 +712,26 @@
     vec_own[...] = vec_in[0] + vec_in[1] + vec_in[2] + vec_in[3]
 
 
-def last_exchange(share, base, grads, vectors):
-    half, cols = grads.shape[1] // 2, grads.shape[2]
+def last_exchange(share, base, grads, down, vectors):
+    cols = grads.shape[2]
     rows_w = grads.shape[1] // 4
     vmem = pl.BlockSpec(memory_space=pltpu.VMEM)
     return pl.pallas_call(
         last_kernel,
-        in_specs=[vmem] * 4,
-        out_specs=[vmem] * 4,
+        in_specs=[vmem] * 5,
+        out_specs=[vmem] * 5,
         out_shape=[
             jax.ShapeDtypeStruct(base.shape, F32),
             jax.ShapeDtypeStruct((4, rows_w, cols), BF),
             jax.ShapeDtypeStruct((4, rows_w, cols), F32),
+            jax.ShapeDtypeStruct(down.shape[1:], F32),
             jax.ShapeDtypeStruct(vectors.shape[2:], F32),
         ],
         scratch_shapes=[
             pltpu.VMEM((2,) + share.shape[1:], BF),
             pltpu.VMEM(share.shape[1:], BF),
             pltpu.VMEM(share.shape[1:], BF),
-            pltpu.VMEM((2, 7, half, cols), BF),
+            pltpu.VMEM((2, 7) + grads.shape[1:], BF),
             pltpu.VMEM((7,) + vectors.shape[1:], F32),
             pltpu.VMEM((4, rows_w, cols), BF),
             pltpu.VMEM(vectors.shape[1:], F32),
@@ -750,7 +750,473 @@
         ),
         cost_estimate=pl.CostEstimate(flops=0, bytes_accessed=150 << 20, transcendentals=0),
         name="last_exchange",
-    )(share, base, grads, vectors)
+    )(share, base, grads, down, vectors)
+
+
+CHUNK = 128
+TILE = 256
+
+
+def tile(index, base=0):
+    return pl.ds(pl.multiple_of(base + index * TILE, TILE), TILE)
+
+
+def nt(a, b):
+    return lax.dot_general(a, b, (((1,), (1,)), ((), ())), preferred_element_type=F32)
+
+
+def middle_kernel(share, states, teacher, weight, mask, w_all, rates, scales,
+                  out_states, hidden, attn_unit, back, attn_inv, hidden_inv, sums, gd_all, ht_all, act_all, ug_all,
+                  part, core, x_buf, tok, gd, act, ug, ht,
+                  ld_sem, core_send, core_recv, x_send, x_recv, tok_send, tok_recv, gd_send, gd_recv, gd_own,
+                  out_sem):
+    sibling, across, _ = group_peers()
+    count = part.shape[0]
+    width = hidden.shape[1]
+    rate_attn, rate_mlp = rates[0:1], rates[1:2]
+
+    def rows(i):
+        return pl.ds(pl.multiple_of(i * CHUNK, CHUNK), CHUNK)
+
+    def load(i):
+        return pltpu.make_async_copy(share.at[:, rows(i)], part.at[i], ld_sem.at[i])
+
+    def core_a(stage, i):
+        return send(part.at[i, 3], core.at[0, i], core_send.at[stage, 0, i], core_recv.at[stage, 0, i], sibling)
+
+    def core_b(stage, i):
+        return send(part.at[i, 1], core.at[1, i], core_send.at[stage, 1, i], core_recv.at[stage, 1, i], sibling)
+
+    def chip(stage, i):
+        return send(part.at[i, 2], x_buf.at[i], x_send.at[stage, i], x_recv.at[stage, i], across)
+
+    def spread(buf, own, sems, recvs, i):
+        return [
+            send(own, buf.at[i, 1], sems.at[0, i], recvs.at[0, i], sibling),
+            send(own, buf.at[i, 2], sems.at[1, i], recvs.at[1, i], across),
+            send(buf.at[i, 2], buf.at[i, 3], sems.at[2, i], recvs.at[2, i], sibling),
+        ]
+
+    def tok_copies(i):
+        return spread(tok, tok.at[i, 0], tok_send, tok_recv, i)
+
+    def gd_copies(i):
+        return spread(gd_all, gd.at[i], gd_send, gd_recv, i)
+
+    def gd_local(i):
+        return pltpu.make_async_copy(gd.at[i], gd_all.at[i, 0], gd_own.at[i])
+
+    def outs(i):
+        slot = i % 2
+        return [
+            pltpu.make_async_copy(ht.at[slot], ht_all.at[i], out_sem.at[0, slot]),
+            pltpu.make_async_copy(act.at[slot], act_all.at[i], out_sem.at[1, slot]),
+            pltpu.make_async_copy(ug.at[slot], ug_all.at[i], out_sem.at[2, slot]),
+        ]
+
+    def forward_far(stage, i):
+        core_a(stage, i).wait_recv()
+        part[i, 2] = (part[i, 2].astype(F32) + core[0, i].astype(F32)).astype(BF)
+        chip(stage, i).start()
+
+    def reduced(stage, i):
+        core_b(stage, i).wait_recv()
+        chip(stage, i).wait_recv()
+        total = part[i, 0].astype(F32) + core[1, i].astype(F32) + x_buf[i].astype(F32)
+        core_a(stage, i).wait_send()
+        core_b(stage, i).wait_send()
+        chip(stage, i).wait_send()
+        return total
+
+    sums[...] = jnp.zeros_like(sums)
+    lax.fori_loop(0, count, lambda i, c: (load(i).start(), c)[1], 0)
+    greet([sibling, across])
+
+    def open_core(i, carry):
+        load(i).wait()
+        core_a(0, i).start()
+        core_b(0, i).start()
+        return carry
+
+    lax.fori_loop(0, count, open_core, 0)
+    lax.fori_loop(0, count, lambda i, c: (forward_far(0, i), c)[1], 0)
+
+    def norm_hidden(i):
+        unit, inverse = unit_rows(reduced(0, i))
+        own = states[rows(i)].astype(F32)
+        value, value_inv = unit_rows(own + rate_attn * (unit - own))
+        hidden[rows(i)] = value
+        attn_unit[rows(i)] = unit.astype(BF)
+        attn_inv[rows(i)] = inverse
+        hidden_inv[rows(i)] = value_inv
+        tok[i, 0] = value.astype(BF)
+        copies = tok_copies(i)
+        copies[0].start()
+        copies[1].start()
+
+    def pass_tokens(i):
+        copies = tok_copies(i)
+        copies[1].wait_recv()
+        copies[2].start()
+
+    def feed(i):
+        copies = tok_copies(i)
+        copies[0].wait()
+        copies[1].wait_send()
+        copies[2].wait()
+        slot = i % 2
+
+        @pl.when(i >= 2)
+        def _():
+            for copy in outs(i - 2):
+                copy.wait()
+
+        def up(n, carry):
+            here = tok[i].reshape(4 * CHUNK, width)
+            up_proj = nn(here, w_all[:, tile(n)])
+            gate_proj = nn(here, w_all[:, tile(n, width)])
+            gated = gate_proj * scales[1:2, tile(n)]
+            value = up_proj * scales[0:1, tile(n)] * (gated * jax.nn.sigmoid(gated))
+            act[slot, :, tile(n)] = value.astype(BF)
+            ug[slot, :, tile(n)] = up_proj.astype(BF)
+            ug[slot, :, tile(n, width)] = gate_proj.astype(BF)
+            return carry
+
+        lax.fori_loop(0, width // TILE, up, 0)
+
+        def down(n, carry):
+            value = nn(act[slot], w_all[:, tile(n, 2 * width)])
+            part[i, :, :, tile(n)] = value.astype(BF).reshape(4, CHUNK, TILE)
+            ht[slot, tile(n)] = tok[i, :, :, tile(n)].reshape(4 * CHUNK, TILE).T
+            return carry
+
+        lax.fori_loop(0, width // TILE, down, 0)
+        core_a(1, i).start()
+        core_b(1, i).start()
+        for copy in outs(i):
+            copy.start()
+        forward_far(1, i)
+
+    def finish(i):
+        unit, inverse = unit_rows(reduced(1, i))
+        own = hidden[rows(i)]
+        result, result_inv = unit_rows(own + rate_mlp * (unit - own))
+        out_states[rows(i)] = result.astype(BF)
+        diff = result - teacher[rows(i)]
+        sums[1:2] = sums[1:2] + jnp.sum(mask[rows(i)] * (diff * diff), axis=0, keepdims=True)
+        g_last = unit_back(weight[rows(i)] * diff, result, result_inv)
+        sums[0:1] = sums[0:1] + jnp.sum(g_last * (unit - own), axis=0, keepdims=True)
+        back[rows(i)] = g_last * (1.0 - rate_mlp)
+        gd[i] = unit_back(g_last * rate_mlp, unit, inverse).astype(BF)
+        copies = gd_copies(i)
+        copies[0].start()
+        copies[1].start()
+        gd_local(i).start()
+
+    def pass_grads(i):
+        copies = gd_copies(i)
+        copies[1].wait_recv()
+        copies[2].start()
+
+    stages = (norm_hidden, pass_tokens, feed, finish, pass_grads)
+
+    def step(t, carry):
+        for lag, stage in enumerate(stages):
+            pl.when((t >= lag) & (t < lag + count))(functools.partial(stage, t - lag))
+        return carry
+
+    lax.fori_loop(0, count + len(stages) - 1, step, 0)
+
+    def close(i, carry):
+        copies = gd_copies(i)
+        copies[0].wait()
+        copies[1].wait_send()
+        copies[2].wait()
+        gd_local(i).wait()
+        return carry
+
+    lax.fori_loop(0, count, close, 0)
+    for i in (count - 2, count - 1):
+        for copy in outs(i):
+            copy.wait()
+
+
+def middle(share, states, teacher, weight, mask, w_all, rates, scales):
+    rows, width = states.shape
+    count = rows // CHUNK
+    vmem, hbm = pl.BlockSpec(memory_space=pltpu.VMEM), pl.BlockSpec(memory_space=pl.ANY)
+    dma = pltpu.SemaphoreType.DMA
+    return pl.pallas_call(
+        middle_kernel,
+        in_specs=[hbm] + [vmem] * 7,
+        out_specs=[vmem] * 7 + [hbm] * 4,
+        out_shape=[
+            jax.ShapeDtypeStruct((rows, width), BF),
+            jax.ShapeDtypeStruct((rows, width), F32),
+            jax.ShapeDtypeStruct((rows, width), BF),
+            jax.ShapeDtypeStruct((rows, width), F32),
+            jax.ShapeDtypeStruct((rows, 1), F32),
+            jax.ShapeDtypeStruct((rows, 1), F32),
+            jax.ShapeDtypeStruct((2, width), F32),
+            jax.ShapeDtypeStruct((count, 4, CHUNK, width), BF),
+            jax.ShapeDtypeStruct((count, width, 4 * CHUNK), BF),
+            jax.ShapeDtypeStruct((count, 4 * CHUNK, width), BF),
+            jax.ShapeDtypeStruct((count, 4 * CHUNK, 2 * width), BF),
+        ],
+        scratch_shapes=[
+            pltpu.VMEM((count, 4, CHUNK, width), BF),
+            pltpu.VMEM((2, count, CHUNK, width), BF),
+            pltpu.VMEM((count, CHUNK, width), BF),
+            pltpu.VMEM((count, 4, CHUNK, width), BF),
+            pltpu.VMEM((count, CHUNK, width), BF),
+            pltpu.VMEM((2, 4 * CHUNK, width), BF),
+            pltpu.VMEM((2, 4 * CHUNK, 2 * width), BF),
+            pltpu.VMEM((2, width, 4 * CHUNK), BF),
+            dma((count,)),
+            dma((2, 2, count)),
+            dma((2, 2, count)),
+            dma((2, count)),
+            dma((2, count)),
+            dma((3, count)),
+            dma((3, count)),
+            dma((3, count)),
+            dma((3, count)),
+            dma((count,)),
+            dma((3, 2)),
+        ],
+        compiler_params=pltpu.CompilerParams(
+            collective_id=3, has_side_effects=True, vmem_limit_bytes=60 << 20
+        ),
+        cost_estimate=pl.CostEstimate(flops=26 * 10**9, bytes_accessed=400 << 20, transcendentals=4 << 20),
+        name="middle",
+    )(share, states, teacher, weight, mask, w_all, rates, scales)
+
+
+def middle_back_kernel(gd_all, ht_all, ug_all, hidden, attn_unit, states, back, attn_inv, hidden_inv, w_all, rates,
+                       scales, base, ga_all, grad_ug, sums, ff_sums,
+                       part, core, x_buf, ga, gd, ht, ug, gug, acc, stage_buf, own_f, own_b, base_buf,
+                       in_sem, own_sem, core_send, core_recv, x_send, x_recv, ga_send, ga_recv, ga_own, base_sem,
+                       out_sem):
+    sibling, across, _ = group_peers()
+    count = core.shape[1]
+    width = w_all.shape[0]
+    rate_attn = rates[0:1]
+
+    def rows(i):
+        return pl.ds(pl.multiple_of(i * CHUNK, CHUNK), CHUNK)
+
+    def stream(i):
+        slot = i % 2
+        return [
+            pltpu.make_async_copy(gd_all.at[i], gd.at[slot], in_sem.at[0, slot]),
+            pltpu.make_async_copy(ht_all.at[i], ht.at[slot], in_sem.at[1, slot]),
+            pltpu.make_async_copy(ug_all.at[i], ug.at[slot], in_sem.at[2, slot]),
+        ]
+
+    def own_rows(i):
+        return [
+            pltpu.make_async_copy(hidden.at[rows(i)], own_f.at[0], own_sem.at[0]),
+            pltpu.make_async_copy(back.at[rows(i)], own_f.at[1], own_sem.at[1]),
+            pltpu.make_async_copy(attn_unit.at[rows(i)], own_b.at[0], own_sem.at[2]),
+            pltpu.make_async_copy(states.at[rows(i)], own_b.at[1], own_sem.at[3]),
+        ]
+
+    def core_a(i):
+        return send(part.at[i % 3, 3], core.at[0, i], core_send.at[0, i], core_recv.at[0, i], sibling)
+
+    def core_b(i):
+        return send(part.at[i % 3, 1], core.at[1, i], core_send.at[1, i], core_recv.at[1, i], sibling)
+
+    def chip(i):
+        return send(part.at[i % 3, 2], x_buf.at[i], x_send.at[i], x_recv.at[i], across)
+
+    def ga_copies(i):
+        return [
+            send(ga.at[i], ga_all.at[1, rows(i)], ga_send.at[0, i], ga_recv.at[0, i], sibling),
+            send(ga.at[i], ga_all.at[2, rows(i)], ga_send.at[1, i], ga_recv.at[1, i], across),
+            send(ga_all.at[2, rows(i)], ga_all.at[3, rows(i)], ga_send.at[2, i], ga_recv.at[2, i], sibling),
+        ]
+
+    def ga_local(i):
+        return pltpu.make_async_copy(ga.at[i], ga_all.at[0, rows(i)], ga_own.at[i])
+
+    def base_copy(i):
+        return pltpu.make_async_copy(base_buf.at[i % 2], base.at[rows(i)], base_sem.at[i % 2])
+
+    for copy in stream(0) + own_rows(0):
+        copy.start()
+    sums[...] = jnp.zeros_like(sums)
+    ff_sums[...] = jnp.zeros_like(ff_sums)
+    acc[...] = jnp.zeros_like(acc)
+    greet([sibling, across])
+
+    def feed(i):
+        slot = i % 2
+        for copy in stream(i):
+            copy.wait()
+
+        @pl.when(i + 1 < count)
+        def _():
+            for copy in stream(i + 1):
+                copy.start()
+
+        def grads(n, carry):
+            g_act = nt(gd[slot].reshape(4 * CHUNK, width), w_all[tile(n), pl.ds(2 * width, width)])
+            up_proj = ug[slot, :, tile(n)].astype(F32)
+            gate_proj = ug[slot, :, tile(n, width)].astype(F32)
+            scale_up, scale_gate = scales[0:1, tile(n)], scales[1:2, tile(n)]
+            gated = gate_proj * scale_gate
+            sigmoid = jax.nn.sigmoid(gated)
+            g_upscaled = g_act * (gated * sigmoid)
+            g_gated = g_act * (up_proj * scale_up) * sigmoid * (1.0 + gated * (1.0 - sigmoid))
+            ff_sums[0:1, tile(n)] = ff_sums[0:1, tile(n)] + jnp.sum(g_upscaled * up_proj, axis=0, keepdims=True)
+            ff_sums[1:2, tile(n)] = ff_sums[1:2, tile(n)] + jnp.sum(g_gated * gate_proj, axis=0, keepdims=True)
+            gug[:, tile(n)] = (g_upscaled * scale_up).astype(BF)
+            gug[:, tile(n, width)] = (g_gated * scale_gate).astype(BF)
+            return carry
+
+        lax.fori_loop(0, width // TILE, grads, 0)
+
+        def through(n, carry):
+            value = nt(gug[...], w_all[tile(n), pl.ds(0, 2 * width)])
+            part[i % 3, :, :, tile(n)] = value.astype(BF).reshape(4, CHUNK, TILE)
+            return carry
+
+        lax.fori_loop(0, width // TILE, through, 0)
+        core_a(i).start()
+        core_b(i).start()
+        core_a(i).wait_recv()
+        part[i % 3, 2] = (part[i % 3, 2].astype(F32) + core[0, i].astype(F32)).astype(BF)
+        chip(i).start()
+
+        def outer(n, carry):
+            acc[:, tile(n)] = acc[:, tile(n)] + nn(ht[slot], gug[:, tile(n)])
+            return carry
+
+        lax.fori_loop(0, 2 * width // TILE, outer, 0)
+
+    def finish(i):
+        core_b(i).wait_recv()
+        chip(i).wait_recv()
+        through = part[i % 3, 0].astype(F32) + core[1, i].astype(F32) + x_buf[i].astype(F32)
+        core_a(i).wait_send()
+        core_b(i).wait_send()
+        chip(i).wait_send()
+        for copy in own_rows(i):
+            copy.wait()
+        value, unit, own = own_f[0], own_b[0].astype(F32), own_b[1].astype(F32)
+        g_pre = unit_back(own_f[1] + through, value, hidden_inv[rows(i)])
+
+        @pl.when(i + 1 < count)
+        def _():
+            for copy in own_rows(i + 1):
+                copy.start()
+
+        @pl.when(i >= 2)
+        def _():
+            base_copy(i - 2).wait()
+
+        base_buf[i % 2] = g_pre * (1.0 - rate_attn)
+        base_copy(i).start()
+        sums[0:1] = sums[0:1] + jnp.sum(g_pre * (unit - own), axis=0, keepdims=True)
+        ga[i] = unit_back(g_pre * rate_attn, unit, attn_inv[rows(i)]).astype(BF)
+        copies = ga_copies(i)
+        copies[0].start()
+        copies[1].start()
+        ga_local(i).start()
+
+    def pass_grads(i):
+        copies = ga_copies(i)
+        copies[1].wait_recv()
+        copies[2].start()
+
+    stages = (feed, finish, pass_grads)
+
+    def step(t, carry):
+        for lag, stage in enumerate(stages):
+            pl.when((t >= lag) & (t < lag + count))(functools.partial(stage, t - lag))
+        return carry
+
+    lax.fori_loop(0, count + len(stages) - 1, step, 0)
+
+    def out_copy(n):
+        return pltpu.make_async_copy(stage_buf.at[n % 2], grad_ug.at[tile(n)], out_sem.at[n % 2])
+
+    def store(n, carry):
+        @pl.when(n >= 2)
+        def _():
+            out_copy(n - 2).wait()
+
+        stage_buf[n % 2] = acc[tile(n)].astype(BF)
+        out_copy(n).start()
+        return carry
+
+    blocks = width // TILE
+    lax.fori_loop(0, blocks, store, 0)
+
+    def close(i, carry):
+        copies = ga_copies(i)
+        copies[0].wait()
+        copies[1].wait_send()
+        copies[2].wait()
+        ga_local(i).wait()
+        return carry
+
+    lax.fori_loop(0, count, close, 0)
+    for i in (count - 2, count - 1):
+        base_copy(i).wait()
+    for n in (blocks - 2, blocks - 1):
+        out_copy(n).wait()
+
+
+def middle_back(gd_all, ht_all, ug_all, hidden, attn_unit, states, back, attn_inv, hidden_inv, w_all, rates, scales):
+    rows, width = states.shape
+    count = rows // CHUNK
+    vmem, hbm = pl.BlockSpec(memory_space=pltpu.VMEM), pl.BlockSpec(memory_space=pl.ANY)
+    dma = pltpu.SemaphoreType.DMA
+    return pl.pallas_call(
+        middle_back_kernel,
+        in_specs=[hbm] * 7 + [vmem] * 5,
+        out_specs=[hbm, hbm, hbm, vmem, vmem],
+        out_shape=[
+            jax.ShapeDtypeStruct((rows, width), F32),
+            jax.ShapeDtypeStruct((4, rows, width), BF),
+            jax.ShapeDtypeStruct((width, 2 * width), BF),
+            jax.ShapeDtypeStruct((1, width), F32),
+            jax.ShapeDtypeStruct((2, width), F32),
+        ],
+        scratch_shapes=[
+            pltpu.VMEM((3, 4, CHUNK, width), BF),
+            pltpu.VMEM((2, count, CHUNK, width), BF),
+            pltpu.VMEM((count, CHUNK, width), BF),
+            pltpu.VMEM((count, CHUNK, width), BF),
+            pltpu.VMEM((2, 4, CHUNK, width), BF),
+            pltpu.VMEM((2, width, 4 * CHUNK), BF),
+            pltpu.VMEM((2, 4 * CHUNK, 2 * width), BF),
+            pltpu.VMEM((4 * CHUNK, 2 * width), BF),
+            pltpu.VMEM((width, 2 * width), F32),
+            pltpu.VMEM((2, TILE, 2 * width), BF),
+            pltpu.VMEM((2, CHUNK, width), F32),
+            pltpu.VMEM((2, CHUNK, width), BF),
+            pltpu.VMEM((2, CHUNK, width), F32),
+            dma((3, 2)),
+            dma((4,)),
+            dma((2, count)),
+            dma((2, count)),
+            dma((count,)),
+            dma((count,)),
+            dma((3, count)),
+            dma((3, count)),
+            dma((count,)),
+            dma((2,)),
+            dma((2,)),
+        ],
+        compiler_params=pltpu.CompilerParams(
+            collective_id=4, has_side_effects=True, vmem_limit_bytes=60 << 20
+        ),
+        cost_estimate=pl.CostEstimate(flops=42 * 10**9, bytes_accessed=200 << 20, transcendentals=4 << 20),
+        name="middle_back",
+    )(gd_all, ht_all, ug_all, hidden, attn_unit, states, back, attn_inv, hidden_inv, w_all, rates, scales)
 
 
 def order_kernel(where_ref, parent_ref, perm_ref, branch_ref, leaf_ref):
@@ -807,24 +1273,6 @@
         scratch_shapes=[pltpu.SMEM((NB,), jnp.int32), pltpu.SMEM((NB,), jnp.int32)],
         name="tree_order",
     )(where, parents)
-
-
-def swap(value, step):
-    return lax.ppermute(value, "fsdp", [(i, i ^ step) for i in range(4)])
-
-
-def gather_tokens(mine):
-    across = swap(mine, 2)
-    return jnp.concatenate((mine, swap(mine, 1), across, swap(across, 1)), axis=0)
-
-
-def reduce_tokens(share):
-    rows = share.shape[0] // 4
-    part = [share[i * rows : (i + 1) * rows] for i in range(4)]
-    other = swap(jnp.concatenate((part[3], part[1]), axis=0).astype(BF), 1)
-    far = part[2] + other[:rows]
-    near = part[0] + other[rows:]
-    return near + swap(far.astype(BF), 2)
 
 
 def dot(left, right, contract):
@@ -893,8 +1341,7 @@
         axis=2,
     )
     ug_group = lax.all_to_all(ug_send, "fsdp", 0, 0, tiled=True).reshape(tps * rows_w, 2 * hid)
-    w_ug = lax.all_gather(ug_group, "dp", axis=0, tiled=True)
-    w_d = lax.all_gather(w_down, "dp", axis=0, tiled=True)
+    w_all = lax.all_gather(jnp.concatenate((ug_group, w_down), axis=1), "dp", axis=0, tiled=True)
 
     w_qkv = first[:, : 3 * cols]
     small_all = first[:, 3 * cols :].astype(F32)
@@ -907,50 +1354,22 @@
 
     qkv = dot(w_qkv, tokens, (0, 1)).reshape(3, cols, TOK)
     mixed, sums = attn_fwd(perm, qkv, scale_qk)
-    attn = reduce_tokens(dot(mixed, w_o, (0, 0)))
-    inputs = states.astype(F32)
-    attn_unit, attn_inv = unit_rows(attn)
-    hidden, hidden_inv = unit_rows(inputs + rate_attn * (attn_unit - inputs))
-    hidden_all = gather_tokens(hidden.astype(BF))
-    raw = dot(hidden_all, w_ug, (1, 0))
-    up_proj, gate_proj = raw[:, :hid], raw[:, hid:]
-    upscaled = up_proj * scale_up
-    gated = gate_proj * scale_gate * root_width
-    sigmoid_gate = jax.nn.sigmoid(gated)
-    act = (upscaled * (gated * sigmoid_gate)).astype(BF)
-    down = reduce_tokens(dot(act, w_d, (1, 0)))
-    down_unit, down_inv = unit_rows(down)
-    result, result_inv = unit_rows(hidden + rate_mlp * (down_unit - hidden))
-    loss_local = jnp.sum(mask_f[:, None] * (result - teacher) ** 2)
-
-    g_result = 2.0 * mask_f[:, None] * (result - teacher) / valid_count
-    g_last = unit_back(g_result, result, result_inv)
-    g_rate_mlp = jnp.sum(g_last * (down_unit - hidden), axis=0)
-    g_down = unit_back(g_last * rate_mlp, down_unit, down_inv).astype(BF)
-    g_down_all = gather_tokens(g_down)
-    g_act = dot(g_down_all, w_d, (1, 1))
-    g_upscaled = g_act * (gated * sigmoid_gate)
-    g_gated = g_act * upscaled * sigmoid_gate * (1.0 + gated * (1.0 - sigmoid_gate))
-    grad_up_scale = jnp.sum(g_upscaled * up_proj, axis=0)
-    grad_gate_scale = jnp.sum(g_gated * gate_proj * root_width, axis=0)
-    g_ug = jnp.concatenate(
-        ((g_upscaled * scale_up).astype(BF), (g_gated * scale_gate * root_width).astype(BF)), axis=1
-    )
-    back_hidden, part_down, part_ug = lax.optimization_barrier(
-        (
-            reduce_tokens(dot(g_ug, w_ug, (1, 1))),
-            dot(act, g_down_all, (0, 0)).astype(BF),
-            dot(hidden_all, g_ug, (0, 0)).astype(BF),
-        )
-    )
-    g_hidden = g_last * (1.0 - rate_mlp) + back_hidden
+    rates = jnp.stack((rate_attn, rate_mlp))
+    scales = jnp.stack((scale_up, scale_gate * root_width))
+    share = dot(mixed, w_o, (0, 0)).astype(BF).reshape(tps, TOK // tps, D)
+    mask_col = mask_f[:, None]
+    out_states, hidden, attn_unit, back, attn_inv, hidden_inv, sums_mid, gd_all, ht_all, act_all, ug_all = middle(
+        share, states, teacher, mask_col * (2.0 / valid_count), mask_col, w_all, rates, scales
+    )
+    base, ga_all, part_ug, sums_back, ff_sums = middle_back(
+        gd_all, ht_all, ug_all, hidden, attn_unit, states, back, attn_inv, hidden_inv, w_all, rates, scales
+    )
     grad_ug = lax.psum_scatter(part_ug, "dp", scatter_dimension=0, tiled=True)
-    grad_down = lax.psum_scatter(part_down, "dp", scatter_dimension=0, tiled=True).astype(F32)
-
-    g_pre = unit_back(g_hidden, hidden, hidden_inv)
-    g_rate_attn = jnp.sum(g_pre * (attn_unit - inputs), axis=0)
-    g_attn = unit_back(g_pre * rate_attn, attn_unit, attn_inv).astype(BF)
-    g_attn_all = gather_tokens(g_attn)
+    part_down = dot(act_all.reshape(TOK, hid), gd_all.reshape(TOK, D), (0, 0)).astype(BF)
+    loss_local = jnp.sum(sums_mid[1])
+    g_rate_mlp, g_rate_attn = sums_mid[0], sums_back[0]
+    grad_up_scale, grad_gate_scale = ff_sums[0], ff_sums[1] * root_width
+    g_attn_all = ga_all.reshape(TOK, D)
     g_mixed = dot(w_o, g_attn_all, (1, 1)).astype(BF)
     g_qkv, g_scale = attn_bwd(perm, qkv, scale_qk, sums, mixed, g_mixed)
     g_qkv = g_qkv.reshape(3 * cols, TOK)
@@ -970,7 +1389,9 @@
     part_out = dot(mixed, g_attn_all, (1, 0)).astype(BF).reshape(dps, rows_w, tps, cols).transpose(0, 2, 1, 3)
     part_qkv = dot(tokens, g_qkv, (0, 1)).astype(BF).reshape(dps, tps * rows_w, 3 * cols)
     parts = jnp.concatenate((part_qkv, part_out.reshape(dps, tps * rows_w, cols)), axis=2)
-    grad_states, qkv_back, out_back, vector_share = last_exchange(share, g_pre * (1.0 - rate_attn), parts, vectors)
+    grad_states, qkv_back, out_back, grad_down, vector_share = last_exchange(
+        share, base, parts, part_down.reshape(dps, ff_rows, D), vectors
+    )
     vector_share = vector_share.reshape(512)
     out_back = out_back[:, :, 3 * cols :].transpose(1, 0, 2).reshape(rows_w, D)
     grad_out = lax.ppermute(out_back, both, [(b, a) for a, b in spread])
@@ -981,7 +1402,7 @@
     cuts = (0, rows_w, 2 * rows_w, 3 * rows_w, 3 * rows_w + ff_rows, 3 * rows_w + 2 * ff_rows)
     v = [vector_share[a:b] for a, b in zip(cuts, cuts[1:])]
     return (
-        result.astype(BF),
+        out_states,
         vector_share[-1] / valid_count,
         grad_states,
         qkv_back[0],

time: 837 us -> 722 us (0.86)
  Pallas kernels: 214 us -> 541 us
  waiting for transfers between devices: 260 us -> 7.07 us
  matrix products: 184 us -> 63.6 us
  other arithmetic: 70.6 us -> 9.74 us
  blocking collectives: 0 us -> 14.7 us
  starting transfers between devices: 24 us -> 11.9 us
  local copies, waits for them, and re-layouts: 60 us -> 50.2 us
    pallas_call x1 -> x3, Pallas kernels: 74.4 us -> 354 us  [the longest x1 161 us: middle(): pl.pallas_call(middle_kernel, in_specs=[hbm] + [vmem] * 7, out_specs=[vme...]
    ppermute x15 -> x0, waiting for transfers between devices: 222 us -> none  [swap(): return lax.ppermute(value, 'fsdp', [(i, i ^ step) for i in range(4)])]
    dot_general x12 -> x7, matrix products: 184 us -> 63.6 us  [dot(): lax.dot_general(left, right, ((contract[:1], contract[1:]), ((), ())), pr...]
    pallas_call x1, Pallas kernels: 59.8 us -> 107 us  [first_exchange(): pl.pallas_call(first_kernel, in_specs=[hbm, vmem, vmem, vmem], out_specs=...]
    convert_element_type x9 -> x0, other arithmetic: 33.3 us -> none  [the longest x1 12.5 us: local(): act = (upscaled * (gated * sigmoid_gate)).astype(BF)]
    all_gather x2 -> x1, waiting for transfers between devices: 27.7 us -> 0.01 us  [local(): lax.all_gather(jnp.concatenate((ug_group, w_down), axis=1), 'dp', axis=0,...]
    reduce_sum x9 -> x1, other arithmetic: 20.7 us -> 0.61 us  [local(): loss_local = jnp.sum(sums_mid[1])]
    all_to_all x0 -> x1, blocking collectives: none -> 14.7 us  [local(): lax.all_to_all(ug_send, 'fsdp', 0, 0, tiled=True)]
  transfers between devices with their start and end apart: 23 -> 5, of which waited for: 14 -> 2; matrix products, arithmetic and copies ran while one was open for 23% -> 13% of each run, Pallas kernels for 26% -> 38%
where the time goes in v3:
time: 722 us; the launch traced here: 719 us
  Pallas kernels  541 us (75%)
  matrix products  63.6 us (9%)
  local copies, waits for them, and re-layouts  50.2 us (7%)
  between operations  21 us (3%)
  blocking collectives  14.7 us (2%)
  starting transfers between devices  11.9 us (2%)
  other arithmetic  9.74 us (1%)
    pallas_call x1, Pallas kernels, middle(): pl.pallas_call(middle_kernel, in_specs=[hbm] + [vmem] * 7, out_specs=[vme...  161 us
    pallas_call x1, Pallas kernels, middle_back(): pl.pallas_call(middle_back_kernel, in_specs=[hbm] * 7 + [vmem] * 5, out_s...  107 us
    pallas_call x1, Pallas kernels, first_exchange(): pl.pallas_call(first_kernel, in_specs=[hbm, vmem, vmem, vmem], out_specs=...  107 us
    pallas_call x1, Pallas kernels, last_exchange(): pl.pallas_call(last_kernel, in_specs=[vmem] * 5, out_specs=[vmem] * 5, ou...  86 us
    dot_general x7, matrix products, dot(): lax.dot_general(left, right, ((contract[:1], contract[1:]), ((), ())), pr...  63.6 us
    pallas_call x1, Pallas kernels, attn_bwd(): pl.pallas_call(bwd_kernel, grid_spec=pltpu.PrefetchScalarGridSpec(num_sca...  48.9 us
    pallas_call x1, Pallas kernels, attn_fwd(): pl.pallas_call(fwd_kernel, grid_spec=pltpu.PrefetchScalarGridSpec(num_sca...  24.7 us
    all_to_all x1, blocking collectives, local(): lax.all_to_all(ug_send, 'fsdp', 0, 0, tiled=True)  14.7 us
  transfers between devices with their start and end apart: 5, of which 2 were waited for; matrix products, arithmetic and copies ran while one was open for 13% of the time, Pallas kernels for 38%

profile of v3, /device:TPU:4, one launch (start us, length us, event | category | flops | bytes accessed | tf_op | source)
XLA Modules:
  0.0 719.1 jit_solution(15823880315042055970)
XLA Ops:
  11.5 14.7 %all_to_all.14 = bf16[4,40,2560]{2,1,0:T(8,128)(2,1)S(1)} all-to-all(bf16[4,40,2560]{2,1,0:T(8,128)(2,1)S(1)} %pad_maximum_fusion.2), channel_id=1, replica_groups=mesh['dp'=8,'fsdp'=4] {'fsdp'}, dimensions={0} | all-to-all | bytes 1638400 | tf_op jit(solution)/shard_map/all_to_all | solution.py:1343
  27.4 4.7 collective-permute-start
  37.9 6.4 tree_order.1.perm_ref
  46.0 107.0 %first_exchange.1 = (bf16[4,640,1280]{2,1,0:T(8,128)(2,1)S(1)}, bf16[8,4,40,1024]{3,2,1,0:T(8,128)(2,1)S(1)}, bf16[8,40,1280]{2,1,0:T(8,128)(2,1)S(1)}) custom-call(bf16[640,1280]{1,0:T(8,128)(2,1)S(1)} %copy-done, bf16[4,40,1024]{2,1,0:T(8,128)(2,1)S(1)} %pad_maximum_fusion.3.qkv_send, bf16[4,40,128]{2,1,0:T(8,128)(2,1)S(1)} %bitcast.74, ...), custom_call_target="tpu_custom_call" | custom-call | bytes 157286400 | tf_op jit(solution)/shard_map/first_exchange/pallas_call | solution.py:595
  153.0 2.7 copy-done.1
  161.9 4.3 copy.64
  167.5 11.8 %fusion.9.qkv_ref = f32[3,320,2560]{2,1,0:T(8,128)} fusion(bf16[3,320,1280]{2,1,0:T(8,128)(2,1)} %bitcast.91, bf16[2560,1280,1]{1,0,2:T(8,128)(2,1)} %bitcast.78), kind=kOutput, calls=%fused_computation.48 | convolution fusion | flops 6291456000 | bytes 18841600 | tf_op jit(solution)/shard_map/dot_general | solution.py:1279
  179.3 24.7 %tree_attention.1 = (bf16[320,2560]{1,0:T(8,128)(2,1)S(1)}, f32[5,8,2560]{2,1,0:T(8,128)S(1)}) custom-call(s32[20]{0:T(128)S(1)} %copy-done.4, f32[3,320,2560]{2,1,0:T(8,128)} %fusion.9.qkv_ref, f32[5,64,1]{2,1,0:T(8,128)S(1)} %reshape.228.scale_ref), custom_call_target="tpu_custom_call" | custom-call | flops 3523215360 | bytes 12582912 | tf_op jit(solution)/shard_map/tree_attention/pallas_call | solution.py:372
  204.0 5.5 convolution_convert_fusion.1
  210.6 160.7 %middle.1 = (bf16[640,1280]{1,0:T(8,128)(2,1)}, f32[640,1280]{1,0:T(8,128)}, bf16[640,1280]{1,0:T(8,128)(2,1)}, f32[640,1280]{1,0:T(8,128)}, f32[640,1]{1,0:T(8,...) custom-call(bf16[4,640,1280]{2,1,0:T(8,128)(2,1)} %bitcast.101, ...), custom_call_target="tpu_custom_call" | custom-call | flops 25999998976 | bytes 419430400 | tf_op jit(solution)/shard_map/middle/pallas_call | solution.py:949
  371.4 107.2 %middle_back.1 = (f32[640,1280]{1,0:T(8,128)}, bf16[4,640,1280]{2,1,0:T(8,128)(2,1)}, bf16[1280,2560]{1,0:T(8,128)(2,1)}, f32[1,1280]{1,0:T(1,128)}, f32[2,1280]{1,0:T(2,128)}) custom-call(bf16[5,4,128,1280]{3,2,1,0:T(8,128)(2,1)} %get-tuple-element.49.gd_all, bf16[5,1280,512]{2,1,0:T(8,128)(2,1)} %get-tuple-element.50.ht_all, ...), custom_call_target="tpu_custom_call" | custom-call | flops 41999998976 | bytes 209715200 | tf_op jit(solution)/shard_map/middle_back/pallas_call | solution.py:1177
  480.3 5.5 convolution_convert_fusion.3.g_ref
  485.9 48.9 %tree_attention_grad.1 = (bf16[3,320,2560]{2,1,0:T(8,128)(2,1)}, f32[5,64,1]{2,1,0:T(8,128)S(1)}) custom-call(s32[20]{0:T(128)S(1)} %copy-done.4, f32[3,320,2560]{2,1,0:T(8,128)} %fusion.9.qkv_ref, f32[5,64,1]{2,1,0:T(8,128)S(1)} %reshape.228.scale_ref, f32[5,8,2560]{2,1,0:T(8,128)S(1)} %get-tuple-element.48.sum_ref, bf16[320,2560]{1,0:T(8,128)(2,1)S(1)} %copy-done.6, ...), custom_call_target="tpu_custom_call" | custom-call | flops 8808038400 | bytes 20971520 | tf_op jit(solution)/shard_map/tree_attention_grad/pallas_call | solution.py:453
  536.0 11.4 %convolution_convert_fusion.4 = bf16[1280,960]{0,1:T(8,128)(2,1)} fusion(bf16[960,2560]{1,0:T(8,128)(2,1)} %bitcast.102, bf16[2560,1280]{1,0:T(8,128)(2,1)} %bitcast.79), kind=kOutput, calls=%fused_computation.4 | convolution fusion | flops 6292684800 | bytes 13926400 | tf_op jit(solution)/shard_map/dot_general | solution.py:1279
  547.4 4.7 copy.72
  552.2 5.7 convolution_convert_fusion.5
  561.2 4.3 pad_maximum_fusion.grads
  565.6 14.1 %convolution_convert_fusion.2 = bf16[1280,1280]{1,0:T(8,128)(2,1)} fusion(bf16[2560,1280]{1,0:T(8,128)(2,1)} %bitcast.98, bf16[2560,1280]{1,0:T(8,128)(2,1)} %bitcast.97), kind=kOutput, calls=%fused_computation.2 | convolution fusion | flops 8390246400 | bytes 16384000 | tf_op jit(solution)/shard_map/dot_general | solution.py:1279
  579.7 9.4 %convolution_convert_fusion = bf16[2560,1280]{1,0:T(8,128)(2,1)} fusion(bf16[960,2560]{1,0:T(8,128)(2,1)S(1)} %bitcast.105, bf16[1280,1024]{1,0:T(8,128)(2,1)S(1)} %bitcast.73), kind=kOutput, calls=%fused_computation | convolution fusion | flops 6294732800 | bytes 14090240 | tf_op jit(solution)/shard_map/dot_general | solution.py:1279
  589.1 86.0 %last_exchange.1 = (f32[640,1280]{1,0:T(8,128)}, bf16[4,40,1280]{2,1,0:T(8,128)(2,1)S(1)}, f32[4,40,1280]{2,1,0:T(8,128)S(1)}, f32[160,1280]{1,0:T(8,128)}, f32[4,128]{1,0:T(4,128)S(1)}) custom-call(bf16[4,640,1280]{2,1,0:T(8,128)(2,1)} %bitcast.84, f32[640,1280]{1,0:T(8,128)} %get-tuple-element.59.base, bf16[8,160,1280]{2,1,0:T(8,128)(2,1)} %pad_maximum_fusion.grads, ...), custom_call_target="tpu_custom_call" | custom-call | bytes 157286400 | tf_op jit(solution)/shard_map/last_exchange/pallas_call | solution.py:719
  676.8 3.3 collective-permute-start.1
  680.6 3.7 all-to-all-start.1
  692.1 4.4 all-to-all-done.1
  704.5 2.8 copy.92
  (151 shorter events, 43.7 us)
Async XLA Ops:
  7.2 2.6 copy-start.10
  7.2 203.5 %all-gather.2.cloned.1.call-start = ((), (), s32[]{:S(2)}) async-start(), calls=%async_computation.3 | async-start | bytes 11059200 | tf_op jit(solution)/shard_map/all_gather | solution.py:1344
  9.8 16.4 %copy-start.9 = (bf16[160,1280]{1,0:T(8,128)(2,1)S(1)}, bf16[160,1280]{1,0:T(8,128)(2,1)}, u32[]{:S(2)}) copy-start(bf16[160,1280]{1,0:T(8,128)(2,1)} %param.26) | copy-start | bytes 1228804
  11.3 16.1 %copy-start.23 = (bf16[40,1280]{1,0:T(8,128)(2,1)S(1)}, bf16[40,1280]{1,0:T(8,128)(2,1)}, u32[]{:S(2)}) copy-start(bf16[40,1280]{1,0:T(8,128)(2,1)} %param.23) | copy-start | bytes 307204
  11.3 20.8 %copy-start.16 = (s32[640]{0:T(1024)S(1)}, s32[640]{0:T(1024)}, u32[]{:S(2)}) copy-start(s32[640]{0:T(1024)} %param.19) | copy-start | bytes 7684
  11.3 24.1 %copy-start.24 = (bf16[160]{0:T(256)(128)(2,1)S(1)}, bf16[160]{0:T(256)(128)(2,1)}, u32[]{:S(2)}) copy-start(bf16[160]{0:T(256)(128)(2,1)} %param.30) | copy-start | bytes 964
  11.3 24.1 %copy-start.25 = (bf16[160]{0:T(256)(128)(2,1)S(1)}, bf16[160]{0:T(256)(128)(2,1)}, u32[]{:S(2)}) copy-start(bf16[160]{0:T(256)(128)(2,1)} %param.31) | copy-start | bytes 964
  11.4 24.1 %copy-start.20 = (bf16[40]{0:T(256)(128)(2,1)S(1)}, bf16[40]{0:T(256)(128)(2,1)}, u32[]{:S(2)}) copy-start(bf16[40]{0:T(256)(128)(2,1)} %param.27) | copy-start | bytes 244
  11.4 24.1 %copy-start.21 = (bf16[40]{0:T(256)(128)(2,1)S(1)}, bf16[40]{0:T(256)(128)(2,1)}, u32[]{:S(2)}) copy-start(bf16[40]{0:T(256)(128)(2,1)} %param.28) | copy-start | bytes 244
  11.4 24.1 %copy-start.22 = (bf16[40]{0:T(256)(128)(2,1)S(1)}, bf16[40]{0:T(256)(128)(2,1)}, u32[]{:S(2)}) copy-start(bf16[40]{0:T(256)(128)(2,1)} %param.29) | copy-start | bytes 244
  11.4 24.5 %copy-start.13 = (bf16[40,1280]{1,0:T(8,128)(2,1)S(1)}, bf16[40,1280]{1,0:T(8,128)(2,1)}, u32[]{:S(2)}) copy-start(bf16[40,1280]{1,0:T(8,128)(2,1)} %param.20) | copy-start | bytes 307204
  11.5 24.6 %copy-start.14 = (bf16[40,1280]{1,0:T(8,128)(2,1)S(1)}, bf16[40,1280]{1,0:T(8,128)(2,1)}, u32[]{:S(2)}) copy-start(bf16[40,1280]{1,0:T(8,128)(2,1)} %param.21) | copy-start | bytes 307204
  11.5 24.8 %copy-start.15 = (bf16[40,1280]{1,0:T(8,128)(2,1)S(1)}, bf16[40,1280]{1,0:T(8,128)(2,1)}, u32[]{:S(2)}) copy-start(bf16[40,1280]{1,0:T(8,128)(2,1)} %param.22) | copy-start | bytes 307204
  27.3 653.2 %reduce-scatter.2.cloned.1.call-start = ((), (), s32[]{:S(2)}) async-start(), calls=%async_computation.4 | async-start | bytes 7372800 | tf_op jit(solution)/shard_map/reduce_scatter | solution.py:1367
  27.4 17.2 %collective-permute-start = (bf16[40,1280]{1,0:T(8,128)(2,1)S(1)}, bf16[40,1280]{1,0:T(8,128)(2,1)S(1)}, u32[]{:S(2)}, u32[]{:S(2)}) collective-permute-start(bf16[40,1280]{1,0:T(8,128)(2,1)S(1)} %copy-done.23), channel_id=1, source_target_pairs={{0,0},{1,4},{2,8},{3,12},{4,16},{5,20},{6,24},{7,28},{8,1},{9,5},{... | collective-permute-start | bytes 307208 | tf_op jit(solution)/shard_map/ppermute | solution.py:1332
  153.0 2.7 copy-start.1
  167.5 11.8 %copy-start.4 = (s32[20]{0:T(128)S(1)}, s32[20]{0:T(128)}, u32[]{:S(2)}) copy-start(s32[20]{0:T(128)} %tree_order.1.perm_ref) | copy-start | bytes 244
  179.3 24.7 %copy-start.3 = (bf16[8,40,1280]{2,1,0:T(8,128)(2,1)S(1)}, bf16[8,40,1280]{2,1,0:T(8,128)(2,1)}, u32[]{:S(2)}) copy-start(bf16[8,40,1280]{2,1,0:T(8,128)(2,1)} %copy-done.2) | copy-start | bytes 2457604
  480.3 5.6 copy-start.6
  561.2 18.5 %slice-start = ((s8[4915200]{0:T(1024)(128)(4,1)}), s8[720896]{0:T(1024)(128)(4,1)S(1)}, s32[]{:S(2)}) async-start(s8[4915200]{0:T(1024)(128)(4,1)} %bitcast.103), calls=%async_computation.5 | async-start | bytes 1441792
  565.6 14.1 %slice-start.1 = ((s8[4915200]{0:T(1024)(128)(4,1)}), s8[4194304]{0:T(1024)(128)(4,1)S(1)}, s32[]{:S(2)}) async-start(s8[4915200]{0:T(1024)(128)(4,1)} %bitcast.103), calls=%async_computation.6 | async-start | bytes 8388608
  676.8 14.7 %collective-permute-start.1 = (f32[40,1280]{1,0:T(8,128)S(1)}, f32[40,1280]{1,0:T(8,128)S(1)}, u32[]{:S(2)}, u32[]{:S(2)}) collective-permute-start(f32[40,1280]{1,0:T(8,128)S(1)} %reshape.224), channel_id=1, source_target_pairs={{0,0},{4,1},{8,2},{12,3},{16,4},{20,5},{24,6},{28,7},{1,8},{5,9},{... | collective-permute-start | bytes 614408 | tf_op jit(solution)/shard_map/ppermute | solution.py:1397
  680.6 16.0 %all-to-all-start.1 = ((bf16[4,40,2560]{2,1,0:T(8,128)(2,1)}), bf16[4,40,2560]{2,1,0:T(8,128)(2,1)S(1)}, u32[]{:S(2)}, u32[]{:S(2)}) async-start(bf16[4,40,2560]{2,1,0:T(8,128)(2,1)} %bitcast.92), calls=%async_computation.2 | async-start | bytes 1638400 | tf_op jit(solution)/shard_map/all_to_all | solution.py:1398
  704.5 2.9 copy-start.7
  (9 other events, 11.9 us)
Sparse Core Ops, SparseCore 0:
  27.5 167.2 all-gather.1
  478.7 123.3 reduce-scatter.1

commit v4 on v3

v4 whole, which is shorter than its diff:
```python
import functools
import math

import jax
import jax.numpy as jnp
from jax import lax
from jax.experimental import pallas as pl
from jax.experimental.pallas import tpu as pltpu
from jax.sharding import PartitionSpec as P


D = 1280
HEADS = 20
HEAD_DIM = 64
FF = 5120
BLOCK = 128
DEPTH = 10


EPS = 1e-06


def unit_rows(vector):
    inverse = lax.rsqrt(jnp.sum(vector * vector, axis=-1, keepdims=True) + EPS)
    return (vector * inverse, inverse)


def unit_back(grad, unit, inverse):
    return (grad - unit * jnp.sum(grad * unit, axis=-1, keepdims=True)) * inverse


def project(left, right):
    return jnp.dot(left, right, preferred_element_type=jnp.float32)


def project_back(grad, weight):
    return jnp.einsum("te,de->td", grad, weight, preferred_element_type=jnp.float32)


def ancestors(local_parent):
    column = jnp.arange(local_parent.shape[0], dtype=jnp.int32)
    columns = [column]
    for depth_step in range(DEPTH - 1):
        column = jnp.where(column >= 0, local_parent[jnp.maximum(column, 0)], -1)
        columns.append(column)
    return jnp.stack(columns, axis=1)


def head_back(grad_flat, unit, inverse, scale):
    scaled = (grad_flat * scale).reshape(unit.shape)
    raw = unit_back(scaled, unit, inverse).reshape(grad_flat.shape)
    scale_grad = jnp.sum(grad_flat * unit.reshape(grad_flat.shape), axis=0)
    return (raw, scale_grad)


def general(
    states,
    teacher,
    parent_ids,
    valid_mask,
    w_query,
    w_key,
    w_value,
    w_out,
    w_up,
    w_gate,
    w_down,
    qk_scale,
    attn_rate,
    mlp_rate,
    up_scale,
    gate_scale,
):
    rows_dev = states.shape[0]
    blocks_dev = rows_dev // BLOCK
    width_rows = w_query.shape[0]
    span = DEPTH * BLOCK
    factor = math.sqrt(HEAD_DIM)
    root_width = math.sqrt(D)
    mask_f = valid_mask.astype(jnp.float32)
    qkv_local = jnp.concatenate((w_query, w_key, w_value), axis=1)
    scal_width_local = jnp.stack((qk_scale, attn_rate, mlp_rate), axis=1)
    piece_qkv = lax.all_gather(qkv_local, ("dp", "fsdp"), axis=0, tiled=True)
    piece_out = lax.all_gather(w_out, ("dp", "fsdp"), axis=0, tiled=True)
    piece_scal = lax.all_gather(scal_width_local, ("dp", "fsdp"), axis=0, tiled=True)
    lefts = states
    total = jnp.dot(lefts, piece_qkv, preferred_element_type=jnp.float32)
    scal_whole = piece_scal
    qkv_raw = total
    scal_width = scal_whole
    scale_qk = scal_width[:, 0].astype(jnp.float32)
    rate_attn = scal_width[:, 1].astype(jnp.float32)
    rate_mlp = scal_width[:, 2].astype(jnp.float32)
    query_raw = qkv_raw[:, :D]
    key_raw = qkv_raw[:, D : 2 * D]
    values = qkv_raw[:, 2 * D :].astype(jnp.bfloat16)
    query_unit, query_inv = unit_rows(query_raw.reshape(rows_dev, HEADS, HEAD_DIM))
    key_unit, key_inv = unit_rows(key_raw.reshape(rows_dev, HEADS, HEAD_DIM))
    query_n = (query_unit.reshape(rows_dev, D) * scale_qk).astype(jnp.bfloat16)
    key_n = (key_unit.reshape(rows_dev, D) * scale_qk).astype(jnp.bfloat16)
    key_group, value_group = (
        lax.all_gather(key_n, "fsdp", axis=0, tiled=True),
        lax.all_gather(values, "fsdp", axis=0, tiled=True),
    )
    group_blocks = parent_ids.shape[0]
    group_base = lax.axis_index("dp") * group_blocks
    local_parent = jnp.where(parent_ids >= 0, parent_ids - group_base, -1)
    paths_all = ancestors(local_parent)
    own_first = lax.axis_index("fsdp") * blocks_dev
    paths = lax.dynamic_slice_in_dim(paths_all, own_first, blocks_dev, 0)
    safe_paths = jnp.maximum(paths, 0)
    key_rows = key_group.reshape(group_blocks, BLOCK, D)[safe_paths].reshape(
        blocks_dev, span, HEADS, HEAD_DIM
    )
    value_rows = value_group.reshape(group_blocks, BLOCK, D)[safe_paths].reshape(
        blocks_dev, span, HEADS, HEAD_DIM
    )
    slot_of = jnp.arange(span, dtype=jnp.int32) // BLOCK
    offset = jnp.arange(span, dtype=jnp.int32) % BLOCK
    row_pos = jnp.arange(BLOCK, dtype=jnp.int32)
    causal = offset[None, :] <= row_pos[:, None]
    is_live = jnp.take(paths, slot_of, axis=1) >= 0
    allowed = jnp.where(slot_of[None, None, :] == 0, causal[None], is_live[:, None, :])[:, None]
    query_heads = query_n.reshape(blocks_dev, BLOCK, HEADS, HEAD_DIM)
    scores = factor * jnp.einsum(
        "bqhd,bkhd->bhqk", query_heads, key_rows, preferred_element_type=jnp.float32
    )
    scores = jnp.where(allowed, scores, jnp.float32(-1e30))
    row_max = jnp.max(scores, axis=-1, keepdims=True)
    powers = jnp.exp(scores - row_max)
    row_sum = jnp.sum(powers, axis=-1, keepdims=True)
    probs_b = (powers / row_sum).astype(jnp.bfloat16)
    log_total = row_max + jnp.log(row_sum)
    mixed = jnp.einsum("bhqk,bkhd->bqhd", probs_b, value_rows, preferred_element_type=jnp.float32)
    mixed = mixed.reshape(rows_dev, D).astype(jnp.bfloat16)
    inputs = states.astype(jnp.float32)
    attn = project(mixed, piece_out)
    attn_unit, attn_inv = unit_rows(attn)
    hidden, hidden_inv = unit_rows(inputs + rate_attn * (attn_unit - inputs))
    hidden_b = hidden.astype(jnp.bfloat16)
    ffn_local = jnp.concatenate((w_up, w_gate), axis=1)
    scal_hidden_local = jnp.concatenate(
        (up_scale.reshape(width_rows, 4), gate_scale.reshape(width_rows, 4)), axis=1
    )
    piece_ffn = lax.all_gather(ffn_local, ("dp", "fsdp"), axis=0, tiled=True)
    piece_scal = lax.all_gather(scal_hidden_local, ("dp", "fsdp"), axis=0, tiled=True)
    lefts = hidden_b
    total = jnp.dot(lefts, piece_ffn, preferred_element_type=jnp.float32)
    scal_whole = piece_scal
    scale_up = scal_whole[:, :4].reshape(FF).astype(jnp.float32)
    scale_gate = scal_whole[:, 4:].reshape(FF).astype(jnp.float32)
    up_proj = total[:, :FF]
    gate_proj = total[:, FF:]
    upscaled = up_proj * scale_up
    gated = gate_proj * scale_gate * root_width
    sigmoid_gate = jax.nn.sigmoid(gated)
    act = (upscaled * (gated * sigmoid_gate)).astype(jnp.bfloat16)
    lefts = act
    down = jnp.dot(
        lefts,
        lax.all_gather(w_down, ("dp", "fsdp"), axis=0, tiled=True),
        preferred_element_type=jnp.float32,
    )
    down_unit, down_inv = unit_rows(down)
    result, result_inv = unit_rows(hidden + rate_mlp * (down_unit - hidden))
    loss_local = jnp.sum(mask_f[:, None] * (result - teacher) ** 2)
    valid_count, loss_sum = lax.psum((jnp.sum(mask_f), loss_local), ("dp", "fsdp"))
    loss = loss_sum / valid_count
    g_result = 2.0 * mask_f[:, None] * (result - teacher) / valid_count
    g_last = unit_back(g_result, result, result_inv)
    g_hidden = g_last * (1.0 - rate_mlp)
    g_rate_mlp = jnp.sum(g_last * (down_unit - hidden), axis=0)
    g_down = unit_back(g_last * rate_mlp, down_unit, down_inv).astype(jnp.bfloat16)
    g_act = jnp.einsum(
        "te,fe->tf",
        g_down,
        lax.all_gather(w_down, ("dp", "fsdp"), axis=0, tiled=True),
        preferred_element_type=jnp.float32,
    )
    g_upscaled = g_act * (gated * sigmoid_gate)
    g_gated = g_act * upscaled * sigmoid_gate * (1.0 + gated * (1.0 - sigmoid_gate))
    grad_up_scale = jnp.sum(g_upscaled * up_proj, axis=0)
    grad_gate_scale = jnp.sum(g_gated * gate_proj * root_width, axis=0)
    g_up = (g_upscaled * scale_up).astype(jnp.bfloat16)
    g_gate = (g_gated * scale_gate * root_width).astype(jnp.bfloat16)
    g_both = jnp.concatenate((g_up, g_gate), axis=1)
    g_hidden = g_hidden + jnp.einsum(
        "tc,dc->td",
        g_both,
        lax.all_gather(ffn_local, ("dp", "fsdp"), axis=0, tiled=True),
        preferred_element_type=jnp.float32,
    )
    scal_terms = jnp.concatenate(
        (grad_up_scale.reshape(D, 4), grad_gate_scale.reshape(D, 4)), axis=1
    )
    lefts = hidden_b
    main = jnp.einsum("td,tc->dc", lefts, g_both, preferred_element_type=jnp.float32)
    ffn_share = lax.psum_scatter(
        jnp.concatenate((main, scal_terms), axis=1), ("dp", "fsdp"), scatter_dimension=0, tiled=True
    )
    lefts = act
    grad_down = lax.psum_scatter(
        jnp.einsum("tf,te->fe", lefts, g_down, preferred_element_type=jnp.float32),
        ("dp", "fsdp"),
        scatter_dimension=0,
        tiled=True,
    )
    g_pre = unit_back(g_hidden, hidden, hidden_inv)
    g_states = g_pre * (1.0 - rate_attn)
    g_rate_attn = jnp.sum(g_pre * (attn_unit - inputs), axis=0)
    g_attn = unit_back(g_pre * rate_attn, attn_unit, attn_inv).astype(jnp.bfloat16)
    g_mixed = project_back(g_attn, piece_out).astype(jnp.bfloat16)
    scores = factor * jnp.einsum(
        "bqhd,bkhd->bhqk", query_heads, key_rows, preferred_element_type=jnp.float32
    )
    probs = jnp.where(allowed, jnp.exp(scores - log_total), jnp.float32(0.0))
    probs_again = probs.astype(jnp.bfloat16)
    g_heads = g_mixed.reshape(blocks_dev, BLOCK, HEADS, HEAD_DIM)
    g_probs = jnp.einsum("bqhd,bkhd->bhqk", g_heads, value_rows, preferred_element_type=jnp.float32)
    delta = jnp.sum(probs * g_probs, axis=-1, keepdims=True)
    g_scores = (probs * (g_probs - delta)).astype(jnp.bfloat16)
    g_query_n = factor * jnp.einsum(
        "bhqk,bkhd->bqhd", g_scores, key_rows, preferred_element_type=jnp.float32
    )
    g_key_rows = factor * jnp.einsum(
        "bhqk,bqhd->bkhd", g_scores, query_heads, preferred_element_type=jnp.float32
    )
    g_value_rows = jnp.einsum(
        "bhqk,bqhd->bkhd", probs_again, g_heads, preferred_element_type=jnp.float32
    )
    flat_paths = safe_paths.reshape(blocks_dev * DEPTH)
    g_key_group = (
        jnp.zeros((group_blocks, BLOCK, D), jnp.float32)
        .at[flat_paths]
        .add(g_key_rows.reshape(blocks_dev * DEPTH, BLOCK, D))
    )
    g_value_group = (
        jnp.zeros((group_blocks, BLOCK, D), jnp.float32)
        .at[flat_paths]
        .add(g_value_rows.reshape(blocks_dev * DEPTH, BLOCK, D))
    )
    g_key_n, g_values = (
        lax.psum_scatter(
            g_key_group.reshape(group_blocks * BLOCK, D).astype(jnp.bfloat16),
            "fsdp",
            scatter_dimension=0,
            tiled=True,
        ).astype(jnp.float32),
        lax.psum_scatter(
            g_value_group.reshape(group_blocks * BLOCK, D).astype(jnp.bfloat16),
            "fsdp",
            scatter_dimension=0,
            tiled=True,
        ).astype(jnp.float32),
    )
    g_query_raw, scale_from_query = head_back(
        g_query_n.reshape(rows_dev, D), query_unit, query_inv, scale_qk
    )
    g_key_raw, scale_from_key = head_back(g_key_n, key_unit, key_inv, scale_qk)
    grad_qk_scale = scale_from_query + scale_from_key
    g_qkv = jnp.concatenate(
        (
            g_query_raw.astype(jnp.bfloat16),
            g_key_raw.astype(jnp.bfloat16),
            g_values.astype(jnp.bfloat16),
        ),
        axis=1,
    )
    g_states = g_states + jnp.einsum(
        "tc,dc->td",
        g_qkv,
        lax.all_gather(qkv_local, ("dp", "fsdp"), axis=0, tiled=True),
        preferred_element_type=jnp.float32,
    )
    vector_terms = jnp.stack((grad_qk_scale, g_rate_attn, g_rate_mlp), axis=1)
    lefts = states
    main = jnp.einsum("td,tc->dc", lefts, g_qkv, preferred_element_type=jnp.float32)
    outer = jnp.einsum("td,tc->dc", mixed, g_attn, preferred_element_type=jnp.float32)
    attn_share = lax.psum_scatter(
        jnp.concatenate((main, outer, vector_terms), axis=1),
        ("dp", "fsdp"),
        scatter_dimension=0,
        tiled=True,
    )
    return (
        result.astype(jnp.bfloat16),
        loss,
        g_states,
        attn_share[:, :D],
        attn_share[:, D : 2 * D],
        attn_share[:, 2 * D : 3 * D],
        attn_share[:, 3 * D : 4 * D],
        ffn_share[:, :FF],
        ffn_share[:, FF : 2 * FF],
        grad_down,
        attn_share[:, 4 * D],
        attn_share[:, 4 * D + 1],
        attn_share[:, 4 * D + 2],
        ffn_share[:, 2 * FF : 2 * FF + 4].reshape(-1),
        ffn_share[:, 2 * FF + 4 : 2 * FF + 8].reshape(-1),
    )

TRUNK = 8
NB = 20
TOK = NB * BLOCK
F32 = jnp.float32
BF = jnp.bfloat16


def head_norm(raw):
    inv = lax.rsqrt(jnp.sum(raw * raw, axis=0, keepdims=True) + EPS)
    return raw * inv, inv


def lanes_at(start, size):
    return pl.ds(pl.multiple_of(start, 128), size)


def rows_at(start, size):
    return pl.ds(pl.multiple_of(start, 16), size)


def each_chunk(visit):
    for j in range(TRUNK // 2):
        parts = [(0, 256 * j, "all")] if j else []
        visit(256 * j, parts + [(256 * j, 256, "causal")])
    trunk = TRUNK * BLOCK

    def branches(j, carry):
        start = trunk + 256 * j
        visit(start, [(0, trunk, "all"), (start, 256, "pair")])
        return carry

    def leaves(j, carry):
        start = trunk + 4 * BLOCK + 256 * j
        visit(start, [(0, trunk, "all"), (trunk + BLOCK * j, BLOCK, "all"), (start, 256, "pair")])
        return carry

    for j in range(2):
        branches(j, 0)
    for j in range(4):
        leaves(j, 0)


def masked(kind, value):
    if kind == "all":
        return value
    key = lax.broadcasted_iota(jnp.int32, (256, 256), 0)
    query = lax.broadcasted_iota(jnp.int32, (256, 256), 1)
    keep = key <= query
    if kind == "pair":
        keep = keep & ((key < 128) == (query < 128))
    return jnp.where(keep, value, jnp.zeros_like(value))


def nn(a, b):
    return lax.dot_general(a, b, (((1,), (0,)), ((), ())), preferred_element_type=F32)


def nt(a, b):
    return lax.dot_general(a, b, (((1,), (1,)), ((), ())), preferred_element_type=F32)


def attention_back_kernel(order, qkv, scales, sums, mixed, ga_all, w_o, ht_all, gug_all,
                          g_qkv, g_scale, part_out, g_up, g_gate,
                          ga_b, ga, gm, raw, out_b, qT, q, k, kT, v, gT, g, dq, dk, dv, delta, inv,
                          gug_b, ht_r, ht_l, ring_r, ring_l, next_r, next_l, hid_buf, hid_in,
                          ga_sem, gug_sem, row_sem, raw_sem, out_sem, ring_send, ring_recv, a2a_send, a2a_recv):
    me = lax.axis_index("fsdp")
    place = ring_place()
    peers = group_peers()
    right, left = {"dp": ring_dp(place + 1)}, {"dp": ring_dp(place - 1)}
    count, chunk, side = gug_b.shape[0], ring_r.shape[1], ring_r.shape[2]
    heads = g_scale.shape[0]
    rows_w = hid_buf.shape[1]

    def slices(step):
        slot = step % 2
        cut_r = rows_at(ring_dp(place - 1 - step) * chunk, chunk)
        cut_l = rows_at(ring_dp(place + 1 + step) * chunk, chunk)
        return [
            pltpu.make_async_copy(ht_all.at[:, cut_r], ht_r.at[slot], row_sem.at[0, slot]),
            pltpu.make_async_copy(ht_all.at[:, cut_l], ht_l.at[slot], row_sem.at[1, slot]),
        ]

    def raw_copy(head):
        slot = head % 2
        return pltpu.make_async_copy(
            qkv.at[:, rows_at(head * HEAD_DIM, HEAD_DIM)], raw.at[slot], raw_sem.at[slot]
        )

    def out_copy(head):
        slot = head % 2
        return pltpu.make_async_copy(
            out_b.at[slot], g_qkv.at[:, rows_at(head * HEAD_DIM, HEAD_DIM)], out_sem.at[slot]
        )

    load_ga = pltpu.make_async_copy(ga_all, ga_b, ga_sem.at[0])
    load_ga.start()
    raw_copy(0).start()
    for copy in slices(0):
        copy.start()
    loads = [pltpu.make_async_copy(gug_all.at[i], gug_b.at[i], gug_sem.at[i]) for i in range(count)]
    for copy in loads:
        copy.start()
    for copy in slices(1):
        copy.start()
    greet([*peers, right, left])
    load_ga.wait()

    def pick(i, carry):
        ga[lanes_at(i * BLOCK, BLOCK)] = ga_b[order[0, i]]
        return carry

    lax.fori_loop(0, NB, pick, 0)

    def back(n, carry):
        gm[:, tile(n)] = nt(w_o[...], ga[tile(n)]).astype(BF)
        return carry

    lax.fori_loop(0, TOK // TILE, back, 0)

    def outer(n, carry):
        part_out[:, tile(n)] = nn(mixed[...], ga[:, tile(n)]).astype(BF)
        return carry

    lax.fori_loop(0, D // TILE, outer, 0)

    def parts(step):
        slot = step % 2
        for copy in slices(step):
            copy.wait()
        next_r[...] = jnp.zeros_like(next_r)
        next_l[...] = jnp.zeros_like(next_l)

        def add(i, carry):
            next_r[...] = next_r[...] + nn(ht_r[slot, i], gug_b[i, :, pl.ds(0, side)])
            next_l[...] = next_l[...] + nn(ht_l[slot, i], gug_b[i, :, pl.ds(side, side)])
            return carry

        lax.fori_loop(0, count, add, 0)

        @pl.when(step + 2 < 8)
        def _():
            for copy in slices(step + 2):
                copy.start()

    def hop_copies(step):
        return [
            send(ring_r.at[step], ring_r.at[step + 1], ring_send.at[0, step], ring_recv.at[0, step], right),
            send(ring_l.at[step], ring_l.at[step + 1], ring_send.at[1, step], ring_recv.at[1, step], left),
        ]

    def exchange():
        return [
            send(hid_buf.at[peer["fsdp"]], hid_in.at[me], a2a_send.at[i], a2a_recv.at[i], peer)
            for i, peer in enumerate(peers)
        ]

    def hop(step):
        parts(step + 1)
        for copy in hop_copies(step):
            copy.wait()

        @pl.when(step < 6)
        def _():
            ring_r[step + 1] = (ring_r[step + 1].astype(F32) + next_r[...]).astype(BF)
            ring_l[step + 1] = (ring_l[step + 1].astype(F32) + next_l[...]).astype(BF)
            for copy in hop_copies(step + 1):
                copy.start()

        @pl.when(step == 6)
        def _():
            for start, ring, own in ((0, ring_r, next_r), (side, ring_l, next_l)):
                total = ring[7].astype(F32) + own[...]
                for i in range(4):
                    hid_buf[i, :, start : start + side] = total[i * rows_w : (i + 1) * rows_w].astype(BF)
            for copy in exchange():
                copy.start()

    for copy in loads:
        copy.wait()
    parts(0)
    ring_r[0] = next_r[...].astype(BF)
    ring_l[0] = next_l[...].astype(BF)
    for copy in hop_copies(0):
        copy.start()

    def open_head(head):
        slot = head % 2
        raw_copy(head).wait()

        @pl.when(head + 1 < heads)
        def _():
            raw_copy(head + 1).start()

        @pl.when(head >= 2)
        def _():
            out_copy(head - 2).wait()

        scale = scales[head]
        mine = rows_at(head * HEAD_DIM, HEAD_DIM)

        for i in range(NB):
            here = slice(i * BLOCK, (i + 1) * BLOCK)
            q_unit, _ = head_norm(raw[slot, 0, :, here])
            k_unit, _ = head_norm(raw[slot, 1, :, here])
            q8 = (q_unit * scale).astype(BF) * BF(8.0)
            qT[:, here] = q8
            q[here, :] = q8.T
            kn = (k_unit * scale).astype(BF)
            kT[:, here] = kn
            k[here, :] = kn.T
            v[here, :] = raw[slot, 2, :, here].astype(BF).T
            gh = gm[mine, here]
            gT[:, here] = gh
            g[here, :] = gh.T
            delta[:, here] = jnp.sum(gh.astype(F32) * mixed[mine, here].astype(F32), axis=0, keepdims=True)
            inv[:, here] = sums[head, 0:1, here]
        dk[...] = jnp.zeros_like(dk)
        dv[...] = jnp.zeros_like(dv)

    def close_head(head):
        slot = head % 2
        scale = scales[head]

        def visit(start, pieces):
            span = lanes_at(start, 256)
            query, grad = qT[:, span], gT[:, span]
            query_rows, grad_rows = q[span, :], g[span, :]
            scale_row, delta_row = inv[:, span], delta[:, span]
            acc = jnp.zeros((64, 256), F32)
            for kstart, size, kind in pieces:
                keys = lanes_at(kstart, size)
                probs = masked(kind, jnp.exp(nn(k[keys, :], query)) * scale_row)
                g_probs = nn(v[keys, :], grad)
                g_scores = (probs * (g_probs - delta_row)).astype(BF)
                dv[keys, :] += nn(probs.astype(BF), grad_rows)
                dk[keys, :] += nn(g_scores, query_rows)
                acc = acc + nn(kT[:, keys], g_scores)
            dq[:, span] = acc * 8.0

        each_chunk(visit)
        total = jnp.zeros((64, BLOCK), F32)
        for i in range(NB):
            here = slice(i * BLOCK, (i + 1) * BLOCK)
            for which, grad in ((0, dq[:, here]), (1, dk[here, :].T)):
                unit, inverse = head_norm(raw[slot, which, :, here])
                total = total + grad * unit
                scaled = grad * scale
                value = (scaled - unit * jnp.sum(scaled * unit, axis=0, keepdims=True)) * inverse
                out_b[slot, which, :, here] = value.astype(BF)
            out_b[slot, 2, :, here] = dv[here, :].T.astype(BF)
        g_scale[head] = jnp.sum(total, axis=1, keepdims=True)
        out_copy(head).start()

    def work(i, carry):
        pl.when(i % 2 == 0)(functools.partial(open_head, i // 2))
        pl.when(i % 2 == 1)(functools.partial(close_head, i // 2))
        pl.when(i < 7)(functools.partial(hop, i))
        return carry

    lax.fori_loop(0, 2 * heads, work, 0)
    for copy in exchange():
        copy.wait()
    hid_in[me] = hid_buf[me]
    size = g_up.shape[1] // 32
    for which, out in enumerate((g_up, g_gate)):
        for d in range(8):
            start = (8 * which + d) * size
            block = [hid_in[i, :, start : start + size].astype(F32) for i in range(4)]
            out[:, d * 4 * size : (d + 1) * 4 * size] = jnp.concatenate(block, axis=1)
    for head in (heads - 2, heads - 1):
        out_copy(head).wait()


def attention_back(order, qkv, scales, sums, mixed, ga_all, w_o, ht_all, gug_all):
    heads = scales.shape[0]
    count, tokens, hidden_width = gug_all.shape
    chunk = ht_all.shape[1] // 8
    side = hidden_width // 2
    rows_w = chunk // 4
    vmem, hbm = pl.BlockSpec(memory_space=pltpu.VMEM), pl.BlockSpec(memory_space=pl.ANY)
    smem = pl.BlockSpec(memory_space=pltpu.SMEM)
    dma = pltpu.SemaphoreType.DMA
    return pl.pallas_call(
        attention_back_kernel,
        in_specs=[smem, hbm, vmem, vmem, vmem, hbm, vmem, hbm, hbm],
        out_specs=[hbm, vmem, vmem, vmem, vmem],
        out_shape=[
            jax.ShapeDtypeStruct(qkv.shape, BF),
            jax.ShapeDtypeStruct(scales.shape, F32),
            jax.ShapeDtypeStruct(w_o.shape, BF),
            jax.ShapeDtypeStruct((rows_w, 2 * hidden_width), F32),
            jax.ShapeDtypeStruct((rows_w, 2 * hidden_width), F32),
        ],
        scratch_shapes=[
            pltpu.VMEM(ga_all.shape, BF),
            pltpu.VMEM((TOK, w_o.shape[1]), BF),
            pltpu.VMEM(mixed.shape, BF),
            pltpu.VMEM((2, 3, HEAD_DIM, TOK), F32),
            pltpu.VMEM((2, 3, HEAD_DIM, TOK), BF),
            pltpu.VMEM((HEAD_DIM, TOK), BF),
            pltpu.VMEM((TOK, HEAD_DIM), BF),
            pltpu.VMEM((TOK, HEAD_DIM), BF),
            pltpu.VMEM((HEAD_DIM, TOK), BF),
            pltpu.VMEM((TOK, HEAD_DIM), BF),
            pltpu.VMEM((HEAD_DIM, TOK), BF),
            pltpu.VMEM((TOK, HEAD_DIM), BF),
            pltpu.VMEM((HEAD_DIM, TOK), F32),
            pltpu.VMEM((TOK, HEAD_DIM), F32),
            pltpu.VMEM((TOK, HEAD_DIM), F32),
            pltpu.VMEM((1, TOK), F32),
            pltpu.VMEM((1, TOK), F32),
            pltpu.VMEM(gug_all.shape, BF),
            pltpu.VMEM((2, count, chunk, tokens), BF),
            pltpu.VMEM((2, count, chunk, tokens), BF),
            pltpu.VMEM((8, chunk, side), BF),
            pltpu.VMEM((8, chunk, side), BF),
            pltpu.VMEM((chunk, side), F32),
            pltpu.VMEM((chunk, side), F32),
            pltpu.VMEM((4, rows_w, hidden_width), BF),
            pltpu.VMEM((4, rows_w, hidden_width), BF),
            dma((1,)),
            dma((count,)),
            dma((2, 2)),
            dma((2,)),
            dma((2,)),
            dma((2, 7)),
            dma((2, 7)),
            dma((3,)),
            dma((3,)),
        ],
        compiler_params=pltpu.CompilerParams(
            collective_id=5, has_side_effects=True, vmem_limit_bytes=62 << 20
        ),
        name="attention_back",
        cost_estimate=pl.CostEstimate(flops=40 * 10**9, bytes_accessed=60 << 20, transcendentals=14 << 20),
    )(order, qkv, scales, sums, mixed, ga_all, w_o, ht_all, gug_all)


MESH = pl.DeviceIdType.MESH


def ring_place():
    dp = lax.axis_index("dp")
    z, y = dp // 2, dp % 2
    return z + y * (7 - 2 * z)


def ring_dp(place):
    place = (place + 16) % 8
    y = place // 4
    return 2 * (place + y * (7 - 2 * place)) + y


def greet(peers):
    barrier = pltpu.get_barrier_semaphore()
    for peer in peers:
        pl.semaphore_signal(barrier, inc=1, device_id=peer, device_id_type=MESH)
    pl.semaphore_wait(barrier, len(peers))


def group_peers():
    me = lax.axis_index("fsdp")
    core = 1 - 2 * (me % 2)
    chip = 2 - 4 * (me // 2)
    return {"fsdp": me + core}, {"fsdp": me + chip}, {"fsdp": me + core + chip}


def send(src, dst, send_sem, recv_sem, peer):
    return pltpu.make_async_remote_copy(
        src_ref=src, dst_ref=dst, send_sem=send_sem, recv_sem=recv_sem, device_id=peer, device_id_type=MESH
    )


def forward_kernel(order, states, qkv_send, extra, out_piece, ug_send,
                   tokens_t, w_t, w_o, w_ug, qkv, mixed, sums, share,
                   land, weights, tok, turned, tok_t, out_w, ug_land, ug_own, raw, qs, ks, vs, blocks, stage,
                   tok_send, tok_recv, a2a_send, a2a_recv, ring_send, ring_recv, ug_s, ug_r, local_sem, raw_sem,
                   stage_sem):
    me, dp = lax.axis_index("fsdp"), lax.axis_index("dp")
    place = ring_place()
    sibling, across, corner = group_peers()
    right, left = {"dp": ring_dp(place + 1)}, {"dp": ring_dp(place - 1)}
    rows, width = states.shape
    piece = land.shape[1]
    chunk = 4 * piece
    half = chunk // 2
    cols = mixed.shape[0]
    heads = cols // HEAD_DIM
    greet([sibling, across, corner, right, left])

    exchange, ug_exchange = [], []
    for i, peer in enumerate((sibling, across, corner)):
        copy = send(qkv_send.at[peer["fsdp"]], land.at[me], a2a_send.at[i], a2a_recv.at[i], peer)
        copy.start()
        exchange.append(copy)
    far = []
    for i in range(2):
        part = pl.ds(i * (rows // 2), rows // 2)
        here = pl.ds(2 * rows + i * (rows // 2), rows // 2)
        copy = send(states.at[part], tok.at[here], tok_send.at[i], tok_recv.at[i], across)
        copy.start()
        far.append(copy)
    near = send(states, tok.at[pl.ds(rows, rows)], tok_send.at[2], tok_recv.at[2], sibling)
    near.start()
    own = pltpu.make_async_copy(states, tok.at[pl.ds(0, rows)], local_sem.at[0])
    own.start()
    for i, peer in enumerate((sibling, across, corner)):
        copy = send(ug_send.at[peer["fsdp"]], ug_land.at[me], a2a_send.at[3 + i], a2a_recv.at[3 + i], peer)
        copy.start()
        ug_exchange.append(copy)
    land[me] = qkv_send[me]
    ug_land[me] = ug_send[me]
    out_w[dp] = out_piece[...]
    vs[HEAD_DIM:, :] = jnp.ones((vs.shape[0] - HEAD_DIM, TOK), BF)
    for copy in exchange:
        copy.wait()
    weights[rows_at(dp * chunk, chunk)] = jnp.concatenate([land[i].astype(F32) for i in range(4)], axis=0).astype(BF)
    last = pl.ds(weights.shape[1] - 128, 128)
    weights[rows_at(dp * chunk, chunk), last] = weights[rows_at(dp * chunk, chunk), last] + extra[...]

    def hop(step, carry):
        to_right, to_left = ring_dp(place - step), ring_dp(place + step)
        first, second = rows_at(to_right * chunk, half), rows_at(to_left * chunk + half, half)
        copies = [
            send(weights.at[first], weights.at[first], ring_send.at[0, step], ring_recv.at[0, step], right),
            send(weights.at[second], weights.at[second], ring_send.at[1, step], ring_recv.at[1, step], left),
            send(out_w.at[to_right, :, pl.ds(0, 640)], out_w.at[to_right, :, pl.ds(0, 640)],
                 ring_send.at[2, step], ring_recv.at[2, step], right),
            send(out_w.at[to_left, :, pl.ds(640, 640)], out_w.at[to_left, :, pl.ds(640, 640)],
                 ring_send.at[3, step], ring_recv.at[3, step], left),
        ]
        for copy in copies:
            copy.start()
        for copy in copies:
            copy.wait()
        return carry

    def ug_copies(step):
        first = rows_at(ring_dp(place - step) * chunk, half)
        second = rows_at(ring_dp(place + step) * chunk + half, half)
        return [
            send(w_ug.at[first], w_ug.at[first], ug_s.at[0, step], ug_r.at[0, step], right),
            send(w_ug.at[second], w_ug.at[second], ug_s.at[1, step], ug_r.at[1, step], left),
        ]

    def ug_hop(step):
        for copy in ug_copies(step):
            copy.wait()

        @pl.when(step < 6)
        def _():
            for copy in ug_copies(step + 1):
                copy.start()

    def turn(i, carry):
        turned[i] = tok[lanes_at(i * BLOCK, BLOCK)].T
        return carry

    lax.fori_loop(0, 1, hop, 0)
    near.wait()
    own.wait()
    lax.fori_loop(0, 4, turn, 0)
    lax.fori_loop(1, 2, hop, 0)
    lax.fori_loop(4, 7, turn, 0)
    lax.fori_loop(2, 3, hop, 0)
    lax.fori_loop(7, 10, turn, 0)
    lax.fori_loop(3, 5, hop, 0)
    passed = []
    for i in range(2):
        far[i].wait()
        here = pl.ds(2 * rows + i * (rows // 2), rows // 2)
        there = pl.ds(3 * rows + i * (rows // 2), rows // 2)
        copy = send(tok.at[here], tok.at[there], tok_send.at[3 + i], tok_recv.at[3 + i], sibling)
        copy.start()
        passed.append(copy)
    for copy in ug_exchange:
        copy.wait()
    ug_own[...] = jnp.concatenate([ug_land[i].astype(F32) for i in range(4)], axis=0).astype(BF)
    ug_store = pltpu.make_async_copy(ug_own, w_ug.at[rows_at(dp * chunk, chunk)], local_sem.at[1])
    ug_store.start()
    lax.fori_loop(5, 6, hop, 0)
    lax.fori_loop(10, 15, turn, 0)
    lax.fori_loop(6, 7, hop, 0)
    ug_store.wait()
    for copy in ug_copies(0):
        copy.start()
    for copy in passed:
        copy.wait()

    lax.fori_loop(15, NB, turn, 0)

    def arrange(i, carry):
        tok_t[:, lanes_at(i * BLOCK, BLOCK)] = turned[order[0, i]]
        return carry

    lax.fori_loop(0, NB, arrange, 0)
    keep = pltpu.make_async_copy(tok_t, tokens_t, local_sem.at[2])
    keep.start()

    def turn_weights(i, carry):
        w_t[:, lanes_at(i * BLOCK, BLOCK)] = weights[rows_at(i * BLOCK, BLOCK)].T
        return carry

    lax.fori_loop(0, width // BLOCK, turn_weights, 0)
    w_o[...] = jnp.concatenate([out_w[i].astype(F32) for i in range(8)], axis=0).astype(BF)

    def raw_copies(head):
        slot = head % 2
        return [
            pltpu.make_async_copy(
                raw.at[slot, pl.ds(which * HEAD_DIM, HEAD_DIM)],
                qkv.at[which, rows_at(head * HEAD_DIM, HEAD_DIM)],
                raw_sem.at[slot, which],
            )
            for which in range(3)
        ]

    def attend(head, carry):
        slot = head % 2

        @pl.when(head >= 2)
        def _():
            for copy in raw_copies(head - 2):
                copy.wait()

        left_rows = jnp.concatenate(
            [w_t[rows_at(which * cols + head * HEAD_DIM, HEAD_DIM)] for which in range(3)], axis=0
        )

        def project_tile(n, carry):
            raw[slot, :, tile(n)] = nn(left_rows, tok_t[:, tile(n)])
            return carry

        lax.fori_loop(0, TOK // TILE, project_tile, 0, unroll=2)
        for copy in raw_copies(head):
            copy.start()
        scale = weights[rows_at(me * cols + head * HEAD_DIM, HEAD_DIM), last][:, HEAD_DIM : HEAD_DIM + 1].astype(F32)

        def prepare(i, carry):
            here = lanes_at(i * BLOCK, BLOCK)
            q_unit, _ = head_norm(raw[slot, pl.ds(0, HEAD_DIM), here])
            k_unit, _ = head_norm(raw[slot, pl.ds(HEAD_DIM, HEAD_DIM), here])
            qs[:, here] = (q_unit * scale).astype(BF) * BF(8.0)
            ks[here, :] = (k_unit * scale).astype(BF).T
            vs[0:HEAD_DIM, here] = raw[slot, pl.ds(2 * HEAD_DIM, HEAD_DIM), here].astype(BF)
            return carry

        lax.fori_loop(0, NB, prepare, 0, unroll=NB)

        def visit(start, parts):
            span = lanes_at(start, 256)
            query = qs[:, span]
            acc = jnp.zeros((vs.shape[0], 256), F32)
            for kstart, count, kind in parts:
                keys = lanes_at(kstart, count)
                powers = masked(kind, jnp.exp(nn(ks[keys, :], query))).astype(BF)
                acc = acc + nn(vs[:, keys], powers)
            total = 1.0 / acc[HEAD_DIM : HEAD_DIM + 1, :]
            mixed[rows_at(head * HEAD_DIM, HEAD_DIM), span] = (acc[0:HEAD_DIM, :] * total).astype(BF)
            sums[head, :, span] = jnp.broadcast_to(total, (8, 256))

        each_chunk(visit)

        @pl.when(head % 2 == 1)
        def _():
            ug_hop(head // 2)

        return carry

    lax.fori_loop(0, heads, attend, 0)
    ug_hop(2)

    def share_copy(b):
        slot = b % 2
        return pltpu.make_async_copy(
            stage.at[slot], share.at[b // 5, lanes_at((b % 5) * BLOCK, BLOCK)], stage_sem.at[slot]
        )

    def split(i, carry):
        blocks[i] = mixed[:, lanes_at(i * BLOCK, BLOCK)]
        return carry

    lax.fori_loop(0, NB, split, 0)

    def out_project(b, carry):
        @pl.when(b >= 2)
        def _():
            share_copy(b - 2).wait()

        stage[b % 2] = nn(blocks[order[1, b]].T, w_o[...]).astype(BF)
        share_copy(b).start()
        return carry

    lax.fori_loop(0, NB, out_project, 0, unroll=4)
    lax.fori_loop(3, 7, lambda step, c: (ug_hop(step), c)[1], 0)
    keep.wait()
    for b in (NB - 2, NB - 1):
        share_copy(b).wait()
    for head in (heads - 2, heads - 1):
        for copy in raw_copies(head):
            copy.wait()


def forward(order, states, qkv_send, extra, out_piece, ug_send):
    tps, rows_w, packed = qkv_send.shape
    tokens, width = states.shape
    hidden_width = ug_send.shape[2]
    cols = 8 * rows_w
    vmem, hbm = pl.BlockSpec(memory_space=pltpu.VMEM), pl.BlockSpec(memory_space=pl.ANY)
    smem = pl.BlockSpec(memory_space=pltpu.SMEM)
    dma = pltpu.SemaphoreType.DMA
    return pl.pallas_call(
        forward_kernel,
        in_specs=[smem, hbm] + [vmem] * 4,
        out_specs=[hbm, vmem, vmem, hbm, hbm, vmem, vmem, hbm],
        out_shape=[
            jax.ShapeDtypeStruct((width, TOK), BF),
            jax.ShapeDtypeStruct((packed, width), BF),
            jax.ShapeDtypeStruct((cols, width), BF),
            jax.ShapeDtypeStruct((width, hidden_width), BF),
            jax.ShapeDtypeStruct((3, cols, TOK), F32),
            jax.ShapeDtypeStruct((cols, TOK), BF),
            jax.ShapeDtypeStruct((cols // HEAD_DIM, 8, TOK), F32),
            jax.ShapeDtypeStruct((tps, tokens, width), BF),
        ],
        scratch_shapes=[
            pltpu.VMEM((tps, rows_w, packed), BF),
            pltpu.VMEM((width, packed), BF),
            pltpu.VMEM((TOK, width), BF),
            pltpu.VMEM((NB, width, BLOCK), BF),
            pltpu.VMEM((width, TOK), BF),
            pltpu.VMEM((8, rows_w, width), BF),
            pltpu.VMEM((tps, rows_w, hidden_width), BF),
            pltpu.VMEM((tps * rows_w, hidden_width), BF),
            pltpu.VMEM((2, 3 * HEAD_DIM, TOK), F32),
            pltpu.VMEM((HEAD_DIM, TOK), BF),
            pltpu.VMEM((TOK, HEAD_DIM), BF),
            pltpu.VMEM((HEAD_DIM + 16, TOK), BF),
            pltpu.VMEM((NB, cols, BLOCK), BF),
            pltpu.VMEM((2, BLOCK, width), BF),
            dma((5,)),
            dma((5,)),
            dma((6,)),
            dma((6,)),
            dma((4, 7)),
            dma((4, 7)),
            dma((2, 7)),
            dma((2, 7)),
            dma((3,)),
            dma((2, 3)),
            dma((2,)),
        ],
        compiler_params=pltpu.CompilerParams(
            collective_id=1, has_side_effects=True, vmem_limit_bytes=56 << 20
        ),
        cost_estimate=pl.CostEstimate(flops=12 * 10**9, bytes_accessed=200 << 20, transcendentals=14 << 20),
        name="forward",
    )(order, states, qkv_send, extra, out_piece, ug_send)


def last_kernel(order, base, tokens_t, g_qkv, w_t, part_out, vectors,
                g_states, g_query, g_key, g_value, out_rows, vec_own,
                gq_b, blocks, tok_r, tok_l, share, turned, core_buf, x_buf, base_b, gs_b,
                ring_r, ring_l, ring_o, ring_v, next_r, next_l, row_buf, row_in, vec_part, vec_in,
                in_sem, row_sem, base_sem, core_send, core_recv, x_send, x_recv,
                ring_send, ring_recv, a2a_send, a2a_recv):
    me, dp = lax.axis_index("fsdp"), lax.axis_index("dp")
    place = ring_place()
    sibling, across, corner = group_peers()
    right, left = {"dp": ring_dp(place + 1)}, {"dp": ring_dp(place - 1)}
    chunk, side = ring_r.shape[1], ring_r.shape[2]
    rows = share.shape[1]
    quarter = rows // 4
    width = w_t.shape[1]
    heads_width = gq_b.shape[0]
    rows_w = row_buf.shape[1]

    def slices(step):
        slot = step % 2
        cut_r = rows_at(ring_dp(place - 1 - step) * chunk, chunk)
        cut_l = rows_at(ring_dp(place + 1 + step) * chunk, chunk)
        return [
            pltpu.make_async_copy(tokens_t.at[cut_r], tok_r.at[slot], row_sem.at[0, slot]),
            pltpu.make_async_copy(tokens_t.at[cut_l], tok_l.at[slot], row_sem.at[1, slot]),
        ]

    def base_copy(i):
        return pltpu.make_async_copy(base.at[pl.ds(i * quarter, quarter)], base_b.at[i % 2], base_sem.at[0, i % 2])

    def gs_copy(i):
        return pltpu.make_async_copy(gs_b.at[i % 2], g_states.at[pl.ds(i * quarter, quarter)], base_sem.at[1, i % 2])

    load_q = pltpu.make_async_copy(g_qkv, gq_b, in_sem.at[0])
    load_q.start()
    for step in (0, 1):
        for copy in slices(step):
            copy.start()
    greet([sibling, across, corner, right, left])

    def parts(step):
        slot = step % 2
        for copy in slices(step):
            copy.wait()
        next_r[...] = nt(tok_r[slot], gq_b[pl.ds(0, side)])
        next_l[...] = nt(tok_l[slot], gq_b[pl.ds(side, heads_width - side)])

        @pl.when(step + 2 < 8)
        def _():
            for copy in slices(step + 2):
                copy.start()

    def hop_copies(step):
        return [
            send(ring.at[step], ring.at[step + 1], ring_send.at[i, step], ring_recv.at[i, step], peer)
            for i, (ring, peer) in enumerate(((ring_r, right), (ring_l, left), (ring_o, left), (ring_v, right)))
        ]

    def through(r, slot):
        for i in range(rows // BLOCK):
            turned[i * BLOCK : (i + 1) * BLOCK] = blocks[order[1, r * (rows // BLOCK) + i]].T

        def one(n, carry):
            share[slot, :, tile(n)] = nn(turned[...], w_t[pl.ds(0, heads_width), tile(n)]).astype(BF)
            return carry

        lax.fori_loop(0, width // TILE, one, 0)

    core = [
        send(share.at[0], core_buf.at[0], core_send.at[0], core_recv.at[0], sibling),
        send(share.at[2], core_buf.at[1], core_send.at[1], core_recv.at[1], sibling),
    ]
    far = [
        send(share.at[1, pl.ds(i * quarter, quarter)], x_buf.at[pl.ds(i * quarter, quarter)], x_send.at[i],
             x_recv.at[i], across)
        for i in range(4)
    ]
    load_q.wait()

    def split(i, carry):
        blocks[i] = gq_b[:, lanes_at(i * BLOCK, BLOCK)]
        return carry

    def hop(step, carry):
        parts(step)

        @pl.when(step == 0)
        def _():
            ring_r[0] = next_r[...].astype(BF)
            ring_l[0] = next_l[...].astype(BF)
            ring_o[0] = part_out[ring_dp(place + 1)]
            ring_v[0] = vectors[ring_dp(place - 1)]

        @pl.when(step > 0)
        def _():
            for copy in hop_copies(step - 1):
                copy.wait()
            ring_r[step] = (ring_r[step].astype(F32) + next_r[...]).astype(BF)
            ring_l[step] = (ring_l[step].astype(F32) + next_l[...]).astype(BF)
            ring_o[step] = (ring_o[step].astype(F32) + part_out[ring_dp(place + 1 + step)].astype(F32)).astype(BF)
            ring_v[step] = ring_v[step] + vectors[ring_dp(place - 1 - step)]

        for copy in hop_copies(step):
            copy.start()
        @pl.when(step == 0)
        def _():
            lax.fori_loop(0, NB, split, 0)

        pl.when(step < 4)(functools.partial(through, 3 - step, step % 3))

        @pl.when(step == 0)
        def _():
            core[0].start()

        @pl.when(step == 1)
        def _():
            core[0].wait()
            for i in range(4):
                span = pl.ds(i * quarter, quarter)
                share[1, span] = (share[1, span].astype(F32) + core_buf[0, span].astype(F32)).astype(BF)
                far[i].start()

        @pl.when(step == 2)
        def _():
            core[1].start()

        return carry

    lax.fori_loop(0, 7, hop, 0)
    base_copy(0).start()
    base_copy(1).start()
    parts(7)
    for copy in hop_copies(6):
        copy.wait()
    total = jnp.concatenate((ring_r[7].astype(F32) + next_r[...], ring_l[7].astype(F32) + next_l[...]), axis=1)
    for i in range(4):
        row_buf[i] = total[i * rows_w : (i + 1) * rows_w].astype(BF)
    vec_part[...] = ring_v[7] + vectors[dp]
    exchange = []
    for i, peer in enumerate((sibling, across, corner)):
        to = peer["fsdp"]
        copies = [
            send(row_buf.at[to], row_in.at[me], a2a_send.at[i], a2a_recv.at[i], peer),
            send(vec_part.at[to], vec_in.at[me], a2a_send.at[3 + i], a2a_recv.at[3 + i], peer),
        ]
        for copy in copies:
            copy.start()
        exchange += copies
    row_in[me] = row_buf[me]
    vec_in[me] = vec_part[me]
    out_rows[...] = ring_o[7].astype(F32) + part_out[dp].astype(F32)
    core[1].wait()
    for i in range(4):
        span = pl.ds(i * quarter, quarter)
        far[i].wait()
        base_copy(i).wait()
        if i >= 2:
            gs_copy(i - 2).wait()
        gs_b[i % 2] = base_b[i % 2] + (
            share[0, span].astype(F32) + core_buf[1, span].astype(F32) + x_buf[span].astype(F32)
        )
        gs_copy(i).start()
        if i < 2:
            base_copy(i + 2).start()
    for copy in exchange:
        copy.wait()
    vec_own[...] = vec_in[0] + vec_in[1] + vec_in[2] + vec_in[3]
    cols = heads_width // 3
    for which, out in enumerate((g_query, g_key, g_value)):
        out[...] = jnp.concatenate(
            [row_in[i, :, which * cols : (which + 1) * cols].astype(F32) for i in range(4)], axis=1
        )
    for i in (2, 3):
        gs_copy(i).wait()


def last_exchange(order, base, tokens_t, g_qkv, w_t, part_out, vectors):
    rows, width = base.shape
    heads_width = g_qkv.shape[0]
    rows_w = part_out.shape[1]
    chunk = 4 * rows_w
    side = 2 * heads_width // 3
    vmem, hbm = pl.BlockSpec(memory_space=pltpu.VMEM), pl.BlockSpec(memory_space=pl.ANY)
    dma = pltpu.SemaphoreType.DMA
    return pl.pallas_call(
        last_kernel,
        in_specs=[pl.BlockSpec(memory_space=pltpu.SMEM), hbm, hbm, hbm, vmem, vmem, vmem],
        out_specs=[hbm] + [vmem] * 5,
        out_shape=[jax.ShapeDtypeStruct((rows, width), F32)]
        + [jax.ShapeDtypeStruct((rows_w, width), F32)] * 4
        + [jax.ShapeDtypeStruct(vectors.shape[2:], F32)],
        scratch_shapes=[
            pltpu.VMEM(g_qkv.shape, BF),
            pltpu.VMEM((NB, heads_width, BLOCK), BF),
            pltpu.VMEM((2, chunk, tokens_t.shape[1]), BF),
            pltpu.VMEM((2, chunk, tokens_t.shape[1]), BF),
            pltpu.VMEM((3, rows, width), BF),
            pltpu.VMEM((rows, heads_width), BF),
            pltpu.VMEM((2, rows, width), BF),
            pltpu.VMEM((rows, width), BF),
            pltpu.VMEM((2, rows // 4, width), F32),
            pltpu.VMEM((2, rows // 4, width), F32),
            pltpu.VMEM((8, chunk, side), BF),
            pltpu.VMEM((8, chunk, heads_width - side), BF),
            pltpu.VMEM((8, rows_w, width), BF),
            pltpu.VMEM(vectors.shape, F32),
            pltpu.VMEM((chunk, side), F32),
            pltpu.VMEM((chunk, heads_width - side), F32),
            pltpu.VMEM((4, rows_w, heads_width), BF),
            pltpu.VMEM((4, rows_w, heads_width), BF),
            pltpu.VMEM(vectors.shape[1:], F32),
            pltpu.VMEM(vectors.shape[1:], F32),
            dma((1,)),
            dma((2, 2)),
            dma((2, 2)),
            dma((2,)),
            dma((2,)),
            dma((4,)),
            dma((4,)),
            dma((4, 7)),
            dma((4, 7)),
            dma((6,)),
            dma((6,)),
        ],
        compiler_params=pltpu.CompilerParams(
            collective_id=2, has_side_effects=True, vmem_limit_bytes=48 << 20
        ),
        cost_estimate=pl.CostEstimate(flops=13 * 10**9, bytes_accessed=100 << 20, transcendentals=0),
        name="last_exchange",
    )(order, base, tokens_t, g_qkv, w_t, part_out, vectors)


CHUNK = 128
TILE = 256


def tile(index, base=0):
    return pl.ds(pl.multiple_of(base + index * TILE, TILE), TILE)


def nt(a, b):
    return lax.dot_general(a, b, (((1,), (1,)), ((), ())), preferred_element_type=F32)


def middle_kernel(share, states, teacher, weight, mask, w_ug, w_own, rates, scales,
                  w_d, out_states, hidden, attn_unit, back, attn_inv, hidden_inv, sums, gd_all, ht_all, act_all, ug_all,
                  part, core, x_buf, tok, gd, act, act_t, ug, ht,
                  ld_sem, core_send, core_recv, x_send, x_recv, tok_send, tok_recv, gd_send, gd_recv, gd_own,
                  out_sem, ring_send, ring_recv):
    sibling, across, _ = group_peers()
    dp, place = lax.axis_index("dp"), ring_place()
    right, left = {"dp": ring_dp(place + 1)}, {"dp": ring_dp(place - 1)}
    piece = w_own.shape[0]
    count = part.shape[0]
    width = hidden.shape[1]
    rate_attn, rate_mlp = rates[0:1], rates[1:2]

    def rows(i):
        return pl.ds(pl.multiple_of(i * CHUNK, CHUNK), CHUNK)

    def load(i):
        return pltpu.make_async_copy(share.at[:, rows(i)], part.at[i], ld_sem.at[i])

    def core_a(stage, i):
        return send(part.at[i, 3], core.at[0, i], core_send.at[stage, 0, i], core_recv.at[stage, 0, i], sibling)

    def core_b(stage, i):
        return send(part.at[i, 1], core.at[1, i], core_send.at[stage, 1, i], core_recv.at[stage, 1, i], sibling)

    def chip(stage, i):
        return send(part.at[i, 2], x_buf.at[i], x_send.at[stage, i], x_recv.at[stage, i], across)

    def spread(buf, own, sems, recvs, i):
        return [
            send(own, buf.at[i, 1], sems.at[0, i], recvs.at[0, i], sibling),
            send(own, buf.at[i, 2], sems.at[1, i], recvs.at[1, i], across),
            send(buf.at[i, 2], buf.at[i, 3], sems.at[2, i], recvs.at[2, i], sibling),
        ]

    def tok_copies(i):
        return spread(tok, tok.at[i, 0], tok_send, tok_recv, i)

    def gd_copies(i):
        return spread(gd_all, gd.at[i], gd_send, gd_recv, i)

    def gd_local(i):
        return pltpu.make_async_copy(gd.at[i], gd_all.at[i, 0], gd_own.at[i])

    def outs(i):
        slot = i % 2
        return [
            pltpu.make_async_copy(ht.at[slot], ht_all.at[i], out_sem.at[0, slot]),
            pltpu.make_async_copy(act_t.at[slot], act_all.at[i], out_sem.at[1, slot]),
            pltpu.make_async_copy(ug.at[slot], ug_all.at[i], out_sem.at[2, slot]),
        ]

    def ring(step):
        first = rows_at(ring_dp(place - step) * piece, piece // 2)
        second = rows_at(ring_dp(place + step) * piece + piece // 2, piece // 2)
        return [
            send(w_d.at[first], w_d.at[first], ring_send.at[0, step], ring_recv.at[0, step], right),
            send(w_d.at[second], w_d.at[second], ring_send.at[1, step], ring_recv.at[1, step], left),
        ]

    def hop(step, carry):
        for copy in ring(step):
            copy.wait()

        @pl.when(step < 6)
        def _():
            for copy in ring(step + 1):
                copy.start()

        return carry

    def forward_far(stage, i):
        core_a(stage, i).wait_recv()
        part[i, 2] = (part[i, 2].astype(F32) + core[0, i].astype(F32)).astype(BF)
        chip(stage, i).start()

    def reduced(stage, i):
        core_b(stage, i).wait_recv()
        chip(stage, i).wait_recv()
        total = part[i, 0].astype(F32) + core[1, i].astype(F32) + x_buf[i].astype(F32)
        core_a(stage, i).wait_send()
        core_b(stage, i).wait_send()
        chip(stage, i).wait_send()
        return total

    sums[...] = jnp.zeros_like(sums)
    lax.fori_loop(0, count, lambda i, c: (load(i).start(), c)[1], 0)
    w_d[rows_at(dp * piece, piece)] = w_own[...]
    greet([sibling, across, right, left])
    for copy in ring(0):
        copy.start()

    def open_core(i, carry):
        load(i).wait()
        core_a(0, i).start()
        core_b(0, i).start()
        return carry

    lax.fori_loop(0, count, open_core, 0)
    lax.fori_loop(0, count, lambda i, c: (forward_far(0, i), c)[1], 0)

    def norm_hidden(i):
        unit, inverse = unit_rows(reduced(0, i))
        own = states[rows(i)].astype(F32)
        value, value_inv = unit_rows(own + rate_attn * (unit - own))
        hidden[rows(i)] = value
        attn_unit[rows(i)] = unit.astype(BF)
        attn_inv[rows(i)] = inverse
        hidden_inv[rows(i)] = value_inv
        tok[i, 0] = value.astype(BF)
        copies = tok_copies(i)
        copies[0].start()
        copies[1].start()

    def pass_tokens(i):
        copies = tok_copies(i)
        copies[1].wait_recv()
        copies[2].start()

    def feed(i):
        copies = tok_copies(i)
        copies[0].wait()
        copies[1].wait_send()
        copies[2].wait()
        slot = i % 2

        @pl.when(i >= 2)
        def _():
            for copy in outs(i - 2):
                copy.wait()

        def up(n, carry):
            here = tok[i].reshape(4 * CHUNK, width)
            up_proj = nn(here, w_ug[:, tile(n)])
            gate_proj = nn(here, w_ug[:, tile(n, width)])
            gated = gate_proj * scales[1:2, tile(n)]
            value = up_proj * scales[0:1, tile(n)] * (gated * jax.nn.sigmoid(gated))
            act[:, tile(n)] = value.astype(BF)
            act_t[slot, tile(n)] = value.astype(BF).T
            ug[slot, :, tile(n)] = up_proj.astype(BF)
            ug[slot, :, tile(n, width)] = gate_proj.astype(BF)
            return carry

        lax.fori_loop(0, width // TILE, up, 0)

        @pl.when(i == 0)
        def _():
            lax.fori_loop(4, 7, hop, 0)

        def down(n, carry):
            value = nn(act[...], w_d[:, tile(n)])
            part[i, :, :, tile(n)] = value.astype(BF).reshape(4, CHUNK, TILE)
            ht[slot, tile(n)] = tok[i, :, :, tile(n)].reshape(4 * CHUNK, TILE).T
            return carry

        lax.fori_loop(0, width // TILE, down, 0)
        core_a(1, i).start()
        core_b(1, i).start()
        for copy in outs(i):
            copy.start()
        forward_far(1, i)

    def finish(i):
        unit, inverse = unit_rows(reduced(1, i))
        own = hidden[rows(i)]
        result, result_inv = unit_rows(own + rate_mlp * (unit - own))
        out_states[rows(i)] = result.astype(BF)
        diff = result - teacher[rows(i)]
        sums[1:2] = sums[1:2] + jnp.sum(mask[rows(i)] * (diff * diff), axis=0, keepdims=True)
        g_last = unit_back(weight[rows(i)] * diff, result, result_inv)
        sums[0:1] = sums[0:1] + jnp.sum(g_last * (unit - own), axis=0, keepdims=True)
        back[rows(i)] = g_last * (1.0 - rate_mlp)
        gd[i] = unit_back(g_last * rate_mlp, unit, inverse).astype(BF)
        copies = gd_copies(i)
        copies[0].start()
        copies[1].start()
        gd_local(i).start()

    def pass_grads(i):
        copies = gd_copies(i)
        copies[1].wait_recv()
        copies[2].start()

    stages = (norm_hidden, pass_tokens, feed, finish, pass_grads)

    def step(t, carry):
        for lag, stage in enumerate(stages):
            pl.when((t >= lag) & (t < lag + count))(functools.partial(stage, t - lag))

        @pl.when(t < 2)
        def _():
            lax.fori_loop(2 * t, 2 * t + 2, hop, 0)

        return carry

    lax.fori_loop(0, count + len(stages) - 1, step, 0)

    def close(i, carry):
        copies = gd_copies(i)
        copies[0].wait()
        copies[1].wait_send()
        copies[2].wait()
        gd_local(i).wait()
        return carry

    lax.fori_loop(0, count, close, 0)
    for i in (count - 2, count - 1):
        for copy in outs(i):
            copy.wait()


def middle(share, states, teacher, weight, mask, w_ug, w_own, rates, scales):
    rows, width = states.shape
    count = rows // CHUNK
    vmem, hbm = pl.BlockSpec(memory_space=pltpu.VMEM), pl.BlockSpec(memory_space=pl.ANY)
    dma = pltpu.SemaphoreType.DMA
    return pl.pallas_call(
        middle_kernel,
        in_specs=[hbm] + [vmem] * 8,
        out_specs=[vmem] * 8 + [hbm] * 4,
        out_shape=[
            jax.ShapeDtypeStruct((8 * w_own.shape[0], width), BF),
            jax.ShapeDtypeStruct((rows, width), BF),
            jax.ShapeDtypeStruct((rows, width), F32),
            jax.ShapeDtypeStruct((rows, width), BF),
            jax.ShapeDtypeStruct((rows, width), F32),
            jax.ShapeDtypeStruct((rows, 1), F32),
            jax.ShapeDtypeStruct((rows, 1), F32),
            jax.ShapeDtypeStruct((2, width), F32),
            jax.ShapeDtypeStruct((count, 4, CHUNK, width), BF),
            jax.ShapeDtypeStruct((count, width, 4 * CHUNK), BF),
            jax.ShapeDtypeStruct((count, width, 4 * CHUNK), BF),
            jax.ShapeDtypeStruct((count, 4 * CHUNK, 2 * width), BF),
        ],
        scratch_shapes=[
            pltpu.VMEM((count, 4, CHUNK, width), BF),
            pltpu.VMEM((2, count, CHUNK, width), BF),
            pltpu.VMEM((count, CHUNK, width), BF),
            pltpu.VMEM((count, 4, CHUNK, width), BF),
            pltpu.VMEM((count, CHUNK, width), BF),
            pltpu.VMEM((4 * CHUNK, width), BF),
            pltpu.VMEM((2, width, 4 * CHUNK), BF),
            pltpu.VMEM((2, 4 * CHUNK, 2 * width), BF),
            pltpu.VMEM((2, width, 4 * CHUNK), BF),
            dma((count,)),
            dma((2, 2, count)),
            dma((2, 2, count)),
            dma((2, count)),
            dma((2, count)),
            dma((3, count)),
            dma((3, count)),
            dma((3, count)),
            dma((3, count)),
            dma((count,)),
            dma((3, 2)),
            dma((2, 7)),
            dma((2, 7)),
        ],
        compiler_params=pltpu.CompilerParams(
            collective_id=3, has_side_effects=True, vmem_limit_bytes=60 << 20
        ),
        cost_estimate=pl.CostEstimate(flops=26 * 10**9, bytes_accessed=400 << 20, transcendentals=4 << 20),
        name="middle",
    )(share, states, teacher, weight, mask, w_ug, w_own, rates, scales)


def middle_back_kernel(gd_all, act_all, ug_all, hidden, attn_unit, states, back, attn_inv, hidden_inv, w_ug, w_d,
                       rates, scales, base, ga_all, gug_all, down_rows, sums, ff_sums,
                       part, core, x_buf, ga, gd, act, ug, gug, own_f, own_b, base_buf, dwd, column, ring_buf,
                       gd_sem, act_sem, in_sem, own_sem, core_send, core_recv, x_send, x_recv, ga_send, ga_recv,
                       ga_own, base_sem, out_sem, ring_send, ring_recv):
    sibling, across, _ = group_peers()
    dp, place = lax.axis_index("dp"), ring_place()
    right, left = {"dp": ring_dp(place + 1)}, {"dp": ring_dp(place - 1)}
    count = core.shape[1]
    width = w_d.shape[0]
    half = ring_buf.shape[2]
    rate_attn = rates[0:1]

    def rows(i):
        return pl.ds(pl.multiple_of(i * CHUNK, CHUNK), CHUNK)

    def load_gd(i):
        return pltpu.make_async_copy(gd_all.at[i], gd.at[i], gd_sem.at[i])

    def load_act(i):
        return pltpu.make_async_copy(act_all.at[i], act.at[i], act_sem.at[i])

    def load_ug(i):
        return pltpu.make_async_copy(ug_all.at[i], ug.at[i % 2], in_sem.at[i % 2])

    def store_gug(i):
        return pltpu.make_async_copy(gug.at[i % 2], gug_all.at[i], out_sem.at[i % 2])

    def own_rows(i):
        return [
            pltpu.make_async_copy(hidden.at[rows(i)], own_f.at[0], own_sem.at[0]),
            pltpu.make_async_copy(back.at[rows(i)], own_f.at[1], own_sem.at[1]),
            pltpu.make_async_copy(attn_unit.at[rows(i)], own_b.at[0], own_sem.at[2]),
            pltpu.make_async_copy(states.at[rows(i)], own_b.at[1], own_sem.at[3]),
        ]

    def core_a(i):
        return send(part.at[i % 3, 3], core.at[0, i], core_send.at[0, i], core_recv.at[0, i], sibling)

    def core_b(i):
        return send(part.at[i % 3, 1], core.at[1, i], core_send.at[1, i], core_recv.at[1, i], sibling)

    def chip(i):
        return send(part.at[i % 3, 2], x_buf.at[i], x_send.at[i], x_recv.at[i], across)

    def ga_copies(i):
        return [
            send(ga.at[i], ga_all.at[1, rows(i)], ga_send.at[0, i], ga_recv.at[0, i], sibling),
            send(ga.at[i], ga_all.at[2, rows(i)], ga_send.at[1, i], ga_recv.at[1, i], across),
            send(ga_all.at[2, rows(i)], ga_all.at[3, rows(i)], ga_send.at[2, i], ga_recv.at[2, i], sibling),
        ]

    def ga_local(i):
        return pltpu.make_async_copy(ga.at[i], ga_all.at[0, rows(i)], ga_own.at[i])

    def base_copy(i):
        return pltpu.make_async_copy(base_buf.at[i % 2], base.at[rows(i)], base_sem.at[i % 2])

    def right_half(step):
        return rows_at(ring_dp(place - 1 - step) * 2 * half, half)

    def left_half(step):
        return rows_at(ring_dp(place + 1 + step) * 2 * half + half, half)

    def ring(step):
        return [
            send(ring_buf.at[0, step], ring_buf.at[0, step + 1], ring_send.at[0, step], ring_recv.at[0, step], right),
            send(ring_buf.at[1, step], ring_buf.at[1, step + 1], ring_send.at[1, step], ring_recv.at[1, step], left),
        ]

    def hop(step, carry):
        for copy in ring(step):
            copy.wait()

        @pl.when(step < 6)
        def _():
            for side, cut in ((0, right_half(step + 1)), (1, left_half(step + 1))):
                ring_buf[side, step + 1] = (
                    ring_buf[side, step + 1].astype(F32) + dwd[cut].astype(F32)
                ).astype(BF)
            for copy in ring(step + 1):
                copy.start()

        return carry

    for copy in [load_ug(0)] + own_rows(0):
        copy.start()
    lax.fori_loop(0, count, lambda i, c: (load_gd(i).start(), c)[1], 0)
    lax.fori_loop(0, count, lambda i, c: (load_act(i).start(), c)[1], 0)
    sums[...] = jnp.zeros_like(sums)
    ff_sums[...] = jnp.zeros_like(ff_sums)
    greet([sibling, across, right, left])
    lax.fori_loop(0, count, lambda i, c: (load_gd(i).wait(), c)[1], 0)

    def feed(i):
        slot = i % 2
        load_ug(i).wait()

        @pl.when(i + 1 < count)
        def _():
            load_ug(i + 1).start()

        @pl.when(i >= 2)
        def _():
            store_gug(i - 2).wait()

        def grads(n, carry):
            g_act = nt(gd[i].reshape(4 * CHUNK, width), w_d[tile(n)])
            up_proj = ug[slot, :, tile(n)].astype(F32)
            gate_proj = ug[slot, :, tile(n, width)].astype(F32)
            scale_up, scale_gate = scales[0:1, tile(n)], scales[1:2, tile(n)]
            gated = gate_proj * scale_gate
            sigmoid = jax.nn.sigmoid(gated)
            g_upscaled = g_act * (gated * sigmoid)
            g_gated = g_act * (up_proj * scale_up) * sigmoid * (1.0 + gated * (1.0 - sigmoid))
            ff_sums[0:1, tile(n)] = ff_sums[0:1, tile(n)] + jnp.sum(g_upscaled * up_proj, axis=0, keepdims=True)
            ff_sums[1:2, tile(n)] = ff_sums[1:2, tile(n)] + jnp.sum(g_gated * gate_proj, axis=0, keepdims=True)
            gug[slot, :, tile(n)] = (g_upscaled * scale_up).astype(BF)
            gug[slot, :, tile(n, width)] = (g_gated * scale_gate).astype(BF)
            return carry

        lax.fori_loop(0, width // TILE, grads, 0)
        store_gug(i).start()

        def through(n, carry):
            value = nt(gug[slot], w_ug[tile(n)])
            part[i % 3, :, :, tile(n)] = value.astype(BF).reshape(4, CHUNK, TILE)
            return carry

        lax.fori_loop(0, width // TILE, through, 0)
        core_a(i).start()
        core_b(i).start()
        core_a(i).wait_recv()
        part[i % 3, 2] = (part[i % 3, 2].astype(F32) + core[0, i].astype(F32)).astype(BF)
        chip(i).start()

    def down_grads():
        lax.fori_loop(0, count, lambda i, c: (load_act(i).wait(), c)[1], 0)

        def outer(n, carry):
            column[...] = jnp.zeros_like(column)

            def add(k, carry):
                column[...] = column[...] + nn(act[k], gd[k, :, :, tile(n)].reshape(4 * CHUNK, TILE))
                return carry

            lax.fori_loop(0, count, add, 0)
            dwd[:, tile(n)] = column[...].astype(BF)
            return carry

        lax.fori_loop(0, width // TILE, outer, 0)
        ring_buf[0, 0] = dwd[right_half(0)]
        ring_buf[1, 0] = dwd[left_half(0)]
        for copy in ring(0):
            copy.start()

    def finish(i):
        core_b(i).wait_recv()
        chip(i).wait_recv()
        through = part[i % 3, 0].astype(F32) + core[1, i].astype(F32) + x_buf[i].astype(F32)
        core_a(i).wait_send()
        core_b(i).wait_send()
        chip(i).wait_send()
        for copy in own_rows(i):
            copy.wait()
        value, unit, own = own_f[0], own_b[0].astype(F32), own_b[1].astype(F32)
        g_pre = unit_back(own_f[1] + through, value, hidden_inv[rows(i)])

        @pl.when(i + 1 < count)
        def _():
            for copy in own_rows(i + 1):
                copy.start()

        @pl.when(i >= 2)
        def _():
            base_copy(i - 2).wait()

        base_buf[i % 2] = g_pre * (1.0 - rate_attn)
        base_copy(i).start()
        sums[0:1] = sums[0:1] + jnp.sum(g_pre * (unit - own), axis=0, keepdims=True)
        ga[i] = unit_back(g_pre * rate_attn, unit, attn_inv[rows(i)]).astype(BF)
        copies = ga_copies(i)
        copies[0].start()
        copies[1].start()
        ga_local(i).start()

    def pass_grads(i):
        copies = ga_copies(i)
        copies[1].wait_recv()
        copies[2].start()

    stages = (feed, finish, pass_grads)

    def step(t, carry):
        for lag, stage in enumerate(stages):
            pl.when((t >= lag) & (t < lag + count))(functools.partial(stage, t - lag))
        pl.when(t == 0)(down_grads)

        @pl.when((t >= 1) & (t < 4))
        def _():
            lax.fori_loop(2 * t - 2, 2 * t, hop, 0)

        return carry

    lax.fori_loop(0, count + len(stages) - 1, step, 0)
    hop(6, 0)
    own = dp * 2 * half
    down_rows[pl.ds(0, half)] = ring_buf[0, 7].astype(F32) + dwd[rows_at(own, half)].astype(F32)
    down_rows[pl.ds(half, half)] = ring_buf[1, 7].astype(F32) + dwd[rows_at(own + half, half)].astype(F32)

    def close(i, carry):
        copies = ga_copies(i)
        copies[0].wait()
        copies[1].wait_send()
        copies[2].wait()
        ga_local(i).wait()
        return carry

    lax.fori_loop(0, count, close, 0)
    for i in (count - 2, count - 1):
        base_copy(i).wait()
        store_gug(i).wait()


def middle_back(gd_all, act_all, ug_all, hidden, attn_unit, states, back, attn_inv, hidden_inv, w_ug, w_d, rates,
                scales):
    rows, width = states.shape
    count = rows // CHUNK
    piece = width // 8
    vmem, hbm = pl.BlockSpec(memory_space=pltpu.VMEM), pl.BlockSpec(memory_space=pl.ANY)
    dma = pltpu.SemaphoreType.DMA
    return pl.pallas_call(
        middle_back_kernel,
        in_specs=[hbm] * 7 + [vmem] * 6,
        out_specs=[hbm, hbm, hbm, vmem, vmem, vmem],
        out_shape=[
            jax.ShapeDtypeStruct((rows, width), F32),
            jax.ShapeDtypeStruct((4, rows, width), BF),
            jax.ShapeDtypeStruct((count, 4 * CHUNK, 2 * width), BF),
            jax.ShapeDtypeStruct((piece, width), F32),
            jax.ShapeDtypeStruct((1, width), F32),
            jax.ShapeDtypeStruct((2, width), F32),
        ],
        scratch_shapes=[
            pltpu.VMEM((3, 4, CHUNK, width), BF),
            pltpu.VMEM((2, count, CHUNK, width), BF),
            pltpu.VMEM((count, CHUNK, width), BF),
            pltpu.VMEM((count, CHUNK, width), BF),
            pltpu.VMEM((count, 4, CHUNK, width), BF),
            pltpu.VMEM((count, width, 4 * CHUNK), BF),
            pltpu.VMEM((2, 4 * CHUNK, 2 * width), BF),
            pltpu.VMEM((2, 4 * CHUNK, 2 * width), BF),
            pltpu.VMEM((2, CHUNK, width), F32),
            pltpu.VMEM((2, CHUNK, width), BF),
            pltpu.VMEM((2, CHUNK, width), F32),
            pltpu.VMEM((width, width), BF),
            pltpu.VMEM((width, TILE), F32),
            pltpu.VMEM((2, 8, piece // 2, width), BF),
            dma((count,)),
            dma((count,)),
            dma((2,)),
            dma((4,)),
            dma((2, count)),
            dma((2, count)),
            dma((count,)),
            dma((count,)),
            dma((3, count)),
            dma((3, count)),
            dma((count,)),
            dma((2,)),
            dma((2,)),
            dma((2, 7)),
            dma((2, 7)),
        ],
        compiler_params=pltpu.CompilerParams(
            collective_id=4, has_side_effects=True, vmem_limit_bytes=60 << 20
        ),
        cost_estimate=pl.CostEstimate(flops=34 * 10**9, bytes_accessed=200 << 20, transcendentals=4 << 20),
        name="middle_back",
    )(gd_all, act_all, ug_all, hidden, attn_unit, states, back, attn_inv, hidden_inv, w_ug, w_d, rates, scales)


def order_kernel(where_ref, parent_ref, out_ref):
    base, me = where_ref[0], where_ref[1]
    shape = (128, 128)
    row = lax.broadcasted_iota(jnp.int32, shape, 0)
    block = lax.broadcasted_iota(jnp.int32, (8, 128), 1)
    real = block < NB
    parent = jnp.where(real & (parent_ref[...] >= 0), parent_ref[...] - base, -1)
    up = (row == parent[0:1]).astype(F32)
    up2 = nn(up, up)
    near = up + up2
    up4 = nn(up2, up2)
    near = near + nn(near, up2)
    near = near + nn(near, up4)
    above = near + nn(nn(up4, up4), up)
    depth = jnp.broadcast_to(jnp.sum(above, axis=0, keepdims=True), (8, 128)).astype(jnp.int32)
    before = (row < lax.broadcasted_iota(jnp.int32, shape, 1)).astype(F32)
    rank = nn(((depth == TRUNK) & real).astype(F32), before)
    parent_rank = nn(rank, up).astype(jnp.int32)
    sibling = jnp.sum(nn(up.T, up) * before, axis=0, keepdims=True).astype(jnp.int32)
    leaf = TRUNK + 4 + 2 * parent_rank + sibling
    slot = jnp.where(depth < TRUNK, depth, jnp.where(depth == TRUNK, TRUNK + rank.astype(jnp.int32), leaf))
    slot = jnp.where(real, slot, 127)
    mine = jnp.where(real, jnp.bitwise_xor(block // 5, me) * 5 + block % 5, 127)
    order = nt(mine.astype(F32), (row == slot[0:1]).astype(F32))
    back = nt(slot.astype(F32), (row == mine[0:1]).astype(F32))
    which = lax.broadcasted_iota(jnp.int32, (8, 128), 0)
    out_ref[...] = jnp.where(which == 0, order, back).astype(jnp.int32)


def tree_order(where, parents):
    return pl.pallas_call(
        order_kernel,
        in_specs=[pl.BlockSpec(memory_space=pltpu.SMEM), pl.BlockSpec(memory_space=pltpu.VMEM)],
        out_specs=pl.BlockSpec(memory_space=pltpu.VMEM),
        out_shape=jax.ShapeDtypeStruct((8, 128), jnp.int32),
        name="tree_order",
    )(where, jnp.broadcast_to(jnp.pad(parents, (0, 128 - NB), constant_values=-1), (8, 128)))


def local(
    states,
    teacher,
    parent_ids,
    valid_mask,
    w_query,
    w_key,
    w_value,
    w_out,
    w_up,
    w_gate,
    w_down,
    qk_scale,
    attn_rate,
    mlp_rate,
    up_scale,
    gate_scale,
):
    both = ("dp", "fsdp")
    dps, tps = 8, 4
    rows_w = w_query.shape[0]
    cols = D // tps
    hid = FF // tps
    ff_rows = FF // (dps * tps)
    me = lax.axis_index("fsdp")
    root_width = math.sqrt(D)
    mask_f = valid_mask.astype(F32)
    group_base = lax.axis_index("dp") * NB
    order = tree_order(jnp.stack((group_base, me)).astype(jnp.int32), parent_ids)

    count = jnp.sum(valid_mask)
    first_row = jnp.arange(rows_w, dtype=jnp.int32) == 0
    small = jnp.stack(
        (
            qk_scale,
            attn_rate,
            mlp_rate,
            jnp.where(first_row, count // 128, 0).astype(BF),
            jnp.where(first_row, count % 128, 0).astype(BF),
        ),
        axis=1,
    )
    small = jnp.pad(small, ((0, 0), (0, 59)))
    qkv_send = jnp.concatenate(
        [w.reshape(rows_w, tps, cols).transpose(1, 0, 2) for w in (w_query, w_key, w_value)]
        + [jnp.broadcast_to(small[None], (tps, rows_w, 64))],
        axis=2,
    )
    extra = jnp.pad(jnp.stack((up_scale, gate_scale), axis=1), ((0, 0), (69, 57)))
    spread = [(j, tps * (j % dps) + j // dps) for j in range(dps * tps)]
    ug_send = jnp.concatenate(
        [
            w.reshape(rows_w, dps, tps, ff_rows).transpose(2, 0, 1, 3).reshape(tps, rows_w, hid)
            for w in (w_up, w_gate)
        ],
        axis=2,
    )
    tokens_t, w_t, w_o, w_ug, qkv, mixed, sums, share = forward(
        order, states, qkv_send, extra, lax.ppermute(w_out, both, spread), ug_send
    )
    small_all = w_t[3 * cols : 3 * cols + 8].astype(F32)
    rates = small_all[1:3]
    valid_count = 128.0 * jnp.sum(small_all[3]) + jnp.sum(small_all[4])
    scales = small_all[5:7] * jnp.array([[1.0], [root_width]], F32)
    scale_qk = lax.dynamic_slice_in_dim(small_all[0], me * cols, cols).reshape(cols // HEAD_DIM, HEAD_DIM, 1)

    mask_col = mask_f[:, None]
    w_d, out_states, hidden, attn_unit, back, attn_inv, hidden_inv, sums_mid, gd_all, ht_all, act_all, ug_all = middle(
        share, states, teacher, mask_col * (2.0 / valid_count), mask_col, w_ug, w_down, rates, scales
    )
    base, ga_all, gug_all, grad_down, sums_back, ff_sums = middle_back(
        gd_all, act_all, ug_all, hidden, attn_unit, states, back, attn_inv, hidden_inv, w_ug, w_d, rates, scales
    )
    loss_local = jnp.sum(sums_mid[1])
    g_rate_mlp, g_rate_attn = sums_mid[0], sums_back[0]
    grad_up_scale, grad_gate_scale = ff_sums[0], ff_sums[1] * root_width
    g_qkv, g_scale, part_out, grad_up, grad_gate = attention_back(
        order, qkv, scale_qk, sums, mixed, ga_all.reshape(NB, BLOCK, D), w_o, ht_all, gug_all
    )
    g_qkv = g_qkv.reshape(3 * cols, TOK)
    slot = jnp.arange(tps, dtype=jnp.int32) == me
    qk_rows = jnp.where(slot[:, None], g_scale.reshape(1, cols), 0.0).reshape(dps * tps, rows_w)
    ff_terms = [
        jnp.where(slot[None, :, None], term.reshape(dps, 1, ff_rows), 0.0).reshape(dps * tps, ff_rows)
        for term in (grad_up_scale, grad_gate_scale)
    ]
    vectors = jnp.concatenate(
        [g_rate_attn.reshape(dps * tps, rows_w), g_rate_mlp.reshape(dps * tps, rows_w), qk_rows]
        + ff_terms
        + [jnp.broadcast_to(loss_local, (dps * tps, 512 - 3 * rows_w - 2 * ff_rows))],
        axis=1,
    ).reshape(dps, tps, 4, 128)
    part_out = part_out.reshape(dps, rows_w, D)
    grad_states, g_query, g_key, g_value, out_back, vector_share = last_exchange(
        order, base, tokens_t, g_qkv, w_t, part_out, vectors
    )
    vector_share = vector_share.reshape(512)
    grad_out = lax.ppermute(out_back, both, [(b, a) for a, b in spread])
    cuts = (0, rows_w, 2 * rows_w, 3 * rows_w, 3 * rows_w + ff_rows, 3 * rows_w + 2 * ff_rows)
    v = [vector_share[a:b] for a, b in zip(cuts, cuts[1:])]
    return (
        out_states,
        vector_share[-1] / valid_count,
        grad_states,
        g_query,
        g_key,
        g_value,
        grad_out,
        grad_up,
        grad_gate,
        grad_down,
        v[2],
        v[0],
        v[1],
        v[3],
        v[4],
    )


def solution(mesh):
    placed = (
        P(("dp", "fsdp"), None),
        P(("dp", "fsdp"), None),
        P("dp"),
        P(("dp", "fsdp")),
        P(("dp", "fsdp"), None),
        P(("dp", "fsdp"), None),
        P(("dp", "fsdp"), None),
        P(("dp", "fsdp"), None),
        P(("dp", "fsdp"), None),
        P(("dp", "fsdp"), None),
        P(("dp", "fsdp"), None),
        P(("dp", "fsdp")),
        P(("dp", "fsdp")),
        P(("dp", "fsdp")),
        P(("dp", "fsdp")),
        P(("dp", "fsdp")),
    )
    quick = mesh.shape["fsdp"] == 4 and mesh.shape["dp"] == 8
    return jax.shard_map(
        local if quick else general,
        mesh=mesh,
        in_specs=placed,
        out_specs=(
            P(("dp", "fsdp"), None),
            P(),
            P(("dp", "fsdp"), None),
            P(("dp", "fsdp"), None),
            P(("dp", "fsdp"), None),
            P(("dp", "fsdp"), None),
            P(("dp", "fsdp"), None),
            P(("dp", "fsdp"), None),
            P(("dp", "fsdp"), None),
            P(("dp", "fsdp"), None),
            P(("dp", "fsdp")),
            P(("dp", "fsdp")),
            P(("dp", "fsdp")),
            P(("dp", "fsdp")),
            P(("dp", "fsdp")),
        ),
        check_vma=False,
    )
```

time: 722 us -> 676 us (0.936)
  Pallas kernels: 541 us -> 614 us
  matrix products: 63.6 us -> 0 us
  local copies, waits for them, and re-layouts: 50.2 us -> 28 us
  blocking collectives: 14.7 us -> 0 us
  between operations: 21 us -> 6.75 us
    pallas_call x7 -> x6, Pallas kernels: 541 us -> 614 us  [the longest x1 172 us: middle(): pl.pallas_call(middle_kernel, in_specs=[hbm] + [vmem] * 8, out_specs=[vme...]
    dot_general x7 -> x0, matrix products: 63.6 us -> none  [dot(): lax.dot_general(left, right, ((contract[:1], contract[1:]), ((), ())), pr...]
    all_to_all x1 -> x0, blocking collectives: 14.7 us -> none  [local(): lax.all_to_all(ug_send, 'fsdp', 0, 0, tiled=True)]
    convert_element_type x4 -> x0, local copies, waits for them, and re-layouts: 8.3 us -> none  [the longest x1 4.72 us: local(): dot(tokens, g_qkv, (0, 1)).astype(BF).reshape(dps, tps * rows_w, 3 * cols)]
    ppermute x1, waiting for transfers between devices: 2.58 us -> 10.5 us  [local(): grad_out = lax.ppermute(out_back, both, [(b, a) for a, b in spread])]
  transfers between devices with their start and end apart: 5 -> 2, of which waited for: 2 -> 1; matrix products, arithmetic and copies ran while one was open for 13% -> 2% of each run, Pallas kernels for 38% -> 0%
where the time goes in v4:
time: 676 us; the launch traced here: 675 us
  Pallas kernels  614 us (91%)
  local copies, waits for them, and re-layouts  28 us (4%)
  waiting for transfers between devices  10.6 us (2%)
  other arithmetic  8.46 us (1%)
  starting transfers between devices  7.5 us (1%)
    pallas_call x1, Pallas kernels, middle(): pl.pallas_call(middle_kernel, in_specs=[hbm] + [vmem] * 8, out_specs=[vme...  172 us
    pallas_call x1, Pallas kernels, forward(): pl.pallas_call(forward_kernel, in_specs=[smem, hbm] + [vmem] * 4, out_spe...  150 us
    pallas_call x1, Pallas kernels, middle_back(): pl.pallas_call(middle_back_kernel, in_specs=[hbm] * 7 + [vmem] * 6, out_s...  120 us
    pallas_call x1, Pallas kernels, attention_back(): pl.pallas_call(attention_back_kernel, in_specs=[smem, hbm, vmem, vmem, vm...  116 us
    pallas_call x1, Pallas kernels, last_exchange(): pl.pallas_call(last_kernel, in_specs=[pl.BlockSpec(memory_space=pltpu.SME...  53.5 us
  transfers between devices with their start and end apart: 2, of which 1 were waited for; matrix products, arithmetic and copies ran while one was open for 2% of the time, Pallas kernels for 0%

profile of v4, /device:TPU:4, one launch (start us, length us, event | category | flops | bytes accessed | tf_op | source)
XLA Modules:
  0.0 675.1 jit_solution(7935005804603730668)
XLA Ops:
  0.7 4.6 collective-permute-start
  5.2 1.4 fusion.2
  10.1 1.1 reshape.124
  11.1 1.1 reshape.125
  12.2 1.1 reshape.123
  14.0 1.7 reshape.126
  21.3 2.2 tree_order.1.order
  23.5 0.9 pad_maximum_fusion.ug_send
  26.0 149.9 %forward.1 = (bf16[1280,2560]{1,0:T(8,128)(2,1)}, bf16[1024,1280]{1,0:T(8,128)(2,1)}, bf16[320,1280]{1,0:T(8,128)(2,1)}, bf16[1280,2560]{1,0:T(8,128)(2,1)}, f32...) custom-call(s32[8,128]{1,0:T(8,128)} %tree_order.1.order, ...), custom_call_target="tpu_custom_call" | custom-call | flops 12000000000 | bytes 209715200 | tf_op jit(solution)/shard_map/forward/pallas_call | solution.py:915
  180.1 171.6 %middle.1 = (bf16[1280,1280]{1,0:T(8,128)(2,1)}, bf16[640,1280]{1,0:T(8,128)(2,1)}, f32[640,1280]{1,0:T(8,128)}, bf16[640,1280]{1,0:T(8,128)(2,1)}, f32[640,1280...) custom-call(bf16[4,640,1280]{2,1,0:T(8,128)(2,1)} %get-tuple-element, ...), custom_call_target="tpu_custom_call" | custom-call | flops 25999998976 | bytes 419430400 | tf_op jit(solution)/shard_map/middle/pallas_call | solution.py:1423
  351.7 120.4 %middle_back.1 = (f32[640,1280]{1,0:T(8,128)}, bf16[4,640,1280]{2,1,0:T(8,128)(2,1)}, bf16[5,512,2560]{2,1,0:T(8,128)(2,1)}, f32[160,1280]{1,0:T(8,128)}, f32[1,1280]{1,0:T(1,128)}, /*index=5*/f32[2,1280]{1,0:T(2,128)}) custom-call(bf16[5,4,128,1280]{3,2,1,0:T(8,128)(2,1)} %get-tuple-element.56.gd_all, bf16[5,1280,512]{2,1,0:T(8,128)(2,1)} %get-tuple-element.57.act_all, ...), custom_call_target="tpu_custom_call" | custom-call | flops 33999998976 | bytes 209715200 | tf_op jit(solution)/shard_map/middle_back/pallas_call | solution.py:1704
  473.3 0.9 reshape.136.scales
  474.2 116.2 %attention_back.1 = (bf16[3,320,2560]{2,1,0:T(8,128)(2,1)}, f32[5,64,1]{2,1,0:T(8,128)}, bf16[320,1280]{1,0:T(8,128)(2,1)}, f32[40,5120]{1,0:T(8,128)}, f32[40,5120]{1,0:T(8,128)}) custom-call(s32[8,128]{1,0:T(8,128)} %tree_order.1.order, f32[3,320,2560]{2,1,0:T(8,128)} %get-tuple-element.67.qkv, f32[5,64,1]{2,1,0:T(8,128)} %reshape.136.scales, ...), custom_call_target="tpu_custom_call" | custom-call | flops 40000000000 | bytes 62914560 | tf_op jit(solution)/shard_map/attention_back/pallas_call | solution.py:586
  590.4 1.0 reduce.6
  593.3 1.7 copy-done.1
  595.0 1.1 copy-done.2
  596.2 53.5 %last_exchange.1 = (f32[640,1280]{1,0:T(8,128)}, f32[40,1280]{1,0:T(8,128)S(1)}, f32[40,1280]{1,0:T(8,128)S(1)}, f32[40,1280]{1,0:T(8,128)S(1)}, f32[40,1280]{1,0:T(8,128)S(1)}, /*index=5*/f32[4,128]{1,0:T(4,128)S(1)}) custom-call(s32[8,128]{1,0:T(8,128)S(1)} %copy-done, f32[640,1280]{1,0:T(8,128)} %get-tuple-element.65.base, ...), custom_call_target="tpu_custom_call" | custom-call | flops 12999999488 | bytes 104857600 | tf_op jit(solution)/shard_map/last_exchange/pallas_call | solution.py:1147
  650.9 2.9 collective-permute-start.1
  655.1 10.5 %collective-permute-done.1 = f32[40,1280]{1,0:T(8,128)S(1)} collective-permute-done((f32[40,1280]{1,0:T(8,128)S(1)}, f32[40,1280]{1,0:T(8,128)S(1)}, u32[]{:S(2)}, u32[]{:S(2)}) %collective-permute-start.1) | collective-permute-done | bytes 204832 | tf_op jit(solution)/shard_map/ppermute | solution.py:1891
  665.7 1.2 copy.74
  666.8 1.7 copy.75
  671.3 0.9 copy.80
  672.2 0.9 copy.81
  673.1 0.9 copy.82
  (88 shorter events, 18.9 us)
Async XLA Ops:
  0.6 15.9 %copy-start.8 = (bf16[40,5120]{1,0:T(8,128)(2,1)S(1)}, bf16[40,5120]{1,0:T(8,128)(2,1)}, u32[]{:S(2)}) copy-start(bf16[40,5120]{1,0:T(8,128)(2,1)} %param.26) | copy-start | bytes 1228804
  0.7 24.7 %collective-permute-start = (bf16[40,1280]{1,0:T(8,128)(2,1)}, bf16[40,1280]{1,0:T(8,128)(2,1)S(1)}, u32[]{:S(2)}, u32[]{:S(2)}) collective-permute-start(bf16[40,1280]{1,0:T(8,128)(2,1)} %param.24), channel_id=1, source_target_pairs={{0,0},{1,4},{2,8},{3,12},{4,16},{5,20},{6,24},{7,28},{8,1},{9,5},{... | collective-permute-start | bytes 307208 | tf_op jit(solution)/shard_map/ppermute | solution.py:1852
  14.0 4.1 copy-start.14
  14.0 4.1 copy-start.15
  25.4 153.2 %copy-start.9 = (s32[640]{0:T(1024)S(1)}, s32[640]{0:T(1024)}, u32[]{:S(2)}) copy-start(s32[640]{0:T(1024)} %param.20) | copy-start | bytes 7684
  25.4 154.1 %copy-start.12 = (f32[2]{0:T(128)S(1)}, f32[2]{0:T(128)}, u32[]{:S(2)}) copy-start(f32[2]{0:T(128)} %constant.74) | copy-start | bytes 28
  25.4 0.6 copy-start.13
  474.2 117.3 %copy-start.11 = (f32[1,1280]{1,0:T(1,128)S(1)}, f32[1,1280]{1,0:T(1,128)}, u32[]{:S(2)}) copy-start(f32[1,1280]{1,0:T(1,128)} %get-tuple-element.76) | copy-start | bytes 15364
  474.2 117.4 %copy-start.10 = (f32[2,1280]{1,0:T(2,128)S(1)}, f32[2,1280]{1,0:T(2,128)}, u32[]{:S(2)}) copy-start(f32[2,1280]{1,0:T(2,128)} %get-tuple-element.77) | copy-start | bytes 30724
  474.2 119.1 %copy-start = (s32[8,128]{1,0:T(8,128)S(1)}, s32[8,128]{1,0:T(8,128)}, u32[]{:S(2)}) copy-start(s32[8,128]{1,0:T(8,128)} %tree_order.1.order) | copy-start | bytes 12292
  593.3 1.7 copy-start.1
  595.0 1.1 copy-start.2
  596.2 69.5 %copy-start.4 = (bf16[640,1280]{1,0:T(8,128)(2,1)S(1)}, bf16[640,1280]{1,0:T(8,128)(2,1)}, u32[]{:S(2)}) copy-start(bf16[640,1280]{1,0:T(8,128)(2,1)} %get-tuple-element.126) | copy-start | bytes 4915204
  650.9 14.7 %collective-permute-start.1 = (f32[40,1280]{1,0:T(8,128)S(1)}, f32[40,1280]{1,0:T(8,128)S(1)}, u32[]{:S(2)}, u32[]{:S(2)}) collective-permute-start(f32[40,1280]{1,0:T(8,128)S(1)} %get-tuple-element.85), channel_id=1, source_target_pairs={{0,0},{4,1},{8,2},{12,3},{16,4},{20,5},{24,6},{28,7},{1,8},{5,9},{... | collective-permute-start | bytes 614408 | tf_op jit(solution)/shard_map/ppermute | solution.py:1891
  654.5 12.3 %copy-start.3 = (f32[640,1280]{1,0:T(8,128)S(1)}, f32[640,1280]{1,0:T(8,128)}, u32[]{:S(2)}) copy-start(f32[640,1280]{1,0:T(8,128)} %get-tuple-element.128) | copy-start | bytes 9830404
  666.8 4.4 copy-start.7
  666.8 5.3 copy-start.6
  668.5 4.5 copy-start.5

commit v5 on v4

--- a/solution.py
+++ b/solution.py
@@ -320,26 +320,20 @@
     return pl.ds(pl.multiple_of(start, 16), size)
 
 
-def each_chunk(visit):
+def early_chunks(visit):
     for j in range(TRUNK // 2):
         parts = [(0, 256 * j, "all")] if j else []
         visit(256 * j, parts + [(256 * j, 256, "causal")])
     trunk = TRUNK * BLOCK
-
-    def branches(j, carry):
-        start = trunk + 256 * j
+    for start in (trunk, trunk + 256):
         visit(start, [(0, trunk, "all"), (start, 256, "pair")])
-        return carry
-
-    def leaves(j, carry):
+
+
+def late_chunks(visit):
+    trunk = TRUNK * BLOCK
+    for j in range(4):
         start = trunk + 4 * BLOCK + 256 * j
         visit(start, [(0, trunk, "all"), (trunk + BLOCK * j, BLOCK, "all"), (start, 256, "pair")])
-        return carry
-
-    for j in range(2):
-        branches(j, 0)
-    for j in range(4):
-        leaves(j, 0)
 
 
 def masked(kind, value):
@@ -364,13 +358,13 @@
 def attention_back_kernel(order, qkv, scales, sums, mixed, ga_all, w_o, ht_all, gug_all,
                           g_qkv, g_scale, part_out, g_up, g_gate,
                           ga_b, ga, gm, raw, out_b, qT, q, k, kT, v, gT, g, dq, dk, dv, delta, inv,
-                          gug_b, ht_r, ht_l, ring_r, ring_l, next_r, next_l, hid_buf, hid_in,
+                          gug_b, ht_r, ht_l, ring, own, hid_buf, hid_in,
                           ga_sem, gug_sem, row_sem, raw_sem, out_sem, ring_send, ring_recv, a2a_send, a2a_recv):
     me = lax.axis_index("fsdp")
     place = ring_place()
     peers = group_peers()
     right, left = {"dp": ring_dp(place + 1)}, {"dp": ring_dp(place - 1)}
-    count, chunk, side = gug_b.shape[0], ring_r.shape[1], ring_r.shape[2]
+    count, chunk, side = gug_b.shape[0], ring.shape[3], ring.shape[4]
     heads = g_scale.shape[0]
     rows_w = hid_buf.shape[1]
 
@@ -426,29 +420,34 @@
 
     lax.fori_loop(0, D // TILE, outer, 0)
 
-    def parts(step):
+    def parts(step, which):
         slot = step % 2
-        for copy in slices(step):
-            copy.wait()
-        next_r[...] = jnp.zeros_like(next_r)
-        next_l[...] = jnp.zeros_like(next_l)
+
+        @pl.when(which == 0)
+        def _():
+            for copy in slices(step):
+                copy.wait()
+
+        own[...] = jnp.zeros_like(own)
 
         def add(i, carry):
-            next_r[...] = next_r[...] + nn(ht_r[slot, i], gug_b[i, :, pl.ds(0, side)])
-            next_l[...] = next_l[...] + nn(ht_l[slot, i], gug_b[i, :, pl.ds(side, side)])
+            for d, rows in enumerate((ht_r, ht_l)):
+                cut = lanes_at((2 * d + which) * side, side)
+                own[d] = own[d] + nn(rows[slot, i], gug_b[i, :, cut])
             return carry
 
         lax.fori_loop(0, count, add, 0)
 
-        @pl.when(step + 2 < 8)
+        @pl.when((which == 1) & (step + 2 < 8))
         def _():
             for copy in slices(step + 2):
                 copy.start()
 
-    def hop_copies(step):
+    def hop_copies(step, which):
         return [
-            send(ring_r.at[step], ring_r.at[step + 1], ring_send.at[0, step], ring_recv.at[0, step], right),
-            send(ring_l.at[step], ring_l.at[step + 1], ring_send.at[1, step], ring_recv.at[1, step], left),
+            send(ring.at[d, which, step], ring.at[d, which, step + 1], ring_send.at[d, which, step],
+                 ring_recv.at[d, which, step], peer)
+            for d, peer in enumerate((right, left))
         ]
 
     def exchange():
@@ -457,34 +456,45 @@
             for i, peer in enumerate(peers)
         ]
 
-    def hop(step):
-        parts(step + 1)
-        for copy in hop_copies(step):
+    def poll(index):
+        step, which = index // 2, index % 2
+        parts(step + 1, which)
+        for copy in hop_copies(step, which):
             copy.wait()
 
         @pl.when(step < 6)
         def _():
-            ring_r[step + 1] = (ring_r[step + 1].astype(F32) + next_r[...]).astype(BF)
-            ring_l[step + 1] = (ring_l[step + 1].astype(F32) + next_l[...]).astype(BF)
-            for copy in hop_copies(step + 1):
+            for d in range(2):
+                ring[d, which, step + 1] = (ring[d, which, step + 1].astype(F32) + own[d]).astype(BF)
+            for copy in hop_copies(step + 1, which):
                 copy.start()
 
         @pl.when(step == 6)
         def _():
-            for start, ring, own in ((0, ring_r, next_r), (side, ring_l, next_l)):
-                total = ring[7].astype(F32) + own[...]
+            for d in range(2):
+                total = ring[d, which, 7].astype(F32) + own[d]
                 for i in range(4):
-                    hid_buf[i, :, start : start + side] = total[i * rows_w : (i + 1) * rows_w].astype(BF)
+                    hid_buf[i, :, lanes_at((2 * d + which) * side, side)] = total[
+                        i * rows_w : (i + 1) * rows_w
+                    ].astype(BF)
+
+        @pl.when(index == 13)
+        def _():
             for copy in exchange():
                 copy.start()
 
     for copy in loads:
         copy.wait()
-    parts(0)
-    ring_r[0] = next_r[...].astype(BF)
-    ring_l[0] = next_l[...].astype(BF)
-    for copy in hop_copies(0):
-        copy.start()
+
+    def begin(which, carry):
+        parts(0, which)
+        for d in range(2):
+            ring[d, which, 0] = own[d].astype(BF)
+        for copy in hop_copies(0, which):
+            copy.start()
+        return carry
+
+    lax.fori_loop(0, 2, begin, 0)
 
     def open_head(head):
         slot = head % 2
@@ -520,27 +530,26 @@
         dk[...] = jnp.zeros_like(dk)
         dv[...] = jnp.zeros_like(dv)
 
+    def visit(start, pieces):
+        span = lanes_at(start, 256)
+        query, grad = qT[:, span], gT[:, span]
+        query_rows, grad_rows = q[span, :], g[span, :]
+        scale_row, delta_row = inv[:, span], delta[:, span]
+        acc = jnp.zeros((64, 256), F32)
+        for kstart, size, kind in pieces:
+            keys = lanes_at(kstart, size)
+            probs = masked(kind, jnp.exp(nn(k[keys, :], query)) * scale_row)
+            g_probs = nn(v[keys, :], grad)
+            g_scores = (probs * (g_probs - delta_row)).astype(BF)
+            dv[keys, :] += nn(probs.astype(BF), grad_rows)
+            dk[keys, :] += nn(g_scores, query_rows)
+            acc = acc + nn(kT[:, keys], g_scores)
+        dq[:, span] = acc * 8.0
+
+
     def close_head(head):
         slot = head % 2
         scale = scales[head]
-
-        def visit(start, pieces):
-            span = lanes_at(start, 256)
-            query, grad = qT[:, span], gT[:, span]
-            query_rows, grad_rows = q[span, :], g[span, :]
-            scale_row, delta_row = inv[:, span], delta[:, span]
-            acc = jnp.zeros((64, 256), F32)
-            for kstart, size, kind in pieces:
-                keys = lanes_at(kstart, size)
-                probs = masked(kind, jnp.exp(nn(k[keys, :], query)) * scale_row)
-                g_probs = nn(v[keys, :], grad)
-                g_scores = (probs * (g_probs - delta_row)).astype(BF)
-                dv[keys, :] += nn(probs.astype(BF), grad_rows)
-                dk[keys, :] += nn(g_scores, query_rows)
-                acc = acc + nn(kT[:, keys], g_scores)
-            dq[:, span] = acc * 8.0
-
-        each_chunk(visit)
         total = jnp.zeros((64, BLOCK), F32)
         for i in range(NB):
             here = slice(i * BLOCK, (i + 1) * BLOCK)
@@ -555,12 +564,15 @@
         out_copy(head).start()
 
     def work(i, carry):
-        pl.when(i % 2 == 0)(functools.partial(open_head, i // 2))
-        pl.when(i % 2 == 1)(functools.partial(close_head, i // 2))
-        pl.when(i < 7)(functools.partial(hop, i))
-        return carry
-
-    lax.fori_loop(0, 2 * heads, work, 0)
+        head, segment = i // 4, i % 4
+        pl.when(segment == 0)(functools.partial(open_head, head))
+        pl.when(segment == 1)(functools.partial(early_chunks, visit))
+        pl.when(segment == 2)(functools.partial(late_chunks, visit))
+        pl.when(segment == 3)(functools.partial(close_head, head))
+        pl.when(i < 14)(functools.partial(poll, i))
+        return carry
+
+    lax.fori_loop(0, 4 * heads, work, 0)
     for copy in exchange():
         copy.wait()
     hid_in[me] = hid_buf[me]
@@ -578,7 +590,7 @@
     heads = scales.shape[0]
     count, tokens, hidden_width = gug_all.shape
     chunk = ht_all.shape[1] // 8
-    side = hidden_width // 2
+    side = hidden_width // 4
     rows_w = chunk // 4
     vmem, hbm = pl.BlockSpec(memory_space=pltpu.VMEM), pl.BlockSpec(memory_space=pl.ANY)
     smem = pl.BlockSpec(memory_space=pltpu.SMEM)
@@ -615,10 +627,8 @@
             pltpu.VMEM(gug_all.shape, BF),
             pltpu.VMEM((2, count, chunk, tokens), BF),
             pltpu.VMEM((2, count, chunk, tokens), BF),
-            pltpu.VMEM((8, chunk, side), BF),
-            pltpu.VMEM((8, chunk, side), BF),
-            pltpu.VMEM((chunk, side), F32),
-            pltpu.VMEM((chunk, side), F32),
+            pltpu.VMEM((2, 2, 8, chunk, side), BF),
+            pltpu.VMEM((2, chunk, side), F32),
             pltpu.VMEM((4, rows_w, hidden_width), BF),
             pltpu.VMEM((4, rows_w, hidden_width), BF),
             dma((1,)),
@@ -626,8 +636,8 @@
             dma((2, 2)),
             dma((2,)),
             dma((2,)),
-            dma((2, 7)),
-            dma((2, 7)),
+            dma((2, 2, 7)),
+            dma((2, 2, 7)),
             dma((3,)),
             dma((3,)),
         ],
@@ -674,9 +684,27 @@
     )
 
 
-def forward_kernel(order, states, qkv_send, extra, out_piece, ug_send,
+EARLY_HOPS = 5
+
+
+def hidden_ring(ref, sends, recvs, step, base=0):
+    place = ring_place()
+    right, left = {"dp": ring_dp(place + 1)}, {"dp": ring_dp(place - 1)}
+    chunk = ref.shape[0] // 8
+    to_right, to_left = ring_dp(place - step) * chunk, ring_dp(place + step) * chunk
+    first, size = 48, chunk // 2
+    cuts = ((to_right, first, right), (to_left + size, first, left),
+            (to_right + first, size - first, right), (to_left + size + first, size - first, left))
+    return [
+        send(ref.at[rows_at(start, rows)], ref.at[rows_at(start, rows)], sends.at[i, step - base],
+             recvs.at[i, step - base], peer)
+        for i, (start, rows, peer) in enumerate(cuts)
+    ]
+
+
+def forward_kernel(order, states, w_query, w_key, w_value, small, extra, out_piece, w_up, w_gate,
                    tokens_t, w_t, w_o, w_ug, qkv, mixed, sums, share,
-                   land, weights, tok, turned, tok_t, out_w, ug_land, ug_own, raw, qs, ks, vs, blocks, stage,
+                   qkv_send, ug_send, land, weights, tok, turned, tok_t, out_w, ug_land, ug_own, raw, qs, ks, vs, blocks, stage,
                    tok_send, tok_recv, a2a_send, a2a_recv, ring_send, ring_recv, ug_s, ug_r, local_sem, raw_sem,
                    stage_sem):
     me, dp = lax.axis_index("fsdp"), lax.axis_index("dp")
@@ -689,6 +717,12 @@
     half = chunk // 2
     cols = mixed.shape[0]
     heads = cols // HEAD_DIM
+    own = pltpu.make_async_copy(states, tok.at[pl.ds(0, rows)], local_sem.at[0])
+    own.start()
+    for i in range(4):
+        cut = slice(i * cols, (i + 1) * cols)
+        block = [w[:, cut].astype(F32) for w in (w_query, w_key, w_value)] + [small[...].astype(F32)]
+        qkv_send[i] = jnp.concatenate(block, axis=1).astype(BF)
     greet([sibling, across, corner, right, left])
 
     exchange, ug_exchange = [], []
@@ -705,12 +739,16 @@
         far.append(copy)
     near = send(states, tok.at[pl.ds(rows, rows)], tok_send.at[2], tok_recv.at[2], sibling)
     near.start()
-    own = pltpu.make_async_copy(states, tok.at[pl.ds(0, rows)], local_sem.at[0])
-    own.start()
-    for i, peer in enumerate((sibling, across, corner)):
-        copy = send(ug_send.at[peer["fsdp"]], ug_land.at[me], a2a_send.at[3 + i], a2a_recv.at[3 + i], peer)
-        copy.start()
-        ug_exchange.append(copy)
+    size = w_up.shape[1] // 32
+    for i in range(4):
+        for which, w in enumerate((w_up, w_gate)):
+            for half_d in range(2):
+                block = [
+                    w[:, (4 * d + i) * size : (4 * d + i + 1) * size].astype(F32)
+                    for d in range(4 * half_d, 4 * half_d + 4)
+                ]
+                start = (8 * which + 4 * half_d) * size
+                ug_send[i, :, start : start + 4 * size] = jnp.concatenate(block, axis=1).astype(BF)
     land[me] = qkv_send[me]
     ug_land[me] = ug_send[me]
     out_w[dp] = out_piece[...]
@@ -721,39 +759,35 @@
     last = pl.ds(weights.shape[1] - 128, 128)
     weights[rows_at(dp * chunk, chunk), last] = weights[rows_at(dp * chunk, chunk), last] + extra[...]
 
-    def hop(step, carry):
+    def ring_copies(step):
         to_right, to_left = ring_dp(place - step), ring_dp(place + step)
         first, second = rows_at(to_right * chunk, half), rows_at(to_left * chunk + half, half)
-        copies = [
-            send(weights.at[first], weights.at[first], ring_send.at[0, step], ring_recv.at[0, step], right),
-            send(weights.at[second], weights.at[second], ring_send.at[1, step], ring_recv.at[1, step], left),
-            send(out_w.at[to_right, :, pl.ds(0, 640)], out_w.at[to_right, :, pl.ds(0, 640)],
-                 ring_send.at[2, step], ring_recv.at[2, step], right),
-            send(out_w.at[to_left, :, pl.ds(640, 640)], out_w.at[to_left, :, pl.ds(640, 640)],
-                 ring_send.at[3, step], ring_recv.at[3, step], left),
+        lanes_r, lanes_l = pl.ds(0, width // 2), pl.ds(width // 2, width // 2)
+        return [
+            send(ref, ref, ring_send.at[i, step], ring_recv.at[i, step], peer)
+            for i, (ref, peer) in enumerate(
+                (
+                    (weights.at[first], right),
+                    (weights.at[second], left),
+                    (out_w.at[to_right, :, lanes_r], right),
+                    (out_w.at[to_left, :, lanes_l], left),
+                )
+            )
         ]
-        for copy in copies:
-            copy.start()
-        for copy in copies:
+
+    def hop(step, carry):
+        for copy, later in zip(ring_copies(step), ring_copies(step + 1)):
             copy.wait()
-        return carry
-
-    def ug_copies(step):
-        first = rows_at(ring_dp(place - step) * chunk, half)
-        second = rows_at(ring_dp(place + step) * chunk + half, half)
-        return [
-            send(w_ug.at[first], w_ug.at[first], ug_s.at[0, step], ug_r.at[0, step], right),
-            send(w_ug.at[second], w_ug.at[second], ug_s.at[1, step], ug_r.at[1, step], left),
-        ]
+            pl.when(step < 6)(later.start)
+        return carry
 
     def ug_hop(step):
-        for copy in ug_copies(step):
+        for copy, later in zip(hidden_ring(w_ug, ug_s, ug_r, step), hidden_ring(w_ug, ug_s, ug_r, step + 1)):
             copy.wait()
-
-        @pl.when(step < 6)
-        def _():
-            for copy in ug_copies(step + 1):
-                copy.start()
+            pl.when(step < EARLY_HOPS - 1)(later.start)
+
+    for copy in ring_copies(0):
+        copy.start()
 
     def turn(i, carry):
         turned[i] = tok[lanes_at(i * BLOCK, BLOCK)].T
@@ -776,35 +810,39 @@
         copy = send(tok.at[here], tok.at[there], tok_send.at[3 + i], tok_recv.at[3 + i], sibling)
         copy.start()
         passed.append(copy)
+    for i, peer in enumerate((sibling, across, corner)):
+        copy = send(ug_send.at[peer["fsdp"]], ug_land.at[me], a2a_send.at[3 + i], a2a_recv.at[3 + i], peer)
+        copy.start()
+        ug_exchange.append(copy)
+    lax.fori_loop(5, 6, hop, 0)
+    lax.fori_loop(10, 15, turn, 0)
+    lax.fori_loop(6, 7, hop, 0)
+    for copy in passed:
+        copy.wait()
+
+    lax.fori_loop(15, NB, turn, 0)
+
+    def arrange(i, carry):
+        tok_t[:, lanes_at(i * BLOCK, BLOCK)] = turned[order[0, i]]
+        return carry
+
+    lax.fori_loop(0, NB, arrange, 0)
+    keep = pltpu.make_async_copy(tok_t, tokens_t, local_sem.at[2])
+    keep.start()
+
+    def turn_weights(i, carry):
+        w_t[:, lanes_at(i * BLOCK, BLOCK)] = weights[rows_at(i * BLOCK, BLOCK)].T
+        return carry
+
+    lax.fori_loop(0, width // BLOCK, turn_weights, 0)
     for copy in ug_exchange:
         copy.wait()
     ug_own[...] = jnp.concatenate([ug_land[i].astype(F32) for i in range(4)], axis=0).astype(BF)
     ug_store = pltpu.make_async_copy(ug_own, w_ug.at[rows_at(dp * chunk, chunk)], local_sem.at[1])
     ug_store.start()
-    lax.fori_loop(5, 6, hop, 0)
-    lax.fori_loop(10, 15, turn, 0)
-    lax.fori_loop(6, 7, hop, 0)
     ug_store.wait()
-    for copy in ug_copies(0):
+    for copy in hidden_ring(w_ug, ug_s, ug_r, 0):
         copy.start()
-    for copy in passed:
-        copy.wait()
-
-    lax.fori_loop(15, NB, turn, 0)
-
-    def arrange(i, carry):
-        tok_t[:, lanes_at(i * BLOCK, BLOCK)] = turned[order[0, i]]
-        return carry
-
-    lax.fori_loop(0, NB, arrange, 0)
-    keep = pltpu.make_async_copy(tok_t, tokens_t, local_sem.at[2])
-    keep.start()
-
-    def turn_weights(i, carry):
-        w_t[:, lanes_at(i * BLOCK, BLOCK)] = weights[rows_at(i * BLOCK, BLOCK)].T
-        return carry
-
-    lax.fori_loop(0, width // BLOCK, turn_weights, 0)
     w_o[...] = jnp.concatenate([out_w[i].astype(F32) for i in range(8)], axis=0).astype(BF)
 
     def raw_copies(head):
@@ -862,7 +900,8 @@
             mixed[rows_at(head * HEAD_DIM, HEAD_DIM), span] = (acc[0:HEAD_DIM, :] * total).astype(BF)
             sums[head, :, span] = jnp.broadcast_to(total, (8, 256))
 
-        each_chunk(visit)
+        early_chunks(visit)
+        late_chunks(visit)
 
         @pl.when(head % 2 == 1)
         def _():
@@ -871,7 +910,7 @@
         return carry
 
     lax.fori_loop(0, heads, attend, 0)
-    ug_hop(2)
+    ug_hop(heads // 2)
 
     def share_copy(b):
         slot = b % 2
@@ -894,8 +933,10 @@
         share_copy(b).start()
         return carry
 
-    lax.fori_loop(0, NB, out_project, 0, unroll=4)
-    lax.fori_loop(3, 7, lambda step, c: (ug_hop(step), c)[1], 0)
+    lax.fori_loop(0, NB // 2, out_project, 0, unroll=2)
+    ug_hop(heads // 2 + 1)
+    lax.fori_loop(NB // 2, NB, out_project, 0, unroll=2)
+    lax.fori_loop(heads // 2 + 2, EARLY_HOPS, lambda step, c: (ug_hop(step), c)[1], 0)
     keep.wait()
     for b in (NB - 2, NB - 1):
         share_copy(b).wait()
@@ -904,17 +945,18 @@
             copy.wait()
 
 
-def forward(order, states, qkv_send, extra, out_piece, ug_send):
-    tps, rows_w, packed = qkv_send.shape
+def forward(order, states, w_query, w_key, w_value, small, extra, out_piece, w_up, w_gate):
+    tps, rows_w = 4, w_query.shape[0]
     tokens, width = states.shape
-    hidden_width = ug_send.shape[2]
+    packed = 3 * width // tps + small.shape[1]
+    hidden_width = 2 * w_up.shape[1] // tps
     cols = 8 * rows_w
     vmem, hbm = pl.BlockSpec(memory_space=pltpu.VMEM), pl.BlockSpec(memory_space=pl.ANY)
     smem = pl.BlockSpec(memory_space=pltpu.SMEM)
     dma = pltpu.SemaphoreType.DMA
     return pl.pallas_call(
         forward_kernel,
-        in_specs=[smem, hbm] + [vmem] * 4,
+        in_specs=[smem, hbm] + [vmem] * 8,
         out_specs=[hbm, vmem, vmem, hbm, hbm, vmem, vmem, hbm],
         out_shape=[
             jax.ShapeDtypeStruct((width, TOK), BF),
@@ -927,6 +969,8 @@
             jax.ShapeDtypeStruct((tps, tokens, width), BF),
         ],
         scratch_shapes=[
+            pltpu.VMEM((tps, rows_w, packed), BF),
+            pltpu.VMEM((tps, rows_w, hidden_width), BF),
             pltpu.VMEM((tps, rows_w, packed), BF),
             pltpu.VMEM((width, packed), BF),
             pltpu.VMEM((TOK, width), BF),
@@ -947,8 +991,8 @@
             dma((6,)),
             dma((4, 7)),
             dma((4, 7)),
-            dma((2, 7)),
-            dma((2, 7)),
+            dma((4, EARLY_HOPS)),
+            dma((4, EARLY_HOPS)),
             dma((3,)),
             dma((2, 3)),
             dma((2,)),
@@ -958,7 +1002,7 @@
         ),
         cost_estimate=pl.CostEstimate(flops=12 * 10**9, bytes_accessed=200 << 20, transcendentals=14 << 20),
         name="forward",
-    )(order, states, qkv_send, extra, out_piece, ug_send)
+    )(order, states, w_query, w_key, w_value, small, extra, out_piece, w_up, w_gate)
 
 
 def last_kernel(order, base, tokens_t, g_qkv, w_t, part_out, vectors,
@@ -1055,15 +1099,25 @@
 
         @pl.when(step > 0)
         def _():
-            for copy in hop_copies(step - 1):
-                copy.wait()
+            before, now = hop_copies(step - 1), hop_copies(step)
+            before[0].wait()
             ring_r[step] = (ring_r[step].astype(F32) + next_r[...]).astype(BF)
+            now[0].start()
+            before[1].wait()
             ring_l[step] = (ring_l[step].astype(F32) + next_l[...]).astype(BF)
+            now[1].start()
+            before[2].wait()
             ring_o[step] = (ring_o[step].astype(F32) + part_out[ring_dp(place + 1 + step)].astype(F32)).astype(BF)
+            now[2].start()
+            before[3].wait()
             ring_v[step] = ring_v[step] + vectors[ring_dp(place - 1 - step)]
-
-        for copy in hop_copies(step):
-            copy.start()
+            now[3].start()
+
+        @pl.when(step == 0)
+        def _():
+            for copy in hop_copies(0):
+                copy.start()
+
         @pl.when(step == 0)
         def _():
             lax.fori_loop(0, NB, split, 0)
@@ -1194,6 +1248,7 @@
 
 CHUNK = 128
 TILE = 256
+LAG = 3
 
 
 def tile(index, base=0):
@@ -1204,11 +1259,11 @@
     return lax.dot_general(a, b, (((1,), (1,)), ((), ())), preferred_element_type=F32)
 
 
-def middle_kernel(share, states, teacher, weight, mask, w_ug, w_own, rates, scales,
-                  w_d, out_states, hidden, attn_unit, back, attn_inv, hidden_inv, sums, gd_all, ht_all, act_all, ug_all,
+def middle_kernel(share, states, teacher, weight, mask, w_in, w_own, rates, scales,
+                  w_ug, w_d, out_states, hidden, attn_unit, back, attn_inv, hidden_inv, sums, gd_all, ht_all, act_all, ug_all,
                   part, core, x_buf, tok, gd, act, act_t, ug, ht,
                   ld_sem, core_send, core_recv, x_send, x_recv, tok_send, tok_recv, gd_send, gd_recv, gd_own,
-                  out_sem, ring_send, ring_recv):
+                  out_sem, ring_send, ring_recv, ug_s, ug_r, ug_sem):
     sibling, across, _ = group_peers()
     dp, place = lax.axis_index("dp"), ring_place()
     right, left = {"dp": ring_dp(place + 1)}, {"dp": ring_dp(place - 1)}
@@ -1256,24 +1311,17 @@
             pltpu.make_async_copy(ug.at[slot], ug_all.at[i], out_sem.at[2, slot]),
         ]
 
-    def ring(step):
-        first = rows_at(ring_dp(place - step) * piece, piece // 2)
-        second = rows_at(ring_dp(place + step) * piece + piece // 2, piece // 2)
-        return [
-            send(w_d.at[first], w_d.at[first], ring_send.at[0, step], ring_recv.at[0, step], right),
-            send(w_d.at[second], w_d.at[second], ring_send.at[1, step], ring_recv.at[1, step], left),
-        ]
-
-    def hop(step, carry):
-        for copy in ring(step):
+    def hop(step):
+        late = hidden_ring(w_d, ring_send, ring_recv, step + 1)
+        for copy, later in zip(hidden_ring(w_d, ring_send, ring_recv, step), late):
             copy.wait()
-
-        @pl.when(step < 6)
-        def _():
-            for copy in ring(step + 1):
-                copy.start()
-
-        return carry
+            pl.when(step < 6)(later.start)
+
+    def ug_hop(step):
+        late = hidden_ring(w_ug, ug_s, ug_r, step + 1, EARLY_HOPS)
+        for copy, later in zip(hidden_ring(w_ug, ug_s, ug_r, step, EARLY_HOPS), late):
+            copy.wait()
+            pl.when(step < 6)(later.start)
 
     def forward_far(stage, i):
         core_a(stage, i).wait_recv()
@@ -1292,8 +1340,27 @@
     sums[...] = jnp.zeros_like(sums)
     lax.fori_loop(0, count, lambda i, c: (load(i).start(), c)[1], 0)
     w_d[rows_at(dp * piece, piece)] = w_own[...]
+    chunk = w_ug.shape[0] // 8
+
+    def load_w(i):
+        cuts = rows_at(ring_dp(place - i) * chunk, chunk // 2), rows_at(
+            ring_dp(place + i) * chunk + chunk // 2, chunk // 2
+        )
+        return [pltpu.make_async_copy(w_in.at[cut], w_ug.at[cut], ug_sem.at[d, i]) for d, cut in enumerate(cuts)]
+
+    def start_w(i, carry):
+        for copy in load_w(i):
+            copy.start()
+        return carry
+
+    def wait_w(i, carry):
+        for copy in load_w(i):
+            copy.wait()
+        return carry
+
+    lax.fori_loop(0, EARLY_HOPS + 1, start_w, 0)
     greet([sibling, across, right, left])
-    for copy in ring(0):
+    for copy in hidden_ring(w_d, ring_send, ring_recv, 0):
         copy.start()
 
     def open_core(i, carry):
@@ -1303,6 +1370,9 @@
         return carry
 
     lax.fori_loop(0, count, open_core, 0)
+    lax.fori_loop(0, EARLY_HOPS + 1, wait_w, 0)
+    for copy in hidden_ring(w_ug, ug_s, ug_r, EARLY_HOPS, EARLY_HOPS):
+        copy.start()
     lax.fori_loop(0, count, lambda i, c: (forward_far(0, i), c)[1], 0)
 
     def norm_hidden(i):
@@ -1348,10 +1418,6 @@
             return carry
 
         lax.fori_loop(0, width // TILE, up, 0)
-
-        @pl.when(i == 0)
-        def _():
-            lax.fori_loop(4, 7, hop, 0)
 
         def down(n, carry):
             value = nn(act[...], w_d[:, tile(n)])
@@ -1387,19 +1453,20 @@
         copies[1].wait_recv()
         copies[2].start()
 
-    stages = (norm_hidden, pass_tokens, feed, finish, pass_grads)
+    stages = ((0, norm_hidden), (1, pass_tokens), (LAG, feed), (LAG + 1, finish), (LAG + 2, pass_grads))
 
     def step(t, carry):
-        for lag, stage in enumerate(stages):
+        for lag, stage in stages:
+            if lag == LAG:
+                pl.when(t < 7 - EARLY_HOPS)(lambda: ug_hop(EARLY_HOPS + t))
+                pl.when(t < 3)(lambda: hop(2 * t + 1))
+                pl.when(t == 2)(lambda: hop(6))
             pl.when((t >= lag) & (t < lag + count))(functools.partial(stage, t - lag))
-
-        @pl.when(t < 2)
-        def _():
-            lax.fori_loop(2 * t, 2 * t + 2, hop, 0)
-
-        return carry
-
-    lax.fori_loop(0, count + len(stages) - 1, step, 0)
+            if lag == 0:
+                pl.when(t < 3)(lambda: hop(2 * t))
+        return carry
+
+    lax.fori_loop(0, count + LAG + 2, step, 0)
 
     def close(i, carry):
         copies = gd_copies(i)
@@ -1422,9 +1489,10 @@
     dma = pltpu.SemaphoreType.DMA
     return pl.pallas_call(
         middle_kernel,
-        in_specs=[hbm] + [vmem] * 8,
-        out_specs=[vmem] * 8 + [hbm] * 4,
+        in_specs=[hbm] + [vmem] * 4 + [hbm] + [vmem] * 3,
+        out_specs=[vmem] * 9 + [hbm] * 4,
         out_shape=[
+            jax.ShapeDtypeStruct(w_ug.shape, BF),
             jax.ShapeDtypeStruct((8 * w_own.shape[0], width), BF),
             jax.ShapeDtypeStruct((rows, width), BF),
             jax.ShapeDtypeStruct((rows, width), F32),
@@ -1459,8 +1527,11 @@
             dma((3, count)),
             dma((count,)),
             dma((3, 2)),
-            dma((2, 7)),
-            dma((2, 7)),
+            dma((4, 7)),
+            dma((4, 7)),
+            dma((4, 7 - EARLY_HOPS)),
+            dma((4, 7 - EARLY_HOPS)),
+            dma((2, EARLY_HOPS + 1)),
         ],
         compiler_params=pltpu.CompilerParams(
             collective_id=3, has_side_effects=True, vmem_limit_bytes=60 << 20
@@ -1472,14 +1543,17 @@
 
 def middle_back_kernel(gd_all, act_all, ug_all, hidden, attn_unit, states, back, attn_inv, hidden_inv, w_ug, w_d,
                        rates, scales, base, ga_all, gug_all, down_rows, sums, ff_sums,
-                       part, core, x_buf, ga, gd, act, ug, gug, own_f, own_b, base_buf, dwd, column, ring_buf,
+                       w_ug_b, w_d_b, part, core, x_buf, ga, gd, act, ug, gug, own_f, own_b, base_buf, dwd, column, ring_buf,
                        gd_sem, act_sem, in_sem, own_sem, core_send, core_recv, x_send, x_recv, ga_send, ga_recv,
-                       ga_own, base_sem, out_sem, ring_send, ring_recv):
+                       ga_own, base_sem, out_sem, w_sem, ring_send, ring_recv):
     sibling, across, _ = group_peers()
     dp, place = lax.axis_index("dp"), ring_place()
     right, left = {"dp": ring_dp(place + 1)}, {"dp": ring_dp(place - 1)}
     count = core.shape[1]
     width = w_d.shape[0]
+    load_d = pltpu.make_async_copy(w_d, w_d_b, w_sem.at[0])
+    load_u = pltpu.make_async_copy(w_ug, w_ug_b, w_sem.at[1])
+    load_d.start()
     half = ring_buf.shape[2]
     rate_attn = rates[0:1]
 
@@ -1558,11 +1632,13 @@
     for copy in [load_ug(0)] + own_rows(0):
         copy.start()
     lax.fori_loop(0, count, lambda i, c: (load_gd(i).start(), c)[1], 0)
+    load_u.start()
     lax.fori_loop(0, count, lambda i, c: (load_act(i).start(), c)[1], 0)
     sums[...] = jnp.zeros_like(sums)
     ff_sums[...] = jnp.zeros_like(ff_sums)
     greet([sibling, across, right, left])
     lax.fori_loop(0, count, lambda i, c: (load_gd(i).wait(), c)[1], 0)
+    load_d.wait()
 
     def feed(i):
         slot = i % 2
@@ -1577,7 +1653,7 @@
             store_gug(i - 2).wait()
 
         def grads(n, carry):
-            g_act = nt(gd[i].reshape(4 * CHUNK, width), w_d[tile(n)])
+            g_act = nt(gd[i].reshape(4 * CHUNK, width), w_d_b[tile(n)])
             up_proj = ug[slot, :, tile(n)].astype(F32)
             gate_proj = ug[slot, :, tile(n, width)].astype(F32)
             scale_up, scale_gate = scales[0:1, tile(n)], scales[1:2, tile(n)]
@@ -1593,9 +1669,10 @@
 
         lax.fori_loop(0, width // TILE, grads, 0)
         store_gug(i).start()
+        pl.when(i == 0)(load_u.wait)
 
         def through(n, carry):
-            value = nt(gug[slot], w_ug[tile(n)])
+            value = nt(gug[slot], w_ug_b[tile(n)])
             part[i % 3, :, :, tile(n)] = value.astype(BF).reshape(4, CHUNK, TILE)
             return carry
 
@@ -1703,7 +1780,7 @@
     dma = pltpu.SemaphoreType.DMA
     return pl.pallas_call(
         middle_back_kernel,
-        in_specs=[hbm] * 7 + [vmem] * 6,
+        in_specs=[hbm] * 7 + [vmem] * 2 + [hbm] * 2 + [vmem] * 2,
         out_specs=[hbm, hbm, hbm, vmem, vmem, vmem],
         out_shape=[
             jax.ShapeDtypeStruct((rows, width), F32),
@@ -1714,6 +1791,8 @@
             jax.ShapeDtypeStruct((2, width), F32),
         ],
         scratch_shapes=[
+            pltpu.VMEM(w_ug.shape, BF),
+            pltpu.VMEM(w_d.shape, BF),
             pltpu.VMEM((3, 4, CHUNK, width), BF),
             pltpu.VMEM((2, count, CHUNK, width), BF),
             pltpu.VMEM((count, CHUNK, width), BF),
@@ -1739,6 +1818,7 @@
             dma((3, count)),
             dma((3, count)),
             dma((count,)),
+            dma((2,)),
             dma((2,)),
             dma((2,)),
             dma((2, 7)),
@@ -1834,22 +1914,10 @@
         axis=1,
     )
     small = jnp.pad(small, ((0, 0), (0, 59)))
-    qkv_send = jnp.concatenate(
-        [w.reshape(rows_w, tps, cols).transpose(1, 0, 2) for w in (w_query, w_key, w_value)]
-        + [jnp.broadcast_to(small[None], (tps, rows_w, 64))],
-        axis=2,
-    )
     extra = jnp.pad(jnp.stack((up_scale, gate_scale), axis=1), ((0, 0), (69, 57)))
     spread = [(j, tps * (j % dps) + j // dps) for j in range(dps * tps)]
-    ug_send = jnp.concatenate(
-        [
-            w.reshape(rows_w, dps, tps, ff_rows).transpose(2, 0, 1, 3).reshape(tps, rows_w, hid)
-            for w in (w_up, w_gate)
-        ],
-        axis=2,
-    )
     tokens_t, w_t, w_o, w_ug, qkv, mixed, sums, share = forward(
-        order, states, qkv_send, extra, lax.ppermute(w_out, both, spread), ug_send
+        order, states, w_query, w_key, w_value, small, extra, lax.ppermute(w_out, both, spread), w_up, w_gate
     )
     small_all = w_t[3 * cols : 3 * cols + 8].astype(F32)
     rates = small_all[1:3]
@@ -1858,7 +1926,7 @@
     scale_qk = lax.dynamic_slice_in_dim(small_all[0], me * cols, cols).reshape(cols // HEAD_DIM, HEAD_DIM, 1)
 
     mask_col = mask_f[:, None]
-    w_d, out_states, hidden, attn_unit, back, attn_inv, hidden_inv, sums_mid, gd_all, ht_all, act_all, ug_all = middle(
+    w_ug, w_d, out_states, hidden, attn_unit, back, attn_inv, hidden_inv, sums_mid, gd_all, ht_all, act_all, ug_all = middle(
         share, states, teacher, mask_col * (2.0 / valid_count), mask_col, w_ug, w_down, rates, scales
     )
     base, ga_all, gug_all, grad_down, sums_back, ff_sums = middle_back(

time: 676 us -> 618 us (0.914)
  Pallas kernels: 614 us -> 564 us
    pallas_call x3, Pallas kernels: 442 us -> 397 us  [the longest x1 166 us: middle(): pl.pallas_call(middle_kernel, in_specs=[hbm] + [vmem] * 4 + [hbm] + [vmem...]
    reshape x10 -> x0, local copies, waits for them, and re-layouts: 7.2 us -> none  [the longest x6 3.99 us: local(): w.reshape(rows_w, dps, tps, ff_rows).transpose(2, 0, 1, 3)]
    pallas_call x1, Pallas kernels: 116 us -> 109 us  [attention_back(): pl.pallas_call(attention_back_kernel, in_specs=[smem, hbm, vmem, vmem, vm...]
  transfers between devices with their start and end apart: 2 -> 2, of which waited for: 1 -> 1; matrix products, arithmetic and copies ran while one was open for 2% -> 1% of each run, Pallas kernels for 0% -> 0%
where the time goes in v5:
time: 618 us; the launch traced here: 617 us
  Pallas kernels  564 us (91%)
  local copies, waits for them, and re-layouts  22.7 us (4%)
  waiting for transfers between devices  10.5 us (2%)
  starting transfers between devices  7.46 us (1%)
  other arithmetic  6.66 us (1%)
  between operations  6.61 us (1%)
    pallas_call x1, Pallas kernels, middle(): pl.pallas_call(middle_kernel, in_specs=[hbm] + [vmem] * 4 + [hbm] + [vmem...  166 us
    pallas_call x1, Pallas kernels, middle_back(): pl.pallas_call(middle_back_kernel, in_specs=[hbm] * 7 + [vmem] * 2 + [hbm...  118 us
    pallas_call x1, Pallas kernels, forward(): pl.pallas_call(forward_kernel, in_specs=[smem, hbm] + [vmem] * 8, out_spe...  114 us
    pallas_call x1, Pallas kernels, attention_back(): pl.pallas_call(attention_back_kernel, in_specs=[smem, hbm, vmem, vmem, vm...  109 us
    pallas_call x1, Pallas kernels, last_exchange(): pl.pallas_call(last_kernel, in_specs=[pl.BlockSpec(memory_space=pltpu.SME...  54.8 us
  transfers between devices with their start and end apart: 2, of which 1 were waited for; matrix products, arithmetic and copies ran while one was open for 1% of the time, Pallas kernels for 0%

profile of v5, /device:TPU:4, one launch (start us, length us, event | category | flops | bytes accessed | tf_op | source)
XLA Modules:
  0.0 617.5 jit_solution(13510845173786061746)
XLA Ops:
  0.6 4.4 collective-permute-start
  5.1 1.4 fusion.2
  9.1 0.7 stack.38
  13.4 0.9 broadcast_in_dim.110.mask
  15.7 2.2 tree_order.1.order
  18.6 114.0 %forward.1 = (bf16[1280,2560]{1,0:T(8,128)(2,1)}, bf16[1024,1280]{1,0:T(8,128)(2,1)}, bf16[320,1280]{1,0:T(8,128)(2,1)}, bf16[1280,2560]{1,0:T(8,128)(2,1)}, f32...) custom-call(s32[8,128]{1,0:T(8,128)} %tree_order.1.order, ...), custom_call_target="tpu_custom_call" | custom-call | flops 12000000000 | bytes 209715200 | tf_op jit(solution)/shard_map/forward/pallas_call | solution.py:957
  132.6 0.7 slice_convert_fusion
  135.4 0.9 mul.48.weight
  136.9 165.7 %middle.1 = (bf16[1280,2560]{1,0:T(8,128)(2,1)}, bf16[1280,1280]{1,0:T(8,128)(2,1)}, bf16[640,1280]{1,0:T(8,128)(2,1)}, f32[640,1280]{1,0:T(8,128)}, bf16[640,12...) custom-call(bf16[4,640,1280]{2,1,0:T(8,128)(2,1)} %get-tuple-element, ...), custom_call_target="tpu_custom_call" | custom-call | flops 25999998976 | bytes 419430400 | tf_op jit(solution)/shard_map/middle/pallas_call | solution.py:1490
  302.6 117.5 %middle_back.1 = (f32[640,1280]{1,0:T(8,128)}, bf16[4,640,1280]{2,1,0:T(8,128)(2,1)}, bf16[5,512,2560]{2,1,0:T(8,128)(2,1)}, f32[160,1280]{1,0:T(8,128)}, f32[1,1280]{1,0:T(1,128)}, /*index=5*/f32[2,1280]{1,0:T(2,128)}) custom-call(bf16[5,4,128,1280]{3,2,1,0:T(8,128)(2,1)} %get-tuple-element.57.gd_all, bf16[5,1280,512]{2,1,0:T(8,128)(2,1)} %get-tuple-element.58.act_all, ...), custom_call_target="tpu_custom_call" | custom-call | flops 33999998976 | bytes 209715200 | tf_op jit(solution)/shard_map/middle_back/pallas_call | solution.py:1781
  420.1 0.8 multiply_reduce_fusion
  421.3 0.9 reshape.107.scales
  422.2 109.3 %attention_back.1 = (bf16[3,320,2560]{2,1,0:T(8,128)(2,1)}, f32[5,64,1]{2,1,0:T(8,128)}, bf16[320,1280]{1,0:T(8,128)(2,1)}, f32[40,5120]{1,0:T(8,128)}, f32[40,5120]{1,0:T(8,128)}) custom-call(s32[8,128]{1,0:T(8,128)} %tree_order.1.order, f32[3,320,2560]{2,1,0:T(8,128)} %get-tuple-element.69.qkv, f32[5,64,1]{2,1,0:T(8,128)} %reshape.107.scales, ...), custom_call_target="tpu_custom_call" | custom-call | flops 40000000000 | bytes 62914560 | tf_op jit(solution)/shard_map/attention_back/pallas_call | solution.py:598
  531.4 1.0 reduce.6
  534.3 1.7 copy-done.1
  536.1 1.1 copy-done.2
  537.2 54.8 %last_exchange.1 = (f32[640,1280]{1,0:T(8,128)}, f32[40,1280]{1,0:T(8,128)S(1)}, f32[40,1280]{1,0:T(8,128)S(1)}, f32[40,1280]{1,0:T(8,128)S(1)}, f32[40,1280]{1,0:T(8,128)S(1)}, /*index=5*/f32[4,128]{1,0:T(4,128)S(1)}) custom-call(s32[8,128]{1,0:T(8,128)S(1)} %copy-done, f32[640,1280]{1,0:T(8,128)} %get-tuple-element.67.base, ...), custom_call_target="tpu_custom_call" | custom-call | flops 12999999488 | bytes 104857600 | tf_op jit(solution)/shard_map/last_exchange/pallas_call | solution.py:1201
  593.3 3.0 collective-permute-start.1
  597.6 10.5 %collective-permute-done.1 = f32[40,1280]{1,0:T(8,128)S(1)} collective-permute-done((f32[40,1280]{1,0:T(8,128)S(1)}, f32[40,1280]{1,0:T(8,128)S(1)}, u32[]{:S(2)}, u32[]{:S(2)}) %collective-permute-start.1) | collective-permute-done | bytes 204832 | tf_op jit(solution)/shard_map/ppermute | solution.py:1959
  608.1 1.2 copy.57
  609.2 1.7 copy.58
  613.7 0.9 copy.63
  614.6 0.9 copy.64
  615.5 0.9 copy.65
  (68 shorter events, 13.6 us)
Async XLA Ops:
  0.6 17.3 %collective-permute-start = (bf16[40,1280]{1,0:T(8,128)(2,1)}, bf16[40,1280]{1,0:T(8,128)(2,1)S(1)}, u32[]{:S(2)}, u32[]{:S(2)}) collective-permute-start(bf16[40,1280]{1,0:T(8,128)(2,1)} %param.24), channel_id=1, source_target_pairs={{0,0},{1,4},{2,8},{3,12},{4,16},{5,20},{6,24},{7,28},{8,1},{9,5},{... | collective-permute-start | bytes 307208 | tf_op jit(solution)/shard_map/ppermute | solution.py:1920
  17.9 117.4 %copy-start.8 = (s32[640]{0:T(1024)S(1)}, s32[640]{0:T(1024)}, u32[]{:S(2)}) copy-start(s32[640]{0:T(1024)} %param.20) | copy-start | bytes 7684
  17.9 118.3 %copy-start.11 = (f32[2]{0:T(128)S(1)}, f32[2]{0:T(128)}, u32[]{:S(2)}) copy-start(f32[2]{0:T(128)} %constant.74) | copy-start | bytes 28
  18.0 0.6 copy-start.12
  422.1 110.4 %copy-start.10 = (f32[1,1280]{1,0:T(1,128)S(1)}, f32[1,1280]{1,0:T(1,128)}, u32[]{:S(2)}) copy-start(f32[1,1280]{1,0:T(1,128)} %get-tuple-element.78) | copy-start | bytes 15364
  422.1 110.5 %copy-start.9 = (f32[2,1280]{1,0:T(2,128)S(1)}, f32[2,1280]{1,0:T(2,128)}, u32[]{:S(2)}) copy-start(f32[2,1280]{1,0:T(2,128)} %get-tuple-element.79) | copy-start | bytes 30724
  422.2 112.2 %copy-start = (s32[8,128]{1,0:T(8,128)S(1)}, s32[8,128]{1,0:T(8,128)}, u32[]{:S(2)}) copy-start(s32[8,128]{1,0:T(8,128)} %tree_order.1.order) | copy-start | bytes 12292
  534.3 1.7 copy-start.1
  536.1 1.1 copy-start.2
  537.2 70.9 %copy-start.4 = (bf16[640,1280]{1,0:T(8,128)(2,1)S(1)}, bf16[640,1280]{1,0:T(8,128)(2,1)}, u32[]{:S(2)}) copy-start(bf16[640,1280]{1,0:T(8,128)(2,1)} %get-tuple-element.126) | copy-start | bytes 4915204
  593.3 14.8 %collective-permute-start.1 = (f32[40,1280]{1,0:T(8,128)S(1)}, f32[40,1280]{1,0:T(8,128)S(1)}, u32[]{:S(2)}, u32[]{:S(2)}) collective-permute-start(f32[40,1280]{1,0:T(8,128)S(1)} %get-tuple-element.87), channel_id=1, source_target_pairs={{0,0},{4,1},{8,2},{12,3},{16,4},{20,5},{24,6},{28,7},{1,8},{5,9},{... | collective-permute-start | bytes 614408 | tf_op jit(solution)/shard_map/ppermute | solution.py:1959
  597.0 12.3 %copy-start.3 = (f32[640,1280]{1,0:T(8,128)S(1)}, f32[640,1280]{1,0:T(8,128)}, u32[]{:S(2)}) copy-start(f32[640,1280]{1,0:T(8,128)} %get-tuple-element.128) | copy-start | bytes 9830404
  609.2 4.4 copy-start.7
  609.2 5.3 copy-start.6
  611.0 4.5 copy-start.5

commit v6 on v5

--- a/solution.py
+++ b/solution.py
@@ -357,7 +357,7 @@
 
 def attention_back_kernel(order, qkv, scales, sums, mixed, ga_all, w_o, ht_all, gug_all,
                           g_qkv, g_scale, part_out, g_up, g_gate,
-                          ga_b, ga, gm, raw, out_b, qT, q, k, kT, v, gT, g, dq, dk, dv, delta, inv,
+                          w_b, ga_b, ga, gm, raw, out_b, qT, q, k, kT, v, gT, g, dq, dk, dv, delta, inv,
                           gug_b, ht_r, ht_l, ring, own, hid_buf, hid_in,
                           ga_sem, gug_sem, row_sem, raw_sem, out_sem, ring_send, ring_recv, a2a_send, a2a_recv):
     me = lax.axis_index("fsdp")
@@ -391,6 +391,8 @@
 
     load_ga = pltpu.make_async_copy(ga_all, ga_b, ga_sem.at[0])
     load_ga.start()
+    load_w = pltpu.make_async_copy(w_o.at[0], w_b, ga_sem.at[1])
+    load_w.start()
     raw_copy(0).start()
     for copy in slices(0):
         copy.start()
@@ -401,6 +403,7 @@
         copy.start()
     greet([*peers, right, left])
     load_ga.wait()
+    load_w.wait()
 
     def pick(i, carry):
         ga[lanes_at(i * BLOCK, BLOCK)] = ga_b[order[0, i]]
@@ -409,7 +412,7 @@
     lax.fori_loop(0, NB, pick, 0)
 
     def back(n, carry):
-        gm[:, tile(n)] = nt(w_o[...], ga[tile(n)]).astype(BF)
+        gm[:, tile(n)] = nt(w_b[...], ga[tile(n)]).astype(BF)
         return carry
 
     lax.fori_loop(0, TOK // TILE, back, 0)
@@ -597,18 +600,19 @@
     dma = pltpu.SemaphoreType.DMA
     return pl.pallas_call(
         attention_back_kernel,
-        in_specs=[smem, hbm, vmem, vmem, vmem, hbm, vmem, hbm, hbm],
+        in_specs=[smem, hbm, vmem, vmem, vmem, hbm, hbm, hbm, hbm],
         out_specs=[hbm, vmem, vmem, vmem, vmem],
         out_shape=[
             jax.ShapeDtypeStruct(qkv.shape, BF),
             jax.ShapeDtypeStruct(scales.shape, F32),
-            jax.ShapeDtypeStruct(w_o.shape, BF),
+            jax.ShapeDtypeStruct(w_o.shape[1:], BF),
             jax.ShapeDtypeStruct((rows_w, 2 * hidden_width), F32),
             jax.ShapeDtypeStruct((rows_w, 2 * hidden_width), F32),
         ],
         scratch_shapes=[
+            pltpu.VMEM(w_o.shape[1:], BF),
             pltpu.VMEM(ga_all.shape, BF),
-            pltpu.VMEM((TOK, w_o.shape[1]), BF),
+            pltpu.VMEM((TOK, w_o.shape[2]), BF),
             pltpu.VMEM(mixed.shape, BF),
             pltpu.VMEM((2, 3, HEAD_DIM, TOK), F32),
             pltpu.VMEM((2, 3, HEAD_DIM, TOK), BF),
@@ -631,7 +635,7 @@
             pltpu.VMEM((2, chunk, side), F32),
             pltpu.VMEM((4, rows_w, hidden_width), BF),
             pltpu.VMEM((4, rows_w, hidden_width), BF),
-            dma((1,)),
+            dma((2,)),
             dma((count,)),
             dma((2, 2)),
             dma((2,)),
@@ -684,7 +688,7 @@
     )
 
 
-EARLY_HOPS = 5
+EARLY_HOPS = 4
 
 
 def hidden_ring(ref, sends, recvs, step, base=0):
@@ -703,10 +707,10 @@
 
 
 def forward_kernel(order, states, w_query, w_key, w_value, small, extra, out_piece, w_up, w_gate,
-                   tokens_t, w_t, w_o, w_ug, qkv, mixed, sums, share,
-                   qkv_send, ug_send, land, weights, tok, turned, tok_t, out_w, ug_land, ug_own, raw, qs, ks, vs, blocks, stage,
+                   tokens_t, w_t, w_o, w_ug, qkv, mixed, sums, mixed_n,
+                   qkv_send, ug_send, land, weights, tok, turned, tok_t, out_w, ug_land, ug_own, raw, qs, ks, vs, blocks, natural,
                    tok_send, tok_recv, a2a_send, a2a_recv, ring_send, ring_recv, ug_s, ug_r, local_sem, raw_sem,
-                   stage_sem):
+                   w_send, w_recv):
     me, dp = lax.axis_index("fsdp"), lax.axis_index("dp")
     place = ring_place()
     sibling, across, corner = group_peers()
@@ -843,7 +847,13 @@
     ug_store.wait()
     for copy in hidden_ring(w_ug, ug_s, ug_r, 0):
         copy.start()
-    w_o[...] = jnp.concatenate([out_w[i].astype(F32) for i in range(8)], axis=0).astype(BF)
+    w_o[0] = jnp.concatenate([out_w[i].astype(F32) for i in range(8)], axis=0).astype(BF)
+    w_copies = [
+        send(w_o.at[0], w_o.at[i + 1], w_send.at[i], w_recv.at[i], peer)
+        for i, peer in enumerate((sibling, across, corner))
+    ]
+    for copy in w_copies:
+        copy.start()
 
     def raw_copies(head):
         slot = head % 2
@@ -912,34 +922,24 @@
     lax.fori_loop(0, heads, attend, 0)
     ug_hop(heads // 2)
 
-    def share_copy(b):
-        slot = b % 2
-        return pltpu.make_async_copy(
-            stage.at[slot], share.at[b // 5, lanes_at((b % 5) * BLOCK, BLOCK)], stage_sem.at[slot]
-        )
-
     def split(i, carry):
         blocks[i] = mixed[:, lanes_at(i * BLOCK, BLOCK)]
         return carry
 
+    def arrange_back(i, carry):
+        natural[i] = blocks[order[1, i]]
+        return carry
+
     lax.fori_loop(0, NB, split, 0)
-
-    def out_project(b, carry):
-        @pl.when(b >= 2)
-        def _():
-            share_copy(b - 2).wait()
-
-        stage[b % 2] = nn(blocks[order[1, b]].T, w_o[...]).astype(BF)
-        share_copy(b).start()
-        return carry
-
-    lax.fori_loop(0, NB // 2, out_project, 0, unroll=2)
+    lax.fori_loop(0, NB, arrange_back, 0)
+    keep_mixed = pltpu.make_async_copy(natural, mixed_n, local_sem.at[3])
+    keep_mixed.start()
     ug_hop(heads // 2 + 1)
-    lax.fori_loop(NB // 2, NB, out_project, 0, unroll=2)
     lax.fori_loop(heads // 2 + 2, EARLY_HOPS, lambda step, c: (ug_hop(step), c)[1], 0)
     keep.wait()
-    for b in (NB - 2, NB - 1):
-        share_copy(b).wait()
+    keep_mixed.wait()
+    for copy in w_copies:
+        copy.wait()
     for head in (heads - 2, heads - 1):
         for copy in raw_copies(head):
             copy.wait()
@@ -961,12 +961,12 @@
         out_shape=[
             jax.ShapeDtypeStruct((width, TOK), BF),
             jax.ShapeDtypeStruct((packed, width), BF),
-            jax.ShapeDtypeStruct((cols, width), BF),
+            jax.ShapeDtypeStruct((tps, cols, width), BF),
             jax.ShapeDtypeStruct((width, hidden_width), BF),
             jax.ShapeDtypeStruct((3, cols, TOK), F32),
             jax.ShapeDtypeStruct((cols, TOK), BF),
             jax.ShapeDtypeStruct((cols // HEAD_DIM, 8, TOK), F32),
-            jax.ShapeDtypeStruct((tps, tokens, width), BF),
+            jax.ShapeDtypeStruct((NB, cols, BLOCK), BF),
         ],
         scratch_shapes=[
             pltpu.VMEM((tps, rows_w, packed), BF),
@@ -984,7 +984,7 @@
             pltpu.VMEM((TOK, HEAD_DIM), BF),
             pltpu.VMEM((HEAD_DIM + 16, TOK), BF),
             pltpu.VMEM((NB, cols, BLOCK), BF),
-            pltpu.VMEM((2, BLOCK, width), BF),
+            pltpu.VMEM((NB, cols, BLOCK), BF),
             dma((5,)),
             dma((5,)),
             dma((6,)),
@@ -993,9 +993,10 @@
             dma((4, 7)),
             dma((4, EARLY_HOPS)),
             dma((4, EARLY_HOPS)),
+            dma((4,)),
+            dma((2, 3)),
             dma((3,)),
-            dma((2, 3)),
-            dma((2,)),
+            dma((3,)),
         ],
         compiler_params=pltpu.CompilerParams(
             collective_id=1, has_side_effects=True, vmem_limit_bytes=56 << 20
@@ -1118,27 +1119,29 @@
             for copy in hop_copies(0):
                 copy.start()
 
-        @pl.when(step == 0)
+        @pl.when(step < 4)
         def _():
-            lax.fori_loop(0, NB, split, 0)
-
-        pl.when(step < 4)(functools.partial(through, 3 - step, step % 3))
-
-        @pl.when(step == 0)
-        def _():
-            core[0].start()
-
-        @pl.when(step == 1)
-        def _():
-            core[0].wait()
-            for i in range(4):
-                span = pl.ds(i * quarter, quarter)
-                share[1, span] = (share[1, span].astype(F32) + core_buf[0, span].astype(F32)).astype(BF)
-                far[i].start()
-
-        @pl.when(step == 2)
-        def _():
-            core[1].start()
+            @pl.when(step == 0)
+            def _():
+                lax.fori_loop(0, NB, split, 0)
+                through(3, 0)
+                core[0].start()
+
+            @pl.when(step < 3)
+            def _():
+                through(2 - step, (step + 1) % 3)
+
+            @pl.when(step == 0)
+            def _():
+                core[0].wait()
+                for i in range(4):
+                    span = pl.ds(i * quarter, quarter)
+                    share[1, span] = (share[1, span].astype(F32) + core_buf[0, span].astype(F32)).astype(BF)
+                    far[i].start()
+
+            @pl.when(step == 1)
+            def _():
+                core[1].start()
 
         return carry
 
@@ -1259,33 +1262,50 @@
     return lax.dot_general(a, b, (((1,), (1,)), ((), ())), preferred_element_type=F32)
 
 
-def middle_kernel(share, states, teacher, weight, mask, w_in, w_own, rates, scales,
-                  w_ug, w_d, out_states, hidden, attn_unit, back, attn_inv, hidden_inv, sums, gd_all, ht_all, act_all, ug_all,
-                  part, core, x_buf, tok, gd, act, act_t, ug, ht,
-                  ld_sem, core_send, core_recv, x_send, x_recv, tok_send, tok_recv, gd_send, gd_recv, gd_own,
+def middle_kernel(mixed_n, states, teacher, weight, mask, w_in, w_own, w_o, rates, scales,
+                  w_ug_out, w_d_out, hidden_out, back_out, out_states, attn_unit, attn_inv, hidden_inv, sums, gd_all,
+                  ht_all, act_all, ug_all, w_ug, w_d, hidden, back, mx, part, core, x_buf, tok, gd, act, act_t, ug, ht,
+                  mx_send, mx_recv, mx_own, keep_sem, core_send, core_recv, x_send, x_recv, tok_send, tok_recv, gd_send, gd_recv, gd_own,
                   out_sem, ring_send, ring_recv, ug_s, ug_r, ug_sem):
-    sibling, across, _ = group_peers()
+    sibling, across, corner = group_peers()
     dp, place = lax.axis_index("dp"), ring_place()
     right, left = {"dp": ring_dp(place + 1)}, {"dp": ring_dp(place - 1)}
     piece = w_own.shape[0]
-    count = part.shape[0]
+    count = x_buf.shape[0]
     width = hidden.shape[1]
     rate_attn, rate_mlp = rates[0:1], rates[1:2]
 
     def rows(i):
         return pl.ds(pl.multiple_of(i * CHUNK, CHUNK), CHUNK)
 
-    def load(i):
-        return pltpu.make_async_copy(share.at[:, rows(i)], part.at[i], ld_sem.at[i])
+    def mx_copies(i):
+        return [
+            send(mixed_n.at[(r + 1) * count + i], mx.at[i, r + 1], mx_send.at[r, i], mx_recv.at[r, i], peer)
+            for r, peer in enumerate((sibling, across, corner))
+        ]
+
+    def mx_local(i):
+        return pltpu.make_async_copy(mixed_n.at[i], mx.at[i, 0], mx_own.at[i])
+
+    def keep_rows(i):
+        return [
+            pltpu.make_async_copy(hidden.at[rows(i)], hidden_out.at[rows(i)], keep_sem.at[0, i]),
+            pltpu.make_async_copy(back.at[rows(i)], back_out.at[rows(i)], keep_sem.at[1, i]),
+        ]
+
+    keep_w = [
+        pltpu.make_async_copy(w_ug, w_ug_out, keep_sem.at[2, 0]),
+        pltpu.make_async_copy(w_d, w_d_out, keep_sem.at[2, 1]),
+    ]
 
     def core_a(stage, i):
-        return send(part.at[i, 3], core.at[0, i], core_send.at[stage, 0, i], core_recv.at[stage, 0, i], sibling)
+        return send(part.at[i % 3, 3], core.at[0, i], core_send.at[stage, 0, i], core_recv.at[stage, 0, i], sibling)
 
     def core_b(stage, i):
-        return send(part.at[i, 1], core.at[1, i], core_send.at[stage, 1, i], core_recv.at[stage, 1, i], sibling)
+        return send(part.at[i % 3, 1], core.at[1, i], core_send.at[stage, 1, i], core_recv.at[stage, 1, i], sibling)
 
     def chip(stage, i):
-        return send(part.at[i, 2], x_buf.at[i], x_send.at[stage, i], x_recv.at[stage, i], across)
+        return send(part.at[i % 3, 2], x_buf.at[i], x_send.at[stage, i], x_recv.at[stage, i], across)
 
     def spread(buf, own, sems, recvs, i):
         return [
@@ -1325,20 +1345,19 @@
 
     def forward_far(stage, i):
         core_a(stage, i).wait_recv()
-        part[i, 2] = (part[i, 2].astype(F32) + core[0, i].astype(F32)).astype(BF)
+        part[i % 3, 2] = (part[i % 3, 2].astype(F32) + core[0, i].astype(F32)).astype(BF)
         chip(stage, i).start()
 
     def reduced(stage, i):
         core_b(stage, i).wait_recv()
         chip(stage, i).wait_recv()
-        total = part[i, 0].astype(F32) + core[1, i].astype(F32) + x_buf[i].astype(F32)
+        total = part[i % 3, 0].astype(F32) + core[1, i].astype(F32) + x_buf[i].astype(F32)
         core_a(stage, i).wait_send()
         core_b(stage, i).wait_send()
         chip(stage, i).wait_send()
         return total
 
     sums[...] = jnp.zeros_like(sums)
-    lax.fori_loop(0, count, lambda i, c: (load(i).start(), c)[1], 0)
     w_d[rows_at(dp * piece, piece)] = w_own[...]
     chunk = w_ug.shape[0] // 8
 
@@ -1359,24 +1378,29 @@
         return carry
 
     lax.fori_loop(0, EARLY_HOPS + 1, start_w, 0)
-    greet([sibling, across, right, left])
+    greet([sibling, across, corner, right, left])
     for copy in hidden_ring(w_d, ring_send, ring_recv, 0):
         copy.start()
 
-    def open_core(i, carry):
-        load(i).wait()
-        core_a(0, i).start()
-        core_b(0, i).start()
-        return carry
-
-    lax.fori_loop(0, count, open_core, 0)
+    def open_mixed(i, carry):
+        mx_local(i).start()
+        for copy in mx_copies(i):
+            copy.start()
+        return carry
+
+    lax.fori_loop(0, count, open_mixed, 0)
     lax.fori_loop(0, EARLY_HOPS + 1, wait_w, 0)
     for copy in hidden_ring(w_ug, ug_s, ug_r, EARLY_HOPS, EARLY_HOPS):
         copy.start()
-    lax.fori_loop(0, count, lambda i, c: (forward_far(0, i), c)[1], 0)
 
     def norm_hidden(i):
-        unit, inverse = unit_rows(reduced(0, i))
+        mx_local(i).wait()
+        for copy in mx_copies(i):
+            copy.wait()
+        attn = nn(mx[i, 0].T, w_o[0])
+        for r in range(1, 4):
+            attn = attn + nn(mx[i, r].T, w_o[r])
+        unit, inverse = unit_rows(attn)
         own = states[rows(i)].astype(F32)
         value, value_inv = unit_rows(own + rate_attn * (unit - own))
         hidden[rows(i)] = value
@@ -1421,19 +1445,19 @@
 
         def down(n, carry):
             value = nn(act[...], w_d[:, tile(n)])
-            part[i, :, :, tile(n)] = value.astype(BF).reshape(4, CHUNK, TILE)
+            part[i % 3, :, :, tile(n)] = value.astype(BF).reshape(4, CHUNK, TILE)
             ht[slot, tile(n)] = tok[i, :, :, tile(n)].reshape(4 * CHUNK, TILE).T
             return carry
 
         lax.fori_loop(0, width // TILE, down, 0)
-        core_a(1, i).start()
-        core_b(1, i).start()
+        core_a(0, i).start()
+        core_b(0, i).start()
         for copy in outs(i):
             copy.start()
-        forward_far(1, i)
+        forward_far(0, i)
 
     def finish(i):
-        unit, inverse = unit_rows(reduced(1, i))
+        unit, inverse = unit_rows(reduced(0, i))
         own = hidden[rows(i)]
         result, result_inv = unit_rows(own + rate_mlp * (unit - own))
         out_states[rows(i)] = result.astype(BF)
@@ -1447,6 +1471,8 @@
         copies[0].start()
         copies[1].start()
         gd_local(i).start()
+        for copy in keep_rows(i):
+            copy.start()
 
     def pass_grads(i):
         copies = gd_copies(i)
@@ -1461,6 +1487,12 @@
                 pl.when(t < 7 - EARLY_HOPS)(lambda: ug_hop(EARLY_HOPS + t))
                 pl.when(t < 3)(lambda: hop(2 * t + 1))
                 pl.when(t == 2)(lambda: hop(6))
+
+                @pl.when(t == 2)
+                def _():
+                    for copy in keep_w:
+                        copy.start()
+
             pl.when((t >= lag) & (t < lag + count))(functools.partial(stage, t - lag))
             if lag == 0:
                 pl.when(t < 3)(lambda: hop(2 * t))
@@ -1474,30 +1506,34 @@
         copies[1].wait_send()
         copies[2].wait()
         gd_local(i).wait()
+        for copy in keep_rows(i):
+            copy.wait()
         return carry
 
     lax.fori_loop(0, count, close, 0)
     for i in (count - 2, count - 1):
         for copy in outs(i):
             copy.wait()
-
-
-def middle(share, states, teacher, weight, mask, w_ug, w_own, rates, scales):
+    for copy in keep_w:
+        copy.wait()
+
+
+def middle(mixed_n, states, teacher, weight, mask, w_ug, w_own, w_o, rates, scales):
     rows, width = states.shape
     count = rows // CHUNK
     vmem, hbm = pl.BlockSpec(memory_space=pltpu.VMEM), pl.BlockSpec(memory_space=pl.ANY)
     dma = pltpu.SemaphoreType.DMA
     return pl.pallas_call(
         middle_kernel,
-        in_specs=[hbm] + [vmem] * 4 + [hbm] + [vmem] * 3,
-        out_specs=[vmem] * 9 + [hbm] * 4,
+        in_specs=[hbm] + [vmem] * 4 + [hbm] + [vmem] * 4,
+        out_specs=[hbm] * 4 + [vmem] * 5 + [hbm] * 4,
         out_shape=[
             jax.ShapeDtypeStruct(w_ug.shape, BF),
             jax.ShapeDtypeStruct((8 * w_own.shape[0], width), BF),
-            jax.ShapeDtypeStruct((rows, width), BF),
+            jax.ShapeDtypeStruct((rows, width), F32),
             jax.ShapeDtypeStruct((rows, width), F32),
             jax.ShapeDtypeStruct((rows, width), BF),
-            jax.ShapeDtypeStruct((rows, width), F32),
+            jax.ShapeDtypeStruct((rows, width), BF),
             jax.ShapeDtypeStruct((rows, 1), F32),
             jax.ShapeDtypeStruct((rows, 1), F32),
             jax.ShapeDtypeStruct((2, width), F32),
@@ -1507,7 +1543,12 @@
             jax.ShapeDtypeStruct((count, 4 * CHUNK, 2 * width), BF),
         ],
         scratch_shapes=[
-            pltpu.VMEM((count, 4, CHUNK, width), BF),
+            pltpu.VMEM(w_ug.shape, BF),
+            pltpu.VMEM((8 * w_own.shape[0], width), BF),
+            pltpu.VMEM((rows, width), F32),
+            pltpu.VMEM((rows, width), F32),
+            pltpu.VMEM((count, 4) + mixed_n.shape[1:], BF),
+            pltpu.VMEM((3, 4, CHUNK, width), BF),
             pltpu.VMEM((2, count, CHUNK, width), BF),
             pltpu.VMEM((count, CHUNK, width), BF),
             pltpu.VMEM((count, 4, CHUNK, width), BF),
@@ -1516,11 +1557,14 @@
             pltpu.VMEM((2, width, 4 * CHUNK), BF),
             pltpu.VMEM((2, 4 * CHUNK, 2 * width), BF),
             pltpu.VMEM((2, width, 4 * CHUNK), BF),
+            dma((3, count)),
+            dma((3, count)),
             dma((count,)),
-            dma((2, 2, count)),
-            dma((2, 2, count)),
-            dma((2, count)),
-            dma((2, count)),
+            dma((3, count)),
+            dma((1, 2, count)),
+            dma((1, 2, count)),
+            dma((1, count)),
+            dma((1, count)),
             dma((3, count)),
             dma((3, count)),
             dma((3, count)),
@@ -1534,11 +1578,11 @@
             dma((2, EARLY_HOPS + 1)),
         ],
         compiler_params=pltpu.CompilerParams(
-            collective_id=3, has_side_effects=True, vmem_limit_bytes=60 << 20
+            collective_id=3, has_side_effects=True, vmem_limit_bytes=62 << 20
         ),
         cost_estimate=pl.CostEstimate(flops=26 * 10**9, bytes_accessed=400 << 20, transcendentals=4 << 20),
         name="middle",
-    )(share, states, teacher, weight, mask, w_ug, w_own, rates, scales)
+    )(mixed_n, states, teacher, weight, mask, w_ug, w_own, w_o, rates, scales)
 
 
 def middle_back_kernel(gd_all, act_all, ug_all, hidden, attn_unit, states, back, attn_inv, hidden_inv, w_ug, w_d,
@@ -1916,7 +1960,7 @@
     small = jnp.pad(small, ((0, 0), (0, 59)))
     extra = jnp.pad(jnp.stack((up_scale, gate_scale), axis=1), ((0, 0), (69, 57)))
     spread = [(j, tps * (j % dps) + j // dps) for j in range(dps * tps)]
-    tokens_t, w_t, w_o, w_ug, qkv, mixed, sums, share = forward(
+    tokens_t, w_t, w_o, w_ug, qkv, mixed, sums, mixed_n = forward(
         order, states, w_query, w_key, w_value, small, extra, lax.ppermute(w_out, both, spread), w_up, w_gate
     )
     small_all = w_t[3 * cols : 3 * cols + 8].astype(F32)
@@ -1926,8 +1970,8 @@
     scale_qk = lax.dynamic_slice_in_dim(small_all[0], me * cols, cols).reshape(cols // HEAD_DIM, HEAD_DIM, 1)
 
     mask_col = mask_f[:, None]
-    w_ug, w_d, out_states, hidden, attn_unit, back, attn_inv, hidden_inv, sums_mid, gd_all, ht_all, act_all, ug_all = middle(
-        share, states, teacher, mask_col * (2.0 / valid_count), mask_col, w_ug, w_down, rates, scales
+    w_ug, w_d, hidden, back, out_states, attn_unit, attn_inv, hidden_inv, sums_mid, gd_all, ht_all, act_all, ug_all = middle(
+        mixed_n, states, teacher, mask_col * (2.0 / valid_count), mask_col, w_ug, w_down, w_o, rates, scales
     )
     base, ga_all, gug_all, grad_down, sums_back, ff_sums = middle_back(
         gd_all, act_all, ug_all, hidden, attn_unit, states, back, attn_inv, hidden_inv, w_ug, w_d, rates, scales

time: 618 us -> 603 us (0.976)
  Pallas kernels: 564 us -> 548 us
    pallas_call x1, Pallas kernels: 114 us -> 106 us  [forward(): pl.pallas_call(forward_kernel, in_specs=[smem, hbm] + [vmem] * 8, out_spe...]
    pallas_call x1, Pallas kernels: 166 us -> 159 us  [middle(): pl.pallas_call(middle_kernel, in_specs=[hbm] + [vmem] * 4 + [hbm] + [vmem...]
where the time goes in v6:
time: 603 us; the launch traced here: 602 us
  Pallas kernels  548 us (91%)
  local copies, waits for them, and re-layouts  22.7 us (4%)
  waiting for transfers between devices  10.5 us (2%)
  starting transfers between devices  7.61 us (1%)
  other arithmetic  6.66 us (1%)
  between operations  6.61 us (1%)
    pallas_call x1, Pallas kernels, middle(): pl.pallas_call(middle_kernel, in_specs=[hbm] + [vmem] * 4 + [hbm] + [vmem...  159 us
    pallas_call x1, Pallas kernels, middle_back(): pl.pallas_call(middle_back_kernel, in_specs=[hbm] * 7 + [vmem] * 2 + [hbm...  117 us
    pallas_call x1, Pallas kernels, attention_back(): pl.pallas_call(attention_back_kernel, in_specs=[smem, hbm, vmem, vmem, vm...  109 us
    pallas_call x1, Pallas kernels, forward(): pl.pallas_call(forward_kernel, in_specs=[smem, hbm] + [vmem] * 8, out_spe...  106 us
    pallas_call x1, Pallas kernels, last_exchange(): pl.pallas_call(last_kernel, in_specs=[pl.BlockSpec(memory_space=pltpu.SME...  54.1 us
  transfers between devices with their start and end apart: 2, of which 1 were waited for; matrix products, arithmetic and copies ran while one was open for 1% of the time, Pallas kernels for 0%

profile of v6, /device:TPU:4, one launch (start us, length us, event | category | flops | bytes accessed | tf_op | source)
XLA Modules:
  0.0 602.1 jit_solution(16937447850173891986)
XLA Ops:
  0.6 4.4 collective-permute-start
  5.1 1.4 fusion.2
  9.1 0.7 stack.38
  13.4 0.9 broadcast_in_dim.110.mask
  15.7 2.2 tree_order.1.order
  18.6 105.9 %forward.1 = (bf16[1280,2560]{1,0:T(8,128)(2,1)}, bf16[1024,1280]{1,0:T(8,128)(2,1)}, bf16[4,320,1280]{2,1,0:T(8,128)(2,1)}, bf16[1280,2560]{1,0:T(8,128)(2,1)},...) custom-call(s32[8,128]{1,0:T(8,128)} %tree_order.1.order, ...), custom_call_target="tpu_custom_call" | custom-call | flops 12000000000 | bytes 209715200 | tf_op jit(solution)/shard_map/forward/pallas_call | solution.py:957
  124.5 0.7 slice_convert_fusion
  127.2 0.9 mul.48.weight
  128.8 159.4 %middle.1 = (bf16[1280,2560]{1,0:T(8,128)(2,1)}, bf16[1280,1280]{1,0:T(8,128)(2,1)}, f32[640,1280]{1,0:T(8,128)}, f32[640,1280]{1,0:T(8,128)}, bf16[640,1280]{1,...) custom-call(bf16[20,320,128]{2,1,0:T(8,128)(2,1)} %get-tuple-element, ...), custom_call_target="tpu_custom_call" | custom-call | flops 25999998976 | bytes 419430400 | tf_op jit(solution)/shard_map/middle/pallas_call | solution.py:1526
  288.2 117.2 %middle_back.1 = (f32[640,1280]{1,0:T(8,128)}, bf16[4,640,1280]{2,1,0:T(8,128)(2,1)}, bf16[5,512,2560]{2,1,0:T(8,128)(2,1)}, f32[160,1280]{1,0:T(8,128)}, f32[1,1280]{1,0:T(1,128)}, /*index=5*/f32[2,1280]{1,0:T(2,128)}) custom-call(bf16[5,4,128,1280]{3,2,1,0:T(8,128)(2,1)} %get-tuple-element.58.gd_all, bf16[5,1280,512]{2,1,0:T(8,128)(2,1)} %get-tuple-element.59.act_all, ...), custom_call_target="tpu_custom_call" | custom-call | flops 33999998976 | bytes 209715200 | tf_op jit(solution)/shard_map/middle_back/pallas_call | solution.py:1825
  405.4 0.8 multiply_reduce_fusion
  406.5 0.9 reshape.107.scales
  407.4 109.2 %attention_back.1 = (bf16[3,320,2560]{2,1,0:T(8,128)(2,1)}, f32[5,64,1]{2,1,0:T(8,128)}, bf16[320,1280]{1,0:T(8,128)(2,1)}, f32[40,5120]{1,0:T(8,128)}, f32[40,5120]{1,0:T(8,128)}) custom-call(s32[8,128]{1,0:T(8,128)} %tree_order.1.order, f32[3,320,2560]{2,1,0:T(8,128)} %get-tuple-element.70.qkv, f32[5,64,1]{2,1,0:T(8,128)} %reshape.107.scales, ...), custom_call_target="tpu_custom_call" | custom-call | flops 40000000000 | bytes 62914560 | tf_op jit(solution)/shard_map/attention_back/pallas_call | solution.py:601
  516.7 1.0 reduce.6
  519.6 1.7 copy-done.1
  521.3 1.1 copy-done.2
  522.5 54.1 %last_exchange.1 = (f32[640,1280]{1,0:T(8,128)}, f32[40,1280]{1,0:T(8,128)S(1)}, f32[40,1280]{1,0:T(8,128)S(1)}, f32[40,1280]{1,0:T(8,128)S(1)}, f32[40,1280]{1,0:T(8,128)S(1)}, /*index=5*/f32[4,128]{1,0:T(4,128)S(1)}) custom-call(s32[8,128]{1,0:T(8,128)S(1)} %copy-done, f32[640,1280]{1,0:T(8,128)} %get-tuple-element.68.base, ...), custom_call_target="tpu_custom_call" | custom-call | flops 12999999488 | bytes 104857600 | tf_op jit(solution)/shard_map/last_exchange/pallas_call | solution.py:1204
  577.8 3.2 collective-permute-start.1
  582.2 10.5 %collective-permute-done.1 = f32[40,1280]{1,0:T(8,128)S(1)} collective-permute-done((f32[40,1280]{1,0:T(8,128)S(1)}, f32[40,1280]{1,0:T(8,128)S(1)}, u32[]{:S(2)}, u32[]{:S(2)}) %collective-permute-start.1) | collective-permute-done | bytes 204832 | tf_op jit(solution)/shard_map/ppermute | solution.py:2003
  592.7 1.2 copy.57
  593.9 1.7 copy.58
  598.3 0.9 copy.63
  599.2 0.9 copy.64
  600.1 0.9 copy.65
  (68 shorter events, 13.6 us)
Async XLA Ops:
  0.6 17.3 %collective-permute-start = (bf16[40,1280]{1,0:T(8,128)(2,1)}, bf16[40,1280]{1,0:T(8,128)(2,1)S(1)}, u32[]{:S(2)}, u32[]{:S(2)}) collective-permute-start(bf16[40,1280]{1,0:T(8,128)(2,1)} %param.24), channel_id=1, source_target_pairs={{0,0},{1,4},{2,8},{3,12},{4,16},{5,20},{6,24},{7,28},{8,1},{9,5},{... | collective-permute-start | bytes 307208 | tf_op jit(solution)/shard_map/ppermute | solution.py:1964
  17.9 109.3 %copy-start.8 = (s32[640]{0:T(1024)S(1)}, s32[640]{0:T(1024)}, u32[]{:S(2)}) copy-start(s32[640]{0:T(1024)} %param.20) | copy-start | bytes 7684
  17.9 110.2 %copy-start.11 = (f32[2]{0:T(128)S(1)}, f32[2]{0:T(128)}, u32[]{:S(2)}) copy-start(f32[2]{0:T(128)} %constant.74) | copy-start | bytes 28
  18.0 0.6 copy-start.12
  407.4 110.4 %copy-start.10 = (f32[1,1280]{1,0:T(1,128)S(1)}, f32[1,1280]{1,0:T(1,128)}, u32[]{:S(2)}) copy-start(f32[1,1280]{1,0:T(1,128)} %get-tuple-element.78) | copy-start | bytes 15364
  407.4 110.5 %copy-start.9 = (f32[2,1280]{1,0:T(2,128)S(1)}, f32[2,1280]{1,0:T(2,128)}, u32[]{:S(2)}) copy-start(f32[2,1280]{1,0:T(2,128)} %get-tuple-element.79) | copy-start | bytes 30724
  407.4 112.1 %copy-start = (s32[8,128]{1,0:T(8,128)S(1)}, s32[8,128]{1,0:T(8,128)}, u32[]{:S(2)}) copy-start(s32[8,128]{1,0:T(8,128)} %tree_order.1.order) | copy-start | bytes 12292
  519.6 1.7 copy-start.1
  521.3 1.1 copy-start.2
  522.5 70.3 %copy-start.4 = (bf16[640,1280]{1,0:T(8,128)(2,1)S(1)}, bf16[640,1280]{1,0:T(8,128)(2,1)}, u32[]{:S(2)}) copy-start(bf16[640,1280]{1,0:T(8,128)(2,1)} %get-tuple-element.126) | copy-start | bytes 4915204
  577.8 14.9 %collective-permute-start.1 = (f32[40,1280]{1,0:T(8,128)S(1)}, f32[40,1280]{1,0:T(8,128)S(1)}, u32[]{:S(2)}, u32[]{:S(2)}) collective-permute-start(f32[40,1280]{1,0:T(8,128)S(1)} %get-tuple-element.87), channel_id=1, source_target_pairs={{0,0},{4,1},{8,2},{12,3},{16,4},{20,5},{24,6},{28,7},{1,8},{5,9},{... | collective-permute-start | bytes 614408 | tf_op jit(solution)/shard_map/ppermute | solution.py:2003
  581.6 12.3 %copy-start.3 = (f32[640,1280]{1,0:T(8,128)S(1)}, f32[640,1280]{1,0:T(8,128)}, u32[]{:S(2)}) copy-start(f32[640,1280]{1,0:T(8,128)} %get-tuple-element.128) | copy-start | bytes 9830404
  593.9 4.4 copy-start.7
  593.9 5.3 copy-start.6
  595.6 4.5 copy-start.5

commit v7 on v6

--- a/solution.py
+++ b/solution.py
@@ -688,7 +688,7 @@
     )
 
 
-EARLY_HOPS = 4
+EARLY_HOPS = 5
 
 
 def hidden_ring(ref, sends, recvs, step, base=0):
@@ -785,10 +785,17 @@
             pl.when(step < 6)(later.start)
         return carry
 
-    def ug_hop(step):
-        for copy, later in zip(hidden_ring(w_ug, ug_s, ug_r, step), hidden_ring(w_ug, ug_s, ug_r, step + 1)):
-            copy.wait()
-            pl.when(step < EARLY_HOPS - 1)(later.start)
+    def ug_poll(index):
+        step = index // 2
+        now, late = hidden_ring(w_ug, ug_s, ug_r, step), hidden_ring(w_ug, ug_s, ug_r, step + 1)
+
+        def pass_on(first):
+            for copy, later in zip(now[first : first + 2], late[first : first + 2]):
+                copy.wait()
+                pl.when(step < EARLY_HOPS - 1)(later.start)
+
+        pl.when(index % 2 == 0)(functools.partial(pass_on, 0))
+        pl.when(index % 2 == 1)(functools.partial(pass_on, 2))
 
     for copy in ring_copies(0):
         copy.start()
@@ -866,7 +873,7 @@
             for which in range(3)
         ]
 
-    def attend(head, carry):
+    def open_head(head):
         slot = head % 2
 
         @pl.when(head >= 2)
@@ -898,29 +905,27 @@
 
         lax.fori_loop(0, NB, prepare, 0, unroll=NB)
 
-        def visit(start, parts):
-            span = lanes_at(start, 256)
-            query = qs[:, span]
-            acc = jnp.zeros((vs.shape[0], 256), F32)
-            for kstart, count, kind in parts:
-                keys = lanes_at(kstart, count)
-                powers = masked(kind, jnp.exp(nn(ks[keys, :], query))).astype(BF)
-                acc = acc + nn(vs[:, keys], powers)
-            total = 1.0 / acc[HEAD_DIM : HEAD_DIM + 1, :]
-            mixed[rows_at(head * HEAD_DIM, HEAD_DIM), span] = (acc[0:HEAD_DIM, :] * total).astype(BF)
-            sums[head, :, span] = jnp.broadcast_to(total, (8, 256))
-
-        early_chunks(visit)
-        late_chunks(visit)
-
-        @pl.when(head % 2 == 1)
-        def _():
-            ug_hop(head // 2)
-
-        return carry
-
-    lax.fori_loop(0, heads, attend, 0)
-    ug_hop(heads // 2)
+    def visit(head, start, parts):
+        span = lanes_at(start, 256)
+        query = qs[:, span]
+        acc = jnp.zeros((vs.shape[0], 256), F32)
+        for kstart, count, kind in parts:
+            keys = lanes_at(kstart, count)
+            powers = masked(kind, jnp.exp(nn(ks[keys, :], query))).astype(BF)
+            acc = acc + nn(vs[:, keys], powers)
+        total = 1.0 / acc[HEAD_DIM : HEAD_DIM + 1, :]
+        mixed[rows_at(head * HEAD_DIM, HEAD_DIM), span] = (acc[0:HEAD_DIM, :] * total).astype(BF)
+        sums[head, :, span] = jnp.broadcast_to(total, (8, 256))
+
+    def work(i, carry):
+        head, segment = i // 3, i % 3
+        pl.when(segment == 0)(functools.partial(open_head, head))
+        pl.when(segment == 1)(lambda: early_chunks(functools.partial(visit, head)))
+        pl.when(segment == 2)(lambda: late_chunks(functools.partial(visit, head)))
+        pl.when(i % 2 == 1)(lambda: ug_poll(i // 2))
+        return carry
+
+    lax.fori_loop(0, 3 * heads, work, 0)
 
     def split(i, carry):
         blocks[i] = mixed[:, lanes_at(i * BLOCK, BLOCK)]
@@ -934,8 +939,7 @@
     lax.fori_loop(0, NB, arrange_back, 0)
     keep_mixed = pltpu.make_async_copy(natural, mixed_n, local_sem.at[3])
     keep_mixed.start()
-    ug_hop(heads // 2 + 1)
-    lax.fori_loop(heads // 2 + 2, EARLY_HOPS, lambda step, c: (ug_hop(step), c)[1], 0)
+    lax.fori_loop(3 * heads // 2, 2 * EARLY_HOPS, lambda index, c: (ug_poll(index), c)[1], 0)
     keep.wait()
     keep_mixed.wait()
     for copy in w_copies:
@@ -1009,14 +1013,14 @@
 def last_kernel(order, base, tokens_t, g_qkv, w_t, part_out, vectors,
                 g_states, g_query, g_key, g_value, out_rows, vec_own,
                 gq_b, blocks, tok_r, tok_l, share, turned, core_buf, x_buf, base_b, gs_b,
-                ring_r, ring_l, ring_o, ring_v, next_r, next_l, row_buf, row_in, vec_part, vec_in,
+                ring_r, ring_m, ring_l, ring_o, ring_v, next_r, next_l, row_buf, row_in, vec_part, vec_in,
                 in_sem, row_sem, base_sem, core_send, core_recv, x_send, x_recv,
                 ring_send, ring_recv, a2a_send, a2a_recv):
     me, dp = lax.axis_index("fsdp"), lax.axis_index("dp")
     place = ring_place()
     sibling, across, corner = group_peers()
     right, left = {"dp": ring_dp(place + 1)}, {"dp": ring_dp(place - 1)}
-    chunk, side = ring_r.shape[1], ring_r.shape[2]
+    chunk, side, cut = ring_r.shape[1], next_r.shape[1], ring_r.shape[2]
     rows = share.shape[1]
     quarter = rows // 4
     width = w_t.shape[1]
@@ -1060,7 +1064,9 @@
     def hop_copies(step):
         return [
             send(ring.at[step], ring.at[step + 1], ring_send.at[i, step], ring_recv.at[i, step], peer)
-            for i, (ring, peer) in enumerate(((ring_r, right), (ring_l, left), (ring_o, left), (ring_v, right)))
+            for i, (ring, peer) in enumerate(
+                ((ring_r, right), (ring_l, left), (ring_m, right), (ring_o, left), (ring_v, right))
+            )
         ]
 
     def through(r, slot):
@@ -1093,7 +1099,8 @@
 
         @pl.when(step == 0)
         def _():
-            ring_r[0] = next_r[...].astype(BF)
+            ring_r[0] = next_r[:, :cut].astype(BF)
+            ring_m[0] = next_r[:, cut:].astype(BF)
             ring_l[0] = next_l[...].astype(BF)
             ring_o[0] = part_out[ring_dp(place + 1)]
             ring_v[0] = vectors[ring_dp(place - 1)]
@@ -1102,17 +1109,20 @@
         def _():
             before, now = hop_copies(step - 1), hop_copies(step)
             before[0].wait()
-            ring_r[step] = (ring_r[step].astype(F32) + next_r[...]).astype(BF)
+            ring_r[step] = (ring_r[step].astype(F32) + next_r[:, :cut]).astype(BF)
             now[0].start()
             before[1].wait()
             ring_l[step] = (ring_l[step].astype(F32) + next_l[...]).astype(BF)
             now[1].start()
             before[2].wait()
-            ring_o[step] = (ring_o[step].astype(F32) + part_out[ring_dp(place + 1 + step)].astype(F32)).astype(BF)
+            ring_m[step] = (ring_m[step].astype(F32) + next_r[:, cut:]).astype(BF)
             now[2].start()
             before[3].wait()
+            ring_o[step] = (ring_o[step].astype(F32) + part_out[ring_dp(place + 1 + step)].astype(F32)).astype(BF)
+            now[3].start()
+            before[4].wait()
             ring_v[step] = ring_v[step] + vectors[ring_dp(place - 1 - step)]
-            now[3].start()
+            now[4].start()
 
         @pl.when(step == 0)
         def _():
@@ -1151,7 +1161,8 @@
     parts(7)
     for copy in hop_copies(6):
         copy.wait()
-    total = jnp.concatenate((ring_r[7].astype(F32) + next_r[...], ring_l[7].astype(F32) + next_l[...]), axis=1)
+    total = jnp.concatenate((ring_r[7], ring_m[7], ring_l[7]), axis=1).astype(F32)
+    total = total + jnp.concatenate((next_r[...], next_l[...]), axis=1)
     for i in range(4):
         row_buf[i] = total[i * rows_w : (i + 1) * rows_w].astype(BF)
     vec_part[...] = ring_v[7] + vectors[dp]
@@ -1219,7 +1230,8 @@
             pltpu.VMEM((rows, width), BF),
             pltpu.VMEM((2, rows // 4, width), F32),
             pltpu.VMEM((2, rows // 4, width), F32),
-            pltpu.VMEM((8, chunk, side), BF),
+            pltpu.VMEM((8, chunk, 384), BF),
+            pltpu.VMEM((8, chunk, side - 384), BF),
             pltpu.VMEM((8, chunk, heads_width - side), BF),
             pltpu.VMEM((8, rows_w, width), BF),
             pltpu.VMEM(vectors.shape, F32),
@@ -1236,8 +1248,8 @@
             dma((2,)),
             dma((4,)),
             dma((4,)),
-            dma((4, 7)),
-            dma((4, 7)),
+            dma((5, 7)),
+            dma((5, 7)),
             dma((6,)),
             dma((6,)),
         ],
@@ -1264,7 +1276,7 @@
 
 def middle_kernel(mixed_n, states, teacher, weight, mask, w_in, w_own, w_o, rates, scales,
                   w_ug_out, w_d_out, hidden_out, back_out, out_states, attn_unit, attn_inv, hidden_inv, sums, gd_all,
-                  ht_all, act_all, ug_all, w_ug, w_d, hidden, back, mx, part, core, x_buf, tok, gd, act, act_t, ug, ht,
+                  ht_all, act_all, ug_all, w_ug, w_d, hidden, back, target, mx, part, core, x_buf, tok, gd, act, act_t, ug, ht,
                   mx_send, mx_recv, mx_own, keep_sem, core_send, core_recv, x_send, x_recv, tok_send, tok_recv, gd_send, gd_recv, gd_own,
                   out_sem, ring_send, ring_recv, ug_s, ug_r, ug_sem):
     sibling, across, corner = group_peers()
@@ -1284,6 +1296,9 @@
             for r, peer in enumerate((sibling, across, corner))
         ]
 
+    def load_teacher(i):
+        return pltpu.make_async_copy(teacher.at[rows(i)], target.at[i % 2], keep_sem.at[2, 2 + i % 2])
+
     def mx_local(i):
         return pltpu.make_async_copy(mixed_n.at[i], mx.at[i, 0], mx_own.at[i])
 
@@ -1358,6 +1373,8 @@
         return total
 
     sums[...] = jnp.zeros_like(sums)
+    load_teacher(0).start()
+    load_teacher(1).start()
     w_d[rows_at(dp * piece, piece)] = w_own[...]
     chunk = w_ug.shape[0] // 8
 
@@ -1435,16 +1452,21 @@
             gate_proj = nn(here, w_ug[:, tile(n, width)])
             gated = gate_proj * scales[1:2, tile(n)]
             value = up_proj * scales[0:1, tile(n)] * (gated * jax.nn.sigmoid(gated))
-            act[:, tile(n)] = value.astype(BF)
+            act[slot, :, tile(n)] = value.astype(BF)
             act_t[slot, tile(n)] = value.astype(BF).T
             ug[slot, :, tile(n)] = up_proj.astype(BF)
             ug[slot, :, tile(n, width)] = gate_proj.astype(BF)
             return carry
 
         lax.fori_loop(0, width // TILE, up, 0)
+        for copy in outs(i)[1:]:
+            copy.start()
+
+    def feed_down(i):
+        slot = i % 2
 
         def down(n, carry):
-            value = nn(act[...], w_d[:, tile(n)])
+            value = nn(act[slot], w_d[:, tile(n)])
             part[i % 3, :, :, tile(n)] = value.astype(BF).reshape(4, CHUNK, TILE)
             ht[slot, tile(n)] = tok[i, :, :, tile(n)].reshape(4 * CHUNK, TILE).T
             return carry
@@ -1452,8 +1474,7 @@
         lax.fori_loop(0, width // TILE, down, 0)
         core_a(0, i).start()
         core_b(0, i).start()
-        for copy in outs(i):
-            copy.start()
+        outs(i)[0].start()
         forward_far(0, i)
 
     def finish(i):
@@ -1461,7 +1482,13 @@
         own = hidden[rows(i)]
         result, result_inv = unit_rows(own + rate_mlp * (unit - own))
         out_states[rows(i)] = result.astype(BF)
-        diff = result - teacher[rows(i)]
+        load_teacher(i).wait()
+        diff = result - target[i % 2]
+
+        @pl.when(i + 2 < count)
+        def _():
+            load_teacher(i + 2).start()
+
         sums[1:2] = sums[1:2] + jnp.sum(mask[rows(i)] * (diff * diff), axis=0, keepdims=True)
         g_last = unit_back(weight[rows(i)] * diff, result, result_inv)
         sums[0:1] = sums[0:1] + jnp.sum(g_last * (unit - own), axis=0, keepdims=True)
@@ -1479,26 +1506,25 @@
         copies[1].wait_recv()
         copies[2].start()
 
-    stages = ((0, norm_hidden), (1, pass_tokens), (LAG, feed), (LAG + 1, finish), (LAG + 2, pass_grads))
+    stages = (norm_hidden, pass_tokens, feed, feed_down, finish, pass_grads)
 
     def step(t, carry):
-        for lag, stage in stages:
-            if lag == LAG:
+        for lag, stage in enumerate(stages):
+            if lag == 2:
                 pl.when(t < 7 - EARLY_HOPS)(lambda: ug_hop(EARLY_HOPS + t))
-                pl.when(t < 3)(lambda: hop(2 * t + 1))
-                pl.when(t == 2)(lambda: hop(6))
-
-                @pl.when(t == 2)
+            if lag == 3:
+                pl.when(t < 4)(lambda: hop(jnp.maximum(2 * t - 1, 0)))
+                pl.when((t >= 1) & (t < 4))(lambda: hop(2 * t))
+
+                @pl.when(t == 3)
                 def _():
                     for copy in keep_w:
                         copy.start()
 
             pl.when((t >= lag) & (t < lag + count))(functools.partial(stage, t - lag))
-            if lag == 0:
-                pl.when(t < 3)(lambda: hop(2 * t))
-        return carry
-
-    lax.fori_loop(0, count + LAG + 2, step, 0)
+        return carry
+
+    lax.fori_loop(0, count + len(stages) - 1, step, 0)
 
     def close(i, carry):
         copies = gd_copies(i)
@@ -1525,7 +1551,7 @@
     dma = pltpu.SemaphoreType.DMA
     return pl.pallas_call(
         middle_kernel,
-        in_specs=[hbm] + [vmem] * 4 + [hbm] + [vmem] * 4,
+        in_specs=[hbm, vmem, hbm, vmem, vmem, hbm] + [vmem] * 4,
         out_specs=[hbm] * 4 + [vmem] * 5 + [hbm] * 4,
         out_shape=[
             jax.ShapeDtypeStruct(w_ug.shape, BF),
@@ -1547,13 +1573,14 @@
             pltpu.VMEM((8 * w_own.shape[0], width), BF),
             pltpu.VMEM((rows, width), F32),
             pltpu.VMEM((rows, width), F32),
+            pltpu.VMEM((2, CHUNK, width), F32),
             pltpu.VMEM((count, 4) + mixed_n.shape[1:], BF),
             pltpu.VMEM((3, 4, CHUNK, width), BF),
             pltpu.VMEM((2, count, CHUNK, width), BF),
             pltpu.VMEM((count, CHUNK, width), BF),
             pltpu.VMEM((count, 4, CHUNK, width), BF),
             pltpu.VMEM((count, CHUNK, width), BF),
-            pltpu.VMEM((4 * CHUNK, width), BF),
+            pltpu.VMEM((2, 4 * CHUNK, width), BF),
             pltpu.VMEM((2, width, 4 * CHUNK), BF),
             pltpu.VMEM((2, 4 * CHUNK, 2 * width), BF),
             pltpu.VMEM((2, width, 4 * CHUNK), BF),

time: 603 us -> 596 us (0.988)
    pallas_call x1, Pallas kernels: 159 us -> 150 us  [middle(): pl.pallas_call(middle_kernel, in_specs=[hbm, vmem, hbm, vmem, vmem, hbm]...]
where the time goes in v7:
time: 596 us; the launch traced here: 595 us
  Pallas kernels  542 us (91%)
  local copies, waits for them, and re-layouts  22.7 us (4%)
  waiting for transfers between devices  10.6 us (2%)
  starting transfers between devices  6.85 us (1%)
  other arithmetic  6.66 us (1%)
  between operations  6.61 us (1%)
    pallas_call x1, Pallas kernels, middle(): pl.pallas_call(middle_kernel, in_specs=[hbm, vmem, hbm, vmem, vmem, hbm]...  150 us
    pallas_call x1, Pallas kernels, middle_back(): pl.pallas_call(middle_back_kernel, in_specs=[hbm] * 7 + [vmem] * 2 + [hbm...  117 us
    pallas_call x1, Pallas kernels, attention_back(): pl.pallas_call(attention_back_kernel, in_specs=[smem, hbm, vmem, vmem, vm...  109 us
    pallas_call x1, Pallas kernels, forward(): pl.pallas_call(forward_kernel, in_specs=[smem, hbm] + [vmem] * 8, out_spe...  108 us
    pallas_call x1, Pallas kernels, last_exchange(): pl.pallas_call(last_kernel, in_specs=[pl.BlockSpec(memory_space=pltpu.SME...  54.7 us
  transfers between devices with their start and end apart: 2, of which 1 were waited for; matrix products, arithmetic and copies ran while one was open for 1% of the time, Pallas kernels for 0%

profile of v7, /device:TPU:4, one launch (start us, length us, event | category | flops | bytes accessed | tf_op | source)
XLA Modules:
  0.0 595.1 jit_solution(15605336436643891212)
XLA Ops:
  0.6 4.4 collective-permute-start
  5.1 1.4 fusion.2
  9.1 0.7 stack.38
  13.4 0.9 broadcast_in_dim.110.mask
  15.7 2.2 tree_order.1.order
  18.6 108.3 %forward.1 = (bf16[1280,2560]{1,0:T(8,128)(2,1)}, bf16[1024,1280]{1,0:T(8,128)(2,1)}, bf16[4,320,1280]{2,1,0:T(8,128)(2,1)}, bf16[1280,2560]{1,0:T(8,128)(2,1)},...) custom-call(s32[8,128]{1,0:T(8,128)} %tree_order.1.order, ...), custom_call_target="tpu_custom_call" | custom-call | flops 12000000000 | bytes 209715200 | tf_op jit(solution)/shard_map/forward/pallas_call | solution.py:961
  126.9 0.7 slice_convert_fusion
  129.6 0.9 mul.48.weight
  131.1 149.8 %middle.1 = (bf16[1280,2560]{1,0:T(8,128)(2,1)}, bf16[1280,1280]{1,0:T(8,128)(2,1)}, f32[640,1280]{1,0:T(8,128)}, f32[640,1280]{1,0:T(8,128)}, bf16[640,1280]{1,...) custom-call(bf16[20,320,128]{2,1,0:T(8,128)(2,1)} %get-tuple-element, ...), custom_call_target="tpu_custom_call" | custom-call | flops 25999998976 | bytes 419430400 | tf_op jit(solution)/shard_map/middle/pallas_call | solution.py:1552
  281.0 117.5 %middle_back.1 = (f32[640,1280]{1,0:T(8,128)}, bf16[4,640,1280]{2,1,0:T(8,128)(2,1)}, bf16[5,512,2560]{2,1,0:T(8,128)(2,1)}, f32[160,1280]{1,0:T(8,128)}, f32[1,1280]{1,0:T(1,128)}, /*index=5*/f32[2,1280]{1,0:T(2,128)}) custom-call(bf16[5,4,128,1280]{3,2,1,0:T(8,128)(2,1)} %get-tuple-element.58.gd_all, bf16[5,1280,512]{2,1,0:T(8,128)(2,1)} %get-tuple-element.59.act_all, ...), custom_call_target="tpu_custom_call" | custom-call | flops 33999998976 | bytes 209715200 | tf_op jit(solution)/shard_map/middle_back/pallas_call | solution.py:1852
  398.5 0.8 multiply_reduce_fusion
  399.6 0.9 reshape.107.scales
  400.5 109.2 %attention_back.1 = (bf16[3,320,2560]{2,1,0:T(8,128)(2,1)}, f32[5,64,1]{2,1,0:T(8,128)}, bf16[320,1280]{1,0:T(8,128)(2,1)}, f32[40,5120]{1,0:T(8,128)}, f32[40,5120]{1,0:T(8,128)}) custom-call(s32[8,128]{1,0:T(8,128)} %tree_order.1.order, f32[3,320,2560]{2,1,0:T(8,128)} %get-tuple-element.70.qkv, f32[5,64,1]{2,1,0:T(8,128)} %reshape.107.scales, ...), custom_call_target="tpu_custom_call" | custom-call | flops 40000000000 | bytes 62914560 | tf_op jit(solution)/shard_map/attention_back/pallas_call | solution.py:601
  509.7 1.0 reduce.6
  512.6 1.7 copy-done.1
  514.3 1.1 copy-done.2
  515.5 54.7 %last_exchange.1 = (f32[640,1280]{1,0:T(8,128)}, f32[40,1280]{1,0:T(8,128)S(1)}, f32[40,1280]{1,0:T(8,128)S(1)}, f32[40,1280]{1,0:T(8,128)S(1)}, f32[40,1280]{1,0:T(8,128)S(1)}, /*index=5*/f32[4,128]{1,0:T(4,128)S(1)}) custom-call(s32[8,128]{1,0:T(8,128)S(1)} %copy-done, f32[640,1280]{1,0:T(8,128)} %get-tuple-element.68.base, ...), custom_call_target="tpu_custom_call" | custom-call | flops 12999999488 | bytes 104857600 | tf_op jit(solution)/shard_map/last_exchange/pallas_call | solution.py:1215
  571.3 2.4 collective-permute-start.1
  575.0 10.6 %collective-permute-done.1 = f32[40,1280]{1,0:T(8,128)S(1)} collective-permute-done((f32[40,1280]{1,0:T(8,128)S(1)}, f32[40,1280]{1,0:T(8,128)S(1)}, u32[]{:S(2)}, u32[]{:S(2)}) %collective-permute-start.1) | collective-permute-done | bytes 204832 | tf_op jit(solution)/shard_map/ppermute | solution.py:2030
  585.6 1.2 copy.57
  586.8 1.7 copy.58
  591.3 0.9 copy.63
  592.1 0.9 copy.64
  593.0 0.9 copy.65
  (68 shorter events, 13.6 us)
Async XLA Ops:
  0.6 17.3 %collective-permute-start = (bf16[40,1280]{1,0:T(8,128)(2,1)}, bf16[40,1280]{1,0:T(8,128)(2,1)S(1)}, u32[]{:S(2)}, u32[]{:S(2)}) collective-permute-start(bf16[40,1280]{1,0:T(8,128)(2,1)} %param.24), channel_id=1, source_target_pairs={{0,0},{1,4},{2,8},{3,12},{4,16},{5,20},{6,24},{7,28},{8,1},{9,5},{... | collective-permute-start | bytes 307208 | tf_op jit(solution)/shard_map/ppermute | solution.py:1991
  17.9 111.6 %copy-start.8 = (s32[640]{0:T(1024)S(1)}, s32[640]{0:T(1024)}, u32[]{:S(2)}) copy-start(s32[640]{0:T(1024)} %param.20) | copy-start | bytes 7684
  17.9 112.5 %copy-start.11 = (f32[2]{0:T(128)S(1)}, f32[2]{0:T(128)}, u32[]{:S(2)}) copy-start(f32[2]{0:T(128)} %constant.74) | copy-start | bytes 28
  18.0 0.6 copy-start.12
  400.5 110.3 %copy-start.10 = (f32[1,1280]{1,0:T(1,128)S(1)}, f32[1,1280]{1,0:T(1,128)}, u32[]{:S(2)}) copy-start(f32[1,1280]{1,0:T(1,128)} %get-tuple-element.78) | copy-start | bytes 15364
  400.5 110.4 %copy-start.9 = (f32[2,1280]{1,0:T(2,128)S(1)}, f32[2,1280]{1,0:T(2,128)}, u32[]{:S(2)}) copy-start(f32[2,1280]{1,0:T(2,128)} %get-tuple-element.79) | copy-start | bytes 30724
  400.5 112.1 %copy-start = (s32[8,128]{1,0:T(8,128)S(1)}, s32[8,128]{1,0:T(8,128)}, u32[]{:S(2)}) copy-start(s32[8,128]{1,0:T(8,128)} %tree_order.1.order) | copy-start | bytes 12292
  512.6 1.7 copy-start.1
  514.3 1.1 copy-start.2
  515.4 70.2 %copy-start.4 = (bf16[640,1280]{1,0:T(8,128)(2,1)S(1)}, bf16[640,1280]{1,0:T(8,128)(2,1)}, u32[]{:S(2)}) copy-start(bf16[640,1280]{1,0:T(8,128)(2,1)} %get-tuple-element.126) | copy-start | bytes 4915204
  571.3 14.3 %collective-permute-start.1 = (f32[40,1280]{1,0:T(8,128)S(1)}, f32[40,1280]{1,0:T(8,128)S(1)}, u32[]{:S(2)}, u32[]{:S(2)}) collective-permute-start(f32[40,1280]{1,0:T(8,128)S(1)} %get-tuple-element.87), channel_id=1, source_target_pairs={{0,0},{4,1},{8,2},{12,3},{16,4},{20,5},{24,6},{28,7},{1,8},{5,9},{... | collective-permute-start | bytes 614408 | tf_op jit(solution)/shard_map/ppermute | solution.py:2030
  574.4 12.4 %copy-start.3 = (f32[640,1280]{1,0:T(8,128)S(1)}, f32[640,1280]{1,0:T(8,128)}, u32[]{:S(2)}) copy-start(f32[640,1280]{1,0:T(8,128)} %get-tuple-element.128) | copy-start | bytes 9830404
  586.8 4.4 copy-start.7
  586.8 5.3 copy-start.6
  588.5 4.5 copy-start.5

commit v8 on v7

--- a/solution.py
+++ b/solution.py
@@ -1814,11 +1814,11 @@
     def step(t, carry):
         for lag, stage in enumerate(stages):
             pl.when((t >= lag) & (t < lag + count))(functools.partial(stage, t - lag))
-        pl.when(t == 0)(down_grads)
-
-        @pl.when((t >= 1) & (t < 4))
+        pl.when(t == 2)(down_grads)
+
+        @pl.when((t >= 3) & (t < 6))
         def _():
-            lax.fori_loop(2 * t - 2, 2 * t, hop, 0)
+            lax.fori_loop(2 * t - 6, 2 * t - 4, hop, 0)
 
         return carry
 

time: 596 us -> 589 us (0.988)
  Pallas kernels: 542 us -> 534 us
    pallas_call x1, Pallas kernels: 117 us -> 110 us  [middle_back(): pl.pallas_call(middle_back_kernel, in_specs=[hbm] * 7 + [vmem] * 2 + [hbm...]
where the time goes in v8:
time: 589 us; the launch traced here: 588 us
  Pallas kernels  534 us (91%)
  local copies, waits for them, and re-layouts  22.7 us (4%)
  waiting for transfers between devices  10.6 us (2%)
  starting transfers between devices  7.21 us (1%)
  other arithmetic  6.66 us (1%)
  between operations  6.61 us (1%)
    pallas_call x1, Pallas kernels, middle(): pl.pallas_call(middle_kernel, in_specs=[hbm, vmem, hbm, vmem, vmem, hbm]...  150 us
    pallas_call x1, Pallas kernels, middle_back(): pl.pallas_call(middle_back_kernel, in_specs=[hbm] * 7 + [vmem] * 2 + [hbm...  110 us
    pallas_call x1, Pallas kernels, attention_back(): pl.pallas_call(attention_back_kernel, in_specs=[smem, hbm, vmem, vmem, vm...  110 us
    pallas_call x1, Pallas kernels, forward(): pl.pallas_call(forward_kernel, in_specs=[smem, hbm] + [vmem] * 8, out_spe...  108 us
    pallas_call x1, Pallas kernels, last_exchange(): pl.pallas_call(last_kernel, in_specs=[pl.BlockSpec(memory_space=pltpu.SME...  53.4 us
    unnamed x35, local copies, waits for them, and re-layouts  11.8 us
  transfers between devices with their start and end apart: 2, of which 1 were waited for; matrix products, arithmetic and copies ran while one was open for 1% of the time, Pallas kernels for 0%

profile of v8, /device:TPU:4, one launch (start us, length us, event | category | flops | bytes accessed | tf_op | source)
XLA Modules:
  0.0 588.1 jit_solution(14964986827105795214)
XLA Ops:
  0.6 4.4 collective-permute-start
  5.1 1.4 fusion.2
  9.1 0.7 stack.38
  13.4 0.9 broadcast_in_dim.110.mask
  15.7 2.2 tree_order.1.order
  18.6 108.3 %forward.1 = (bf16[1280,2560]{1,0:T(8,128)(2,1)}, bf16[1024,1280]{1,0:T(8,128)(2,1)}, bf16[4,320,1280]{2,1,0:T(8,128)(2,1)}, bf16[1280,2560]{1,0:T(8,128)(2,1)},...) custom-call(s32[8,128]{1,0:T(8,128)} %tree_order.1.order, ...), custom_call_target="tpu_custom_call" | custom-call | flops 12000000000 | bytes 209715200 | tf_op jit(solution)/shard_map/forward/pallas_call | solution.py:961
  126.9 0.7 slice_convert_fusion
  129.6 0.9 mul.48.weight
  131.1 149.8 %middle.1 = (bf16[1280,2560]{1,0:T(8,128)(2,1)}, bf16[1280,1280]{1,0:T(8,128)(2,1)}, f32[640,1280]{1,0:T(8,128)}, f32[640,1280]{1,0:T(8,128)}, bf16[640,1280]{1,...) custom-call(bf16[20,320,128]{2,1,0:T(8,128)(2,1)} %get-tuple-element, ...), custom_call_target="tpu_custom_call" | custom-call | flops 25999998976 | bytes 419430400 | tf_op jit(solution)/shard_map/middle/pallas_call | solution.py:1552
  281.0 110.4 %middle_back.1 = (f32[640,1280]{1,0:T(8,128)}, bf16[4,640,1280]{2,1,0:T(8,128)(2,1)}, bf16[5,512,2560]{2,1,0:T(8,128)(2,1)}, f32[160,1280]{1,0:T(8,128)}, f32[1,1280]{1,0:T(1,128)}, /*index=5*/f32[2,1280]{1,0:T(2,128)}) custom-call(bf16[5,4,128,1280]{3,2,1,0:T(8,128)(2,1)} %get-tuple-element.58.gd_all, bf16[5,1280,512]{2,1,0:T(8,128)(2,1)} %get-tuple-element.59.act_all, ...), custom_call_target="tpu_custom_call" | custom-call | flops 33999998976 | bytes 209715200 | tf_op jit(solution)/shard_map/middle_back/pallas_call | solution.py:1852
  391.4 0.8 multiply_reduce_fusion
  392.5 0.9 reshape.107.scales
  393.4 110.3 %attention_back.1 = (bf16[3,320,2560]{2,1,0:T(8,128)(2,1)}, f32[5,64,1]{2,1,0:T(8,128)}, bf16[320,1280]{1,0:T(8,128)(2,1)}, f32[40,5120]{1,0:T(8,128)}, f32[40,5120]{1,0:T(8,128)}) custom-call(s32[8,128]{1,0:T(8,128)} %tree_order.1.order, f32[3,320,2560]{2,1,0:T(8,128)} %get-tuple-element.70.qkv, f32[5,64,1]{2,1,0:T(8,128)} %reshape.107.scales, ...), custom_call_target="tpu_custom_call" | custom-call | flops 40000000000 | bytes 62914560 | tf_op jit(solution)/shard_map/attention_back/pallas_call | solution.py:601
  503.7 1.0 reduce.6
  506.6 1.7 copy-done.1
  508.4 1.1 copy-done.2
  509.5 53.4 %last_exchange.1 = (f32[640,1280]{1,0:T(8,128)}, f32[40,1280]{1,0:T(8,128)S(1)}, f32[40,1280]{1,0:T(8,128)S(1)}, f32[40,1280]{1,0:T(8,128)S(1)}, f32[40,1280]{1,0:T(8,128)S(1)}, /*index=5*/f32[4,128]{1,0:T(4,128)S(1)}) custom-call(s32[8,128]{1,0:T(8,128)S(1)} %copy-done, f32[640,1280]{1,0:T(8,128)} %get-tuple-element.68.base, ...), custom_call_target="tpu_custom_call" | custom-call | flops 12999999488 | bytes 104857600 | tf_op jit(solution)/shard_map/last_exchange/pallas_call | solution.py:1215
  564.1 2.8 collective-permute-start.1
  568.2 10.5 %collective-permute-done.1 = f32[40,1280]{1,0:T(8,128)S(1)} collective-permute-done((f32[40,1280]{1,0:T(8,128)S(1)}, f32[40,1280]{1,0:T(8,128)S(1)}, u32[]{:S(2)}, u32[]{:S(2)}) %collective-permute-start.1) | collective-permute-done | bytes 204832 | tf_op jit(solution)/shard_map/ppermute | solution.py:2030
  578.7 1.2 copy.57
  579.9 1.7 copy.58
  584.3 0.9 copy.63
  585.2 0.9 copy.64
  586.1 0.9 copy.65
  (68 shorter events, 13.6 us)
Async XLA Ops:
  0.6 17.3 %collective-permute-start = (bf16[40,1280]{1,0:T(8,128)(2,1)}, bf16[40,1280]{1,0:T(8,128)(2,1)S(1)}, u32[]{:S(2)}, u32[]{:S(2)}) collective-permute-start(bf16[40,1280]{1,0:T(8,128)(2,1)} %param.24), channel_id=1, source_target_pairs={{0,0},{1,4},{2,8},{3,12},{4,16},{5,20},{6,24},{7,28},{8,1},{9,5},{... | collective-permute-start | bytes 307208 | tf_op jit(solution)/shard_map/ppermute | solution.py:1991
  17.9 111.6 %copy-start.8 = (s32[640]{0:T(1024)S(1)}, s32[640]{0:T(1024)}, u32[]{:S(2)}) copy-start(s32[640]{0:T(1024)} %param.20) | copy-start | bytes 7684
  17.9 112.5 %copy-start.11 = (f32[2]{0:T(128)S(1)}, f32[2]{0:T(128)}, u32[]{:S(2)}) copy-start(f32[2]{0:T(128)} %constant.74) | copy-start | bytes 28
  18.0 0.6 copy-start.12
  393.4 111.4 %copy-start.10 = (f32[1,1280]{1,0:T(1,128)S(1)}, f32[1,1280]{1,0:T(1,128)}, u32[]{:S(2)}) copy-start(f32[1,1280]{1,0:T(1,128)} %get-tuple-element.78) | copy-start | bytes 15364
  393.4 111.6 %copy-start.9 = (f32[2,1280]{1,0:T(2,128)S(1)}, f32[2,1280]{1,0:T(2,128)}, u32[]{:S(2)}) copy-start(f32[2,1280]{1,0:T(2,128)} %get-tuple-element.79) | copy-start | bytes 30724
  393.4 113.2 %copy-start = (s32[8,128]{1,0:T(8,128)S(1)}, s32[8,128]{1,0:T(8,128)}, u32[]{:S(2)}) copy-start(s32[8,128]{1,0:T(8,128)} %tree_order.1.order) | copy-start | bytes 12292
  506.6 1.7 copy-start.1
  508.4 1.1 copy-start.2
  509.5 69.2 %copy-start.4 = (bf16[640,1280]{1,0:T(8,128)(2,1)S(1)}, bf16[640,1280]{1,0:T(8,128)(2,1)}, u32[]{:S(2)}) copy-start(bf16[640,1280]{1,0:T(8,128)(2,1)} %get-tuple-element.126) | copy-start | bytes 4915204
  564.1 14.6 %collective-permute-start.1 = (f32[40,1280]{1,0:T(8,128)S(1)}, f32[40,1280]{1,0:T(8,128)S(1)}, u32[]{:S(2)}, u32[]{:S(2)}) collective-permute-start(f32[40,1280]{1,0:T(8,128)S(1)} %get-tuple-element.87), channel_id=1, source_target_pairs={{0,0},{4,1},{8,2},{12,3},{16,4},{20,5},{24,6},{28,7},{1,8},{5,9},{... | collective-permute-start | bytes 614408 | tf_op jit(solution)/shard_map/ppermute | solution.py:2030
  567.6 12.3 %copy-start.3 = (f32[640,1280]{1,0:T(8,128)S(1)}, f32[640,1280]{1,0:T(8,128)}, u32[]{:S(2)}) copy-start(f32[640,1280]{1,0:T(8,128)} %get-tuple-element.128) | copy-start | bytes 9830404
  579.9 4.4 copy-start.7
  579.9 5.3 copy-start.6
  581.6 4.5 copy-start.5

commit v9 on v8

--- a/solution.py
+++ b/solution.py
@@ -1012,7 +1012,7 @@
 
 def last_kernel(order, base, tokens_t, g_qkv, w_t, part_out, vectors,
                 g_states, g_query, g_key, g_value, out_rows, vec_own,
-                gq_b, blocks, tok_r, tok_l, share, turned, core_buf, x_buf, base_b, gs_b,
+                w_b, gq_b, blocks, tok_r, tok_l, share, turned, core_buf, x_buf, base_b, gs_b,
                 ring_r, ring_m, ring_l, ring_o, ring_v, next_r, next_l, row_buf, row_in, vec_part, vec_in,
                 in_sem, row_sem, base_sem, core_send, core_recv, x_send, x_recv,
                 ring_send, ring_recv, a2a_send, a2a_recv):
@@ -1044,9 +1044,11 @@
 
     load_q = pltpu.make_async_copy(g_qkv, gq_b, in_sem.at[0])
     load_q.start()
+    load_w = pltpu.make_async_copy(w_t.at[pl.ds(0, g_qkv.shape[0])], w_b, in_sem.at[1])
     for step in (0, 1):
         for copy in slices(step):
             copy.start()
+    load_w.start()
     greet([sibling, across, corner, right, left])
 
     def parts(step):
@@ -1074,7 +1076,7 @@
             turned[i * BLOCK : (i + 1) * BLOCK] = blocks[order[1, r * (rows // BLOCK) + i]].T
 
         def one(n, carry):
-            share[slot, :, tile(n)] = nn(turned[...], w_t[pl.ds(0, heads_width), tile(n)]).astype(BF)
+            share[slot, :, tile(n)] = nn(turned[...], w_b[:, tile(n)]).astype(BF)
             return carry
 
         lax.fori_loop(0, width // TILE, one, 0)
@@ -1134,6 +1136,7 @@
             @pl.when(step == 0)
             def _():
                 lax.fori_loop(0, NB, split, 0)
+                load_w.wait()
                 through(3, 0)
                 core[0].start()
 
@@ -1214,12 +1217,13 @@
     dma = pltpu.SemaphoreType.DMA
     return pl.pallas_call(
         last_kernel,
-        in_specs=[pl.BlockSpec(memory_space=pltpu.SMEM), hbm, hbm, hbm, vmem, vmem, vmem],
+        in_specs=[pl.BlockSpec(memory_space=pltpu.SMEM), hbm, hbm, hbm, hbm, vmem, vmem],
         out_specs=[hbm] + [vmem] * 5,
         out_shape=[jax.ShapeDtypeStruct((rows, width), F32)]
         + [jax.ShapeDtypeStruct((rows_w, width), F32)] * 4
         + [jax.ShapeDtypeStruct(vectors.shape[2:], F32)],
         scratch_shapes=[
+            pltpu.VMEM((heads_width, width), BF),
             pltpu.VMEM(g_qkv.shape, BF),
             pltpu.VMEM((NB, heads_width, BLOCK), BF),
             pltpu.VMEM((2, chunk, tokens_t.shape[1]), BF),
@@ -1241,7 +1245,7 @@
             pltpu.VMEM((4, rows_w, heads_width), BF),
             pltpu.VMEM(vectors.shape[1:], F32),
             pltpu.VMEM(vectors.shape[1:], F32),
-            dma((1,)),
+            dma((2,)),
             dma((2, 2)),
             dma((2, 2)),
             dma((2,)),
@@ -1276,7 +1280,7 @@
 
 def middle_kernel(mixed_n, states, teacher, weight, mask, w_in, w_own, w_o, rates, scales,
                   w_ug_out, w_d_out, hidden_out, back_out, out_states, attn_unit, attn_inv, hidden_inv, sums, gd_all,
-                  ht_all, act_all, ug_all, w_ug, w_d, hidden, back, target, mx, part, core, x_buf, tok, gd, act, act_t, ug, ht,
+                  ht_all, act_all, ug_all, w_ob, w_ug, w_d, hidden, back, target, mx, part, core, x_buf, tok, gd, act, act_t, ug, ht,
                   mx_send, mx_recv, mx_own, keep_sem, core_send, core_recv, x_send, x_recv, tok_send, tok_recv, gd_send, gd_recv, gd_own,
                   out_sem, ring_send, ring_recv, ug_s, ug_r, ug_sem):
     sibling, across, corner = group_peers()
@@ -1373,6 +1377,8 @@
         return total
 
     sums[...] = jnp.zeros_like(sums)
+    load_o = pltpu.make_async_copy(w_o, w_ob, keep_sem.at[2, 4])
+    load_o.start()
     load_teacher(0).start()
     load_teacher(1).start()
     w_d[rows_at(dp * piece, piece)] = w_own[...]
@@ -1406,6 +1412,7 @@
         return carry
 
     lax.fori_loop(0, count, open_mixed, 0)
+    load_o.wait()
     lax.fori_loop(0, EARLY_HOPS + 1, wait_w, 0)
     for copy in hidden_ring(w_ug, ug_s, ug_r, EARLY_HOPS, EARLY_HOPS):
         copy.start()
@@ -1414,9 +1421,9 @@
         mx_local(i).wait()
         for copy in mx_copies(i):
             copy.wait()
-        attn = nn(mx[i, 0].T, w_o[0])
+        attn = nn(mx[i, 0].T, w_ob[0])
         for r in range(1, 4):
-            attn = attn + nn(mx[i, r].T, w_o[r])
+            attn = attn + nn(mx[i, r].T, w_ob[r])
         unit, inverse = unit_rows(attn)
         own = states[rows(i)].astype(F32)
         value, value_inv = unit_rows(own + rate_attn * (unit - own))
@@ -1551,7 +1558,7 @@
     dma = pltpu.SemaphoreType.DMA
     return pl.pallas_call(
         middle_kernel,
-        in_specs=[hbm, vmem, hbm, vmem, vmem, hbm] + [vmem] * 4,
+        in_specs=[hbm, vmem, hbm, vmem, vmem, hbm, vmem, hbm, vmem, vmem],
         out_specs=[hbm] * 4 + [vmem] * 5 + [hbm] * 4,
         out_shape=[
             jax.ShapeDtypeStruct(w_ug.shape, BF),
@@ -1569,6 +1576,7 @@
             jax.ShapeDtypeStruct((count, 4 * CHUNK, 2 * width), BF),
         ],
         scratch_shapes=[
+            pltpu.VMEM(w_o.shape, BF),
             pltpu.VMEM(w_ug.shape, BF),
             pltpu.VMEM((8 * w_own.shape[0], width), BF),
             pltpu.VMEM((rows, width), F32),

time: 589 us -> 588 us (level)
  no operation moved by 1% of the time
where the time goes in v9:
time: 588 us; the launch traced here: 587 us
  Pallas kernels  533 us (91%)
  local copies, waits for them, and re-layouts  22.7 us (4%)
  waiting for transfers between devices  10.6 us (2%)
  starting transfers between devices  7.22 us (1%)
  other arithmetic  6.66 us (1%)
  between operations  6.61 us (1%)
    pallas_call x1, Pallas kernels, middle(): pl.pallas_call(middle_kernel, in_specs=[hbm, vmem, hbm, vmem, vmem, hbm,...  149 us
    pallas_call x1, Pallas kernels, middle_back(): pl.pallas_call(middle_back_kernel, in_specs=[hbm] * 7 + [vmem] * 2 + [hbm...  110 us
    pallas_call x1, Pallas kernels, attention_back(): pl.pallas_call(attention_back_kernel, in_specs=[smem, hbm, vmem, vmem, vm...  110 us
    pallas_call x1, Pallas kernels, forward(): pl.pallas_call(forward_kernel, in_specs=[smem, hbm] + [vmem] * 8, out_spe...  108 us
    pallas_call x1, Pallas kernels, last_exchange(): pl.pallas_call(last_kernel, in_specs=[pl.BlockSpec(memory_space=pltpu.SME...  53.4 us
    unnamed x35, local copies, waits for them, and re-layouts  11.8 us
  transfers between devices with their start and end apart: 2, of which 1 were waited for; matrix products, arithmetic and copies ran while one was open for 1% of the time, Pallas kernels for 0%

profile of v9, /device:TPU:4, one launch (start us, length us, event | category | flops | bytes accessed | tf_op | source)
XLA Modules:
  0.0 587.0 jit_solution(6112271315859812018)
XLA Ops:
  0.6 4.4 collective-permute-start
  5.1 1.4 fusion.2
  9.1 0.7 stack.38
  13.4 0.9 broadcast_in_dim.110.mask
  15.7 2.2 tree_order.1.order
  18.6 108.3 %forward.1 = (bf16[1280,2560]{1,0:T(8,128)(2,1)}, bf16[1024,1280]{1,0:T(8,128)(2,1)}, bf16[4,320,1280]{2,1,0:T(8,128)(2,1)}, bf16[1280,2560]{1,0:T(8,128)(2,1)},...) custom-call(s32[8,128]{1,0:T(8,128)} %tree_order.1.order, ...), custom_call_target="tpu_custom_call" | custom-call | flops 12000000000 | bytes 209715200 | tf_op jit(solution)/shard_map/forward/pallas_call | solution.py:961
  126.9 0.7 slice_convert_fusion
  129.6 0.9 mul.48.weight
  131.1 148.8 %middle.1 = (bf16[1280,2560]{1,0:T(8,128)(2,1)}, bf16[1280,1280]{1,0:T(8,128)(2,1)}, f32[640,1280]{1,0:T(8,128)}, f32[640,1280]{1,0:T(8,128)}, bf16[640,1280]{1,...) custom-call(bf16[20,320,128]{2,1,0:T(8,128)(2,1)} %get-tuple-element, ...), custom_call_target="tpu_custom_call" | custom-call | flops 25999998976 | bytes 419430400 | tf_op jit(solution)/shard_map/middle/pallas_call | solution.py:1559
  279.9 110.3 %middle_back.1 = (f32[640,1280]{1,0:T(8,128)}, bf16[4,640,1280]{2,1,0:T(8,128)(2,1)}, bf16[5,512,2560]{2,1,0:T(8,128)(2,1)}, f32[160,1280]{1,0:T(8,128)}, f32[1,1280]{1,0:T(1,128)}, /*index=5*/f32[2,1280]{1,0:T(2,128)}) custom-call(bf16[5,4,128,1280]{3,2,1,0:T(8,128)(2,1)} %get-tuple-element.58.gd_all, bf16[5,1280,512]{2,1,0:T(8,128)(2,1)} %get-tuple-element.59.act_all, ...), custom_call_target="tpu_custom_call" | custom-call | flops 33999998976 | bytes 209715200 | tf_op jit(solution)/shard_map/middle_back/pallas_call | solution.py:1860
  390.2 0.8 multiply_reduce_fusion
  391.4 0.9 reshape.107.scales
  392.3 110.2 %attention_back.1 = (bf16[3,320,2560]{2,1,0:T(8,128)(2,1)}, f32[5,64,1]{2,1,0:T(8,128)}, bf16[320,1280]{1,0:T(8,128)(2,1)}, f32[40,5120]{1,0:T(8,128)}, f32[40,5120]{1,0:T(8,128)}) custom-call(s32[8,128]{1,0:T(8,128)} %tree_order.1.order, f32[3,320,2560]{2,1,0:T(8,128)} %get-tuple-element.70.qkv, f32[5,64,1]{2,1,0:T(8,128)} %reshape.107.scales, ...), custom_call_target="tpu_custom_call" | custom-call | flops 40000000000 | bytes 62914560 | tf_op jit(solution)/shard_map/attention_back/pallas_call | solution.py:601
  502.5 1.0 reduce.6
  505.4 1.7 copy-done.1
  507.1 1.1 copy-done.2
  508.3 53.4 %last_exchange.1 = (f32[640,1280]{1,0:T(8,128)}, f32[40,1280]{1,0:T(8,128)S(1)}, f32[40,1280]{1,0:T(8,128)S(1)}, f32[40,1280]{1,0:T(8,128)S(1)}, f32[40,1280]{1,0:T(8,128)S(1)}, /*index=5*/f32[4,128]{1,0:T(4,128)S(1)}) custom-call(s32[8,128]{1,0:T(8,128)S(1)} %copy-done, f32[640,1280]{1,0:T(8,128)} %get-tuple-element.68.base, ...), custom_call_target="tpu_custom_call" | custom-call | flops 12999999488 | bytes 104857600 | tf_op jit(solution)/shard_map/last_exchange/pallas_call | solution.py:1218
  562.9 2.8 collective-permute-start.1
  567.0 10.6 %collective-permute-done.1 = f32[40,1280]{1,0:T(8,128)S(1)} collective-permute-done((f32[40,1280]{1,0:T(8,128)S(1)}, f32[40,1280]{1,0:T(8,128)S(1)}, u32[]{:S(2)}, u32[]{:S(2)}) %collective-permute-start.1) | collective-permute-done | bytes 204832 | tf_op jit(solution)/shard_map/ppermute | solution.py:2038
  577.5 1.2 copy.57
  578.7 1.7 copy.58
  583.1 0.9 copy.63
  584.0 0.9 copy.64
  584.9 0.9 copy.65
  (68 shorter events, 13.6 us)
Async XLA Ops:
  0.6 17.3 %collective-permute-start = (bf16[40,1280]{1,0:T(8,128)(2,1)}, bf16[40,1280]{1,0:T(8,128)(2,1)S(1)}, u32[]{:S(2)}, u32[]{:S(2)}) collective-permute-start(bf16[40,1280]{1,0:T(8,128)(2,1)} %param.24), channel_id=1, source_target_pairs={{0,0},{1,4},{2,8},{3,12},{4,16},{5,20},{6,24},{7,28},{8,1},{9,5},{... | collective-permute-start | bytes 307208 | tf_op jit(solution)/shard_map/ppermute | solution.py:1999
  17.9 111.6 %copy-start.8 = (s32[640]{0:T(1024)S(1)}, s32[640]{0:T(1024)}, u32[]{:S(2)}) copy-start(s32[640]{0:T(1024)} %param.20) | copy-start | bytes 7684
  17.9 112.5 %copy-start.11 = (f32[2]{0:T(128)S(1)}, f32[2]{0:T(128)}, u32[]{:S(2)}) copy-start(f32[2]{0:T(128)} %constant.74) | copy-start | bytes 28
  18.0 0.6 copy-start.12
  392.2 111.3 %copy-start.10 = (f32[1,1280]{1,0:T(1,128)S(1)}, f32[1,1280]{1,0:T(1,128)}, u32[]{:S(2)}) copy-start(f32[1,1280]{1,0:T(1,128)} %get-tuple-element.78) | copy-start | bytes 15364
  392.3 111.5 %copy-start.9 = (f32[2,1280]{1,0:T(2,128)S(1)}, f32[2,1280]{1,0:T(2,128)}, u32[]{:S(2)}) copy-start(f32[2,1280]{1,0:T(2,128)} %get-tuple-element.79) | copy-start | bytes 30724
  392.3 113.1 %copy-start = (s32[8,128]{1,0:T(8,128)S(1)}, s32[8,128]{1,0:T(8,128)}, u32[]{:S(2)}) copy-start(s32[8,128]{1,0:T(8,128)} %tree_order.1.order) | copy-start | bytes 12292
  505.4 1.7 copy-start.1
  507.1 1.1 copy-start.2
  508.3 69.3 %copy-start.4 = (bf16[640,1280]{1,0:T(8,128)(2,1)S(1)}, bf16[640,1280]{1,0:T(8,128)(2,1)}, u32[]{:S(2)}) copy-start(bf16[640,1280]{1,0:T(8,128)(2,1)} %get-tuple-element.126) | copy-start | bytes 4915204
  562.9 14.6 %collective-permute-start.1 = (f32[40,1280]{1,0:T(8,128)S(1)}, f32[40,1280]{1,0:T(8,128)S(1)}, u32[]{:S(2)}, u32[]{:S(2)}) collective-permute-start(f32[40,1280]{1,0:T(8,128)S(1)} %get-tuple-element.87), channel_id=1, source_target_pairs={{0,0},{4,1},{8,2},{12,3},{16,4},{20,5},{24,6},{28,7},{1,8},{5,9},{... | collective-permute-start | bytes 614408 | tf_op jit(solution)/shard_map/ppermute | solution.py:2038
  566.4 12.3 %copy-start.3 = (f32[640,1280]{1,0:T(8,128)S(1)}, f32[640,1280]{1,0:T(8,128)}, u32[]{:S(2)}) copy-start(f32[640,1280]{1,0:T(8,128)} %get-tuple-element.128) | copy-start | bytes 9830404
  578.7 4.4 copy-start.7
  578.7 5.3 copy-start.6
  580.4 4.5 copy-start.5
